TPU v7x, 32 devices: a whole 2x2x4 slice. The times are simulated.
32 devices in a mesh: branch: 2 (over x), tok: 16 (over z, y, core).
Axes of the slice: x: 2, y: 2, z: 4, core: 2. Of those that a mesh axis runs over, the one named last changes fastest.
Arguments:
- teacher_hidden: bfloat16 [2, 256, 4096], P('branch', 'tok'), may hold values from -400 to 400
- teacher_gain: float32 [2, 4096], P('branch'), may hold values from 0.5 to 1.5
- teacher_head: bfloat16 [2, 4096, 20480], P('branch', None, 'tok'), may hold values from -30 to 30
- student_hidden: bfloat16 [256, 4096], P('branch'), may hold values from -400 to 400
- student_gain: float32 [4096], replicated, may hold values from 0.5 to 1.5
- student_head: bfloat16 [4096, 20480], P('branch', 'tok'), may hold values from -30 to 30
- cluster_weights: int32 [256, 2], P(None, 'branch'), may hold values from 0 to 64, as said below
- token_ids: int32 [256], P('branch'), may hold values from 0 to 20479
Outputs:
- grad_head: float32 [4096, 20480], P('branch', 'tok')
- grad_hidden: float32 [256, 4096], P('branch', 'tok')
- grad_gain: float32 [4096], P('tok')
Inputs may be any that keep to these rules, and one draw needn't show every extreme that they name: `cluster_weights`: each token's 2 weights sum to 64.
All inputs are finite; a program needn't handle non-finite values.
Results may differ from a plain program's by a relative error of at most 0.0063.
Values may be sent and summed in bfloat16 or wider, within the bound.
No kernel may reach another device: no remote copies, remote signals or barrier semaphores. Data moves between devices by JAX's collectives and lax.ppermute only.
A program may use at most 128 MiB of HBM per device.

v0:
```python
import jax
import jax.numpy as jnp
from jax import lax
from jax.sharding import PartitionSpec as P

DEN = 64


eps = 1e-05
mix_label = 0.25
loss_scale = 64.0


def merged(value, axis, combine):
    everything = jax.tree.map(lambda part: lax.all_gather(part, axis), value)
    leading = jax.tree.map(lambda part: part[0], everything)

    def step(k, so_far):
        return combine(so_far, jax.tree.map(lambda part: part[k], everything))

    return lax.fori_loop(1, lax.axis_size(axis), step, leading)


def normalize(hidden, gain):
    values = hidden.astype(jnp.float32)
    inv_scale = lax.rsqrt(jnp.mean(values * values, axis=-1, keepdims=True) + eps)
    return ((values * inv_scale * gain).astype(jnp.bfloat16), inv_scale)


def combine_stats(first, second):
    top = jnp.maximum(first[0], second[0])
    return (top, first[1] * jnp.exp(first[0] - top) + second[1] * jnp.exp(second[0] - top))


def probabilities(logits):
    local_max = jnp.max(logits, axis=1)
    local_scaled = jnp.exp(logits - local_max[:, None])
    row_max, row_total = merged((local_max, jnp.sum(local_scaled, axis=1)), "tok", combine_stats)
    scaled = local_scaled * jnp.exp(local_max - row_max)[:, None]
    return scaled / row_total[:, None]


def per_device(
    teacher_hidden,
    teacher_gain,
    teacher_head,
    student_hidden,
    student_gain,
    student_head,
    cluster_weights,
    token_ids,
):
    rows_here = student_hidden.shape[0]
    width = student_hidden.shape[1]
    head_cols = teacher_head.shape[2]
    branch_gain = teacher_gain[0]
    branch_head = teacher_head[0]
    normed, unused_scale = normalize(
        lax.all_gather(teacher_hidden[0], "tok", axis=0, tiled=True), branch_gain
    )
    teacher_logits = jnp.dot(normed, branch_head, preferred_element_type=jnp.float32)
    weight = cluster_weights[:, 0].astype(jnp.float32) / DEN
    terms = probabilities(teacher_logits) * weight[:, None]
    mixed_all = lax.psum(terms, "branch")
    mixed = lax.dynamic_slice_in_dim(mixed_all, lax.axis_index("branch") * rows_here, rows_here, 0)
    student_normed, inv_scale = normalize(student_hidden, student_gain)
    student_logits = jnp.dot(
        student_normed,
        lax.all_gather(student_head, "branch", axis=0, tiled=True),
        preferred_element_type=jnp.float32,
    )
    student_probs = probabilities(student_logits)
    offset = lax.axis_index("tok") * head_cols
    onehot = (
        token_ids[:, None] == offset + jnp.arange(head_cols, dtype=jnp.int32)[None, :]
    ).astype(jnp.float32)
    targets = (1.0 - mix_label) * mixed + mix_label * onehot
    logit_grads = (loss_scale * (student_probs - targets)).astype(jnp.bfloat16)
    contract = (((1,), (1,)), ((), ()))
    partial_grads = lax.dot_general(
        logit_grads,
        lax.all_gather(student_head, "branch", axis=0, tiled=True),
        contract,
        preferred_element_type=jnp.float32,
    )
    normed_grads = lax.psum_scatter(partial_grads, "tok", scatter_dimension=1, tiled=True)
    slice_width = normed_grads.shape[1]
    col_start = lax.axis_index("tok") * slice_width
    hidden_cols = lax.dynamic_slice_in_dim(student_hidden, col_start, slice_width, 1).astype(
        jnp.float32
    )
    gain_cols = lax.dynamic_slice_in_dim(student_gain, col_start, slice_width, 0)
    grad_gain = lax.psum(jnp.sum(normed_grads * hidden_cols * inv_scale, axis=0), "branch")
    row_dots = lax.psum(jnp.sum(gain_cols[None, :] * normed_grads * hidden_cols, axis=1), "tok")
    grad_hidden = (
        inv_scale * gain_cols[None, :] * normed_grads
        - hidden_cols * inv_scale**3 * row_dots[:, None] / width
    )
    exchanged = lax.all_to_all(student_normed, "branch", split_axis=1, concat_axis=0, tiled=True)
    all_grads = lax.all_gather(logit_grads, "branch", axis=0, tiled=True)
    grad_head = lax.dot_general(
        exchanged, all_grads, (((0,), (0,)), ((), ())), preferred_element_type=jnp.float32
    )
    return (grad_head, grad_hidden, grad_gain)


def solution(mesh):
    in_specs = (
        P("branch", "tok", None),
        P("branch", None),
        P("branch", None, "tok"),
        P("branch", None),
        P(),
        P("branch", "tok"),
        P(None, "branch"),
        P("branch"),
    )
    out_specs = (P("branch", "tok"), P("branch", "tok"), P("tok"))
    return jax.shard_map(
        per_device, mesh=mesh, in_specs=in_specs, out_specs=out_specs, check_vma=False
    )
```

profile of v0, /device:TPU:0, one launch (start us, length us, event | category | flops | bytes accessed | tf_op | source)
XLA Modules:
  0.0 349.2 jit_solution(5427056235205396135)
XLA Ops:
  7.2 0.0 all-gather.14.cloned.1.call-start
  7.2 0.7 all-gather.14.cloned.1.call-update
  7.9 0.0 copy-start.1
  7.9 0.0 all-gather.12.cloned.1.call-start
  8.0 0.7 all-gather.12.cloned.1.call-update
  8.7 0.0 copy-start.3
  8.7 0.0 copy-start.2
  8.7 0.0 all-reduce.2.cloned.1.call-start
  8.7 0.4 copy-done.1
  9.1 0.7 copy.13
  9.8 0.6 fusion.7
  10.4 0.0 copy-done.3
  10.4 0.0 copy-done.2
  10.4 0.0 copy-start.5
  10.4 1.6 fusion.9
  12.0 42.4 %all-gather.14.cloned.1.call-done = bf16[1,256,4096]{2,1,0:T(8,128)(2,1)} async-done(((bf16[1,16,4096]{2,1,0:T(8,128)(2,1)}), bf16[1,256,4096]{2,1,0:T(8,128)(2,1)}) %all-gather.14.cloned.1.call-update) | async-done | bytes 2097168 | tf_op jit(solution)/shard_map/all_gather | solution.py:59
  54.4 2.2 fusion.4
  56.6 0.0 copy-done.5
  56.6 7.1 %fusion.22 = (f32[256]{0:T(256)S(1)}, f32[256,1280]{1,0:T(8,128)S(1)}) fusion(bf16[1,4096,1280]{2,1,0:T(8,128)(2,1)} %param.14, bf16[1,256,4096]{2,1,0:T(8,128)(2,1)S(1)} %copy-done, f32[4096]{0:T(1024)S(1)} %bitcast.78, f32[256]{0:T(256)S(1)} %add_rsqrt_fusion), kind=kOutput, calls=%fused_computation.50 | convolution fusion | flops 2688876288 | bytes 13912064 | tf_op jit(solution)/shard_map/dot_general | solution.py:61
  63.7 0.3 fusion.14
  64.0 19.1 %all-gather.8 = f32[16,1,256]{2,1,0:T(1,128)S(1)} all-gather(f32[1,1,256]{2,1,0:T(1,128)S(1)} %bitcast.76), channel_id=6, replica_groups=mesh['branch'=2,'tok'=16] {'tok'}, dimensions={0}, use_global_device_ids=true | all-gather | bytes 17408 | tf_op jit(solution)/shard_map/all_gather | solution.py:15
  83.1 17.4 %all-gather.7 = f32[16,1,256]{2,1,0:T(1,128)S(1)} all-gather(f32[1,1,256]{2,1,0:T(1,128)S(1)} %bitcast.71), channel_id=5, replica_groups=mesh['branch'=2,'tok'=16] {'tok'}, dimensions={0}, use_global_device_ids=true | all-gather | bytes 17408 | tf_op jit(solution)/shard_map/all_gather | solution.py:15
  100.6 0.8 while.35
  101.4 1.4 divide_multiply_fusion
  102.8 0.0 all-reduce.2.cloned.1.call-update
  102.9 0.0 copy-start.4
  102.9 0.0 reduce-scatter.2.cloned.1.call-start
  102.9 81.2 %all-gather.12.cloned.1.call-done = bf16[4096,1280]{1,0:T(8,128)(2,1)} async-done(((bf16[2048,1280]{1,0:T(8,128)(2,1)}), bf16[4096,1280]{1,0:T(8,128)(2,1)}) %all-gather.12.cloned.1.call-update) | async-done | bytes 10485776 | tf_op jit(solution)/shard_map/all_gather | solution.py:69
  184.1 6.0 %fusion.23 = (f32[128]{0:T(128)S(1)}, f32[128,1280]{1,0:T(8,128)S(1)}) fusion(bf16[128,4096]{0,1:T(8,128)(2,1)} %fusion.9, bf16[4096,1280]{1,0:T(8,128)(2,1)} %all-gather.12.cloned.1.call-done), kind=kOutput, calls=%fused_computation.51 | convolution fusion | flops 1342340992 | bytes 12190208 | tf_op jit(solution)/shard_map/dot_general | solution.py:67
  190.1 0.3 fusion.15
  190.4 21.3 %all-gather.6 = f32[16,1,128]{2,1,0:T(1,128)S(1)} all-gather(f32[1,1,128]{2,1,0:T(1,128)S(1)} %bitcast.77), channel_id=3, replica_groups=mesh['branch'=2,'tok'=16] {'tok'}, dimensions={0}, use_global_device_ids=true | all-gather | bytes 8704 | tf_op jit(solution)/shard_map/all_gather | solution.py:15
  211.7 17.4 %all-gather.5 = f32[16,1,128]{2,1,0:T(1,128)S(1)} all-gather(f32[1,1,128]{2,1,0:T(1,128)S(1)} %bitcast.74), channel_id=2, replica_groups=mesh['branch'=2,'tok'=16] {'tok'}, dimensions={0}, use_global_device_ids=true | all-gather | bytes 8704 | tf_op jit(solution)/shard_map/all_gather | solution.py:15
  229.1 0.7 while.34
  229.8 3.1 all-reduce.2.cloned.1.call-done
  232.9 1.4 multiply_convert_fusion
  234.3 8.7 %fusion.25 = f32[128,4096]{1,0:T(8,128)} fusion(bf16[128,1280]{1,0:T(8,128)(2,1)S(1)} %multiply_convert_fusion, bf16[4096,1280]{1,0:T(8,128)(2,1)} %all-gather.12.cloned.1.call-done), kind=kOutput, calls=%fused_computation.53 | convolution fusion | flops 1342177280 | bytes 12910592 | tf_op jit(solution)/shard_map/dot_general | solution.py:80
  243.0 0.0 reduce-scatter.2.cloned.1.call-update
  243.0 3.6 %all-to-all-start = ((bf16[128,2,2048]{0,2,1:T(8,128)(2,1)}), bf16[128,2,2048]{0,2,1:T(8,128)(2,1)S(1)}, u32[]{:S(2)}, u32[]{:S(2)}) async-start(bf16[128,2,2048]{0,2,1:T(8,128)(2,1)} %bitcast.4), calls=%async_computation | async-start | bytes 2097152 | tf_op jit(solution)/shard_map/all_to_all | solution.py:99
  246.6 0.1 dynamic_slice.50
  246.7 13.6 %all-to-all-done = bf16[128,2,2048]{0,2,1:T(8,128)(2,1)S(1)} async-done(((bf16[128,2,2048]{0,2,1:T(8,128)(2,1)}), bf16[128,2,2048]{0,2,1:T(8,128)(2,1)S(1)}, u32[]{:S(2)}, u32[]{:S(2)}) %all-to-all-start) | async-done | bytes 1048608 | tf_op jit(solution)/shard_map/all_to_all | solution.py:99
  260.3 0.5 copy.14
  260.9 9.1 %all_gather.44 = bf16[256,1280]{1,0:T(8,128)(2,1)S(1)} all-gather(bf16[128,1280]{1,0:T(8,128)(2,1)S(1)} %multiply_convert_fusion), channel_id=1, replica_groups=mesh['branch'=2,'tok'=16] {'branch'}, dimensions={0}, use_global_device_ids=true | all-gather | bytes 983040 | tf_op jit(solution)/shard_map/all_gather | solution.py:100
  269.9 5.7 %fusion.24 = f32[2048,1280]{1,0:T(8,128)} fusion(bf16[256,2048]{1,0:T(8,128)(2,1)S(1)} %bitcast.63, bf16[256,1280]{1,0:T(8,128)(2,1)S(1)} %all_gather.44), kind=kOutput, calls=%fused_computation.52 | convolution fusion | flops 1342177280 | bytes 12189696 | tf_op jit(solution)/shard_map/dot_general | solution.py:101
  275.6 29.3 %reduce-scatter.2.cloned.1.call-done = f32[128,256]{1,0:T(8,128)} async-done(((f32[128,4096]{1,0:T(8,128)}), f32[128,256]{1,0:T(8,128)}) %reduce-scatter.2.cloned.1.call-update) | async-done | bytes 131088 | tf_op jit(solution)/shard_map/reduce_scatter | solution.py:86
  305.0 1.0 fusion.21
  306.0 29.5 %psum.22 = f32[128]{0:T(128)S(1)} all-reduce(f32[128]{0:T(128)S(1)} %get-tuple-element.274), channel_id=1, replica_groups=mesh['branch'=2,'tok'=16] {'tok'}, use_global_device_ids=true, to_apply=%region_13.0 | all-reduce | flops 128 | bytes 1024 | tf_op jit(solution)/shard_map/psum | solution.py:94
  335.5 5.5 %psum.23 = f32[256]{0:T(256)} all-reduce(f32[256]{0:T(256)S(1)} %get-tuple-element.273), channel_id=1, replica_groups=mesh['branch'=2,'tok'=16] {'branch'}, use_global_device_ids=true, to_apply=%region_15.0 | all-reduce | flops 256 | bytes 2048 | tf_op jit(solution)/shard_map/psum | solution.py:93
  341.0 1.7 fusion.18
  (60 shorter events, 0.9 us)
Async XLA Ops:
  7.2 47.2 %all-gather.14.cloned.1.call-start = ((), (), s32[]{:S(2)}) async-start(), calls=%async_computation.5 | async-start | bytes 2228224 | tf_op jit(solution)/shard_map/all_gather | solution.py:59
  7.9 1.2 copy-start.1
  7.9 176.2 %all-gather.12.cloned.1.call-start = ((), (), s32[]{:S(2)}) async-start(), calls=%async_computation.2 | async-start | bytes 15728640 | tf_op jit(solution)/shard_map/all_gather | solution.py:69
  8.7 1.7 copy-start.3
  8.7 1.7 copy-start.2
  8.7 224.2 %all-reduce.2.cloned.1.call-start = ((), (), s32[]{:S(2)}) async-start(), calls=%async_computation.3 | async-start | bytes 2621440 | tf_op jit(solution)/shard_map/psum | solution.py:64
  10.4 46.2 %copy-start.5 = (f32[1,4096]{1,0:T(1,128)S(1)}, f32[1,4096]{1,0:T(1,128)}, u32[]{:S(2)}) copy-start(f32[1,4096]{1,0:T(1,128)} %param.13) | copy-start | bytes 49156
  54.3 2.3 copy-start
  102.9 130.0 %copy-start.4 = (s32[128]{0:T(128)S(1)}, s32[128]{0:T(128)}, u32[]{:S(2)}) copy-start(s32[128]{0:T(128)} %param.19) | copy-start | bytes 1540
  102.9 202.1 %reduce-scatter.2.cloned.1.call-start = ((), (), s32[]{:S(2)}) async-start(), calls=%async_computation.4 | async-start | bytes 2228224 | tf_op jit(solution)/shard_map/reduce_scatter | solution.py:86
  243.0 17.3 %all-to-all-start = ((bf16[128,2,2048]{0,2,1:T(8,128)(2,1)}), bf16[128,2,2048]{0,2,1:T(8,128)(2,1)S(1)}, u32[]{:S(2)}, u32[]{:S(2)}) async-start(bf16[128,2,2048]{0,2,1:T(8,128)(2,1)} %bitcast.4), calls=%async_computation | async-start | bytes 2097152 | tf_op jit(solution)/shard_map/all_to_all | solution.py:99
Sparse Core Ops, SparseCore 0:
  10.1 44.1 all-gather.13
  55.9 128.1 all-gather.11
  187.0 45.8 all-reduce.1
  243.2 61.7 reduce-scatter.1
where the time goes:
time: 350 us; the launch traced here: 349 us
  waiting for transfers between devices  171 us (49%)
  blocking collectives  119 us (34%)
  matrix products  27.5 us (8%)
  between operations  13.9 us (4%)
  other arithmetic  11.2 us (3%)
  starting transfers between devices  3.75 us (1%)
    all_gather x1, waiting for transfers between devices, per_device(): lax.all_gather(student_head, 'branch', axis=0, tiled=True)  81.2 us
    all_gather x4, blocking collectives, merged(): everything = jax.tree.map(lambda part: lax.all_gather(part, axis), value)  75.3 us
    all_gather x1, waiting for transfers between devices, per_device(): lax.all_gather(teacher_hidden[0], 'tok', axis=0, tiled=True)  42.4 us
    psum x1, blocking collectives, per_device(): lax.psum(jnp.sum(gain_cols[None, :] * normed_grads * hidden_cols, axis=1)...  29.5 us
    reduce_scatter x1, waiting for transfers between devices, per_device(): lax.psum_scatter(partial_grads, 'tok', scatter_dimension=1, tiled=True)  29.3 us
    all_to_all x1, waiting for transfers between devices, per_device(): lax.all_to_all(student_normed, 'branch', split_axis=1, concat_axis=0, til...  13.6 us
    all_gather x1, blocking collectives, per_device(): all_grads = lax.all_gather(logit_grads, 'branch', axis=0, tiled=True)  9.09 us
    dot_general x1, matrix products, per_device(): lax.dot_general(logit_grads, lax.all_gather(student_head, 'branch', axis=...  8.73 us
  transfers between devices with their start and end apart: 5, of which 5 were waited for; matrix products, arithmetic and copies ran while one was open for 8% of the time, Pallas kernels for 0%

commit v1 on v0

v1 whole, which is shorter than its diff:
```python
import functools

import jax
import jax.numpy as jnp
from jax import lax
from jax.experimental import pallas as pl
from jax.experimental.pallas import tpu as pltpu
from jax.sharding import PartitionSpec as P

DEN = 64

eps = 1e-05
mix_label = 0.25
loss_scale = 64.0


def swap(value, axis, flip):
    size = lax.axis_size(axis)
    return lax.ppermute(value, axis, [(i, i ^ flip) for i in range(size)])


def normalize(hidden, gain):
    values = hidden.astype(jnp.float32)
    inv_scale = lax.rsqrt(jnp.mean(values * values, axis=-1, keepdims=True) + eps)
    return ((values * inv_scale * gain).astype(jnp.bfloat16), inv_scale)


def gather_blocks(block, size):
    got = {0: block}
    for k in range(4, size, 4):
        got[k] = swap(block, "tok", k)
    for k in range(0, size, 4):
        got[k + 2] = swap(got[k], "tok", 2)
    evens = sorted(got)
    half = len(evens) // 2
    for part in (evens[:half], evens[half:]):
        joined = swap(jnp.concatenate([got[k] for k in part], axis=0), "tok", 1)
        for place, k in enumerate(part):
            got[k + 1] = lax.slice_in_dim(joined, place * block.shape[0], (place + 1) * block.shape[0])
    return got


def grad_kernel(place_ref, g_ref, w_ref, out_ref):
    acc = lax.dot_general(g_ref[...], w_ref[...], (((1,), (1,)), ((), ())), preferred_element_type=jnp.float32)
    rows = out_ref.shape[2]
    count = out_ref.shape[0]
    parts = [acc[k * rows : (k + 1) * rows].astype(out_ref.dtype) for k in range(count)]
    for k in range(count):
        for r in range(count):

            @pl.when((place_ref[1] ^ k) == r)
            def _():
                out_ref[k, 0] = parts[r]


def normed_grad_pieces(grads, head, place, blocks, branches):
    tokens, cols = grads.shape
    width = head.shape[0] // blocks
    rows = tokens // branches
    return pl.pallas_call(
        grad_kernel,
        out_shape=jax.ShapeDtypeStruct((branches, blocks, rows, width), jnp.bfloat16),
        grid_spec=pltpu.PrefetchScalarGridSpec(
            num_scalar_prefetch=1,
            grid=(blocks,),
            in_specs=[
                pl.BlockSpec((tokens, cols), lambda i, place: (0, 0)),
                pl.BlockSpec((width, cols), lambda i, place: (i ^ place[0], 0)),
            ],
            out_specs=pl.BlockSpec((branches, 1, rows, width), lambda i, place: (0, i, 0, 0)),
        ),
        cost_estimate=pl.CostEstimate(
            flops=2 * tokens * cols * head.shape[0], bytes_accessed=2 * head.size + 4 * grads.size, transcendentals=0
        ),
    )(place, grads, head)


def per_device(
    teacher_hidden,
    teacher_gain,
    teacher_head,
    student_hidden,
    student_gain,
    student_head,
    cluster_weights,
    token_ids,
):
    branches = lax.axis_size("branch")
    size = lax.axis_size("tok")
    b = lax.axis_index("branch")
    t = lax.axis_index("tok")
    rows, width = student_hidden.shape
    head_cols = teacher_head.shape[2]
    part = width // branches
    blocks = size // branches
    f32 = jnp.float32

    student_normed, inv_scale = normalize(student_hidden, student_gain)

    def features(r):
        return lax.dynamic_slice_in_dim(student_normed, (b ^ r) * part, part, 1)

    student_parts = [features(0)] + [swap(features(r), "branch", r) for r in range(1, branches)]
    student_rows = jnp.concatenate(student_parts, axis=0)

    teacher_block, unused = normalize(teacher_hidden[0], teacher_gain[0])
    got = gather_blocks(teacher_block, size)
    count = teacher_block.shape[0]
    teacher_rows = jnp.zeros((count * size, width), jnp.bfloat16)
    for k in range(size):
        place = (t ^ k) ^ (b * blocks)
        teacher_rows = lax.dynamic_update_slice_in_dim(teacher_rows, got[k], place * count, 0)

    partial_logits = jnp.dot(student_rows, student_head, preferred_element_type=f32)
    logits = partial_logits[:rows]
    for r in range(1, branches):
        logits = logits + swap(partial_logits[r * rows : (r + 1) * rows], "branch", r)
    student_max = jnp.max(logits, axis=1)
    student_exp = jnp.exp(logits - student_max[:, None])
    student_sum = jnp.sum(student_exp, axis=1)

    teacher_logits = jnp.dot(teacher_rows, teacher_head[0], preferred_element_type=f32)
    teacher_max = jnp.max(teacher_logits, axis=1)
    teacher_exp = jnp.exp(teacher_logits - teacher_max[:, None])
    teacher_sum = jnp.sum(teacher_exp, axis=1)
    teacher_exp = teacher_exp.astype(jnp.bfloat16)
    terms = [teacher_exp[:rows]] + [
        swap(teacher_exp[r * rows : (r + 1) * rows], "branch", r) for r in range(1, branches)
    ]

    order = jnp.arange(branches) ^ b
    weights = cluster_weights[:, 0].astype(f32).reshape(branches, rows)
    stats = jnp.stack(
        [
            teacher_max.reshape(branches, rows)[order],
            teacher_sum.reshape(branches, rows)[order],
            weights,
            jnp.broadcast_to(student_max, (branches, rows)),
            jnp.broadcast_to(student_sum, (branches, rows)),
        ],
        axis=1,
    )
    stats = jnp.broadcast_to(stats[:, None], (branches, size, 5, rows)).reshape(branches * size, 5, rows)
    stats = lax.all_to_all(stats, ("branch", "tok"), 0, 0, tiled=True).reshape(branches, size, 5, rows)
    peak = jnp.max(stats[:, :, 0], axis=1)
    total = jnp.sum(stats[:, :, 1] * jnp.exp(stats[:, :, 0] - peak[:, None]), axis=1)
    here = lax.dynamic_index_in_dim(stats, t, 1, keepdims=False)
    scale = ((1.0 - mix_label) / DEN) * here[:, 2] * jnp.exp(here[:, 0] - peak) / total
    scale = scale[order]
    student_stats = lax.dynamic_index_in_dim(stats, b, 0, keepdims=False)
    student_peak = jnp.max(student_stats[:, 3], axis=0)
    student_total = jnp.sum(student_stats[:, 4] * jnp.exp(student_stats[:, 3] - student_peak), axis=0)
    student_scale = jnp.exp(student_max - student_peak) / student_total

    ids = token_ids - t * head_cols
    onehot = (ids[:, None] == jnp.arange(head_cols, dtype=jnp.int32)[None, :]).astype(f32)
    targets = mix_label * onehot
    for r in range(branches):
        targets = targets + terms[r].astype(f32) * scale[r][:, None]
    logit_grads = (loss_scale * (student_exp * student_scale[:, None] - targets)).astype(jnp.bfloat16)
    dots = jnp.sum(logit_grads.astype(f32) * logits, axis=1)
    all_grads = jnp.concatenate(
        [logit_grads] + [swap(logit_grads, "branch", r) for r in range(1, branches)], axis=0
    )

    place = jnp.stack([t % blocks, (t // blocks) ^ b]).astype(jnp.int32)
    pieces = normed_grad_pieces(all_grads, student_head, place, blocks, branches)
    pieces = pieces.reshape(size // 2, 2, rows, width // size)
    core = pieces[:, 0].astype(f32) + swap(pieces[:, 1], "tok", 1).astype(f32)
    core = core.astype(jnp.bfloat16).reshape(size // 4, 2, rows, width // size)
    pair = core[:, 0].astype(f32) + swap(core[:, 1], "tok", 2).astype(f32)
    sent = pair.astype(jnp.bfloat16)
    normed_grads = pair[0]
    for k in range(1, size // 4):
        normed_grads = normed_grads + swap(sent[k], "tok", 4 * k).astype(f32)
    perm = []
    for i in range(branches * size):
        bb, h, q = i // size, (i % size) // blocks, i % blocks
        perm.append((i, (h * branches + bb) * blocks + q))
    normed_grads = lax.ppermute(normed_grads, ("branch", "tok"), perm)
    row_dots = lax.psum(dots, "tok") / inv_scale[:, 0]

    slice_width = width // size
    hidden_cols = lax.dynamic_slice_in_dim(student_hidden, t * slice_width, slice_width, 1).astype(f32)
    gain_cols = lax.dynamic_slice_in_dim(student_gain, t * slice_width, slice_width, 0)
    grad_gain = jnp.sum(normed_grads * hidden_cols * inv_scale, axis=0)
    flip = 1
    while flip < branches:
        grad_gain = grad_gain + swap(grad_gain, "branch", flip)
        flip *= 2
    grad_hidden = (
        inv_scale * gain_cols[None, :] * normed_grads
        - hidden_cols * inv_scale**3 * row_dots[:, None] / width
    )
    grad_head = lax.dot_general(
        student_rows, all_grads, (((0,), (0,)), ((), ())), preferred_element_type=f32
    )
    return (grad_head, grad_hidden, grad_gain)


def solution(mesh):
    in_specs = (
        P("branch", "tok", None),
        P("branch", None),
        P("branch", None, "tok"),
        P("branch", None),
        P(),
        P("branch", "tok"),
        P(None, "branch"),
        P("branch"),
    )
    out_specs = (P("branch", "tok"), P("branch", "tok"), P("tok"))
    return jax.shard_map(
        per_device, mesh=mesh, in_specs=in_specs, out_specs=out_specs, check_vma=False
    )
```

time: 350 us -> 154 us (0.44)
  waiting for transfers between devices: 171 us -> 30.5 us
  blocking collectives: 119 us -> 31.5 us
  starting transfers between devices: 3.75 us -> 36.3 us
  local copies, waits for them, and re-layouts: 1.85 us -> 17.5 us
  matrix products: 27.5 us -> 14.5 us
  between operations: 13.9 us -> 1.01 us
  Pallas kernels: 0 us -> 8.4 us
    all_gather x2 -> x0, waiting for transfers between devices: 124 us -> none  [the longest x1 81.2 us: per_device(): lax.all_gather(student_head, 'branch', axis=0, tiled=True)]
    all_gather x5 -> x0, blocking collectives: 84.4 us -> none  [the longest x4 75.3 us: merged(): everything = jax.tree.map(lambda part: lax.all_gather(part, axis), value)]
    ppermute x0 -> x20, starting transfers between devices: none -> 31.8 us  [the longest x19 31.1 us: swap(): return lax.ppermute(value, axis, [(i, i ^ flip) for i in range(size)])]
    reduce_scatter x1 -> x0, waiting for transfers between devices: 29.3 us -> none  [per_device(): lax.psum_scatter(partial_grads, 'tok', scatter_dimension=1, tiled=True)]
    ppermute x0 -> x20, waiting for transfers between devices: none -> 24.2 us  [the longest x19 24.2 us: swap(): return lax.ppermute(value, axis, [(i, i ^ flip) for i in range(size)])]
    dot_general x4 -> x3, matrix products: 27.5 us -> 14.5 us  [the longest x1 5.67 us: per_device(): lax.dot_general(student_rows, all_grads, (((0,), (0,)), ((), ())), prefer...]
    dynamic_update_slice x0 -> x15, local copies, waits for them, and re-layouts: none -> 9.95 us  [per_device(): lax.dynamic_update_slice_in_dim(teacher_rows, got[k], place * count, 0)]
    pallas_call x0 -> x1, Pallas kernels: none -> 8.4 us  [normed_grad_pieces(): pl.pallas_call(grad_kernel, out_shape=jax.ShapeDtypeStruct((branches, blo...]
  transfers between devices with their start and end apart: 5 -> 21, of which waited for: 5 -> 11; matrix products, arithmetic and copies ran while one was open for 8% -> 20% of each run, Pallas kernels for 0% -> 0%
where the time goes in v1:
time: 154 us; the launch traced here: 153 us
  starting transfers between devices  36.3 us (24%)
  blocking collectives  31.5 us (20%)
  waiting for transfers between devices  30.5 us (20%)
  local copies, waits for them, and re-layouts  17.5 us (11%)
  matrix products  14.5 us (9%)
  other arithmetic  13.4 us (9%)
  Pallas kernels  8.4 us (5%)
    psum x1, blocking collectives, per_device(): row_dots = lax.psum(dots, 'tok') / inv_scale[:, 0]  31.5 us
    ppermute x19, starting transfers between devices, swap(): return lax.ppermute(value, axis, [(i, i ^ flip) for i in range(size)])  31.1 us
    ppermute x19, waiting for transfers between devices, swap(): return lax.ppermute(value, axis, [(i, i ^ flip) for i in range(size)])  24.2 us
    dynamic_update_slice x15, local copies, waits for them, and re-layouts, per_device(): lax.dynamic_update_slice_in_dim(teacher_rows, got[k], place * count, 0)  9.95 us
    pallas_call x1, Pallas kernels, normed_grad_pieces(): pl.pallas_call(grad_kernel, out_shape=jax.ShapeDtypeStruct((branches, blo...  8.4 us
    all_to_all x1, waiting for transfers between devices, per_device(): lax.all_to_all(stats, ('branch', 'tok'), 0, 0, tiled=True)  6.32 us
    dot_general x1, matrix products, per_device(): lax.dot_general(student_rows, all_grads, (((0,), (0,)), ((), ())), prefer...  5.67 us
    dot_general x1, matrix products, per_device(): jnp.dot(teacher_rows, teacher_head[0], preferred_element_type=f32)  4.55 us
  transfers between devices with their start and end apart: 21, of which 11 were waited for; matrix products, arithmetic and copies ran while one was open for 20% of the time, Pallas kernels for 0%

profile of v1, /device:TPU:0, one launch (start us, length us, event | category | flops | bytes accessed | tf_op | source)
XLA Modules:
  0.0 153.0 jit_solution(15297890151153997268)
XLA Ops:
  0.7 1.1 fusion.11
  1.8 1.6 %broadcast_in_dim.4 = bf16[256,4096]{1,0:T(8,128)(2,1)} broadcast(bf16[]{:T(256)} %constant.28.clone.1), dimensions={} | broadcast | bytes 2097154 | tf_op jit(solution)/shard_map/broadcast_in_dim | solution.py:109
  3.4 0.8 constant_dynamic-update-slice_fusion.12
  4.2 4.1 %collective-permute-start.6 = (bf16[16,4096]{1,0:T(8,128)(2,1)S(1)}, bf16[16,4096]{1,0:T(8,128)(2,1)S(1)}, u32[]{:S(2)}, u32[]{:S(2)}) collective-permute-start(bf16[16,4096]{1,0:T(8,128)(2,1)S(1)} %get-tuple-element.8), channel_id=1, source_target_pairs={{0,8},{1,9},{2,10},{3,11},{4,12},{5,13},{6,14},{7,15},{8,0},{9,1},... | collective-permute-start | bytes 393224 | tf_op jit(solution)/shard_map/ppermute | solution.py:19
  8.2 1.6 %collective-permute-start.3 = (bf16[16,4096]{1,0:T(8,128)(2,1)S(1)}, bf16[16,4096]{1,0:T(8,128)(2,1)S(1)}, u32[]{:S(2)}, u32[]{:S(2)}) collective-permute-start(bf16[16,4096]{1,0:T(8,128)(2,1)S(1)} %get-tuple-element.8), channel_id=1, source_target_pairs={{0,4},{1,5},{2,6},{3,7},{4,0},{5,1},{6,2},{7,3},{8,12},{9,13},{10,... | collective-permute-start | bytes 393224 | tf_op jit(solution)/shard_map/ppermute | solution.py:19
  9.8 1.5 collective-permute-start.2
  12.9 1.6 %collective-permute-start = (bf16[128,2048]{1,0:T(8,128)(2,1)S(1)}, bf16[128,2048]{1,0:T(8,128)(2,1)S(1)}, u32[]{:S(2)}, u32[]{:S(2)}) collective-permute-start(bf16[128,2048]{1,0:T(8,128)(2,1)S(1)} %get-tuple-element.14), channel_id=1, source_target_pairs={{0,16},{16,0},{1,17},{17,1},{2,18},{18,2},{3,19},{19,3},{4,20},{20... | collective-permute-start | bytes 1572872 | tf_op jit(solution)/shard_map/ppermute | solution.py:19
  14.9 1.5 collective-permute-start.4
  17.6 0.7 collective-permute-start.7
  18.5 1.5 collective-permute-start.9
  20.1 1.0 collective-permute-done.4
  21.2 2.2 %collective-permute-done.7 = bf16[16,4096]{1,0:T(8,128)(2,1)S(1)} collective-permute-done((bf16[16,4096]{1,0:T(8,128)(2,1)S(1)}, bf16[16,4096]{1,0:T(8,128)(2,1)S(1)}, u32[]{:S(2)}, u32[]{:S(2)}) %collective-permute-start.7) | collective-permute-done | bytes 131104 | tf_op jit(solution)/shard_map/ppermute | solution.py:19
  23.4 1.4 collective-permute-done.9
  25.5 4.2 %fusion.9 = f32[256,1280]{1,0:T(8,128)S(1)} fusion(bf16[2048,1280]{1,0:T(8,128)(2,1)} %w_ref.1, bf16[128,2048]{1,0:T(8,128)(2,1)S(1)} %collective-permute-done, bf16[128,2048]{1,0:T(8,128)(2,1)S(1)} %get-tuple-element.13), kind=kOutput, calls=%fused_computation.17 | convolution fusion | flops 1344274432 | bytes 7602176 | tf_op jit(solution)/shard_map/dot_general | solution.py:114
  29.9 1.6 %collective-permute-start.1 = (f32[128,1280]{1,0:T(8,128)S(1)}, f32[128,1280]{1,0:T(8,128)}, u32[]{:S(2)}, u32[]{:S(2)}) collective-permute-start(f32[128,1280]{1,0:T(8,128)S(1)} %slice.121), channel_id=1, source_target_pairs={{0,16},{16,0},{1,17},{17,1},{2,18},{18,2},{3,19},{19,3},{4,20},{20... | collective-permute-start | bytes 1966088 | tf_op jit(solution)/shard_map/ppermute | solution.py:19
  31.4 0.7 slice_dynamic-update-slice_fusion.7
  33.4 0.7 constant_dynamic-update-slice_fusion.10
  36.7 0.7 slice_dynamic-update-slice_fusion.3
  38.7 0.7 constant_dynamic-update-slice_fusion.6
  41.4 4.6 %fusion.40 = (f32[256]{0:T(256)S(1)}, f32[256,1280]{1,0:T(8,128)S(1)}) fusion(bf16[256,4096]{1,0:T(8,128)(2,1)} %slice_dynamic-update-slice_fusion, bf16[1,4096,1280]{2,1,0:T(8,128)(2,1)S(1)} %copy-done.13), kind=kOutput, calls=%fused_computation.112 | convolution fusion | flops 2684681984 | bytes 13894656 | tf_op jit(solution)/shard_map/dot_general | solution.py:122
  46.3 0.7 gather_fusion.1
  47.0 0.7 gather_fusion
  47.7 1.4 fusion.38
  49.4 0.7 broadcast_in_dim.5
  50.1 4.5 %all-to-all-start = ((f32[32,5,128]{2,1,0:T(8,128)}), f32[32,5,128]{2,1,0:T(8,128)S(1)}, u32[]{:S(2)}, u32[]{:S(2)}) async-start(f32[32,5,128]{2,1,0:T(8,128)} %bitcast.10), calls=%async_computation | async-start | bytes 262144 | tf_op jit(solution)/shard_map/all_to_all | solution.py:144
  54.7 1.8 %collective-permute-start.11 = (bf16[128,1280]{1,0:T(8,128)(2,1)S(1)}, bf16[128,1280]{1,0:T(8,128)(2,1)}, u32[]{:S(2)}, u32[]{:S(2)}) collective-permute-start(bf16[128,1280]{1,0:T(8,128)(2,1)S(1)} %slice.137), channel_id=1, source_target_pairs={{0,16},{16,0},{1,17},{17,1},{2,18},{18,2},{3,19},{19,3},{4,20},{20... | collective-permute-start | bytes 983048 | tf_op jit(solution)/shard_map/ppermute | solution.py:19
  56.5 6.3 %all-to-all-done = f32[32,5,128]{2,1,0:T(8,128)S(1)} async-done(((f32[32,5,128]{2,1,0:T(8,128)}), f32[32,5,128]{2,1,0:T(8,128)S(1)}, u32[]{:S(2)}, u32[]{:S(2)}) %all-to-all-start) | async-done | bytes 81952 | tf_op jit(solution)/shard_map/all_to_all | solution.py:144
  62.9 0.7 gather_fusion.2
  63.7 2.3 %collective-permute-done.11 = bf16[128,1280]{1,0:T(8,128)(2,1)} collective-permute-done((bf16[128,1280]{1,0:T(8,128)(2,1)S(1)}, bf16[128,1280]{1,0:T(8,128)(2,1)}, u32[]{:S(2)}, u32[]{:S(2)}) %collective-permute-start.11) | collective-permute-done | bytes 327712 | tf_op jit(solution)/shard_map/ppermute | solution.py:19
  66.0 2.0 %multiply_reduce_fusion = (f32[128]{0:T(128)}, bf16[128,1280]{1,0:T(8,128)(2,1)S(1)}) fusion(f32[128,1280]{1,0:T(8,128)S(1)} %get-tuple-element.6, f32[128]{0:T(128)S(1)} %get-tuple-element.21, bf16[128,1280]{1,0:T(8,128)(2,1)} %collective-permute-done.11, f32[128]{0:T(128)S(1)} %get-tuple-element.20, bf16[256,1280]{1,0:T(8,128)(2,1)S(1)} %get-tuple-element.9, ...), kind=kLoop, calls=%fused_computation.20 | loop fusion | flops 2621312 | bytes 1641472 | tf_op jit(solution)/shard_map/reduce_sum | solution.py:161
  68.0 1.3 collective-permute-start.12
  69.9 7.3 %collective-permute-done.12 = bf16[128,1280]{1,0:T(8,128)(2,1)S(1)} collective-permute-done((bf16[128,1280]{1,0:T(8,128)(2,1)S(1)}, bf16[128,1280]{1,0:T(8,128)(2,1)S(1)}, u32[]{:S(2)}, u32[]{:S(2)}) %collective-permute-start.12) | collective-permute-done | bytes 327712 | tf_op jit(solution)/shard_map/ppermute | solution.py:19
  77.1 0.9 pad_maximum_fusion.3.g_ref
  78.0 8.4 %shard_map.103 = bf16[2,8,128,256]{3,2,1,0:T(8,128)(2,1)} custom-call(s32[2]{0:T(128)} %pad_add_fusion.place_ref, bf16[256,1280]{1,0:T(8,128)(2,1)} %pad_maximum_fusion.3.g_ref, bf16[2048,1280]{1,0:T(8,128)(2,1)} %w_ref.1), custom_call_target="tpu_custom_call" | custom-call | flops 1342177280 | bytes 6553600 | tf_op jit(solution)/shard_map/pallas_call | solution.py:60
  86.4 1.1 slice_bitcast_fusion
  87.6 1.9 %collective-permute-done.13 = bf16[8,128,256]{2,1,0:T(8,128)(2,1)S(1)} collective-permute-done((bf16[8,128,256]{2,1,0:T(8,128)(2,1)S(1)}, bf16[8,128,256]{2,1,0:T(8,128)(2,1)S(1)}, u32[]{:S(2)}, u32[]{:S(2)}) %collective-permute-start.13) | collective-permute-done | bytes 524320 | tf_op jit(solution)/shard_map/ppermute | solution.py:19
  89.5 1.2 fusion.7
  90.7 1.7 %collective-permute-start.14 = (bf16[4,128,256]{2,1,0:T(8,128)(2,1)S(1)}, bf16[4,128,256]{2,1,0:T(8,128)(2,1)S(1)}, u32[]{:S(2)}, u32[]{:S(2)}) collective-permute-start(bf16[4,128,256]{2,1,0:T(8,128)(2,1)S(1)} %slice_bitcast_fusion.2), channel_id=1, source_target_pairs={{0,2},{1,3},{2,0},{3,1},{4,6},{5,7},{6,4},{7,5},{8,10},{9,11},{10,... | collective-permute-start | bytes 786440 | tf_op jit(solution)/shard_map/ppermute | solution.py:19
  92.4 6.7 %collective-permute-done.14 = bf16[4,128,256]{2,1,0:T(8,128)(2,1)S(1)} collective-permute-done((bf16[4,128,256]{2,1,0:T(8,128)(2,1)S(1)}, bf16[4,128,256]{2,1,0:T(8,128)(2,1)S(1)}, u32[]{:S(2)}, u32[]{:S(2)}) %collective-permute-start.14) | collective-permute-done | bytes 262176 | tf_op jit(solution)/shard_map/ppermute | solution.py:19
  99.2 0.7 slice_bitcast_fusion.7
  99.8 1.6 %collective-permute-start.15 = (bf16[128,256]{1,0:T(8,128)(2,1)}, bf16[128,256]{1,0:T(8,128)(2,1)S(1)}, u32[]{:S(2)}, u32[]{:S(2)}) collective-permute-start(bf16[128,256]{1,0:T(8,128)(2,1)} %get-tuple-element.17), channel_id=1, source_target_pairs={{0,4},{1,5},{2,6},{3,7},{4,0},{5,1},{6,2},{7,3},{8,12},{9,13},{10,... | collective-permute-start | bytes 196616 | tf_op jit(solution)/shard_map/ppermute | solution.py:19
  101.4 2.5 %collective-permute-start.17 = (bf16[128,256]{1,0:T(8,128)(2,1)}, bf16[128,256]{1,0:T(8,128)(2,1)S(1)}, u32[]{:S(2)}, u32[]{:S(2)}) collective-permute-start(bf16[128,256]{1,0:T(8,128)(2,1)} %get-tuple-element.18), channel_id=1, source_target_pairs={{0,12},{1,13},{2,14},{3,15},{4,8},{5,9},{6,10},{7,11},{8,4},{9,5},... | collective-permute-start | bytes 196616 | tf_op jit(solution)/shard_map/ppermute | solution.py:19
  104.6 31.5 %psum.7 = f32[128]{0:T(128)S(1)} all-reduce(f32[128]{0:T(128)} %get-tuple-element.3), channel_id=1, replica_groups=mesh['branch'=2,'tok'=16] {'tok'}, use_global_device_ids=true, to_apply=%region_11.12 | all-reduce | flops 128 | bytes 1024 | tf_op jit(solution)/shard_map/psum | solution.py:181
  136.2 0.7 collective-permute-start.18
  136.8 0.7 multiply_multiply_fusion
  137.5 1.5 fusion.18
  139.0 7.7 %collective-permute-start.19 = (f32[256]{0:T(256)S(1)}, f32[256]{0:T(256)S(1)}, u32[]{:S(2)}, u32[]{:S(2)}) collective-permute-start(f32[256]{0:T(256)S(1)} %get-tuple-element.11), channel_id=1, source_target_pairs={{0,16},{16,0},{1,17},{17,1},{2,18},{18,2},{3,19},{19,3},{4,20},{20... | collective-permute-start | bytes 3080 | tf_op jit(solution)/shard_map/ppermute | solution.py:19
  146.7 5.7 %fusion.8 = f32[2048,1280]{1,0:T(8,128)} fusion(bf16[128,2048]{1,0:T(8,128)(2,1)S(1)} %copy-done.3, bf16[128,2048]{1,0:T(8,128)(2,1)S(1)} %get-tuple-element.13, bf16[128,1280]{1,0:T(8,128)(2,1)S(1)} %collective-permute-done.12, bf16[128,1280]{1,0:T(8,128)(2,1)S(1)} %get-tuple-element.4), kind=kOutput, calls=%fused_computation.16 | convolution fusion | flops 1345585152 | bytes 12189696 | tf_op jit(solution)/shard_map/dot_general | solution.py:195
  (96 shorter events, 14.5 us)
Async XLA Ops:
  0.6 2.8 %copy-start.4 = (bf16[1,16,4096]{2,1,0:T(8,128)(2,1)S(1)}, bf16[1,16,4096]{2,1,0:T(8,128)(2,1)}, u32[]{:S(2)}) copy-start(bf16[1,16,4096]{2,1,0:T(8,128)(2,1)} %param.8) | copy-start | bytes 393220
  0.6 2.8 %copy-start.8 = (f32[1,4096]{1,0:T(1,128)S(1)}, f32[1,4096]{1,0:T(1,128)}, u32[]{:S(2)}) copy-start(f32[1,4096]{1,0:T(1,128)} %param.9) | copy-start | bytes 49156
  0.7 10.9 %copy-start = (bf16[128,4096]{1,0:T(8,128)(2,1)S(1)}, bf16[128,4096]{1,0:T(8,128)(2,1)}, u32[]{:S(2)}) copy-start(bf16[128,4096]{1,0:T(8,128)(2,1)} %param.11) | copy-start | bytes 3145732
  0.7 11.8 %copy-start.7 = (f32[4096]{0:T(1024)S(1)}, f32[4096]{0:T(1024)}, u32[]{:S(2)}) copy-start(f32[4096]{0:T(1024)} %param.12) | copy-start | bytes 49156
  4.2 13.5 %collective-permute-start.6 = (bf16[16,4096]{1,0:T(8,128)(2,1)S(1)}, bf16[16,4096]{1,0:T(8,128)(2,1)S(1)}, u32[]{:S(2)}, u32[]{:S(2)}) collective-permute-start(bf16[16,4096]{1,0:T(8,128)(2,1)S(1)} %get-tuple-element.8), channel_id=1, source_target_pairs={{0,8},{1,9},{2,10},{3,11},{4,12},{5,13},{6,14},{7,15},{8,0},{9,1},... | collective-permute-start | bytes 393224 | tf_op jit(solution)/shard_map/ppermute | solution.py:19
  8.2 6.7 %collective-permute-start.3 = (bf16[16,4096]{1,0:T(8,128)(2,1)S(1)}, bf16[16,4096]{1,0:T(8,128)(2,1)S(1)}, u32[]{:S(2)}, u32[]{:S(2)}) collective-permute-start(bf16[16,4096]{1,0:T(8,128)(2,1)S(1)} %get-tuple-element.8), channel_id=1, source_target_pairs={{0,4},{1,5},{2,6},{3,7},{4,0},{5,1},{6,2},{7,3},{8,12},{9,13},{10,... | collective-permute-start | bytes 393224 | tf_op jit(solution)/shard_map/ppermute | solution.py:19
  9.8 10.3 %collective-permute-start.2 = (bf16[16,4096]{1,0:T(8,128)(2,1)S(1)}, bf16[16,4096]{1,0:T(8,128)(2,1)S(1)}, u32[]{:S(2)}, u32[]{:S(2)}) collective-permute-start(bf16[16,4096]{1,0:T(8,128)(2,1)S(1)} %get-tuple-element.8), channel_id=1, source_target_pairs={{0,2},{1,3},{2,0},{3,1},{4,6},{5,7},{6,4},{7,5},{8,10},{9,11},{10,... | collective-permute-start | bytes 393224 | tf_op jit(solution)/shard_map/ppermute | solution.py:19
  11.3 7.2 %collective-permute-start.8 = (bf16[16,4096]{1,0:T(8,128)(2,1)S(1)}, bf16[16,4096]{1,0:T(8,128)(2,1)S(1)}, u32[]{:S(2)}, u32[]{:S(2)}) collective-permute-start(bf16[16,4096]{1,0:T(8,128)(2,1)S(1)} %get-tuple-element.8), channel_id=1, source_target_pairs={{0,12},{1,13},{2,14},{3,15},{4,8},{5,9},{6,10},{7,11},{8,4},{9,5},... | collective-permute-start | bytes 393224 | tf_op jit(solution)/shard_map/ppermute | solution.py:19
  11.8 0.6 copy-start.11
  11.9 0.6 copy-start.10
  12.4 4.0 %copy-start.12 = (s32[256,1]{0,1:T(1,128)S(1)}, s32[256,1]{0,1:T(1,128)}, u32[]{:S(2)}) copy-start(s32[256,1]{0,1:T(1,128)} %param.14) | copy-start | bytes 3076
  12.9 12.7 %collective-permute-start = (bf16[128,2048]{1,0:T(8,128)(2,1)S(1)}, bf16[128,2048]{1,0:T(8,128)(2,1)S(1)}, u32[]{:S(2)}, u32[]{:S(2)}) collective-permute-start(bf16[128,2048]{1,0:T(8,128)(2,1)S(1)} %get-tuple-element.14), channel_id=1, source_target_pairs={{0,16},{16,0},{1,17},{17,1},{2,18},{18,2},{3,19},{19,3},{4,20},{20... | collective-permute-start | bytes 1572872 | tf_op jit(solution)/shard_map/ppermute | solution.py:19
  14.9 10.6 %copy-start.5 = (bf16[16,4096]{1,0:T(8,128)(2,1)}, bf16[16,4096]{1,0:T(8,128)(2,1)S(1)}, u32[]{:S(2)}) copy-start(bf16[16,4096]{1,0:T(8,128)(2,1)S(1)} %collective-permute-done.3) | copy-start | bytes 393220
  14.9 6.1 %collective-permute-start.4 = (bf16[16,4096]{1,0:T(8,128)(2,1)S(1)}, bf16[16,4096]{1,0:T(8,128)(2,1)S(1)}, u32[]{:S(2)}, u32[]{:S(2)}) collective-permute-start(bf16[16,4096]{1,0:T(8,128)(2,1)S(1)} %collective-permute-done.3), channel_id=1, source_target_pairs={{0,2},{1,3},{2,0},{3,1},{4,6},{5,7},{6,4},{7,5},{8,10},{9,11},{10,... | collective-permute-start | bytes 393224 | tf_op jit(solution)/shard_map/ppermute | solution.py:19
  17.6 5.8 %collective-permute-start.7 = (bf16[16,4096]{1,0:T(8,128)(2,1)S(1)}, bf16[16,4096]{1,0:T(8,128)(2,1)S(1)}, u32[]{:S(2)}, u32[]{:S(2)}) collective-permute-start(bf16[16,4096]{1,0:T(8,128)(2,1)S(1)} %collective-permute-done.6), channel_id=1, source_target_pairs={{0,2},{1,3},{2,0},{3,1},{4,6},{5,7},{6,4},{7,5},{8,10},{9,11},{10,... | collective-permute-start | bytes 393224 | tf_op jit(solution)/shard_map/ppermute | solution.py:19
  18.5 6.3 %collective-permute-start.9 = (bf16[16,4096]{1,0:T(8,128)(2,1)S(1)}, bf16[16,4096]{1,0:T(8,128)(2,1)S(1)}, u32[]{:S(2)}, u32[]{:S(2)}) collective-permute-start(bf16[16,4096]{1,0:T(8,128)(2,1)S(1)} %collective-permute-done.8), channel_id=1, source_target_pairs={{0,2},{1,3},{2,0},{3,1},{4,6},{5,7},{6,4},{7,5},{8,10},{9,11},{10,... | collective-permute-start | bytes 393224 | tf_op jit(solution)/shard_map/ppermute | solution.py:19
  21.1 10.3 %collective-permute-start.5 = (bf16[64,4096]{1,0:T(8,128)(2,1)S(1)}, bf16[64,4096]{1,0:T(8,128)(2,1)S(1)}, u32[]{:S(2)}, u32[]{:S(2)}) collective-permute-start(bf16[64,4096]{1,0:T(8,128)(2,1)S(1)} %pad_maximum_fusion.4), channel_id=1, source_target_pairs={{0,1},{1,0},{2,3},{3,2},{4,5},{5,4},{6,7},{7,6},{8,9},{9,8},{10,11... | collective-permute-start | bytes 1572872 | tf_op jit(solution)/shard_map/ppermute | solution.py:19
  24.8 11.9 %collective-permute-start.10 = (bf16[64,4096]{1,0:T(8,128)(2,1)S(1)}, bf16[64,4096]{1,0:T(8,128)(2,1)S(1)}, u32[]{:S(2)}, u32[]{:S(2)}) collective-permute-start(bf16[64,4096]{1,0:T(8,128)(2,1)S(1)} %pad_maximum_fusion.5), channel_id=1, source_target_pairs={{0,1},{1,0},{2,3},{3,2},{4,5},{5,4},{6,7},{7,6},{8,9},{9,8},{10,11... | collective-permute-start | bytes 1572872 | tf_op jit(solution)/shard_map/ppermute | solution.py:19
  25.5 4.3 %copy-start.2 = (bf16[128,2048]{1,0:T(8,128)(2,1)}, bf16[128,2048]{1,0:T(8,128)(2,1)S(1)}, u32[]{:S(2)}) copy-start(bf16[128,2048]{1,0:T(8,128)(2,1)S(1)} %collective-permute-done) | copy-start | bytes 1572868
  25.5 15.9 %copy-start.13 = (bf16[1,4096,1280]{2,1,0:T(8,128)(2,1)S(1)}, bf16[1,4096,1280]{2,1,0:T(8,128)(2,1)}, u32[]{:S(2)}) copy-start(bf16[1,4096,1280]{2,1,0:T(8,128)(2,1)} %param.10) | copy-start | bytes 31457284
  29.8 8.9 %copy-start.1 = (f32[256,1280]{1,0:T(8,128)}, f32[256,1280]{1,0:T(8,128)S(1)}, u32[]{:S(2)}) copy-start(f32[256,1280]{1,0:T(8,128)S(1)} %fusion.9) | copy-start | bytes 3932164
  29.8 3.6 %copy-start.6 = (bf16[16,4096]{1,0:T(8,128)(2,1)S(1)}, bf16[16,4096]{1,0:T(8,128)(2,1)}, u32[]{:S(2)}) copy-start(bf16[16,4096]{1,0:T(8,128)(2,1)} %copy-done.5) | copy-start | bytes 393220
  29.9 17.9 %collective-permute-start.1 = (f32[128,1280]{1,0:T(8,128)S(1)}, f32[128,1280]{1,0:T(8,128)}, u32[]{:S(2)}, u32[]{:S(2)}) collective-permute-start(f32[128,1280]{1,0:T(8,128)S(1)} %slice.121), channel_id=1, source_target_pairs={{0,16},{16,0},{1,17},{17,1},{2,18},{18,2},{3,19},{19,3},{4,20},{20... | collective-permute-start | bytes 1966088 | tf_op jit(solution)/shard_map/ppermute | solution.py:19
  41.4 6.3 %copy-start.9 = (f32[256,1]{0,1:T(1,128)S(1)}, f32[256,1]{0,1:T(1,128)}, u32[]{:S(2)}) copy-start(f32[256,1]{0,1:T(1,128)} %convert_element_type.85) | copy-start | bytes 3076
  46.0 8.7 %copy-start.14 = (s32[128]{0:T(128)S(1)}, s32[128]{0:T(128)}, u32[]{:S(2)}) copy-start(s32[128]{0:T(128)} %param.15) | copy-start | bytes 1540
  50.1 12.7 %all-to-all-start = ((f32[32,5,128]{2,1,0:T(8,128)}), f32[32,5,128]{2,1,0:T(8,128)S(1)}, u32[]{:S(2)}, u32[]{:S(2)}) async-start(f32[32,5,128]{2,1,0:T(8,128)} %bitcast.10), calls=%async_computation | async-start | bytes 262144 | tf_op jit(solution)/shard_map/all_to_all | solution.py:144
  54.7 11.3 %collective-permute-start.11 = (bf16[128,1280]{1,0:T(8,128)(2,1)S(1)}, bf16[128,1280]{1,0:T(8,128)(2,1)}, u32[]{:S(2)}, u32[]{:S(2)}) collective-permute-start(bf16[128,1280]{1,0:T(8,128)(2,1)S(1)} %slice.137), channel_id=1, source_target_pairs={{0,16},{16,0},{1,17},{17,1},{2,18},{18,2},{3,19},{19,3},{4,20},{20... | collective-permute-start | bytes 983048 | tf_op jit(solution)/shard_map/ppermute | solution.py:19
  68.0 9.2 %collective-permute-start.12 = (bf16[128,1280]{1,0:T(8,128)(2,1)S(1)}, bf16[128,1280]{1,0:T(8,128)(2,1)S(1)}, u32[]{:S(2)}, u32[]{:S(2)}) collective-permute-start(bf16[128,1280]{1,0:T(8,128)(2,1)S(1)} %get-tuple-element.4), channel_id=1, source_target_pairs={{0,16},{16,0},{1,17},{17,1},{2,18},{18,2},{3,19},{19,3},{4,20},{20... | collective-permute-start | bytes 983048 | tf_op jit(solution)/shard_map/ppermute | solution.py:19
  87.5 59.2 %copy-start.3 = (bf16[128,2048]{1,0:T(8,128)(2,1)S(1)}, bf16[128,2048]{1,0:T(8,128)(2,1)}, u32[]{:S(2)}) copy-start(bf16[128,2048]{1,0:T(8,128)(2,1)} %copy-done.2) | copy-start | bytes 1572868
  87.5 2.0 %collective-permute-start.13 = (bf16[8,128,256]{2,1,0:T(8,128)(2,1)S(1)}, bf16[8,128,256]{2,1,0:T(8,128)(2,1)S(1)}, u32[]{:S(2)}, u32[]{:S(2)}) collective-permute-start(bf16[8,128,256]{2,1,0:T(8,128)(2,1)S(1)} %slice_bitcast_fusion), channel_id=1, source_target_pairs={{0,1},{1,0},{2,3},{3,2},{4,5},{5,4},{6,7},{7,6},{8,9},{9,8},{10,11... | collective-permute-start | bytes 1572872 | tf_op jit(solution)/shard_map/ppermute | solution.py:19
  90.7 8.4 %collective-permute-start.14 = (bf16[4,128,256]{2,1,0:T(8,128)(2,1)S(1)}, bf16[4,128,256]{2,1,0:T(8,128)(2,1)S(1)}, u32[]{:S(2)}, u32[]{:S(2)}) collective-permute-start(bf16[4,128,256]{2,1,0:T(8,128)(2,1)S(1)} %slice_bitcast_fusion.2), channel_id=1, source_target_pairs={{0,2},{1,3},{2,0},{3,1},{4,6},{5,7},{6,4},{7,5},{8,10},{9,11},{10,... | collective-permute-start | bytes 786440 | tf_op jit(solution)/shard_map/ppermute | solution.py:19
  99.8 36.3 %collective-permute-start.15 = (bf16[128,256]{1,0:T(8,128)(2,1)}, bf16[128,256]{1,0:T(8,128)(2,1)S(1)}, u32[]{:S(2)}, u32[]{:S(2)}) collective-permute-start(bf16[128,256]{1,0:T(8,128)(2,1)} %get-tuple-element.17), channel_id=1, source_target_pairs={{0,4},{1,5},{2,6},{3,7},{4,0},{5,1},{6,2},{7,3},{8,12},{9,13},{10,... | collective-permute-start | bytes 196616 | tf_op jit(solution)/shard_map/ppermute | solution.py:19
  101.4 34.7 %collective-permute-start.17 = (bf16[128,256]{1,0:T(8,128)(2,1)}, bf16[128,256]{1,0:T(8,128)(2,1)S(1)}, u32[]{:S(2)}, u32[]{:S(2)}) collective-permute-start(bf16[128,256]{1,0:T(8,128)(2,1)} %get-tuple-element.18), channel_id=1, source_target_pairs={{0,12},{1,13},{2,14},{3,15},{4,8},{5,9},{6,10},{7,11},{8,4},{9,5},... | collective-permute-start | bytes 196616 | tf_op jit(solution)/shard_map/ppermute | solution.py:19
  103.9 32.2 %collective-permute-start.16 = (bf16[128,256]{1,0:T(8,128)(2,1)S(1)}, bf16[128,256]{1,0:T(8,128)(2,1)S(1)}, u32[]{:S(2)}, u32[]{:S(2)}) collective-permute-start(bf16[128,256]{1,0:T(8,128)(2,1)S(1)} %get-tuple-element.19), channel_id=1, source_target_pairs={{0,8},{1,9},{2,10},{3,11},{4,12},{5,13},{6,14},{7,15},{8,0},{9,1},... | collective-permute-start | bytes 196616 | tf_op jit(solution)/shard_map/ppermute | solution.py:19
  136.2 1.4 collective-permute-start.18
  139.0 13.4 %collective-permute-start.19 = (f32[256]{0:T(256)S(1)}, f32[256]{0:T(256)S(1)}, u32[]{:S(2)}, u32[]{:S(2)}) collective-permute-start(f32[256]{0:T(256)S(1)} %get-tuple-element.11), channel_id=1, source_target_pairs={{0,16},{16,0},{1,17},{17,1},{2,18},{18,2},{3,19},{19,3},{4,20},{20... | collective-permute-start | bytes 3080 | tf_op jit(solution)/shard_map/ppermute | solution.py:19

commit v2 on v1

v2 whole, which is shorter than its diff:
```python
import functools

import jax
import jax.numpy as jnp
from jax import lax
from jax.experimental import pallas as pl
from jax.experimental.pallas import tpu as pltpu
from jax.sharding import PartitionSpec as P

DEN = 64

eps = 1e-05
mix_label = 0.25
loss_scale = 64.0


def swap(value, axis, flip):
    size = lax.axis_size(axis)
    return lax.ppermute(value, axis, [(i, i ^ flip) for i in range(size)])


def normalize(hidden, gain):
    values = hidden.astype(jnp.float32)
    inv_scale = lax.rsqrt(jnp.mean(values * values, axis=-1, keepdims=True) + eps)
    return ((values * inv_scale * gain).astype(jnp.bfloat16), inv_scale)


def gather_blocks(block, size):
    got = {0: block}
    for k in range(4, size, 4):
        got[k] = swap(block, "tok", k)
    for k in range(0, size, 4):
        got[k + 2] = swap(got[k], "tok", 2)
    evens = sorted(got)
    half = len(evens) // 2
    arrays = [got[k] for k in evens]
    keys = [(k,) for k in evens]
    for group in (evens[:half], evens[half:]):
        arrays.append(swap(jnp.concatenate([got[k] for k in group], axis=0), "tok", 1))
        keys.append(tuple(k + 1 for k in group))
    return arrays, tuple(keys)


def tile_of(cols):
    return next((tile for tile in (256, 128) if cols % tile == 0), cols)


def column(row):
    count = row.shape[1]
    return jnp.transpose(jnp.broadcast_to(row, (128, count)))[:, :1]


def as_row(col):
    return jnp.transpose(jnp.broadcast_to(col, (col.shape[0], 128)))[:1]


def teacher_kernel(keys, half, place_ref, *refs):
    blocks = refs[: len(keys)]
    w_ref, exp_ref, stat_ref, rows_ref, logits_ref = refs[len(keys) :]
    step = pl.program_id(0)

    @pl.when(step == 0)
    def _():
        mine = place_ref[1] ^ (place_ref[0] * half)
        for ref, owned in zip(blocks, keys):
            count = ref.shape[0] // len(owned)
            for j, k in enumerate(owned):
                start = pl.multiple_of((mine ^ k) * count, count)
                rows_ref[pl.ds(start, count), :] = ref[j * count : (j + 1) * count, :]

    tile = w_ref.shape[2]
    place = pl.ds(pl.multiple_of(step * tile, tile), tile) if tile < logits_ref.shape[1] else slice(None)
    logits_ref[:, place] = jnp.dot(rows_ref[...], w_ref[0], preferred_element_type=jnp.float32)

    @pl.when(step == pl.num_programs(0) - 1)
    def _():
        logits = logits_ref[...]
        top = jnp.max(logits, axis=1, keepdims=True)
        scaled = jnp.exp(logits - top)
        exp_ref[...] = scaled.astype(exp_ref.dtype)
        stat_ref[0:1, :] = as_row(top)
        stat_ref[1:2, :] = as_row(jnp.sum(scaled, axis=1, keepdims=True))


def teacher_softmax(got, keys, head, place, half):
    width, cols = head.shape[1:]
    tokens = sum(part.shape[0] for part in got)
    tile = tile_of(cols)
    return pl.pallas_call(
        functools.partial(teacher_kernel, keys, half),
        out_shape=(
            jax.ShapeDtypeStruct((tokens, cols), jnp.bfloat16),
            jax.ShapeDtypeStruct((2, tokens), jnp.float32),
        ),
        grid_spec=pltpu.PrefetchScalarGridSpec(
            num_scalar_prefetch=1,
            grid=(cols // tile,),
            in_specs=[pl.BlockSpec(part.shape, lambda i, place: (0, 0)) for part in got]
            + [pl.BlockSpec((1, width, tile), lambda i, place: (0, 0, i))],
            out_specs=(
                pl.BlockSpec((tokens, cols), lambda i, place: (0, 0)),
                pl.BlockSpec((2, tokens), lambda i, place: (0, 0)),
            ),
            scratch_shapes=[pltpu.VMEM((tokens, width), jnp.bfloat16), pltpu.VMEM((tokens, cols), jnp.float32)],
        ),
        cost_estimate=pl.CostEstimate(
            flops=2 * tokens * width * cols, bytes_accessed=2 * width * cols, transcendentals=tokens * cols
        ),
        name="teacher",
    )(place, *got, head)


def stats_kernel(count, place_ref, *refs):
    parts = refs[:count]
    teacher_ref, weight_ref, logits_ref, out_ref = refs[count:]
    logits = parts[0][...]
    for ref in parts[1:]:
        logits = logits + ref[...]
    logits_ref[...] = logits
    top = jnp.max(logits, axis=1, keepdims=True)
    total = jnp.sum(jnp.exp(logits - top), axis=1, keepdims=True)
    rows = logits.shape[0]
    size = out_ref.shape[0] // count
    student = jnp.concatenate([as_row(top), as_row(total)], axis=0)
    for r in range(count):
        there = place_ref[0] ^ r
        block = jnp.concatenate(
            [
                teacher_ref[:, r * rows : (r + 1) * rows],
                student,
                weight_ref[pl.ds(there, 1), :],
                jnp.zeros((3, rows), jnp.float32),
            ],
            axis=0,
        )
        out_ref[pl.ds(there * size, size)] = jnp.broadcast_to(block[None], (size, 8, rows))


def student_stats(parts, teacher_stats, weights, place, size):
    rows, cols = parts[0].shape
    count = len(parts)
    vmem = pl.BlockSpec(memory_space=pltpu.VMEM)
    return pl.pallas_call(
        functools.partial(stats_kernel, count),
        out_shape=(
            jax.ShapeDtypeStruct((rows, cols), jnp.float32),
            jax.ShapeDtypeStruct((count * size, 8, rows), jnp.float32),
        ),
        in_specs=[pl.BlockSpec(memory_space=pltpu.SMEM)] + [vmem] * (count + 2),
        out_specs=(vmem, vmem),
        cost_estimate=pl.CostEstimate(flops=8 * rows * cols, bytes_accessed=12 * rows * cols, transcendentals=rows * cols),
        name="stats",
    )(place, *parts, teacher_stats, weights)


def grads_kernel(count, size, place_ref, stats_ref, logits_ref, ids_ref, *refs):
    terms = refs[:count]
    grads_ref, dots_ref = refs[count:]
    b, t = place_ref[0], place_ref[1]
    rows, cols = logits_ref.shape
    logits = logits_ref[...]
    shard = lax.broadcasted_iota(jnp.int32, (rows, cols), 1)
    targets = jnp.where(shard == ids_ref[...] - t * cols, mix_label, 0.0)
    probs = None
    for r in range(count):
        start = (b ^ r) * size
        block = stats_ref[pl.ds(start, size)]
        here = stats_ref[start + t]
        peak = jnp.max(block[:, 0, :], axis=0, keepdims=True)
        total = jnp.sum(block[:, 1, :] * jnp.exp(block[:, 0, :] - peak), axis=0, keepdims=True)
        scale = ((1.0 - mix_label) / DEN) * here[4:5] * jnp.exp(here[0:1] - peak) / total
        targets = targets + terms[r][...].astype(jnp.float32) * column(scale)
        if r == 0:
            peak = jnp.max(block[:, 2, :], axis=0, keepdims=True)
            total = jnp.sum(block[:, 3, :] * jnp.exp(block[:, 2, :] - peak), axis=0, keepdims=True)
            probs = jnp.exp(logits - column(peak)) / column(total)
    grads = (loss_scale * (probs - targets)).astype(grads_ref.dtype)
    grads_ref[...] = grads
    dots = as_row(jnp.sum(grads.astype(jnp.float32) * logits, axis=1, keepdims=True))
    dots_ref[...] = jnp.broadcast_to(dots[None], dots_ref.shape)


def make_grads(stats, logits, ids, terms, place, size):
    rows, cols = logits.shape
    count = len(terms)
    vmem = pl.BlockSpec(memory_space=pltpu.VMEM)
    return pl.pallas_call(
        functools.partial(grads_kernel, count, size),
        out_shape=(
            jax.ShapeDtypeStruct((rows, cols), jnp.bfloat16),
            jax.ShapeDtypeStruct((size, 8, rows), jnp.float32),
        ),
        in_specs=[pl.BlockSpec(memory_space=pltpu.SMEM)] + [vmem] * (count + 3),
        out_specs=(vmem, vmem),
        cost_estimate=pl.CostEstimate(flops=16 * rows * cols, bytes_accessed=10 * rows * cols, transcendentals=rows * cols),
        name="grads",
    )(place, stats, logits, ids, *terms)


def pieces_kernel(count, place_ref, *refs):
    grads = refs[:count]
    w_ref, out_ref, turned_ref = refs[count:]
    rows = grads[0].shape[0]

    @pl.when(pl.program_id(0) == 0)
    def _():
        for r in range(count):
            turned_ref[:, r * rows : (r + 1) * rows] = jnp.transpose(grads[r][...])

    acc = jnp.dot(w_ref[...], turned_ref[...], preferred_element_type=jnp.float32)
    parts = [acc[:, r * rows : (r + 1) * rows].astype(out_ref.dtype) for r in range(count)]
    for k in range(count):
        for r in range(count):

            @pl.when((place_ref[3] ^ k) == r)
            def _():
                out_ref[k, 0] = parts[r]


def normed_grad_pieces(grads, head, place, blocks):
    count = len(grads)
    rows, cols = grads[0].shape
    width = head.shape[0] // blocks
    return pl.pallas_call(
        functools.partial(pieces_kernel, count),
        out_shape=jax.ShapeDtypeStruct((count, blocks, width, rows), jnp.bfloat16),
        grid_spec=pltpu.PrefetchScalarGridSpec(
            num_scalar_prefetch=1,
            grid=(blocks,),
            in_specs=[pl.BlockSpec((rows, cols), lambda i, place: (0, 0))] * count
            + [pl.BlockSpec((width, cols), lambda i, place: (i ^ place[2], 0))],
            out_specs=pl.BlockSpec((count, 1, width, rows), lambda i, place: (0, i, 0, 0)),
            scratch_shapes=[pltpu.VMEM((cols, count * rows), jnp.bfloat16)],
        ),
        cost_estimate=pl.CostEstimate(
            flops=2 * count * rows * cols * head.shape[0], bytes_accessed=2 * head.size, transcendentals=0
        ),
        name="pieces",
    )(place, *grads, head)


def per_device(
    teacher_hidden,
    teacher_gain,
    teacher_head,
    student_hidden,
    student_gain,
    student_head,
    cluster_weights,
    token_ids,
):
    branches = lax.axis_size("branch")
    size = lax.axis_size("tok")
    b = lax.axis_index("branch")
    t = lax.axis_index("tok")
    rows, width = student_hidden.shape
    part = width // branches
    blocks = size // branches
    f32 = jnp.float32
    place = jnp.stack([b, t, t % blocks, (t // blocks) ^ b]).astype(jnp.int32)

    student_normed, inv_scale = normalize(student_hidden, student_gain)
    core = t % 2
    half = rows // 2

    def fetched(r):
        sent = lax.dynamic_slice(student_normed, (core * half, (b ^ r) * part), (half, part))
        mine = swap(sent, "branch", r)
        other = swap(mine, "tok", 1)
        first = core == 0
        return jnp.concatenate([jnp.where(first, mine, other), jnp.where(first, other, mine)], axis=0)

    student_parts = [lax.dynamic_slice_in_dim(student_normed, b * part, part, 1)]
    student_parts += [fetched(r) for r in range(1, branches)]
    own_partial = jnp.dot(student_parts[0], student_head, preferred_element_type=f32)
    partials = [own_partial]
    for r in range(1, branches):
        partial = jnp.dot(student_parts[r], student_head, preferred_element_type=f32)
        partials.append(swap(partial, "branch", r))

    teacher_block, unused = normalize(teacher_hidden[0], teacher_gain[0])
    got, keys = gather_blocks(teacher_block, size)
    teacher_exp, teacher_stats = teacher_softmax(got, keys, teacher_head, place, blocks)
    terms = [teacher_exp[:rows]] + [
        swap(teacher_exp[r * rows : (r + 1) * rows], "branch", r) for r in range(1, branches)
    ]

    weights = cluster_weights[:, 0].astype(f32).reshape(branches, rows)
    logits, stats = student_stats(partials, teacher_stats, weights, place, size)
    stats = lax.all_to_all(stats, ("branch", "tok"), 0, 0, tiled=True)
    logit_grads, dots = make_grads(stats, logits, token_ids[:, None], terms, place, size)
    all_grads = [logit_grads] + [swap(logit_grads, "branch", r) for r in range(1, branches)]
    dots = lax.all_to_all(dots, "tok", 0, 0, tiled=True)
    row_dots = jnp.sum(dots[:, 0], axis=0) / inv_scale[:, 0]

    pieces = normed_grad_pieces(all_grads, student_head, place, blocks)
    piece = (width // size, rows)
    pieces = pieces.reshape(size // 2, 2, *piece)
    pieces = (pieces[:, 0].astype(f32) + swap(pieces[:, 1], "tok", 1).astype(f32)).astype(jnp.bfloat16)
    pieces = pieces.reshape(size // 4, 2, *piece)
    pair = pieces[:, 0].astype(f32) + swap(pieces[:, 1], "tok", 2).astype(f32)
    sent = pair.astype(jnp.bfloat16)
    normed_grads = pair[0]
    for k in range(1, size // 4):
        normed_grads = normed_grads + swap(sent[k], "tok", 4 * k).astype(f32)
    perm = []
    for i in range(branches * size):
        bb, h, q = i // size, (i % size) // blocks, i % blocks
        perm.append((i, (h * branches + bb) * blocks + q))
    normed_grads = lax.ppermute(normed_grads, ("branch", "tok"), perm).T

    slice_width = width // size
    hidden_cols = lax.dynamic_slice_in_dim(student_hidden, t * slice_width, slice_width, 1).astype(f32)
    gain_cols = lax.dynamic_slice_in_dim(student_gain, t * slice_width, slice_width, 0)
    grad_gain = jnp.sum(normed_grads * hidden_cols * inv_scale, axis=0)
    flip = 1
    while flip < branches:
        grad_gain = grad_gain + swap(grad_gain, "branch", flip)
        flip *= 2
    grad_hidden = (
        inv_scale * gain_cols[None, :] * normed_grads
        - hidden_cols * inv_scale**3 * row_dots[:, None] / width
    )
    grad_head = lax.dot_general(
        jnp.concatenate(student_parts, axis=0),
        jnp.concatenate(all_grads, axis=0),
        (((0,), (0,)), ((), ())),
        preferred_element_type=f32,
    )
    return (grad_head, grad_hidden, grad_gain)


def solution(mesh):
    in_specs = (
        P("branch", "tok", None),
        P("branch", None),
        P("branch", None, "tok"),
        P("branch", None),
        P(),
        P("branch", "tok"),
        P(None, "branch"),
        P("branch"),
    )
    out_specs = (P("branch", "tok"), P("branch", "tok"), P("tok"))
    return jax.shard_map(
        per_device, mesh=mesh, in_specs=in_specs, out_specs=out_specs, check_vma=False
    )
```

time: 154 us -> 131 us (0.85)
  blocking collectives: 31.5 us -> 0 us
  Pallas kernels: 8.4 us -> 23.1 us
  local copies, waits for them, and re-layouts: 17.5 us -> 11.2 us
  waiting for transfers between devices: 30.5 us -> 35 us
  other arithmetic: 13.4 us -> 9.01 us
    psum x1 -> x0, blocking collectives: 31.5 us -> none  [per_device(): row_dots = lax.psum(dots, 'tok') / inv_scale[:, 0]]
    pallas_call x1 -> x4, Pallas kernels: 8.4 us -> 23.1 us  [the longest x1 9.65 us: teacher_softmax(): pl.pallas_call(functools.partial(teacher_kernel, keys, half), out_shape=(...]
    dynamic_update_slice x15 -> x0, local copies, waits for them, and re-layouts: 9.95 us -> none  [per_device(): lax.dynamic_update_slice_in_dim(teacher_rows, got[k], place * count, 0)]
    unnamed x34, local copies, waits for them, and re-layouts: 0.65 us -> 4.52 us
    all_to_all x1 -> x2, starting transfers between devices: 4.49 us -> 7.99 us  [the longest x1 4.27 us: per_device(): stats = lax.all_to_all(stats, ('branch', 'tok'), 0, 0, tiled=True)]
    all_to_all x1 -> x2, waiting for transfers between devices: 6.32 us -> 9.03 us  [the longest x1 7.45 us: per_device(): stats = lax.all_to_all(stats, ('branch', 'tok'), 0, 0, tiled=True)]
    ppermute x19 -> x20, starting transfers between devices: 31.1 us -> 28.8 us  [swap(): return lax.ppermute(value, axis, [(i, i ^ flip) for i in range(size)])]
    reduce_sum x4 -> x1, other arithmetic: 2.3 us -> 0.03 us  [per_device(): row_dots = jnp.sum(dots[:, 0], axis=0) / inv_scale[:, 0]]
  transfers between devices with their start and end apart: 21 -> 23, of which waited for: 11 -> 11; matrix products, arithmetic and copies ran while one was open for 20% -> 19% of each run, Pallas kernels for 0% -> 9%
where the time goes in v2:
time: 131 us; the launch traced here: 130 us
  starting transfers between devices  37.5 us (29%)
  waiting for transfers between devices  35 us (27%)
  Pallas kernels  23.1 us (18%)
  matrix products  13.2 us (10%)
  local copies, waits for them, and re-layouts  11.2 us (9%)
  other arithmetic  9.01 us (7%)
    ppermute x20, starting transfers between devices, swap(): return lax.ppermute(value, axis, [(i, i ^ flip) for i in range(size)])  28.8 us
    ppermute x20, waiting for transfers between devices, swap(): return lax.ppermute(value, axis, [(i, i ^ flip) for i in range(size)])  26 us
    pallas_call x1, Pallas kernels, teacher_softmax(): pl.pallas_call(functools.partial(teacher_kernel, keys, half), out_shape=(...  9.65 us
    pallas_call x1, Pallas kernels, normed_grad_pieces(): pl.pallas_call(functools.partial(pieces_kernel, count), out_shape=jax.Sha...  8.51 us
    all_to_all x1, waiting for transfers between devices, per_device(): stats = lax.all_to_all(stats, ('branch', 'tok'), 0, 0, tiled=True)  7.45 us
    dot_general x1, matrix products, per_device(): lax.dot_general(jnp.concatenate(student_parts, axis=0), jnp.concatenate(a...  5.66 us
    unnamed x34, local copies, waits for them, and re-layouts  4.52 us
    all_to_all x1, starting transfers between devices, per_device(): stats = lax.all_to_all(stats, ('branch', 'tok'), 0, 0, tiled=True)  4.27 us
  transfers between devices with their start and end apart: 23, of which 11 were waited for; matrix products, arithmetic and copies ran while one was open for 19% of the time, Pallas kernels for 9%

profile of v2, /device:TPU:0, one launch (start us, length us, event | category | flops | bytes accessed | tf_op | source)
XLA Modules:
  0.0 129.9 jit_solution(12672525364226944438)
XLA Ops:
  0.6 1.1 fusion.17
  1.8 1.0 fusion.19.refs_0_
  2.8 5.1 %collective-permute-start.8 = (bf16[16,4096]{1,0:T(8,128)(2,1)S(1)}, bf16[16,4096]{1,0:T(8,128)(2,1)S(1)}, u32[]{:S(2)}, u32[]{:S(2)}) collective-permute-start(bf16[16,4096]{1,0:T(8,128)(2,1)S(1)} %fusion.19.refs_0_), channel_id=1, source_target_pairs={{0,12},{1,13},{2,14},{3,15},{4,8},{5,9},{6,10},{7,11},{8,4},{9,5},... | collective-permute-start | bytes 393224 | tf_op jit(solution)/shard_map/ppermute | solution.py:19
  8.0 0.6 collective-permute-start.4
  8.6 1.7 %collective-permute-start.3 = (bf16[16,4096]{1,0:T(8,128)(2,1)S(1)}, bf16[16,4096]{1,0:T(8,128)(2,1)S(1)}, u32[]{:S(2)}, u32[]{:S(2)}) collective-permute-start(bf16[16,4096]{1,0:T(8,128)(2,1)S(1)} %fusion.19.refs_0_), channel_id=1, source_target_pairs={{0,2},{1,3},{2,0},{3,1},{4,6},{5,7},{6,4},{7,5},{8,10},{9,11},{10,... | collective-permute-start | bytes 393224 | tf_op jit(solution)/shard_map/ppermute | solution.py:19
  10.3 1.5 %fusion = f32[128]{0:T(128)S(1)} fusion(bf16[128,4096]{1,0:T(8,128)(2,1)} %param.11), kind=kLoop, calls=%fused_computation.2 | loop fusion | flops 1572736 | bytes 1049088 | tf_op jit(solution)/shard_map/reduce_sum | solution.py:24
  11.8 1.0 fusion.2
  12.9 0.7 dynamic_slice.13
  13.6 1.5 %collective-permute-start = (bf16[64,2048]{1,0:T(8,128)(2,1)}, bf16[64,2048]{1,0:T(8,128)(2,1)}, u32[]{:S(2)}, u32[]{:S(2)}) collective-permute-start(bf16[64,2048]{1,0:T(8,128)(2,1)} %dynamic_slice.13), channel_id=1, source_target_pairs={{0,16},{16,0},{1,17},{17,1},{2,18},{18,2},{3,19},{19,3},{4,20},{20... | collective-permute-start | bytes 786440 | tf_op jit(solution)/shard_map/ppermute | solution.py:19
  15.6 3.4 %collective-permute-done.6.refs_4_ = bf16[16,4096]{1,0:T(8,128)(2,1)S(1)} collective-permute-done((bf16[16,4096]{1,0:T(8,128)(2,1)S(1)}, bf16[16,4096]{1,0:T(8,128)(2,1)S(1)}, u32[]{:S(2)}, u32[]{:S(2)}) %collective-permute-start.6) | collective-permute-done | bytes 131104 | tf_op jit(solution)/shard_map/ppermute | solution.py:19
  19.0 1.5 %collective-permute-start.7 = (bf16[16,4096]{1,0:T(8,128)(2,1)S(1)}, bf16[16,4096]{1,0:T(8,128)(2,1)S(1)}, u32[]{:S(2)}, u32[]{:S(2)}) collective-permute-start(bf16[16,4096]{1,0:T(8,128)(2,1)S(1)} %collective-permute-done.6.refs_4_), channel_id=1, source_target_pairs={{0,2},{1,3},{2,0},{3,1},{4,6},{5,7},{6,4},{7,5},{8,10},{9,11},{10,... | collective-permute-start | bytes 393224 | tf_op jit(solution)/shard_map/ppermute | solution.py:19
  21.8 3.5 %collective-permute-done.7.refs_5_ = bf16[16,4096]{1,0:T(8,128)(2,1)S(1)} collective-permute-done((bf16[16,4096]{1,0:T(8,128)(2,1)S(1)}, bf16[16,4096]{1,0:T(8,128)(2,1)S(1)}, u32[]{:S(2)}, u32[]{:S(2)}) %collective-permute-start.7) | collective-permute-done | bytes 131104 | tf_op jit(solution)/shard_map/ppermute | solution.py:19
  25.9 0.9 collective-permute-done.5.refs_3_
  27.7 1.0 broadcast_select_fusion.1
  28.7 3.3 %fusion.13 = f32[128,1280]{1,0:T(8,128)S(1)} fusion(bf16[2048,1280]{1,0:T(8,128)(2,1)} %refs_2_.1, bf16[64,2048]{1,0:T(8,128)(2,1)S(1)} %get-tuple-element.23, bf16[64,2048]{1,0:T(8,128)(2,1)S(1)} %get-tuple-element.22), kind=kOutput, calls=%fused_computation.18 | convolution fusion | flops 672137216 | bytes 6422528 | tf_op jit(solution)/shard_map/dot_general | solution.py:278
  32.1 1.6 %collective-permute-start.2 = (f32[128,1280]{1,0:T(8,128)S(1)}, f32[128,1280]{1,0:T(8,128)S(1)}, u32[]{:S(2)}, u32[]{:S(2)}) collective-permute-start(f32[128,1280]{1,0:T(8,128)S(1)} %fusion.13), channel_id=1, source_target_pairs={{0,16},{16,0},{1,17},{17,1},{2,18},{18,2},{3,19},{19,3},{4,20},{20... | collective-permute-start | bytes 1966088 | tf_op jit(solution)/shard_map/ppermute | solution.py:19
  33.6 9.7 %teacher.1 = (bf16[256,1280]{1,0:T(8,128)(2,1)}, f32[2,256]{1,0:T(2,128)}) custom-call(s32[4]{0:T(128)} %pad_add_fusion.place_ref, bf16[16,4096]{1,0:T(8,128)(2,1)} %copy-done.4, bf16[16,4096]{1,0:T(8,128)(2,1)} %copy-done.9, bf16[16,4096]{1,0:T(8,128)(2,1)} %copy-done.8, bf16[16,4096]{1,0:T(8,128)(2,1)} %copy-done.12, bf16[16,4096]{1,0:T(8,128)(2,1)} %copy-done.7, ...), custom_call_target="tpu_custom_call" | custom-call | flops 2684354560 | bytes 10485760 | tf_op jit(solution)/shard_map/teacher/pallas_call | solution.py:89
  43.3 2.0 %fusion.32 = (bf16[128,1280]{1,0:T(8,128)(2,1)}, bf16[128,1280]{1,0:T(8,128)(2,1)}) fusion(bf16[256,1280]{1,0:T(8,128)(2,1)} %get-tuple-element.12), kind=kLoop, calls=%fused_computation.61 | loop fusion | bytes 1310720 | tf_op jit(solution)/shard_map/slice | solution.py:285
  45.8 4.2 %fusion.33.refs_0_ = f32[128,1280]{1,0:T(8,128)} fusion(bf16[128,2048]{1,0:T(8,128)(2,1)S(1)} %constant_dynamic-slice_fusion.1, bf16[2048,1280]{1,0:T(8,128)(2,1)} %refs_2_.1), kind=kOutput, calls=%fused_computation.62 | convolution fusion | flops 671088640 | bytes 6422528 | tf_op jit(solution)/shard_map/dot_general | solution.py:275
  50.5 0.9 copy-done.5
  51.4 2.3 %stats.1 = (f32[128,1280]{1,0:T(8,128)}, f32[32,8,128]{2,1,0:T(8,128)}) custom-call(s32[4]{0:T(128)} %pad_add_fusion.place_ref, f32[128,1280]{1,0:T(8,128)} %fusion.33.refs_0_, f32[128,1280]{1,0:T(8,128)} %copy-done.5, f32[2,256]{1,0:T(2,128)} %get-tuple-element.9.refs_2_, f32[2,128]{1,0:T(2,128)} %bitcast.62), custom_call_target="tpu_custom_call" | custom-call | flops 1310720 | bytes 1966080 | tf_op jit(solution)/shard_map/stats/pallas_call | solution.py:143
  53.6 4.3 %all-to-all-start = ((f32[32,8,128]{2,1,0:T(8,128)}), f32[32,8,128]{2,1,0:T(8,128)S(1)}, u32[]{:S(2)}, u32[]{:S(2)}) async-start(f32[32,8,128]{2,1,0:T(8,128)} %get-tuple-element.10), calls=%async_computation | async-start | bytes 262144 | tf_op jit(solution)/shard_map/all_to_all | solution.py:290
  57.9 0.7 copy.13.ids_ref
  58.7 7.4 %all-to-all-done.stats_ref = f32[32,8,128]{2,1,0:T(8,128)S(1)} async-done(((f32[32,8,128]{2,1,0:T(8,128)}), f32[32,8,128]{2,1,0:T(8,128)S(1)}, u32[]{:S(2)}, u32[]{:S(2)}) %all-to-all-start) | async-done | bytes 131104 | tf_op jit(solution)/shard_map/all_to_all | solution.py:290
  66.1 0.7 copy-done.13
  66.8 2.7 %grads.1 = (bf16[128,1280]{1,0:T(8,128)(2,1)}, f32[16,8,128]{2,1,0:T(8,128)}) custom-call(s32[4]{0:T(128)} %pad_add_fusion.place_ref, f32[32,8,128]{2,1,0:T(8,128)} %copy-done.13, f32[128,1280]{1,0:T(8,128)} %get-tuple-element.11.logits_ref, s32[128,1]{1,0:T(8,128)} %copy.13.ids_ref, bf16[128,1280]{1,0:T(8,128)(2,1)} %get-tuple-element.21.refs_0_, ...), custom_call_target="tpu_custom_call" | custom-call | flops 2621440 | bytes 1638400 | tf_op jit(solution)/shard_map/grads/pallas_call | solution.py:187
  69.4 0.8 collective-permute-start.13
  70.2 9.3 %collective-permute-done.13.refs_1_ = bf16[128,1280]{1,0:T(8,128)(2,1)S(1)} collective-permute-done((bf16[128,1280]{1,0:T(8,128)(2,1)}, bf16[128,1280]{1,0:T(8,128)(2,1)S(1)}, u32[]{:S(2)}, u32[]{:S(2)}) %collective-permute-start.13) | collective-permute-done | bytes 327712 | tf_op jit(solution)/shard_map/ppermute | solution.py:19
  79.5 0.7 copy-done.2
  80.3 8.5 %pieces.1 = bf16[2,8,256,128]{3,2,1,0:T(8,128)(2,1)} custom-call(s32[4]{0:T(128)} %pad_add_fusion.place_ref, bf16[128,1280]{1,0:T(8,128)(2,1)} %get-tuple-element.13.refs_0_, bf16[128,1280]{1,0:T(8,128)(2,1)} %copy-done.2, bf16[2048,1280]{1,0:T(8,128)(2,1)} %refs_2_.1), custom_call_target="tpu_custom_call" | custom-call | flops 1342177280 | bytes 5242880 | tf_op jit(solution)/shard_map/pieces/pallas_call | solution.py:224
  88.8 1.1 slice_bitcast_fusion
  89.9 1.9 %collective-permute-done.14 = bf16[8,256,128]{2,1,0:T(8,128)(2,1)S(1)} collective-permute-done((bf16[8,256,128]{2,1,0:T(8,128)(2,1)S(1)}, bf16[8,256,128]{2,1,0:T(8,128)(2,1)S(1)}, u32[]{:S(2)}, u32[]{:S(2)}) %collective-permute-start.14) | collective-permute-done | bytes 524320 | tf_op jit(solution)/shard_map/ppermute | solution.py:19
  91.8 1.2 fusion.9
  93.0 0.7 slice_bitcast_fusion.2
  94.0 0.8 dynamic_slice.14
  94.8 0.6 constant_dynamic-slice_fusion
  95.4 0.9 copy.22
  96.4 3.7 %all-to-all-start.1 = ((f32[16,8,128]{2,1,0:T(8,128)}), f32[16,8,128]{2,1,0:T(8,128)S(1)}, u32[]{:S(2)}, u32[]{:S(2)}) async-start(f32[16,8,128]{2,1,0:T(8,128)} %get-tuple-element.14), calls=%async_computation.1 | async-start | bytes 131072 | tf_op jit(solution)/shard_map/all_to_all | solution.py:293
  100.1 2.2 %collective-permute-done.15 = bf16[4,256,128]{2,1,0:T(8,128)(2,1)S(1)} collective-permute-done((bf16[4,256,128]{2,1,0:T(8,128)(2,1)}, bf16[4,256,128]{2,1,0:T(8,128)(2,1)S(1)}, u32[]{:S(2)}, u32[]{:S(2)}) %collective-permute-start.15) | collective-permute-done | bytes 262176 | tf_op jit(solution)/shard_map/ppermute | solution.py:19
  102.5 2.1 %collective-permute-start.18 = (bf16[256,128]{1,0:T(8,128)(2,1)S(1)}, bf16[256,128]{1,0:T(8,128)(2,1)S(1)}, u32[]{:S(2)}, u32[]{:S(2)}) collective-permute-start(bf16[256,128]{1,0:T(8,128)(2,1)S(1)} %get-tuple-element.25), channel_id=1, source_target_pairs={{0,12},{1,13},{2,14},{3,15},{4,8},{5,9},{6,10},{7,11},{8,4},{9,5},... | collective-permute-start | bytes 196616 | tf_op jit(solution)/shard_map/ppermute | solution.py:19
  104.6 1.4 %collective-permute-start.17 = (bf16[256,128]{1,0:T(8,128)(2,1)S(1)}, bf16[256,128]{1,0:T(8,128)(2,1)S(1)}, u32[]{:S(2)}, u32[]{:S(2)}) collective-permute-start(bf16[256,128]{1,0:T(8,128)(2,1)S(1)} %get-tuple-element.26), channel_id=1, source_target_pairs={{0,8},{1,9},{2,10},{3,11},{4,12},{5,13},{6,14},{7,15},{8,0},{9,1},... | collective-permute-start | bytes 196616 | tf_op jit(solution)/shard_map/ppermute | solution.py:19
  106.0 1.6 %all-to-all-done.1 = f32[16,8,128]{2,1,0:T(8,128)S(1)} async-done(((f32[16,8,128]{2,1,0:T(8,128)}), f32[16,8,128]{2,1,0:T(8,128)S(1)}, u32[]{:S(2)}, u32[]{:S(2)}) %all-to-all-start.1) | async-done | bytes 65568 | tf_op jit(solution)/shard_map/all_to_all | solution.py:293
  107.6 1.9 %collective-permute-done.18 = bf16[256,128]{1,0:T(8,128)(2,1)S(1)} collective-permute-done((bf16[256,128]{1,0:T(8,128)(2,1)S(1)}, bf16[256,128]{1,0:T(8,128)(2,1)S(1)}, u32[]{:S(2)}, u32[]{:S(2)}) %collective-permute-start.18) | collective-permute-done | bytes 65568 | tf_op jit(solution)/shard_map/ppermute | solution.py:19
  109.5 2.7 %collective-permute-done.17 = bf16[256,128]{1,0:T(8,128)(2,1)S(1)} collective-permute-done((bf16[256,128]{1,0:T(8,128)(2,1)S(1)}, bf16[256,128]{1,0:T(8,128)(2,1)S(1)}, u32[]{:S(2)}, u32[]{:S(2)}) %collective-permute-start.17) | collective-permute-done | bytes 65568 | tf_op jit(solution)/shard_map/ppermute | solution.py:19
  112.2 0.7 collective-permute-start.19
  113.0 9.9 %collective-permute-start.20 = (f32[256]{0:T(256)S(1)}, f32[256]{0:T(256)S(1)}, u32[]{:S(2)}, u32[]{:S(2)}) collective-permute-start(f32[256]{0:T(256)S(1)} %get-tuple-element.27), channel_id=1, source_target_pairs={{0,16},{16,0},{1,17},{17,1},{2,18},{18,2},{3,19},{19,3},{4,20},{20... | collective-permute-start | bytes 3080 | tf_op jit(solution)/shard_map/ppermute | solution.py:19
  123.0 5.7 %fusion.3 = f32[2048,1280]{1,0:T(8,128)} fusion(bf16[64,2048]{1,0:T(8,128)(2,1)S(1)} %get-tuple-element.23, bf16[64,2048]{1,0:T(8,128)(2,1)S(1)} %get-tuple-element.22, bf16[128,2048]{1,0:T(8,128)(2,1)S(1)} %constant_dynamic-slice_fusion.1, bf16[128,1280]{1,0:T(8,128)(2,1)S(1)} %copy-done.3, bf16[128,1280]{1,0:T(8,128)(2,1)S(1)} %copy-done.1), kind=kOutput, calls=%fused_computation.5 | convolution fusion | flops 1346633728 | bytes 12189696 | tf_op jit(solution)/shard_map/dot_general | solution.py:324
  128.6 0.8 copy.18
  (66 shorter events, 5.7 us)
Async XLA Ops:
  0.6 11.2 %copy-start = (bf16[128,4096]{1,0:T(8,128)(2,1)S(1)}, bf16[128,4096]{1,0:T(8,128)(2,1)}, u32[]{:S(2)}) copy-start(bf16[128,4096]{1,0:T(8,128)(2,1)} %param.11) | copy-start | bytes 3145732
  2.8 24.0 %copy-start.4 = (bf16[16,4096]{1,0:T(8,128)(2,1)}, bf16[16,4096]{1,0:T(8,128)(2,1)S(1)}, u32[]{:S(2)}) copy-start(bf16[16,4096]{1,0:T(8,128)(2,1)S(1)} %fusion.19.refs_0_) | copy-start | bytes 393220
  2.8 12.3 %collective-permute-start.8 = (bf16[16,4096]{1,0:T(8,128)(2,1)S(1)}, bf16[16,4096]{1,0:T(8,128)(2,1)S(1)}, u32[]{:S(2)}, u32[]{:S(2)}) collective-permute-start(bf16[16,4096]{1,0:T(8,128)(2,1)S(1)} %fusion.19.refs_0_), channel_id=1, source_target_pairs={{0,12},{1,13},{2,14},{3,15},{4,8},{5,9},{6,10},{7,11},{8,4},{9,5},... | collective-permute-start | bytes 393224 | tf_op jit(solution)/shard_map/ppermute | solution.py:19
  8.0 11.1 %collective-permute-start.6 = (bf16[16,4096]{1,0:T(8,128)(2,1)S(1)}, bf16[16,4096]{1,0:T(8,128)(2,1)S(1)}, u32[]{:S(2)}, u32[]{:S(2)}) collective-permute-start(bf16[16,4096]{1,0:T(8,128)(2,1)S(1)} %fusion.19.refs_0_), channel_id=1, source_target_pairs={{0,8},{1,9},{2,10},{3,11},{4,12},{5,13},{6,14},{7,15},{8,0},{9,1},... | collective-permute-start | bytes 393224 | tf_op jit(solution)/shard_map/ppermute | solution.py:19
  8.0 13.3 %collective-permute-start.4 = (bf16[16,4096]{1,0:T(8,128)(2,1)S(1)}, bf16[16,4096]{1,0:T(8,128)(2,1)S(1)}, u32[]{:S(2)}, u32[]{:S(2)}) collective-permute-start(bf16[16,4096]{1,0:T(8,128)(2,1)S(1)} %fusion.19.refs_0_), channel_id=1, source_target_pairs={{0,4},{1,5},{2,6},{3,7},{4,0},{5,1},{6,2},{7,3},{8,12},{9,13},{10,... | collective-permute-start | bytes 393224 | tf_op jit(solution)/shard_map/ppermute | solution.py:19
  8.6 17.3 %collective-permute-start.3 = (bf16[16,4096]{1,0:T(8,128)(2,1)S(1)}, bf16[16,4096]{1,0:T(8,128)(2,1)S(1)}, u32[]{:S(2)}, u32[]{:S(2)}) collective-permute-start(bf16[16,4096]{1,0:T(8,128)(2,1)S(1)} %fusion.19.refs_0_), channel_id=1, source_target_pairs={{0,2},{1,3},{2,0},{3,1},{4,6},{5,7},{6,4},{7,5},{8,10},{9,11},{10,... | collective-permute-start | bytes 393224 | tf_op jit(solution)/shard_map/ppermute | solution.py:19
  13.6 11.8 %collective-permute-start = (bf16[64,2048]{1,0:T(8,128)(2,1)}, bf16[64,2048]{1,0:T(8,128)(2,1)}, u32[]{:S(2)}, u32[]{:S(2)}) collective-permute-start(bf16[64,2048]{1,0:T(8,128)(2,1)} %dynamic_slice.13), channel_id=1, source_target_pairs={{0,16},{16,0},{1,17},{17,1},{2,18},{18,2},{3,19},{19,3},{4,20},{20... | collective-permute-start | bytes 786440 | tf_op jit(solution)/shard_map/ppermute | solution.py:19
  15.1 13.6 %copy-start.6 = (bf16[16,4096]{1,0:T(8,128)(2,1)}, bf16[16,4096]{1,0:T(8,128)(2,1)S(1)}, u32[]{:S(2)}) copy-start(bf16[16,4096]{1,0:T(8,128)(2,1)S(1)} %collective-permute-done.8.refs_6_) | copy-start | bytes 393220
  15.1 6.7 %collective-permute-start.9 = (bf16[16,4096]{1,0:T(8,128)(2,1)S(1)}, bf16[16,4096]{1,0:T(8,128)(2,1)S(1)}, u32[]{:S(2)}, u32[]{:S(2)}) collective-permute-start(bf16[16,4096]{1,0:T(8,128)(2,1)S(1)} %collective-permute-done.8.refs_6_), channel_id=1, source_target_pairs={{0,2},{1,3},{2,0},{3,1},{4,6},{5,7},{6,4},{7,5},{8,10},{9,11},{10,... | collective-permute-start | bytes 393224 | tf_op jit(solution)/shard_map/ppermute | solution.py:19
  19.0 9.6 %copy-start.7 = (bf16[16,4096]{1,0:T(8,128)(2,1)}, bf16[16,4096]{1,0:T(8,128)(2,1)S(1)}, u32[]{:S(2)}) copy-start(bf16[16,4096]{1,0:T(8,128)(2,1)S(1)} %collective-permute-done.6.refs_4_) | copy-start | bytes 393220
  19.0 6.2 %collective-permute-start.7 = (bf16[16,4096]{1,0:T(8,128)(2,1)S(1)}, bf16[16,4096]{1,0:T(8,128)(2,1)S(1)}, u32[]{:S(2)}, u32[]{:S(2)}) collective-permute-start(bf16[16,4096]{1,0:T(8,128)(2,1)S(1)} %collective-permute-done.6.refs_4_), channel_id=1, source_target_pairs={{0,2},{1,3},{2,0},{3,1},{4,6},{5,7},{6,4},{7,5},{8,10},{9,11},{10,... | collective-permute-start | bytes 393224 | tf_op jit(solution)/shard_map/ppermute | solution.py:19
  21.3 7.4 %copy-start.8 = (bf16[16,4096]{1,0:T(8,128)(2,1)}, bf16[16,4096]{1,0:T(8,128)(2,1)S(1)}, u32[]{:S(2)}) copy-start(bf16[16,4096]{1,0:T(8,128)(2,1)S(1)} %collective-permute-done.4.refs_2_) | copy-start | bytes 393220
  21.3 5.6 %collective-permute-start.5 = (bf16[16,4096]{1,0:T(8,128)(2,1)S(1)}, bf16[16,4096]{1,0:T(8,128)(2,1)S(1)}, u32[]{:S(2)}, u32[]{:S(2)}) collective-permute-start(bf16[16,4096]{1,0:T(8,128)(2,1)S(1)} %collective-permute-done.4.refs_2_), channel_id=1, source_target_pairs={{0,2},{1,3},{2,0},{3,1},{4,6},{5,7},{6,4},{7,5},{8,10},{9,11},{10,... | collective-permute-start | bytes 393224 | tf_op jit(solution)/shard_map/ppermute | solution.py:19
  21.8 6.9 %copy-start.10 = (bf16[16,4096]{1,0:T(8,128)(2,1)}, bf16[16,4096]{1,0:T(8,128)(2,1)S(1)}, u32[]{:S(2)}) copy-start(bf16[16,4096]{1,0:T(8,128)(2,1)S(1)} %collective-permute-done.9.refs_7_) | copy-start | bytes 393220
  25.3 3.4 %copy-start.11 = (bf16[16,4096]{1,0:T(8,128)(2,1)}, bf16[16,4096]{1,0:T(8,128)(2,1)S(1)}, u32[]{:S(2)}) copy-start(bf16[16,4096]{1,0:T(8,128)(2,1)S(1)} %collective-permute-done.7.refs_5_) | copy-start | bytes 393220
  25.3 8.3 %collective-permute-start.11 = (bf16[64,4096]{1,0:T(8,128)(2,1)S(1)}, bf16[64,4096]{1,0:T(8,128)(2,1)}, u32[]{:S(2)}, u32[]{:S(2)}) collective-permute-start(bf16[64,4096]{1,0:T(8,128)(2,1)S(1)} %pad_maximum_fusion.1), channel_id=1, source_target_pairs={{0,1},{1,0},{2,3},{3,2},{4,5},{5,4},{6,7},{7,6},{8,9},{9,8},{10,11... | collective-permute-start | bytes 1572872 | tf_op jit(solution)/shard_map/ppermute | solution.py:19
  25.4 2.3 %collective-permute-start.1 = (bf16[64,2048]{1,0:T(8,128)(2,1)}, bf16[64,2048]{1,0:T(8,128)(2,1)S(1)}, u32[]{:S(2)}, u32[]{:S(2)}) collective-permute-start(bf16[64,2048]{1,0:T(8,128)(2,1)} %collective-permute-done), channel_id=1, source_target_pairs={{0,1},{1,0},{2,3},{3,2},{4,5},{5,4},{6,7},{7,6},{8,9},{9,8},{10,11... | collective-permute-start | bytes 786440 | tf_op jit(solution)/shard_map/ppermute | solution.py:19
  25.9 2.8 %copy-start.9 = (bf16[16,4096]{1,0:T(8,128)(2,1)}, bf16[16,4096]{1,0:T(8,128)(2,1)S(1)}, u32[]{:S(2)}) copy-start(bf16[16,4096]{1,0:T(8,128)(2,1)S(1)} %collective-permute-done.3.refs_1_) | copy-start | bytes 393220
  26.8 0.7 copy-start.12
  26.9 6.8 %collective-permute-start.10 = (bf16[64,4096]{1,0:T(8,128)(2,1)S(1)}, bf16[64,4096]{1,0:T(8,128)(2,1)}, u32[]{:S(2)}, u32[]{:S(2)}) collective-permute-start(bf16[64,4096]{1,0:T(8,128)(2,1)S(1)} %pad_maximum_fusion), channel_id=1, source_target_pairs={{0,1},{1,0},{2,3},{3,2},{4,5},{5,4},{6,7},{7,6},{8,9},{9,8},{10,11... | collective-permute-start | bytes 1572872 | tf_op jit(solution)/shard_map/ppermute | solution.py:19
  32.1 18.5 %collective-permute-start.2 = (f32[128,1280]{1,0:T(8,128)S(1)}, f32[128,1280]{1,0:T(8,128)S(1)}, u32[]{:S(2)}, u32[]{:S(2)}) collective-permute-start(f32[128,1280]{1,0:T(8,128)S(1)} %fusion.13), channel_id=1, source_target_pairs={{0,16},{16,0},{1,17},{17,1},{2,18},{18,2},{3,19},{19,3},{4,20},{20... | collective-permute-start | bytes 1966088 | tf_op jit(solution)/shard_map/ppermute | solution.py:19
  45.2 4.7 %copy-start.14 = (s32[256,1]{0,1:T(1,128)S(1)}, s32[256,1]{0,1:T(1,128)}, u32[]{:S(2)}) copy-start(s32[256,1]{0,1:T(1,128)} %param.14) | copy-start | bytes 3076
  45.2 12.7 %copy-start.15 = (s32[128]{0:T(128)S(1)}, s32[128]{0:T(128)}, u32[]{:S(2)}) copy-start(s32[128]{0:T(128)} %param.15) | copy-start | bytes 1540
  45.2 13.4 %collective-permute-start.12 = (bf16[128,1280]{1,0:T(8,128)(2,1)}, bf16[128,1280]{1,0:T(8,128)(2,1)}, u32[]{:S(2)}, u32[]{:S(2)}) collective-permute-start(bf16[128,1280]{1,0:T(8,128)(2,1)} %get-tuple-element.20), channel_id=1, source_target_pairs={{0,16},{16,0},{1,17},{17,1},{2,18},{18,2},{3,19},{19,3},{4,20},{20... | collective-permute-start | bytes 983048 | tf_op jit(solution)/shard_map/ppermute | solution.py:19
  50.5 0.9 copy-start.5
  53.6 12.5 %all-to-all-start = ((f32[32,8,128]{2,1,0:T(8,128)}), f32[32,8,128]{2,1,0:T(8,128)S(1)}, u32[]{:S(2)}, u32[]{:S(2)}) async-start(f32[32,8,128]{2,1,0:T(8,128)} %get-tuple-element.10), calls=%async_computation | async-start | bytes 262144 | tf_op jit(solution)/shard_map/all_to_all | solution.py:290
  66.1 0.7 copy-start.13
  69.4 10.1 %collective-permute-start.13 = (bf16[128,1280]{1,0:T(8,128)(2,1)}, bf16[128,1280]{1,0:T(8,128)(2,1)S(1)}, u32[]{:S(2)}, u32[]{:S(2)}) collective-permute-start(bf16[128,1280]{1,0:T(8,128)(2,1)} %get-tuple-element.13.refs_0_), channel_id=1, source_target_pairs={{0,16},{16,0},{1,17},{17,1},{2,18},{18,2},{3,19},{19,3},{4,20},{20... | collective-permute-start | bytes 983048 | tf_op jit(solution)/shard_map/ppermute | solution.py:19
  79.5 0.7 copy-start.2
  89.8 2.0 %collective-permute-start.14 = (bf16[8,256,128]{2,1,0:T(8,128)(2,1)S(1)}, bf16[8,256,128]{2,1,0:T(8,128)(2,1)S(1)}, u32[]{:S(2)}, u32[]{:S(2)}) collective-permute-start(bf16[8,256,128]{2,1,0:T(8,128)(2,1)S(1)} %slice_bitcast_fusion), channel_id=1, source_target_pairs={{0,1},{1,0},{2,3},{3,2},{4,5},{5,4},{6,7},{7,6},{8,9},{9,8},{10,11... | collective-permute-start | bytes 1572872 | tf_op jit(solution)/shard_map/ppermute | solution.py:19
  93.0 29.9 %copy-start.1 = (bf16[128,1280]{1,0:T(8,128)(2,1)S(1)}, bf16[128,1280]{1,0:T(8,128)(2,1)}, u32[]{:S(2)}) copy-start(bf16[128,1280]{1,0:T(8,128)(2,1)} %get-tuple-element.13.refs_0_) | copy-start | bytes 983044
  93.0 29.9 %copy-start.3 = (bf16[128,1280]{1,0:T(8,128)(2,1)S(1)}, bf16[128,1280]{1,0:T(8,128)(2,1)}, u32[]{:S(2)}) copy-start(bf16[128,1280]{1,0:T(8,128)(2,1)} %copy-done.2) | copy-start | bytes 983044
  93.8 8.6 %collective-permute-start.15 = (bf16[4,256,128]{2,1,0:T(8,128)(2,1)}, bf16[4,256,128]{2,1,0:T(8,128)(2,1)S(1)}, u32[]{:S(2)}, u32[]{:S(2)}) collective-permute-start(bf16[4,256,128]{2,1,0:T(8,128)(2,1)} %slice_bitcast_fusion.2), channel_id=1, source_target_pairs={{0,2},{1,3},{2,0},{3,1},{4,6},{5,7},{6,4},{7,5},{8,10},{9,11},{10,... | collective-permute-start | bytes 786440 | tf_op jit(solution)/shard_map/ppermute | solution.py:19
  96.4 11.1 %all-to-all-start.1 = ((f32[16,8,128]{2,1,0:T(8,128)}), f32[16,8,128]{2,1,0:T(8,128)S(1)}, u32[]{:S(2)}, u32[]{:S(2)}) async-start(f32[16,8,128]{2,1,0:T(8,128)} %get-tuple-element.14), calls=%async_computation.1 | async-start | bytes 131072 | tf_op jit(solution)/shard_map/all_to_all | solution.py:293
  102.4 5.2 %collective-permute-start.16 = (bf16[256,128]{1,0:T(8,128)(2,1)S(1)}, bf16[256,128]{1,0:T(8,128)(2,1)S(1)}, u32[]{:S(2)}, u32[]{:S(2)}) collective-permute-start(bf16[256,128]{1,0:T(8,128)(2,1)S(1)} %get-tuple-element.24), channel_id=1, source_target_pairs={{0,4},{1,5},{2,6},{3,7},{4,0},{5,1},{6,2},{7,3},{8,12},{9,13},{10,... | collective-permute-start | bytes 196616 | tf_op jit(solution)/shard_map/ppermute | solution.py:19
  102.5 7.0 %collective-permute-start.18 = (bf16[256,128]{1,0:T(8,128)(2,1)S(1)}, bf16[256,128]{1,0:T(8,128)(2,1)S(1)}, u32[]{:S(2)}, u32[]{:S(2)}) collective-permute-start(bf16[256,128]{1,0:T(8,128)(2,1)S(1)} %get-tuple-element.25), channel_id=1, source_target_pairs={{0,12},{1,13},{2,14},{3,15},{4,8},{5,9},{6,10},{7,11},{8,4},{9,5},... | collective-permute-start | bytes 196616 | tf_op jit(solution)/shard_map/ppermute | solution.py:19
  104.6 7.5 %collective-permute-start.17 = (bf16[256,128]{1,0:T(8,128)(2,1)S(1)}, bf16[256,128]{1,0:T(8,128)(2,1)S(1)}, u32[]{:S(2)}, u32[]{:S(2)}) collective-permute-start(bf16[256,128]{1,0:T(8,128)(2,1)S(1)} %get-tuple-element.26), channel_id=1, source_target_pairs={{0,8},{1,9},{2,10},{3,11},{4,12},{5,13},{6,14},{7,15},{8,0},{9,1},... | collective-permute-start | bytes 196616 | tf_op jit(solution)/shard_map/ppermute | solution.py:19
  112.2 0.7 collective-permute-start.19
  113.0 16.4 %collective-permute-start.20 = (f32[256]{0:T(256)S(1)}, f32[256]{0:T(256)S(1)}, u32[]{:S(2)}, u32[]{:S(2)}) collective-permute-start(f32[256]{0:T(256)S(1)} %get-tuple-element.27), channel_id=1, source_target_pairs={{0,16},{16,0},{1,17},{17,1},{2,18},{18,2},{3,19},{19,3},{4,20},{20... | collective-permute-start | bytes 3080 | tf_op jit(solution)/shard_map/ppermute | solution.py:19

commit v3 on v2

v3 whole, which is shorter than its diff:
```python
import functools

import jax
import jax.numpy as jnp
from jax import lax
from jax.experimental import pallas as pl
from jax.experimental.pallas import tpu as pltpu
from jax.sharding import PartitionSpec as P


DEN = 64

eps = 1e-05
mix_label = 0.25
loss_scale = 64.0


def swap(value, axis, flip):
    size = lax.axis_size(axis)
    return lax.ppermute(value, axis, [(i, i ^ flip) for i in range(size)])


VMEM = pl.BlockSpec(memory_space=pltpu.VMEM)
SMEM = pl.BlockSpec(memory_space=pltpu.SMEM)
MIB = 1 << 20


def params(mib):
    return pltpu.CompilerParams(vmem_limit_bytes=mib * MIB)


def cost(flops, nbytes, exps=0):
    return pl.CostEstimate(flops=flops, bytes_accessed=nbytes, transcendentals=exps)


def first_kernel(branches, place_ref, th_ref, tg_ref, sh_ref, sg_ref, block_ref, own_ref, inv_ref, *refs):
    sent, normed_ref = refs[:-1], refs[-1]
    values = th_ref[0].astype(jnp.float32)
    scale = lax.rsqrt(jnp.mean(values * values, axis=-1, keepdims=True) + eps)
    block_ref[...] = (values * scale * tg_ref[...]).astype(jnp.bfloat16)
    values = sh_ref[...].astype(jnp.float32)
    scale = lax.rsqrt(jnp.mean(values * values, axis=-1, keepdims=True) + eps)
    inv_ref[...] = scale
    normed_ref[...] = (values * scale * sg_ref[...]).astype(jnp.bfloat16)
    part = own_ref.shape[1]
    half = own_ref.shape[0] // 2
    b = place_ref[0]
    own_ref[...] = normed_ref[:, pl.ds(pl.multiple_of(b * part, part), part)]
    start = pl.multiple_of((place_ref[1] % 2) * half, half)
    for r in range(1, branches):
        cols = pl.ds(pl.multiple_of((b ^ r) * part, part), part)
        sent[r - 1][...] = normed_ref[pl.ds(start, half), cols]


def normalize_all(teacher_hidden, teacher_gain, student_hidden, student_gain, place, branches):
    rows, width = student_hidden.shape
    part = width // branches
    bf16 = jnp.bfloat16
    return pl.pallas_call(
        functools.partial(first_kernel, branches),
        out_shape=(
            jax.ShapeDtypeStruct(teacher_hidden.shape[1:], bf16),
            jax.ShapeDtypeStruct((rows, part), bf16),
            jax.ShapeDtypeStruct((rows, 1), jnp.float32),
            *[jax.ShapeDtypeStruct((rows // 2, part), bf16)] * (branches - 1),
        ),
        in_specs=[SMEM] + [VMEM] * 4,
        out_specs=(VMEM,) * (2 + branches),
        scratch_shapes=[pltpu.VMEM((rows, width), bf16)],
        compiler_params=params(16),
        cost_estimate=cost(8 * rows * width, 4 * rows * width),
        name="first",
    )(place, teacher_hidden, teacher_gain, student_hidden, student_gain[None])


def gather_blocks(block, size):
    got = {0: block}
    for k in range(4, size, 4):
        got[k] = swap(block, "tok", k)
    for k in range(0, size, 4):
        got[k + 2] = swap(got[k], "tok", 2)
    evens = sorted(got)
    half = len(evens) // 2
    arrays = [got[k] for k in evens]
    keys = [(k,) for k in evens]
    for group in (evens[:half], evens[half:]):
        arrays.append(swap(jnp.concatenate([got[k] for k in group], axis=0), "tok", 1))
        keys.append(tuple(k + 1 for k in group))
    return arrays, tuple(keys)


def own_dot_kernel(rows_ref, w_ref, out_ref):
    out_ref[...] = jnp.dot(rows_ref[...], w_ref[...], preferred_element_type=jnp.float32)


def own_dot(rows, head):
    return pl.pallas_call(
        own_dot_kernel,
        out_shape=jax.ShapeDtypeStruct((rows.shape[0], head.shape[1]), jnp.float32),
        in_specs=[VMEM, VMEM],
        out_specs=VMEM,
        compiler_params=params(16),
        cost_estimate=cost(2 * rows.size * head.shape[1], 2 * head.size),
        name="owndot",
    )(rows, head)


def other_dot_kernel(place_ref, mine_ref, other_ref, w_ref, out_ref, rows_ref):
    half = mine_ref.shape[0]
    core = place_ref[1] % 2
    rows_ref[pl.ds(pl.multiple_of(core * half, half), half), :] = mine_ref[...]
    rows_ref[pl.ds(pl.multiple_of((1 - core) * half, half), half), :] = other_ref[...]
    out_ref[...] = jnp.dot(rows_ref[...], w_ref[...], preferred_element_type=jnp.float32)


def other_dot(mine, other, head, place):
    rows = 2 * mine.shape[0]
    return pl.pallas_call(
        other_dot_kernel,
        out_shape=(
            jax.ShapeDtypeStruct((rows, head.shape[1]), jnp.float32),
            jax.ShapeDtypeStruct((rows, mine.shape[1]), jnp.bfloat16),
        ),
        in_specs=[SMEM, VMEM, VMEM, VMEM],
        out_specs=(VMEM, VMEM),
        compiler_params=params(16),
        cost_estimate=cost(2 * rows * head.size, 2 * head.size),
        name="otherdot",
    )(place, mine, other, head)


def tile_of(cols):
    return next((tile for tile in (256, 128) if cols % tile == 0), cols)


def column(row):
    count = row.shape[1]
    return jnp.transpose(jnp.broadcast_to(row, (128, count)))[:, :1]


def as_row(col):
    return jnp.transpose(jnp.broadcast_to(col, (col.shape[0], 128)))[:1]


def teacher_kernel(keys, half, place_ref, *refs):
    blocks = refs[: len(keys)]
    w_ref, stat_ref, *exps = refs[len(keys) : -2]
    rows_ref, logits_ref = refs[-2:]
    mine = place_ref[1] ^ (place_ref[0] * half)
    for ref, owned in zip(blocks, keys):
        count = ref.shape[0] // len(owned)
        for j, k in enumerate(owned):
            start = pl.multiple_of((mine ^ k) * count, count)
            rows_ref[pl.ds(start, count), :] = ref[j * count : (j + 1) * count, :]

    cols = w_ref.shape[2]
    tile = tile_of(cols)
    if tile == cols:
        logits_ref[...] = jnp.dot(rows_ref[...], w_ref[0], preferred_element_type=jnp.float32)
    else:

        @pl.loop(0, cols // tile)
        def _(step):
            at = pl.ds(pl.multiple_of(step * tile, tile), tile)
            logits_ref[:, at] = jnp.dot(rows_ref[...], w_ref[0, :, at], preferred_element_type=jnp.float32)

    logits = logits_ref[...]
    top = jnp.max(logits, axis=1, keepdims=True)
    scaled = jnp.exp(logits - top)
    rows = exps[0].shape[0]
    for r, ref in enumerate(exps):
        ref[...] = scaled[r * rows : (r + 1) * rows].astype(ref.dtype)
    stat_ref[0:1, :] = as_row(top)
    stat_ref[1:2, :] = as_row(jnp.sum(scaled, axis=1, keepdims=True))


def teacher_softmax(got, keys, head, place, half, branches):
    width, cols = head.shape[1:]
    tokens = sum(part.shape[0] for part in got)
    return pl.pallas_call(
        functools.partial(teacher_kernel, keys, half),
        out_shape=(
            jax.ShapeDtypeStruct((2, tokens), jnp.float32),
            *[jax.ShapeDtypeStruct((tokens // branches, cols), jnp.bfloat16)] * branches,
        ),
        in_specs=[SMEM] + [VMEM] * (len(got) + 1),
        out_specs=(VMEM,) * (1 + branches),
        scratch_shapes=[pltpu.VMEM((tokens, width), jnp.bfloat16), pltpu.VMEM((tokens, cols), jnp.float32)],
        compiler_params=params(28),
        cost_estimate=cost(2 * tokens * width * cols, 2 * width * cols, tokens * cols),
        name="teacher",
    )(place, *got, head)


def stats_kernel(count, place_ref, *refs):
    parts = refs[:count]
    teacher_ref, weight_ref, logits_ref, out_ref = refs[count:]
    logits = parts[0][...]
    for ref in parts[1:]:
        logits = logits + ref[...]
    logits_ref[...] = logits
    top = jnp.max(logits, axis=1, keepdims=True)
    total = jnp.sum(jnp.exp(logits - top), axis=1, keepdims=True)
    rows = logits.shape[0]
    size = out_ref.shape[0] // count
    student = jnp.concatenate([as_row(top), as_row(total)], axis=0)
    for r in range(count):
        there = place_ref[0] ^ r
        block = jnp.concatenate(
            [
                teacher_ref[:, r * rows : (r + 1) * rows],
                student,
                weight_ref[pl.ds(there, 1), :].astype(jnp.float32),
                jnp.zeros((3, rows), jnp.float32),
            ],
            axis=0,
        )
        out_ref[pl.ds(there * size, size)] = jnp.broadcast_to(block[None], (size, 8, rows))


def student_stats(parts, teacher_stats, weights, place, size):
    rows, cols = parts[0].shape
    count = len(parts)
    return pl.pallas_call(
        functools.partial(stats_kernel, count),
        out_shape=(
            jax.ShapeDtypeStruct((rows, cols), jnp.float32),
            jax.ShapeDtypeStruct((count * size, 8, rows), jnp.float32),
        ),
        in_specs=[SMEM] + [VMEM] * (count + 2),
        out_specs=(VMEM, VMEM),
        compiler_params=params(12),
        cost_estimate=cost(8 * rows * cols, 12 * rows * cols, rows * cols),
        name="stats",
    )(place, *parts, teacher_stats, weights)


def grads_kernel(count, size, place_ref, stats_ref, logits_ref, ids_ref, *refs):
    terms = refs[:count]
    grads_ref, dots_ref = refs[count:]
    b, t = place_ref[0], place_ref[1]
    rows, cols = logits_ref.shape
    logits = logits_ref[...]
    shard = lax.broadcasted_iota(jnp.int32, (rows, cols), 1)
    targets = jnp.where(shard == column(ids_ref[...]) - t * cols, mix_label, 0.0)
    probs = None
    for r in range(count):
        start = (b ^ r) * size
        block = stats_ref[pl.ds(start, size)]
        here = stats_ref[start + t]
        peak = jnp.max(block[:, 0, :], axis=0, keepdims=True)
        total = jnp.sum(block[:, 1, :] * jnp.exp(block[:, 0, :] - peak), axis=0, keepdims=True)
        scale = ((1.0 - mix_label) / DEN) * here[4:5] * jnp.exp(here[0:1] - peak) / total
        targets = targets + terms[r][...].astype(jnp.float32) * column(scale)
        if r == 0:
            peak = jnp.max(block[:, 2, :], axis=0, keepdims=True)
            total = jnp.sum(block[:, 3, :] * jnp.exp(block[:, 2, :] - peak), axis=0, keepdims=True)
            probs = jnp.exp(logits - column(peak)) / column(total)
    grads = (loss_scale * (probs - targets)).astype(grads_ref.dtype)
    grads_ref[...] = grads
    dots = as_row(jnp.sum(grads.astype(jnp.float32) * logits, axis=1, keepdims=True))
    dots_ref[...] = jnp.broadcast_to(dots[None], dots_ref.shape)


def make_grads(stats, logits, ids, terms, place, size):
    rows, cols = logits.shape
    count = len(terms)
    return pl.pallas_call(
        functools.partial(grads_kernel, count, size),
        out_shape=(
            jax.ShapeDtypeStruct((rows, cols), jnp.bfloat16),
            jax.ShapeDtypeStruct((size, 8, rows), jnp.float32),
        ),
        in_specs=[SMEM] + [VMEM] * (count + 3),
        out_specs=(VMEM, VMEM),
        compiler_params=params(12),
        cost_estimate=cost(16 * rows * cols, 10 * rows * cols, rows * cols),
        name="grads",
    )(place, stats, logits, ids, *terms)


def pieces_kernel(place_ref, grads_ref, w_ref, keep_ref, send_ref, turned_ref):
    turned_ref[...] = jnp.transpose(grads_ref[...])
    width = keep_ref.shape[1]
    for q in range(2 * keep_ref.shape[0]):
        acc = jnp.dot(w_ref[q * width : (q + 1) * width], turned_ref[...], preferred_element_type=jnp.float32)
        acc = acc.astype(keep_ref.dtype)
        k = place_ref[2] ^ q

        @pl.when(k % 2 == 0)
        def _():
            keep_ref[k // 2] = acc

        @pl.when(k % 2 == 1)
        def _():
            send_ref[k // 2] = acc


def normed_grad_pieces(grads, head, place, blocks):
    rows, cols = grads.shape
    width = head.shape[0] // blocks
    return pl.pallas_call(
        pieces_kernel,
        out_shape=(jax.ShapeDtypeStruct((blocks // 2, width, rows), jnp.bfloat16),) * 2,
        in_specs=[SMEM, VMEM, VMEM],
        out_specs=(VMEM, VMEM),
        scratch_shapes=[pltpu.VMEM((cols, rows), jnp.bfloat16)],
        compiler_params=params(16),
        cost_estimate=cost(2 * rows * head.size, 2 * head.size),
        name="pieces",
    )(place, grads, head)


def fold_kernel(mine_ref, got_ref, keep_ref, send_ref):
    for k in range(mine_ref.shape[0]):
        total = mine_ref[k].astype(jnp.float32) + got_ref[k].astype(jnp.float32)
        (send_ref if k % 2 else keep_ref)[k // 2] = total.astype(keep_ref.dtype)


def fold(mine, got):
    count, width, rows = mine.shape
    return pl.pallas_call(
        fold_kernel,
        out_shape=(jax.ShapeDtypeStruct((count // 2, width, rows), mine.dtype),) * 2,
        in_specs=[VMEM, VMEM],
        out_specs=(VMEM, VMEM),
        compiler_params=params(8),
        cost_estimate=cost(mine.size, 6 * mine.size),
        name="fold",
    )(mine, got)


def split_kernel(count, place_ref, *refs):
    mine, got, out = refs[:count], refs[count : 2 * count], refs[2 * count :]
    lows = mine[0].shape[0]
    for r in range(count):
        for low in range(lows):
            total = (mine[r][low].astype(jnp.float32) + got[r][low].astype(jnp.float32)).astype(mine[r].dtype)
            for kh in range(count):

                @pl.when((place_ref[3] ^ kh) == r)
                def _():
                    out[kh * lows + low][...] = total


def split(mine, got, place):
    count = len(mine)
    lows, width, rows = mine[0].shape
    return pl.pallas_call(
        functools.partial(split_kernel, count),
        out_shape=(jax.ShapeDtypeStruct((width, rows), mine[0].dtype),) * (count * lows),
        in_specs=[SMEM] + [VMEM] * (2 * count),
        out_specs=(VMEM,) * (count * lows),
        compiler_params=params(8),
        cost_estimate=cost(count * mine[0].size, 6 * count * mine[0].size),
        name="split",
    )(place, *mine, *got)


def load_kernel(from_ref, to_ref, sem):
    copy = pltpu.make_async_copy(from_ref, to_ref, sem)
    copy.start()
    copy.wait()


def load(value):
    return pl.pallas_call(
        load_kernel,
        out_shape=jax.ShapeDtypeStruct(value.shape, value.dtype),
        in_specs=[pl.BlockSpec(memory_space=pltpu.HBM)],
        out_specs=VMEM,
        scratch_shapes=[pltpu.SemaphoreType.DMA],
        compiler_params=params(16),
        cost_estimate=cost(0, 4 * value.size),
        name="load",
    )(value)


def head_grad_kernel(count, *refs):
    grads, parts = refs[:count], refs[count : 2 * count]
    out_ref, grads_ref = refs[2 * count :]
    rows = grads[0].shape[0]

    @pl.when(pl.program_id(0) == 0)
    def _():
        for r in range(count):
            grads_ref[r * rows : (r + 1) * rows, :] = grads[r][...]

    turned = jnp.transpose(jnp.concatenate([ref[...] for ref in parts], axis=0))
    out_ref[...] = jnp.dot(turned, grads_ref[...], preferred_element_type=jnp.float32)


def head_grad(grads, parts):
    count = len(grads)
    rows, cols = grads[0].shape
    part = parts[0].shape[1]
    tile = tile_of(part)
    return pl.pallas_call(
        functools.partial(head_grad_kernel, count),
        out_shape=jax.ShapeDtypeStruct((part, cols), jnp.float32),
        grid=(part // tile,),
        in_specs=[pl.BlockSpec((rows, cols), lambda i: (0, 0))] * count
        + [pl.BlockSpec((rows, tile), lambda i: (0, i))] * count,
        out_specs=pl.BlockSpec((tile, cols), lambda i: (i, 0)),
        scratch_shapes=[pltpu.VMEM((count * rows, cols), jnp.bfloat16)],
        compiler_params=params(16),
        cost_estimate=cost(2 * count * rows * part * cols, 4 * part * cols),
        name="headgrad",
    )(*grads, *parts)


def last_kernel(count, width, dots_ref, inv_ref, hidden_ref, gain_ref, *refs):
    parts = refs[:count]
    out_ref, gain_out_ref = refs[count:]
    total = parts[0][...].astype(jnp.float32)
    for ref in parts[1:]:
        total = total + ref[...].astype(jnp.float32)
    normed_grads = jnp.transpose(total)
    inv = inv_ref[...]
    hidden = hidden_ref[...].astype(jnp.float32)
    scaled = hidden * inv
    gain_out_ref[...] = jnp.sum(normed_grads * scaled, axis=0, keepdims=True)
    row_dots = column(jnp.sum(dots_ref[:, 0, :], axis=0, keepdims=True))
    out_ref[...] = inv * gain_ref[...] * normed_grads - scaled * (inv * row_dots / width)


def finish(parts, dots, inv, hidden, gain, width):
    piece, rows = parts[0].shape
    return pl.pallas_call(
        functools.partial(last_kernel, len(parts), width),
        out_shape=(
            jax.ShapeDtypeStruct((rows, piece), jnp.float32),
            jax.ShapeDtypeStruct((1, piece), jnp.float32),
        ),
        in_specs=[VMEM] * (4 + len(parts)),
        out_specs=(VMEM, VMEM),
        compiler_params=params(12),
        cost_estimate=cost(16 * rows * piece, 12 * rows * piece),
        name="last",
    )(dots, inv, hidden, gain, *parts)


def per_device(
    teacher_hidden,
    teacher_gain,
    teacher_head,
    student_hidden,
    student_gain,
    student_head,
    cluster_weights,
    token_ids,
):
    branches = lax.axis_size("branch")
    size = lax.axis_size("tok")
    b = lax.axis_index("branch")
    t = lax.axis_index("tok")
    rows, width = student_hidden.shape
    blocks = size // branches
    place = jnp.stack([b, t, t % blocks, (t // blocks) ^ b]).astype(jnp.int32)
    teacher_block, own, inv_scale, *sent = normalize_all(
        teacher_hidden, teacher_gain, student_hidden, student_gain, place, branches
    )

    loaded = load(student_head)
    student_parts, partials = [own], []
    for r in range(1, branches):
        mine = swap(sent[r - 1], "branch", r)
        other = swap(mine, "tok", 1)
        partial, fetched = other_dot(mine, other, loaded, place)
        student_parts.append(fetched)
        partials.append(swap(partial, "branch", r))
    partials = [own_dot(own, loaded)] + partials

    got, keys = gather_blocks(teacher_block, size)
    teacher_stats, *exps = teacher_softmax(got, keys, teacher_head, place, blocks, branches)
    terms = [exps[0]] + [swap(exps[r], "branch", r) for r in range(1, branches)]

    weights = cluster_weights[:, 0].reshape(branches, rows)
    logits, stats = student_stats(partials, teacher_stats, weights, place, size)
    stats = lax.all_to_all(stats, ("branch", "tok"), 0, 0, tiled=True)
    logit_grads, dots = make_grads(stats, logits, token_ids[None], terms, place, size)
    all_grads = [logit_grads] + [swap(logit_grads, "branch", r) for r in range(1, branches)]
    dots = lax.all_to_all(dots, "tok", 0, 0, tiled=True)

    kept, got = [], []
    for r in range(branches):
        keep, send = normed_grad_pieces(all_grads[r], loaded, place, blocks)
        keep, send = fold(keep, swap(send, "tok", 1))
        kept.append(keep)
        got.append(swap(send, "tok", 2))
    owned = split(kept, got, place)
    arrived = []
    for kh in range(branches):
        for kl in range(blocks // 4):
            perm = []
            for i in range(branches * size):
                bb, h, l, rest = i // size, (i % size) // blocks, (i % blocks) // 4, i % 4
                perm.append((i, (h ^ kh) * size + bb * blocks + (l ^ kl) * 4 + rest))
            arrived.append(lax.ppermute(owned[kh * (blocks // 4) + kl], ("branch", "tok"), perm))

    grad_head = head_grad(all_grads, student_parts)

    slice_width = width // size
    hidden_cols = lax.dynamic_slice_in_dim(student_hidden, t * slice_width, slice_width, 1)
    gain_cols = lax.dynamic_slice_in_dim(student_gain, t * slice_width, slice_width, 0)
    grad_hidden, grad_gain = finish(arrived, dots, inv_scale, hidden_cols, gain_cols[None], width)
    flip = 1
    while flip < branches:
        grad_gain = grad_gain + swap(grad_gain, "branch", flip)
        flip *= 2
    return (grad_head, grad_hidden, grad_gain[0])


def solution(mesh):
    in_specs = (
        P("branch", "tok", None),
        P("branch", None),
        P("branch", None, "tok"),
        P("branch", None),
        P(),
        P("branch", "tok"),
        P(None, "branch"),
        P("branch"),
    )
    out_specs = (P("branch", "tok"), P("branch", "tok"), P("tok"))
    return jax.shard_map(per_device, mesh=mesh, in_specs=in_specs, out_specs=out_specs, check_vma=False)
```

time: 131 us -> 117 us (0.89)
  matrix products: 13.2 us -> 0 us
  waiting for transfers between devices: 35 us -> 44 us
  other arithmetic: 9.01 us -> 0.71 us
  starting transfers between devices: 37.5 us -> 32.1 us
  Pallas kernels: 23.1 us -> 27.8 us
    dot_general x3 -> x0, matrix products: 13.2 us -> none  [the longest x1 5.66 us: per_device(): lax.dot_general(jnp.concatenate(student_parts, axis=0), jnp.concatenate(a...]
    ppermute x20 -> x19, starting transfers between devices: 28.8 us -> 17.7 us  [swap(): return lax.ppermute(value, axis, [(i, i ^ flip) for i in range(size)])]
    pallas_call x1 -> x11, Pallas kernels: 8.51 us -> 19 us  [the longest x2 7.05 us: normed_grad_pieces(): pl.pallas_call(pieces_kernel, out_shape=(jax.ShapeDtypeStruct((blocks //...]
    ppermute x1 -> x4, waiting for transfers between devices: 0.01 us -> 7.96 us  [per_device(): lax.ppermute(owned[kh * (blocks // 4) + kl], ('branch', 'tok'), perm)]
    ppermute x1 -> x4, starting transfers between devices: 0.67 us -> 6.34 us  [per_device(): lax.ppermute(owned[kh * (blocks // 4) + kl], ('branch', 'tok'), perm)]
    unnamed x34 -> x24, local copies, waits for them, and re-layouts: 4.52 us -> 9.51 us
    pallas_call x1, Pallas kernels: 9.65 us -> 5.35 us  [teacher_softmax(): pl.pallas_call(functools.partial(teacher_kernel, keys, half), out_shape=(...]
    convert_element_type x5 -> x0, other arithmetic: 3.87 us -> none  [the longest x2 2.05 us: normalize(): return ((values * inv_scale * gain).astype(jnp.bfloat16), inv_scale)]
  transfers between devices with their start and end apart: 23 -> 25, of which waited for: 11 -> 12; matrix products, arithmetic and copies ran while one was open for 19% -> 1% of each run, Pallas kernels for 9% -> 20%
where the time goes in v3:
time: 117 us
  waiting for transfers between devices  44 us (38%)
  starting transfers between devices  32.1 us (27%)
  Pallas kernels  27.8 us (24%)
  local copies, waits for them, and re-layouts  11.1 us (9%)
    ppermute x19, waiting for transfers between devices, swap(): return lax.ppermute(value, axis, [(i, i ^ flip) for i in range(size)])  28.8 us
    ppermute x19, starting transfers between devices, swap(): return lax.ppermute(value, axis, [(i, i ^ flip) for i in range(size)])  17.7 us
    unnamed x24, local copies, waits for them, and re-layouts  9.51 us
    ppermute x4, waiting for transfers between devices, per_device(): lax.ppermute(owned[kh * (blocks // 4) + kl], ('branch', 'tok'), perm)  7.96 us
    all_to_all x1, waiting for transfers between devices, per_device(): stats = lax.all_to_all(stats, ('branch', 'tok'), 0, 0, tiled=True)  7.24 us
    pallas_call x2, Pallas kernels, normed_grad_pieces(): pl.pallas_call(pieces_kernel, out_shape=(jax.ShapeDtypeStruct((blocks //...  7.05 us
    ppermute x4, starting transfers between devices, per_device(): lax.ppermute(owned[kh * (blocks // 4) + kl], ('branch', 'tok'), perm)  6.34 us
    pallas_call x1, Pallas kernels, head_grad(): pl.pallas_call(functools.partial(head_grad_kernel, count), out_shape=jax....  6.32 us
  transfers between devices with their start and end apart: 25, of which 12 were waited for; matrix products, arithmetic and copies ran while one was open for 1% of the time, Pallas kernels for 20%

profile of v3, /device:TPU:0, one launch (start us, length us, event | category | flops | bytes accessed | tf_op | source)
XLA Modules:
  0.0 116.6 jit_solution(5666904179627562315)
XLA Ops:
  0.7 1.4 %copy-done.3 = bf16[128,4096]{1,0:T(8,128)(2,1)S(1)} copy-done((bf16[128,4096]{1,0:T(8,128)(2,1)S(1)}, bf16[128,4096]{1,0:T(8,128)(2,1)}, u32[]{:S(2)}) %copy-start.3) | copy-done | bytes 1048600
  2.1 0.9 copy-done.4
  3.0 0.7 copy-done.5
  3.7 0.7 copy-done.6
  4.4 1.2 %first.1 = (bf16[16,4096]{1,0:T(8,128)(2,1)S(1)}, bf16[128,2048]{1,0:T(8,128)(2,1)S(1)}, f32[128,1]{1,0:T(8,128)S(1)}, bf16[64,2048]{1,0:T(8,128)(2,1)S(1)}) custom-call(s32[4]{0:T(128)S(1)} %pad_add_fusion.place_ref, bf16[1,16,4096]{2,1,0:T(8,128)(2,1)S(1)} %copy-done.4, f32[1,4096]{1,0:T(1,128)S(1)} %copy-done.6, bf16[128,4096]{1,0:T(8,128)(2,1)S(1)} %copy-done.3, ...), custom_call_target="tpu_custom_call" | custom-call | flops 4194304 | bytes 2097152 | tf_op jit(solution)/shard_map/first/pallas_call | solution.py:59
  5.7 5.1 %collective-permute-start.8 = (bf16[16,4096]{1,0:T(8,128)(2,1)S(1)}, bf16[16,4096]{1,0:T(8,128)(2,1)S(1)}, u32[]{:S(2)}, u32[]{:S(2)}) collective-permute-start(bf16[16,4096]{1,0:T(8,128)(2,1)S(1)} %get-tuple-element.33.refs_0_), channel_id=1, source_target_pairs={{0,12},{1,13},{2,14},{3,15},{4,8},{5,9},{6,10},{7,11},{8,4},{9,5},... | collective-permute-start | bytes 393224 | tf_op jit(solution)/shard_map/ppermute | solution.py:20
  10.8 0.6 collective-permute-start.4
  11.5 3.8 %collective-permute-done.8.refs_6_ = bf16[16,4096]{1,0:T(8,128)(2,1)S(1)} collective-permute-done((bf16[16,4096]{1,0:T(8,128)(2,1)S(1)}, bf16[16,4096]{1,0:T(8,128)(2,1)S(1)}, u32[]{:S(2)}, u32[]{:S(2)}) %collective-permute-start.8) | collective-permute-done | bytes 131104 | tf_op jit(solution)/shard_map/ppermute | solution.py:20
  15.3 1.7 %collective-permute-start.9 = (bf16[16,4096]{1,0:T(8,128)(2,1)S(1)}, bf16[16,4096]{1,0:T(8,128)(2,1)S(1)}, u32[]{:S(2)}, u32[]{:S(2)}) collective-permute-start(bf16[16,4096]{1,0:T(8,128)(2,1)S(1)} %collective-permute-done.8.refs_6_), channel_id=1, source_target_pairs={{0,2},{1,3},{2,0},{3,1},{4,6},{5,7},{6,4},{7,5},{8,10},{9,11},{10,... | collective-permute-start | bytes 393224 | tf_op jit(solution)/shard_map/ppermute | solution.py:20
  17.0 4.9 %collective-permute-done.6.refs_4_ = bf16[16,4096]{1,0:T(8,128)(2,1)S(1)} collective-permute-done((bf16[16,4096]{1,0:T(8,128)(2,1)S(1)}, bf16[16,4096]{1,0:T(8,128)(2,1)S(1)}, u32[]{:S(2)}, u32[]{:S(2)}) %collective-permute-start.6) | collective-permute-done | bytes 131104 | tf_op jit(solution)/shard_map/ppermute | solution.py:20
  21.9 1.5 %collective-permute-start.7 = (bf16[16,4096]{1,0:T(8,128)(2,1)S(1)}, bf16[16,4096]{1,0:T(8,128)(2,1)S(1)}, u32[]{:S(2)}, u32[]{:S(2)}) collective-permute-start(bf16[16,4096]{1,0:T(8,128)(2,1)S(1)} %collective-permute-done.6.refs_4_), channel_id=1, source_target_pairs={{0,2},{1,3},{2,0},{3,1},{4,6},{5,7},{6,4},{7,5},{8,10},{9,11},{10,... | collective-permute-start | bytes 393224 | tf_op jit(solution)/shard_map/ppermute | solution.py:20
  23.4 0.5 collective-permute-start.3
  23.9 1.5 %collective-permute-start = (bf16[64,2048]{1,0:T(8,128)(2,1)S(1)}, bf16[64,2048]{1,0:T(8,128)(2,1)S(1)}, u32[]{:S(2)}, u32[]{:S(2)}) collective-permute-start(bf16[64,2048]{1,0:T(8,128)(2,1)S(1)} %get-tuple-element.31), channel_id=1, source_target_pairs={{0,16},{16,0},{1,17},{17,1},{2,18},{18,2},{3,19},{19,3},{4,20},{20... | collective-permute-start | bytes 786440 | tf_op jit(solution)/shard_map/ppermute | solution.py:20
  25.4 1.5 %collective-permute-start.5 = (bf16[16,4096]{1,0:T(8,128)(2,1)S(1)}, bf16[16,4096]{1,0:T(8,128)(2,1)S(1)}, u32[]{:S(2)}, u32[]{:S(2)}) collective-permute-start(bf16[16,4096]{1,0:T(8,128)(2,1)S(1)} %collective-permute-done.4.refs_2_), channel_id=1, source_target_pairs={{0,2},{1,3},{2,0},{3,1},{4,6},{5,7},{6,4},{7,5},{8,10},{9,11},{10,... | collective-permute-start | bytes 393224 | tf_op jit(solution)/shard_map/ppermute | solution.py:20
  26.9 1.3 %collective-permute-done.7.refs_5_ = bf16[16,4096]{1,0:T(8,128)(2,1)S(1)} collective-permute-done((bf16[16,4096]{1,0:T(8,128)(2,1)S(1)}, bf16[16,4096]{1,0:T(8,128)(2,1)S(1)}, u32[]{:S(2)}, u32[]{:S(2)}) %collective-permute-start.7) | collective-permute-done | bytes 131104 | tf_op jit(solution)/shard_map/ppermute | solution.py:20
  28.4 2.4 %collective-permute-done.mine_ref = bf16[64,2048]{1,0:T(8,128)(2,1)S(1)} collective-permute-done((bf16[64,2048]{1,0:T(8,128)(2,1)S(1)}, bf16[64,2048]{1,0:T(8,128)(2,1)S(1)}, u32[]{:S(2)}, u32[]{:S(2)}) %collective-permute-start) | collective-permute-done | bytes 262176 | tf_op jit(solution)/shard_map/ppermute | solution.py:20
  30.7 1.3 %collective-permute-done.5.refs_3_ = bf16[16,4096]{1,0:T(8,128)(2,1)S(1)} collective-permute-done((bf16[16,4096]{1,0:T(8,128)(2,1)S(1)}, bf16[16,4096]{1,0:T(8,128)(2,1)S(1)}, u32[]{:S(2)}, u32[]{:S(2)}) %collective-permute-start.5) | collective-permute-done | bytes 131104 | tf_op jit(solution)/shard_map/ppermute | solution.py:20
  32.2 2.6 %copy-done.2 = bf16[2048,1280]{1,0:T(8,128)(2,1)S(1)} copy-done((bf16[2048,1280]{1,0:T(8,128)(2,1)S(1)}, bf16[2048,1280]{1,0:T(8,128)(2,1)}, u32[]{:S(2)}) %copy-start.2) | copy-done | bytes 5242904
  35.3 1.5 %otherdot.1 = (f32[128,1280]{1,0:T(8,128)S(1)}, bf16[128,2048]{1,0:T(8,128)(2,1)S(1)}) custom-call(s32[4]{0:T(128)S(1)} %pad_add_fusion.place_ref, bf16[64,2048]{1,0:T(8,128)(2,1)S(1)} %collective-permute-done.mine_ref, bf16[64,2048]{1,0:T(8,128)(2,1)S(1)} %collective-permute-done.1.other_ref, bf16[2048,1280]{1,0:T(8,128)(2,1)S(1)} %load.1.w_ref), custom_call_target="tpu_custom_call" | custom-call | flops 671088640 | bytes 5242880 | tf_op jit(solution)/shard_map/otherdot/pallas_call | solution.py:118
  36.8 1.6 %collective-permute-start.2 = (f32[128,1280]{1,0:T(8,128)S(1)}, f32[128,1280]{1,0:T(8,128)S(1)}, u32[]{:S(2)}, u32[]{:S(2)}) collective-permute-start(f32[128,1280]{1,0:T(8,128)S(1)} %get-tuple-element.32), channel_id=1, source_target_pairs={{0,16},{16,0},{1,17},{17,1},{2,18},{18,2},{3,19},{19,3},{4,20},{20... | collective-permute-start | bytes 1966088 | tf_op jit(solution)/shard_map/ppermute | solution.py:20
  38.4 0.7 slice-done.2
  39.0 5.3 %teacher.1 = (f32[2,256]{1,0:T(2,128)S(1)}, bf16[128,1280]{1,0:T(8,128)(2,1)S(1)}, bf16[128,1280]{1,0:T(8,128)(2,1)}) custom-call(s32[4]{0:T(128)S(1)} %pad_add_fusion.place_ref, bf16[16,4096]{1,0:T(8,128)(2,1)S(1)} %get-tuple-element.33.refs_0_, bf16[16,4096]{1,0:T(8,128)(2,1)S(1)} %collective-permute-done.3.refs_1_, ...), custom_call_target="tpu_custom_call" | custom-call | flops 2684354560 | bytes 10485760 | tf_op jit(solution)/shard_map/teacher/pallas_call | solution.py:180
  44.4 1.5 %collective-permute-start.12 = (bf16[128,1280]{1,0:T(8,128)(2,1)}, bf16[128,1280]{1,0:T(8,128)(2,1)S(1)}, u32[]{:S(2)}, u32[]{:S(2)}) collective-permute-start(bf16[128,1280]{1,0:T(8,128)(2,1)} %get-tuple-element.38), channel_id=1, source_target_pairs={{0,16},{16,0},{1,17},{17,1},{2,18},{18,2},{3,19},{19,3},{4,20},{20... | collective-permute-start | bytes 983048 | tf_op jit(solution)/shard_map/ppermute | solution.py:20
  45.9 0.9 owndot.1.refs_0_
  46.8 7.7 %collective-permute-done.2.refs_1_ = f32[128,1280]{1,0:T(8,128)S(1)} collective-permute-done((f32[128,1280]{1,0:T(8,128)S(1)}, f32[128,1280]{1,0:T(8,128)S(1)}, u32[]{:S(2)}, u32[]{:S(2)}) %collective-permute-start.2) | collective-permute-done | bytes 655392 | tf_op jit(solution)/shard_map/ppermute | solution.py:20
  54.4 1.5 %stats.1 = (f32[128,1280]{1,0:T(8,128)S(1)}, f32[32,8,128]{2,1,0:T(8,128)}) custom-call(s32[4]{0:T(128)S(1)} %pad_add_fusion.place_ref, f32[128,1280]{1,0:T(8,128)S(1)} %owndot.1.refs_0_, f32[128,1280]{1,0:T(8,128)S(1)} %collective-permute-done.2.refs_1_, f32[2,256]{1,0:T(2,128)S(1)} %get-tuple-element.34.refs_2_, s32[2,128]{1,0:T(2,128)S(1)} %bitcast.13), custom_call_target="tpu_custom_call" | custom-call | flops 1310720 | bytes 1966080 | tf_op jit(solution)/shard_map/stats/pallas_call | solution.py:224
  56.0 4.5 %all-to-all-start = ((f32[32,8,128]{2,1,0:T(8,128)}), f32[32,8,128]{2,1,0:T(8,128)S(1)}, u32[]{:S(2)}, u32[]{:S(2)}) async-start(f32[32,8,128]{2,1,0:T(8,128)} %get-tuple-element.35), calls=%async_computation | async-start | bytes 262144 | tf_op jit(solution)/shard_map/all_to_all | solution.py:480
  60.5 1.0 collective-permute-done.12.refs_1_
  61.5 7.2 %all-to-all-done.stats_ref = f32[32,8,128]{2,1,0:T(8,128)S(1)} async-done(((f32[32,8,128]{2,1,0:T(8,128)}), f32[32,8,128]{2,1,0:T(8,128)S(1)}, u32[]{:S(2)}, u32[]{:S(2)}) %all-to-all-start) | async-done | bytes 131104 | tf_op jit(solution)/shard_map/all_to_all | solution.py:480
  68.7 1.9 %grads.1 = (bf16[128,1280]{1,0:T(8,128)(2,1)S(1)}, f32[16,8,128]{2,1,0:T(8,128)}) custom-call(s32[4]{0:T(128)S(1)} %pad_add_fusion.place_ref, f32[32,8,128]{2,1,0:T(8,128)S(1)} %all-to-all-done.stats_ref, f32[128,1280]{1,0:T(8,128)S(1)} %get-tuple-element.36.logits_ref, s32[1,128]{1,0:T(1,128)S(1)} %bitcast.14, ...), custom_call_target="tpu_custom_call" | custom-call | flops 2621440 | bytes 1638400 | tf_op jit(solution)/shard_map/grads/pallas_call | solution.py:268
  70.6 0.8 collective-permute-start.13
  71.4 2.5 %copy-done.1 = bf16[2048,1280]{1,0:T(8,128)(2,1)S(1)} copy-done((bf16[2048,1280]{1,0:T(8,128)(2,1)S(1)}, bf16[2048,1280]{1,0:T(8,128)(2,1)}, u32[]{:S(2)}) %copy-start.1) | copy-done | bytes 5242904
  73.9 3.5 %pieces.2 = (bf16[4,256,128]{2,1,0:T(8,128)(2,1)S(1)}, bf16[4,256,128]{2,1,0:T(8,128)(2,1)S(1)}) custom-call(s32[4]{0:T(128)S(1)} %pad_add_fusion.place_ref, bf16[128,1280]{1,0:T(8,128)(2,1)S(1)} %get-tuple-element.39.refs_0_.grads_ref, bf16[2048,1280]{1,0:T(8,128)(2,1)S(1)} %copy-done.1), custom_call_target="tpu_custom_call" | custom-call | flops 671088640 | bytes 5242880 | tf_op jit(solution)/shard_map/pieces/pallas_call | solution.py:302
  77.5 3.0 %collective-permute-done.13.refs_1_.grads_ref = bf16[128,1280]{1,0:T(8,128)(2,1)S(1)} collective-permute-done((bf16[128,1280]{1,0:T(8,128)(2,1)S(1)}, bf16[128,1280]{1,0:T(8,128)(2,1)S(1)}, u32[]{:S(2)}, u32[]{:S(2)}) %collective-permute-start.13) | collective-permute-done | bytes 327712 | tf_op jit(solution)/shard_map/ppermute | solution.py:20
  80.5 3.5 %pieces.3 = (bf16[4,256,128]{2,1,0:T(8,128)(2,1)S(1)}, bf16[4,256,128]{2,1,0:T(8,128)(2,1)S(1)}) custom-call(s32[4]{0:T(128)S(1)} %pad_add_fusion.place_ref, bf16[128,1280]{1,0:T(8,128)(2,1)S(1)} %collective-permute-done.13.refs_1_.grads_ref, bf16[2048,1280]{1,0:T(8,128)(2,1)S(1)} %copy-done.1), custom_call_target="tpu_custom_call" | custom-call | flops 671088640 | bytes 5242880 | tf_op jit(solution)/shard_map/pieces/pallas_call | solution.py:302
  84.5 1.1 collective-permute-done.15.got_ref
  85.7 0.7 collective-permute-start.17
  86.4 3.5 %all-to-all-start.1 = ((f32[16,8,128]{2,1,0:T(8,128)}), f32[16,8,128]{2,1,0:T(8,128)S(1)}, u32[]{:S(2)}, u32[]{:S(2)}) async-start(f32[16,8,128]{2,1,0:T(8,128)} %get-tuple-element.41), calls=%async_computation.1 | async-start | bytes 131072 | tf_op jit(solution)/shard_map/all_to_all | solution.py:483
  89.9 0.8 dynamic_slice.7
  90.7 2.3 %collective-permute-done.17.refs_3_ = bf16[2,256,128]{2,1,0:T(8,128)(2,1)S(1)} collective-permute-done((bf16[2,256,128]{2,1,0:T(8,128)(2,1)S(1)}, bf16[2,256,128]{2,1,0:T(8,128)(2,1)S(1)}, u32[]{:S(2)}, u32[]{:S(2)}) %collective-permute-start.17) | collective-permute-done | bytes 131104 | tf_op jit(solution)/shard_map/ppermute | solution.py:20
  93.0 0.6 split.1
  93.6 0.7 collective-permute-start.18
  94.4 5.3 %collective-permute-start.20 = (bf16[256,128]{1,0:T(8,128)(2,1)S(1)}, bf16[256,128]{1,0:T(8,128)(2,1)S(1)}, u32[]{:S(2)}, u32[]{:S(2)}) collective-permute-start(bf16[256,128]{1,0:T(8,128)(2,1)S(1)} %get-tuple-element.53), channel_id=1, source_target_pairs={{0,16},{1,17},{2,18},{3,19},{4,20},{5,21},{6,22},{7,23},{8,0},{9,1... | collective-permute-start | bytes 196616 | tf_op jit(solution)/shard_map/ppermute | solution.py:499
  100.0 0.8 constant_dynamic-slice_fusion.hidden_ref
  100.8 8.0 %collective-permute-done.20.refs_2_ = bf16[256,128]{1,0:T(8,128)(2,1)S(1)} collective-permute-done((bf16[256,128]{1,0:T(8,128)(2,1)S(1)}, bf16[256,128]{1,0:T(8,128)(2,1)S(1)}, u32[]{:S(2)}, u32[]{:S(2)}) %collective-permute-start.20) | collective-permute-done | bytes 65568 | tf_op jit(solution)/shard_map/ppermute | solution.py:499
  108.8 0.9 last.1
  109.7 6.3 %headgrad.1 = f32[2048,1280]{1,0:T(8,128)} custom-call(bf16[128,1280]{1,0:T(8,128)(2,1)S(1)} %get-tuple-element.39.refs_0_.grads_ref, bf16[128,1280]{1,0:T(8,128)(2,1)S(1)} %collective-permute-done.13.refs_1_.grads_ref, bf16[128,2048]{1,0:T(8,128)(2,1)S(1)} %get-tuple-element.30.rows_ref.refs_2_, bf16[128,2048]{1,0:T(8,128)(2,1)S(1)} %get-tuple-element.40.refs_3_), custom_call_target="tpu_custom_call" | custom-call | flops 1342177280 | bytes 10485760 | tf_op jit(solution)/shard_map/headgrad/pallas_call | solution.py:398
  116.0 0.6 add.14
  (47 shorter events, 1.8 us)
Async XLA Ops:
  0.6 37.7 %slice-start = ((s8[10485760]{0:T(1024)(128)(4,1)}), s8[2097152]{0:T(1024)(128)(4,1)S(1)}, s32[]{:S(2)}) async-start(s8[10485760]{0:T(1024)(128)(4,1)} %bitcast.9), calls=%async_computation.2 | async-start | bytes 4194304
  0.7 1.4 %copy-start.3 = (bf16[128,4096]{1,0:T(8,128)(2,1)S(1)}, bf16[128,4096]{1,0:T(8,128)(2,1)}, u32[]{:S(2)}) copy-start(bf16[128,4096]{1,0:T(8,128)(2,1)} %sh_ref.1) | copy-start | bytes 3145732
  2.1 0.9 copy-start.4
  3.0 0.7 copy-start.5
  3.7 0.7 copy-start.6
  5.7 9.6 %collective-permute-start.8 = (bf16[16,4096]{1,0:T(8,128)(2,1)S(1)}, bf16[16,4096]{1,0:T(8,128)(2,1)S(1)}, u32[]{:S(2)}, u32[]{:S(2)}) collective-permute-start(bf16[16,4096]{1,0:T(8,128)(2,1)S(1)} %get-tuple-element.33.refs_0_), channel_id=1, source_target_pairs={{0,12},{1,13},{2,14},{3,15},{4,8},{5,9},{6,10},{7,11},{8,4},{9,5},... | collective-permute-start | bytes 393224 | tf_op jit(solution)/shard_map/ppermute | solution.py:20
  10.8 11.1 %collective-permute-start.6 = (bf16[16,4096]{1,0:T(8,128)(2,1)S(1)}, bf16[16,4096]{1,0:T(8,128)(2,1)S(1)}, u32[]{:S(2)}, u32[]{:S(2)}) collective-permute-start(bf16[16,4096]{1,0:T(8,128)(2,1)S(1)} %get-tuple-element.33.refs_0_), channel_id=1, source_target_pairs={{0,8},{1,9},{2,10},{3,11},{4,12},{5,13},{6,14},{7,15},{8,0},{9,1},... | collective-permute-start | bytes 393224 | tf_op jit(solution)/shard_map/ppermute | solution.py:20
  10.8 14.6 %collective-permute-start.4 = (bf16[16,4096]{1,0:T(8,128)(2,1)S(1)}, bf16[16,4096]{1,0:T(8,128)(2,1)S(1)}, u32[]{:S(2)}, u32[]{:S(2)}) collective-permute-start(bf16[16,4096]{1,0:T(8,128)(2,1)S(1)} %get-tuple-element.33.refs_0_), channel_id=1, source_target_pairs={{0,4},{1,5},{2,6},{3,7},{4,0},{5,1},{6,2},{7,3},{8,12},{9,13},{10,... | collective-permute-start | bytes 393224 | tf_op jit(solution)/shard_map/ppermute | solution.py:20
  15.3 11.7 %collective-permute-start.9 = (bf16[16,4096]{1,0:T(8,128)(2,1)S(1)}, bf16[16,4096]{1,0:T(8,128)(2,1)S(1)}, u32[]{:S(2)}, u32[]{:S(2)}) collective-permute-start(bf16[16,4096]{1,0:T(8,128)(2,1)S(1)} %collective-permute-done.8.refs_6_), channel_id=1, source_target_pairs={{0,2},{1,3},{2,0},{3,1},{4,6},{5,7},{6,4},{7,5},{8,10},{9,11},{10,... | collective-permute-start | bytes 393224 | tf_op jit(solution)/shard_map/ppermute | solution.py:20
  21.9 6.4 %collective-permute-start.7 = (bf16[16,4096]{1,0:T(8,128)(2,1)S(1)}, bf16[16,4096]{1,0:T(8,128)(2,1)S(1)}, u32[]{:S(2)}, u32[]{:S(2)}) collective-permute-start(bf16[16,4096]{1,0:T(8,128)(2,1)S(1)} %collective-permute-done.6.refs_4_), channel_id=1, source_target_pairs={{0,2},{1,3},{2,0},{3,1},{4,6},{5,7},{6,4},{7,5},{8,10},{9,11},{10,... | collective-permute-start | bytes 393224 | tf_op jit(solution)/shard_map/ppermute | solution.py:20
  23.4 7.3 %collective-permute-start.3 = (bf16[16,4096]{1,0:T(8,128)(2,1)S(1)}, bf16[16,4096]{1,0:T(8,128)(2,1)S(1)}, u32[]{:S(2)}, u32[]{:S(2)}) collective-permute-start(bf16[16,4096]{1,0:T(8,128)(2,1)S(1)} %get-tuple-element.33.refs_0_), channel_id=1, source_target_pairs={{0,2},{1,3},{2,0},{3,1},{4,6},{5,7},{6,4},{7,5},{8,10},{9,11},{10,... | collective-permute-start | bytes 393224 | tf_op jit(solution)/shard_map/ppermute | solution.py:20
  23.9 6.8 %collective-permute-start = (bf16[64,2048]{1,0:T(8,128)(2,1)S(1)}, bf16[64,2048]{1,0:T(8,128)(2,1)S(1)}, u32[]{:S(2)}, u32[]{:S(2)}) collective-permute-start(bf16[64,2048]{1,0:T(8,128)(2,1)S(1)} %get-tuple-element.31), channel_id=1, source_target_pairs={{0,16},{16,0},{1,17},{17,1},{2,18},{18,2},{3,19},{19,3},{4,20},{20... | collective-permute-start | bytes 786440 | tf_op jit(solution)/shard_map/ppermute | solution.py:20
  25.4 6.7 %collective-permute-start.5 = (bf16[16,4096]{1,0:T(8,128)(2,1)S(1)}, bf16[16,4096]{1,0:T(8,128)(2,1)S(1)}, u32[]{:S(2)}, u32[]{:S(2)}) collective-permute-start(bf16[16,4096]{1,0:T(8,128)(2,1)S(1)} %collective-permute-done.4.refs_2_), channel_id=1, source_target_pairs={{0,2},{1,3},{2,0},{3,1},{4,6},{5,7},{6,4},{7,5},{8,10},{9,11},{10,... | collective-permute-start | bytes 393224 | tf_op jit(solution)/shard_map/ppermute | solution.py:20
  28.3 10.1 %collective-permute-start.11 = (bf16[64,4096]{1,0:T(8,128)(2,1)S(1)}, bf16[64,4096]{1,0:T(8,128)(2,1)S(1)}, u32[]{:S(2)}, u32[]{:S(2)}) collective-permute-start(bf16[64,4096]{1,0:T(8,128)(2,1)S(1)} %pad_maximum_fusion.1), channel_id=1, source_target_pairs={{0,1},{1,0},{2,3},{3,2},{4,5},{5,4},{6,7},{7,6},{8,9},{9,8},{10,11... | collective-permute-start | bytes 1572872 | tf_op jit(solution)/shard_map/ppermute | solution.py:20
  30.7 4.5 %collective-permute-start.1 = (bf16[64,2048]{1,0:T(8,128)(2,1)S(1)}, bf16[64,2048]{1,0:T(8,128)(2,1)S(1)}, u32[]{:S(2)}, u32[]{:S(2)}) collective-permute-start(bf16[64,2048]{1,0:T(8,128)(2,1)S(1)} %collective-permute-done.mine_ref), channel_id=1, source_target_pairs={{0,1},{1,0},{2,3},{3,2},{4,5},{5,4},{6,7},{7,6},{8,9},{9,8},{10,11... | collective-permute-start | bytes 786440 | tf_op jit(solution)/shard_map/ppermute | solution.py:20
  32.1 6.2 %slice-start.1 = ((s8[10485760]{0:T(1024)(128)(4,1)}), s8[4194304]{0:T(1024)(128)(4,1)S(1)}, s32[]{:S(2)}) async-start(s8[10485760]{0:T(1024)(128)(4,1)} %bitcast.9), calls=%async_computation.3 | async-start | bytes 8388608
  32.1 6.9 %slice-start.2 = ((s8[10485760]{0:T(1024)(128)(4,1)}), s8[4194304]{0:T(1024)(128)(4,1)S(1)}, s32[]{:S(2)}) async-start(s8[10485760]{0:T(1024)(128)(4,1)} %bitcast.9), calls=%async_computation.4 | async-start | bytes 8388608
  32.1 6.2 %collective-permute-start.10 = (bf16[64,4096]{1,0:T(8,128)(2,1)S(1)}, bf16[64,4096]{1,0:T(8,128)(2,1)S(1)}, u32[]{:S(2)}, u32[]{:S(2)}) collective-permute-start(bf16[64,4096]{1,0:T(8,128)(2,1)S(1)} %pad_maximum_fusion), channel_id=1, source_target_pairs={{0,1},{1,0},{2,3},{3,2},{4,5},{5,4},{6,7},{7,6},{8,9},{9,8},{10,11... | collective-permute-start | bytes 1572872 | tf_op jit(solution)/shard_map/ppermute | solution.py:20
  32.2 2.6 %copy-start.2 = (bf16[2048,1280]{1,0:T(8,128)(2,1)S(1)}, bf16[2048,1280]{1,0:T(8,128)(2,1)}, u32[]{:S(2)}) copy-start(bf16[2048,1280]{1,0:T(8,128)(2,1)} %from_ref.1) | copy-start | bytes 15728644
  35.2 11.5 %copy-start = (bf16[2048,1280]{1,0:T(8,128)(2,1)}, bf16[2048,1280]{1,0:T(8,128)(2,1)S(1)}, u32[]{:S(2)}) copy-start(bf16[2048,1280]{1,0:T(8,128)(2,1)S(1)} %load.1.w_ref) | copy-start | bytes 15728644
  36.8 17.7 %copy-start.7 = (s32[256,1]{0,1:T(1,128)S(1)}, s32[256,1]{0,1:T(1,128)}, u32[]{:S(2)}) copy-start(s32[256,1]{0,1:T(1,128)} %param.14) | copy-start | bytes 3076
  36.8 31.9 %copy-start.8 = (s32[128]{0:T(128)S(1)}, s32[128]{0:T(128)}, u32[]{:S(2)}) copy-start(s32[128]{0:T(128)} %param.15) | copy-start | bytes 1540
  36.8 17.6 %collective-permute-start.2 = (f32[128,1280]{1,0:T(8,128)S(1)}, f32[128,1280]{1,0:T(8,128)S(1)}, u32[]{:S(2)}, u32[]{:S(2)}) collective-permute-start(f32[128,1280]{1,0:T(8,128)S(1)} %get-tuple-element.32), channel_id=1, source_target_pairs={{0,16},{16,0},{1,17},{17,1},{2,18},{18,2},{3,19},{19,3},{4,20},{20... | collective-permute-start | bytes 1966088 | tf_op jit(solution)/shard_map/ppermute | solution.py:20
  44.4 17.1 %collective-permute-start.12 = (bf16[128,1280]{1,0:T(8,128)(2,1)}, bf16[128,1280]{1,0:T(8,128)(2,1)S(1)}, u32[]{:S(2)}, u32[]{:S(2)}) collective-permute-start(bf16[128,1280]{1,0:T(8,128)(2,1)} %get-tuple-element.38), channel_id=1, source_target_pairs={{0,16},{16,0},{1,17},{17,1},{2,18},{18,2},{3,19},{19,3},{4,20},{20... | collective-permute-start | bytes 983048 | tf_op jit(solution)/shard_map/ppermute | solution.py:20
  56.0 12.7 %all-to-all-start = ((f32[32,8,128]{2,1,0:T(8,128)}), f32[32,8,128]{2,1,0:T(8,128)S(1)}, u32[]{:S(2)}, u32[]{:S(2)}) async-start(f32[32,8,128]{2,1,0:T(8,128)} %get-tuple-element.35), calls=%async_computation | async-start | bytes 262144 | tf_op jit(solution)/shard_map/all_to_all | solution.py:480
  70.6 9.9 %collective-permute-start.13 = (bf16[128,1280]{1,0:T(8,128)(2,1)S(1)}, bf16[128,1280]{1,0:T(8,128)(2,1)S(1)}, u32[]{:S(2)}, u32[]{:S(2)}) collective-permute-start(bf16[128,1280]{1,0:T(8,128)(2,1)S(1)} %get-tuple-element.39.refs_0_.grads_ref), channel_id=1, source_target_pairs={{0,16},{16,0},{1,17},{17,1},{2,18},{18,2},{3,19},{19,3},{4,20},{20... | collective-permute-start | bytes 983048 | tf_op jit(solution)/shard_map/ppermute | solution.py:20
  71.4 2.5 %copy-start.1 = (bf16[2048,1280]{1,0:T(8,128)(2,1)S(1)}, bf16[2048,1280]{1,0:T(8,128)(2,1)}, u32[]{:S(2)}) copy-start(bf16[2048,1280]{1,0:T(8,128)(2,1)} %copy-done) | copy-start | bytes 15728644
  77.4 6.7 %collective-permute-start.14 = (bf16[4,256,128]{2,1,0:T(8,128)(2,1)S(1)}, bf16[4,256,128]{2,1,0:T(8,128)(2,1)S(1)}, u32[]{:S(2)}, u32[]{:S(2)}) collective-permute-start(bf16[4,256,128]{2,1,0:T(8,128)(2,1)S(1)} %get-tuple-element.44), channel_id=1, source_target_pairs={{0,1},{1,0},{2,3},{3,2},{4,5},{5,4},{6,7},{7,6},{8,9},{9,8},{10,11... | collective-permute-start | bytes 786440 | tf_op jit(solution)/shard_map/ppermute | solution.py:20
  84.0 1.6 %collective-permute-start.15 = (bf16[4,256,128]{2,1,0:T(8,128)(2,1)S(1)}, bf16[4,256,128]{2,1,0:T(8,128)(2,1)S(1)}, u32[]{:S(2)}, u32[]{:S(2)}) collective-permute-start(bf16[4,256,128]{2,1,0:T(8,128)(2,1)S(1)} %get-tuple-element.47), channel_id=1, source_target_pairs={{0,1},{1,0},{2,3},{3,2},{4,5},{5,4},{6,7},{7,6},{8,9},{9,8},{10,11... | collective-permute-start | bytes 786440 | tf_op jit(solution)/shard_map/ppermute | solution.py:20
  84.2 6.5 %collective-permute-start.16 = (bf16[2,256,128]{2,1,0:T(8,128)(2,1)S(1)}, bf16[2,256,128]{2,1,0:T(8,128)(2,1)S(1)}, u32[]{:S(2)}, u32[]{:S(2)}) collective-permute-start(bf16[2,256,128]{2,1,0:T(8,128)(2,1)S(1)} %get-tuple-element.49), channel_id=1, source_target_pairs={{0,2},{1,3},{2,0},{3,1},{4,6},{5,7},{6,4},{7,5},{8,10},{9,11},{10,... | collective-permute-start | bytes 393224 | tf_op jit(solution)/shard_map/ppermute | solution.py:20
  85.7 7.3 %collective-permute-start.17 = (bf16[2,256,128]{2,1,0:T(8,128)(2,1)S(1)}, bf16[2,256,128]{2,1,0:T(8,128)(2,1)S(1)}, u32[]{:S(2)}, u32[]{:S(2)}) collective-permute-start(bf16[2,256,128]{2,1,0:T(8,128)(2,1)S(1)} %get-tuple-element.50), channel_id=1, source_target_pairs={{0,2},{1,3},{2,0},{3,1},{4,6},{5,7},{6,4},{7,5},{8,10},{9,11},{10,... | collective-permute-start | bytes 393224 | tf_op jit(solution)/shard_map/ppermute | solution.py:20
  86.4 14.4 %all-to-all-start.1 = ((f32[16,8,128]{2,1,0:T(8,128)}), f32[16,8,128]{2,1,0:T(8,128)S(1)}, u32[]{:S(2)}, u32[]{:S(2)}) async-start(f32[16,8,128]{2,1,0:T(8,128)} %get-tuple-element.41), calls=%async_computation.1 | async-start | bytes 131072 | tf_op jit(solution)/shard_map/all_to_all | solution.py:483
  93.6 7.2 %collective-permute-start.18 = (bf16[256,128]{1,0:T(8,128)(2,1)S(1)}, bf16[256,128]{1,0:T(8,128)(2,1)S(1)}, u32[]{:S(2)}, u32[]{:S(2)}) collective-permute-start(bf16[256,128]{1,0:T(8,128)(2,1)S(1)} %get-tuple-element.51), channel_id=1, source_target_pairs={{0,0},{1,1},{2,2},{3,3},{4,4},{5,5},{6,6},{7,7},{8,16},{9,17},{10,... | collective-permute-start | bytes 196616 | tf_op jit(solution)/shard_map/ppermute | solution.py:499
  94.3 6.5 %collective-permute-start.19 = (bf16[256,128]{1,0:T(8,128)(2,1)S(1)}, bf16[256,128]{1,0:T(8,128)(2,1)S(1)}, u32[]{:S(2)}, u32[]{:S(2)}) collective-permute-start(bf16[256,128]{1,0:T(8,128)(2,1)S(1)} %get-tuple-element.52), channel_id=1, source_target_pairs={{0,4},{1,5},{2,6},{3,7},{4,0},{5,1},{6,2},{7,3},{8,20},{9,21},{10,... | collective-permute-start | bytes 196616 | tf_op jit(solution)/shard_map/ppermute | solution.py:499
  94.4 14.4 %collective-permute-start.20 = (bf16[256,128]{1,0:T(8,128)(2,1)S(1)}, bf16[256,128]{1,0:T(8,128)(2,1)S(1)}, u32[]{:S(2)}, u32[]{:S(2)}) collective-permute-start(bf16[256,128]{1,0:T(8,128)(2,1)S(1)} %get-tuple-element.53), channel_id=1, source_target_pairs={{0,16},{1,17},{2,18},{3,19},{4,20},{5,21},{6,22},{7,23},{8,0},{9,1... | collective-permute-start | bytes 196616 | tf_op jit(solution)/shard_map/ppermute | solution.py:499
  99.7 9.1 %collective-permute-start.21 = (bf16[256,128]{1,0:T(8,128)(2,1)S(1)}, bf16[256,128]{1,0:T(8,128)(2,1)S(1)}, u32[]{:S(2)}, u32[]{:S(2)}) collective-permute-start(bf16[256,128]{1,0:T(8,128)(2,1)S(1)} %get-tuple-element.54), channel_id=1, source_target_pairs={{0,20},{1,21},{2,22},{3,23},{4,16},{5,17},{6,18},{7,19},{8,4},{9,5... | collective-permute-start | bytes 196616 | tf_op jit(solution)/shard_map/ppermute | solution.py:499
  109.7 6.3 %collective-permute-start.22 = (f32[1,256]{1,0:T(1,128)S(1)}, f32[1,256]{1,0:T(1,128)S(1)}, u32[]{:S(2)}, u32[]{:S(2)}) collective-permute-start(f32[1,256]{1,0:T(1,128)S(1)} %get-tuple-element.56), channel_id=1, source_target_pairs={{0,16},{16,0},{1,17},{17,1},{2,18},{18,2},{3,19},{19,3},{4,20},{20... | collective-permute-start | bytes 3080 | tf_op jit(solution)/shard_map/ppermute | solution.py:20

commit v4 on v3

--- a/solution.py
+++ b/solution.py
@@ -33,7 +33,7 @@
     return pl.CostEstimate(flops=flops, bytes_accessed=nbytes, transcendentals=exps)
 
 
-def first_kernel(branches, place_ref, th_ref, tg_ref, sh_ref, sg_ref, block_ref, own_ref, inv_ref, *refs):
+def first_kernel(branches, place_ref, th_ref, tg_ref, sh_ref, sg_ref, block_ref, own_ref, turned_ref, inv_ref, *refs):
     sent, normed_ref = refs[:-1], refs[-1]
     values = th_ref[0].astype(jnp.float32)
     scale = lax.rsqrt(jnp.mean(values * values, axis=-1, keepdims=True) + eps)
@@ -45,7 +45,9 @@
     part = own_ref.shape[1]
     half = own_ref.shape[0] // 2
     b = place_ref[0]
-    own_ref[...] = normed_ref[:, pl.ds(pl.multiple_of(b * part, part), part)]
+    own = normed_ref[:, pl.ds(pl.multiple_of(b * part, part), part)]
+    own_ref[...] = own
+    turned_ref[...] = jnp.transpose(own)
     start = pl.multiple_of((place_ref[1] % 2) * half, half)
     for r in range(1, branches):
         cols = pl.ds(pl.multiple_of((b ^ r) * part, part), part)
@@ -61,11 +63,12 @@
         out_shape=(
             jax.ShapeDtypeStruct(teacher_hidden.shape[1:], bf16),
             jax.ShapeDtypeStruct((rows, part), bf16),
+            jax.ShapeDtypeStruct((part, rows), bf16),
             jax.ShapeDtypeStruct((rows, 1), jnp.float32),
             *[jax.ShapeDtypeStruct((rows // 2, part), bf16)] * (branches - 1),
         ),
         in_specs=[SMEM] + [VMEM] * 4,
-        out_specs=(VMEM,) * (2 + branches),
+        out_specs=(VMEM,) * (3 + branches),
         scratch_shapes=[pltpu.VMEM((rows, width), bf16)],
         compiler_params=params(16),
         cost_estimate=cost(8 * rows * width, 4 * rows * width),
@@ -75,8 +78,10 @@
 
 def gather_blocks(block, size):
     got = {0: block}
-    for k in range(4, size, 4):
+    for k in range(8, size, 8):
         got[k] = swap(block, "tok", k)
+    for k in range(0, size, 8):
+        got[k + 4] = swap(got[k], "tok", 4)
     for k in range(0, size, 4):
         got[k + 2] = swap(got[k], "tok", 2)
     evens = sorted(got)
@@ -105,12 +110,13 @@
     )(rows, head)
 
 
-def other_dot_kernel(place_ref, mine_ref, other_ref, w_ref, out_ref, rows_ref):
+def other_dot_kernel(place_ref, mine_ref, other_ref, w_ref, out_ref, turned_ref, rows_ref):
     half = mine_ref.shape[0]
     core = place_ref[1] % 2
     rows_ref[pl.ds(pl.multiple_of(core * half, half), half), :] = mine_ref[...]
     rows_ref[pl.ds(pl.multiple_of((1 - core) * half, half), half), :] = other_ref[...]
     out_ref[...] = jnp.dot(rows_ref[...], w_ref[...], preferred_element_type=jnp.float32)
+    turned_ref[...] = jnp.transpose(rows_ref[...])
 
 
 def other_dot(mine, other, head, place):
@@ -119,14 +125,30 @@
         other_dot_kernel,
         out_shape=(
             jax.ShapeDtypeStruct((rows, head.shape[1]), jnp.float32),
-            jax.ShapeDtypeStruct((rows, mine.shape[1]), jnp.bfloat16),
+            jax.ShapeDtypeStruct((mine.shape[1], rows), jnp.bfloat16),
         ),
         in_specs=[SMEM, VMEM, VMEM, VMEM],
         out_specs=(VMEM, VMEM),
+        scratch_shapes=[pltpu.VMEM((rows, mine.shape[1]), jnp.bfloat16)],
         compiler_params=params(16),
         cost_estimate=cost(2 * rows * head.size, 2 * head.size),
         name="otherdot",
     )(place, mine, other, head)
+
+
+EXTRA = 8
+
+
+def extra_rows(values, dtype):
+    first = [value.astype(dtype).astype(jnp.float32) for value in values]
+    rest = [value - lead for value, lead in zip(values, first)]
+    empty = jnp.zeros((EXTRA - 2 * len(values), values[0].shape[1]), jnp.float32)
+    return jnp.concatenate(first + rest + [empty], axis=0).astype(dtype)
+
+
+def extra_values(rows, count):
+    rows = rows.astype(jnp.float32)
+    return [rows[i : i + 1] + rows[count + i : count + i + 1] for i in range(count)]
 
 
 def tile_of(cols):
@@ -237,7 +259,7 @@
 
 def grads_kernel(count, size, place_ref, stats_ref, logits_ref, ids_ref, *refs):
     terms = refs[:count]
-    grads_ref, dots_ref = refs[count:]
+    grads_ref = refs[count]
     b, t = place_ref[0], place_ref[1]
     rows, cols = logits_ref.shape
     logits = logits_ref[...]
@@ -257,9 +279,10 @@
             total = jnp.sum(block[:, 3, :] * jnp.exp(block[:, 2, :] - peak), axis=0, keepdims=True)
             probs = jnp.exp(logits - column(peak)) / column(total)
     grads = (loss_scale * (probs - targets)).astype(grads_ref.dtype)
-    grads_ref[...] = grads
+    grads_ref[:rows] = grads
+    grads_ref[rows:] = jnp.zeros((EXTRA, cols), grads.dtype)
     dots = as_row(jnp.sum(grads.astype(jnp.float32) * logits, axis=1, keepdims=True))
-    dots_ref[...] = jnp.broadcast_to(dots[None], dots_ref.shape)
+    grads_ref[rows:, :rows] = extra_rows([dots], grads.dtype)
 
 
 def make_grads(stats, logits, ids, terms, place, size):
@@ -267,61 +290,61 @@
     count = len(terms)
     return pl.pallas_call(
         functools.partial(grads_kernel, count, size),
-        out_shape=(
-            jax.ShapeDtypeStruct((rows, cols), jnp.bfloat16),
-            jax.ShapeDtypeStruct((size, 8, rows), jnp.float32),
-        ),
+        out_shape=jax.ShapeDtypeStruct((rows + EXTRA, cols), jnp.bfloat16),
         in_specs=[SMEM] + [VMEM] * (count + 3),
-        out_specs=(VMEM, VMEM),
+        out_specs=VMEM,
         compiler_params=params(12),
         cost_estimate=cost(16 * rows * cols, 10 * rows * cols, rows * cols),
         name="grads",
     )(place, stats, logits, ids, *terms)
 
 
-def pieces_kernel(place_ref, grads_ref, w_ref, keep_ref, send_ref, turned_ref):
-    turned_ref[...] = jnp.transpose(grads_ref[...])
-    width = keep_ref.shape[1]
-    for q in range(2 * keep_ref.shape[0]):
-        acc = jnp.dot(w_ref[q * width : (q + 1) * width], turned_ref[...], preferred_element_type=jnp.float32)
-        acc = acc.astype(keep_ref.dtype)
-        k = place_ref[2] ^ q
-
-        @pl.when(k % 2 == 0)
-        def _():
-            keep_ref[k // 2] = acc
-
-        @pl.when(k % 2 == 1)
-        def _():
-            send_ref[k // 2] = acc
-
-
-def normed_grad_pieces(grads, head, place, blocks):
-    rows, cols = grads.shape
+def pieces_kernel(parity, width, place_ref, grads_ref, w_ref, out_ref, turned_ref):
+    rows = out_ref.shape[1]
+    turned_ref[...] = jnp.transpose(grads_ref[:rows])
+    count = (out_ref.shape[0] - EXTRA) // width
+    for k in range(count):
+        start = pl.multiple_of((place_ref[2] ^ (2 * k + parity)) * width, width)
+        acc = jnp.dot(w_ref[pl.ds(start, width)], turned_ref[...], preferred_element_type=jnp.float32)
+        out_ref[k * width : (k + 1) * width] = acc.astype(out_ref.dtype)
+    out_ref[count * width :] = grads_ref[rows:, :rows]
+
+
+def normed_grad_pieces(grads, head, place, blocks, parity):
+    rows, cols = grads.shape[0] - EXTRA, grads.shape[1]
     width = head.shape[0] // blocks
     return pl.pallas_call(
-        pieces_kernel,
-        out_shape=(jax.ShapeDtypeStruct((blocks // 2, width, rows), jnp.bfloat16),) * 2,
+        functools.partial(pieces_kernel, parity, width),
+        out_shape=jax.ShapeDtypeStruct((blocks // 2 * width + EXTRA, rows), jnp.bfloat16),
         in_specs=[SMEM, VMEM, VMEM],
-        out_specs=(VMEM, VMEM),
+        out_specs=VMEM,
         scratch_shapes=[pltpu.VMEM((cols, rows), jnp.bfloat16)],
         compiler_params=params(16),
-        cost_estimate=cost(2 * rows * head.size, 2 * head.size),
+        cost_estimate=cost(rows * head.size, head.size),
         name="pieces",
     )(place, grads, head)
 
 
-def fold_kernel(mine_ref, got_ref, keep_ref, send_ref):
-    for k in range(mine_ref.shape[0]):
-        total = mine_ref[k].astype(jnp.float32) + got_ref[k].astype(jnp.float32)
-        (send_ref if k % 2 else keep_ref)[k // 2] = total.astype(keep_ref.dtype)
-
-
-def fold(mine, got):
-    count, width, rows = mine.shape
-    return pl.pallas_call(
-        fold_kernel,
-        out_shape=(jax.ShapeDtypeStruct((count // 2, width, rows), mine.dtype),) * 2,
+def fold_kernel(width, mine_ref, got_ref, keep_ref, send_ref):
+    f32 = jnp.float32
+    count = (mine_ref.shape[0] - EXTRA) // width
+    for k in range(count):
+        at = slice(k * width, (k + 1) * width)
+        total = mine_ref[at].astype(f32) + got_ref[at].astype(f32)
+        to = slice(k // 2 * width, (k // 2 + 1) * width)
+        (send_ref if k % 2 else keep_ref)[to] = total.astype(keep_ref.dtype)
+    dots = extra_values(mine_ref[count * width :], 1)[0] + extra_values(got_ref[count * width :], 1)[0]
+    extra = extra_rows([dots], keep_ref.dtype)
+    keep_ref[count // 2 * width :] = extra
+    send_ref[count // 2 * width :] = extra
+
+
+def fold(mine, got, width):
+    full, rows = mine.shape
+    half = (full - EXTRA) // 2 + EXTRA
+    return pl.pallas_call(
+        functools.partial(fold_kernel, width),
+        out_shape=(jax.ShapeDtypeStruct((half, rows), mine.dtype),) * 2,
         in_specs=[VMEM, VMEM],
         out_specs=(VMEM, VMEM),
         compiler_params=params(8),
@@ -330,31 +353,120 @@
     )(mine, got)
 
 
-def split_kernel(count, place_ref, *refs):
-    mine, got, out = refs[:count], refs[count : 2 * count], refs[2 * count :]
-    lows = mine[0].shape[0]
-    for r in range(count):
-        for low in range(lows):
-            total = (mine[r][low].astype(jnp.float32) + got[r][low].astype(jnp.float32)).astype(mine[r].dtype)
+def split_kernel(count, width, place_ref, *refs):
+    mine, got, turned = (refs[i * count : (i + 1) * count] for i in range(3))
+    out = refs[3 * count :]
+    f32 = jnp.float32
+    lows = (mine[0].shape[0] - EXTRA) // width
+    rows = mine[0].shape[1]
+    dots = [
+        extra_values(mine[r][lows * width :], 1)[0] + extra_values(got[r][lows * width :], 1)[0] for r in range(count)
+    ]
+    for low in range(lows):
+        at = slice(low * width, (low + 1) * width)
+        block = pl.multiple_of((place_ref[2] ^ (4 * low)) * width, width)
+        totals = [mine[r][at].astype(f32) + got[r][at].astype(f32) for r in range(count)]
+        gain = sum(
+            jnp.sum(totals[r] * turned[r][pl.ds(block, width)].astype(f32), axis=1, keepdims=True)
+            for r in range(count)
+        )
+        gain = as_row(gain)
+        lanes = min(width, rows)
+        gains = [gain[:, i : i + lanes] for i in range(0, width, lanes)]
+        if lanes < rows:
+            gains = [jnp.concatenate([row, jnp.zeros((1, rows - lanes), f32)], axis=1) for row in gains]
+        for r in range(count):
+            total = totals[r].astype(mine[r].dtype)
+            extra = extra_rows([dots[r]] + gains, mine[r].dtype)
             for kh in range(count):
 
                 @pl.when((place_ref[3] ^ kh) == r)
                 def _():
-                    out[kh * lows + low][...] = total
-
-
-def split(mine, got, place):
+                    out[kh * lows + low][:width] = total
+                    out[kh * lows + low][width:] = extra
+
+
+def split(mine, got, turned, width, place):
     count = len(mine)
-    lows, width, rows = mine[0].shape
-    return pl.pallas_call(
-        functools.partial(split_kernel, count),
-        out_shape=(jax.ShapeDtypeStruct((width, rows), mine[0].dtype),) * (count * lows),
-        in_specs=[SMEM] + [VMEM] * (2 * count),
+    rows = mine[0].shape[1]
+    lows = (mine[0].shape[0] - EXTRA) // width
+    return pl.pallas_call(
+        functools.partial(split_kernel, count, width),
+        out_shape=(jax.ShapeDtypeStruct((width + EXTRA, rows), mine[0].dtype),) * (count * lows),
+        in_specs=[SMEM] + [VMEM] * (3 * count),
         out_specs=(VMEM,) * (count * lows),
         compiler_params=params(8),
-        cost_estimate=cost(count * mine[0].size, 6 * count * mine[0].size),
+        cost_estimate=cost(4 * count * mine[0].size, 8 * count * mine[0].size),
         name="split",
-    )(place, *mine, *got)
+    )(place, *mine, *got, *turned)
+
+
+def head_grad_kernel(count, *refs):
+    grads, turned = refs[:count], refs[count : 2 * count]
+    out_ref, grads_ref = refs[-2:]
+    rows = grads_ref.shape[0] // count
+
+    @pl.when(pl.program_id(0) == 0)
+    def _():
+        for r in range(count):
+            grads_ref[r * rows : (r + 1) * rows, :] = grads[r][:rows]
+
+    lhs = jnp.concatenate([ref[...] for ref in turned], axis=1)
+    out_ref[...] = jnp.dot(lhs, grads_ref[...], preferred_element_type=jnp.float32)
+
+
+def head_grad(grads, turned, half, done):
+    count = len(grads)
+    full, cols = grads[0].shape
+    part, rows = turned[0].shape
+    tile = tile_of(part)
+    steps = part // tile // 2
+    return pl.pallas_call(
+        functools.partial(head_grad_kernel, count),
+        out_shape=jax.ShapeDtypeStruct((part, cols), jnp.float32),
+        grid=(steps,),
+        in_specs=[pl.BlockSpec((full, cols), lambda i: (0, 0))] * count
+        + [pl.BlockSpec((tile, rows), lambda i: (i + half * steps, 0))] * count
+        + [pl.BlockSpec(memory_space=pl.ANY)] * len(done),
+        out_specs=pl.BlockSpec((tile, cols), lambda i: (i + half * steps, 0)),
+        scratch_shapes=[pltpu.VMEM((count * rows, cols), jnp.bfloat16)],
+        input_output_aliases={2 * count: 0} if done else {},
+        compiler_params=params(16),
+        cost_estimate=cost(count * rows * part * cols, 2 * part * cols),
+        name="headgrad",
+    )(*grads, *turned, *done)
+
+
+def last_kernel(count, width, inv_ref, hidden_ref, gain_ref, *refs):
+    parts = refs[:count]
+    out_ref, gain_out_ref = refs[count:]
+    total = parts[0][...].astype(jnp.float32)
+    for ref in parts[1:]:
+        total = total + ref[...].astype(jnp.float32)
+    piece, rows = total.shape[0] - EXTRA, total.shape[1]
+    lanes = min(piece, rows)
+    dots, *gains = extra_values(total[piece:], 1 + piece // lanes)
+    gain_out_ref[...] = jnp.concatenate([row[:, :lanes] for row in gains], axis=1) / gain_ref[...]
+    normed_grads = jnp.transpose(total[:piece])
+    inv = inv_ref[...]
+    scaled = hidden_ref[...].astype(jnp.float32) * inv
+    out_ref[...] = inv * gain_ref[...] * normed_grads - scaled * (inv * column(dots) / width)
+
+
+def finish(parts, inv, hidden, gain, width):
+    piece, rows = parts[0].shape[0] - EXTRA, parts[0].shape[1]
+    return pl.pallas_call(
+        functools.partial(last_kernel, len(parts), width),
+        out_shape=(
+            jax.ShapeDtypeStruct((rows, piece), jnp.float32),
+            jax.ShapeDtypeStruct((1, piece), jnp.float32),
+        ),
+        in_specs=[VMEM] * (3 + len(parts)),
+        out_specs=(VMEM, VMEM),
+        compiler_params=params(12),
+        cost_estimate=cost(16 * rows * piece, 12 * rows * piece),
+        name="last",
+    )(inv, hidden, gain, *parts)
 
 
 def load_kernel(from_ref, to_ref, sem):
@@ -374,70 +486,6 @@
         cost_estimate=cost(0, 4 * value.size),
         name="load",
     )(value)
-
-
-def head_grad_kernel(count, *refs):
-    grads, parts = refs[:count], refs[count : 2 * count]
-    out_ref, grads_ref = refs[2 * count :]
-    rows = grads[0].shape[0]
-
-    @pl.when(pl.program_id(0) == 0)
-    def _():
-        for r in range(count):
-            grads_ref[r * rows : (r + 1) * rows, :] = grads[r][...]
-
-    turned = jnp.transpose(jnp.concatenate([ref[...] for ref in parts], axis=0))
-    out_ref[...] = jnp.dot(turned, grads_ref[...], preferred_element_type=jnp.float32)
-
-
-def head_grad(grads, parts):
-    count = len(grads)
-    rows, cols = grads[0].shape
-    part = parts[0].shape[1]
-    tile = tile_of(part)
-    return pl.pallas_call(
-        functools.partial(head_grad_kernel, count),
-        out_shape=jax.ShapeDtypeStruct((part, cols), jnp.float32),
-        grid=(part // tile,),
-        in_specs=[pl.BlockSpec((rows, cols), lambda i: (0, 0))] * count
-        + [pl.BlockSpec((rows, tile), lambda i: (0, i))] * count,
-        out_specs=pl.BlockSpec((tile, cols), lambda i: (i, 0)),
-        scratch_shapes=[pltpu.VMEM((count * rows, cols), jnp.bfloat16)],
-        compiler_params=params(16),
-        cost_estimate=cost(2 * count * rows * part * cols, 4 * part * cols),
-        name="headgrad",
-    )(*grads, *parts)
-
-
-def last_kernel(count, width, dots_ref, inv_ref, hidden_ref, gain_ref, *refs):
-    parts = refs[:count]
-    out_ref, gain_out_ref = refs[count:]
-    total = parts[0][...].astype(jnp.float32)
-    for ref in parts[1:]:
-        total = total + ref[...].astype(jnp.float32)
-    normed_grads = jnp.transpose(total)
-    inv = inv_ref[...]
-    hidden = hidden_ref[...].astype(jnp.float32)
-    scaled = hidden * inv
-    gain_out_ref[...] = jnp.sum(normed_grads * scaled, axis=0, keepdims=True)
-    row_dots = column(jnp.sum(dots_ref[:, 0, :], axis=0, keepdims=True))
-    out_ref[...] = inv * gain_ref[...] * normed_grads - scaled * (inv * row_dots / width)
-
-
-def finish(parts, dots, inv, hidden, gain, width):
-    piece, rows = parts[0].shape
-    return pl.pallas_call(
-        functools.partial(last_kernel, len(parts), width),
-        out_shape=(
-            jax.ShapeDtypeStruct((rows, piece), jnp.float32),
-            jax.ShapeDtypeStruct((1, piece), jnp.float32),
-        ),
-        in_specs=[VMEM] * (4 + len(parts)),
-        out_specs=(VMEM, VMEM),
-        compiler_params=params(12),
-        cost_estimate=cost(16 * rows * piece, 12 * rows * piece),
-        name="last",
-    )(dots, inv, hidden, gain, *parts)
 
 
 def per_device(
@@ -457,17 +505,17 @@
     rows, width = student_hidden.shape
     blocks = size // branches
     place = jnp.stack([b, t, t % blocks, (t // blocks) ^ b]).astype(jnp.int32)
-    teacher_block, own, inv_scale, *sent = normalize_all(
+    teacher_block, own, own_turned, inv_scale, *sent = normalize_all(
         teacher_hidden, teacher_gain, student_hidden, student_gain, place, branches
     )
 
     loaded = load(student_head)
-    student_parts, partials = [own], []
+    turned, partials = [own_turned], []
     for r in range(1, branches):
         mine = swap(sent[r - 1], "branch", r)
         other = swap(mine, "tok", 1)
         partial, fetched = other_dot(mine, other, loaded, place)
-        student_parts.append(fetched)
+        turned.append(fetched)
         partials.append(swap(partial, "branch", r))
     partials = [own_dot(own, loaded)] + partials
 
@@ -478,17 +526,19 @@
     weights = cluster_weights[:, 0].reshape(branches, rows)
     logits, stats = student_stats(partials, teacher_stats, weights, place, size)
     stats = lax.all_to_all(stats, ("branch", "tok"), 0, 0, tiled=True)
-    logit_grads, dots = make_grads(stats, logits, token_ids[None], terms, place, size)
+    logit_grads = make_grads(stats, logits, token_ids[None], terms, place, size)
     all_grads = [logit_grads] + [swap(logit_grads, "branch", r) for r in range(1, branches)]
-    dots = lax.all_to_all(dots, "tok", 0, 0, tiled=True)
-
+
+    slice_width = width // size
     kept, got = [], []
     for r in range(branches):
-        keep, send = normed_grad_pieces(all_grads[r], loaded, place, blocks)
-        keep, send = fold(keep, swap(send, "tok", 1))
+        send = normed_grad_pieces(all_grads[r], loaded, place, blocks, 1)
+        send = swap(send, "tok", 1)
+        keep = normed_grad_pieces(all_grads[r], loaded, place, blocks, 0)
+        keep, send = fold(keep, send, slice_width)
         kept.append(keep)
         got.append(swap(send, "tok", 2))
-    owned = split(kept, got, place)
+    owned = split(kept, got, turned, slice_width, place)
     arrived = []
     for kh in range(branches):
         for kl in range(blocks // 4):
@@ -498,16 +548,12 @@
                 perm.append((i, (h ^ kh) * size + bb * blocks + (l ^ kl) * 4 + rest))
             arrived.append(lax.ppermute(owned[kh * (blocks // 4) + kl], ("branch", "tok"), perm))
 
-    grad_head = head_grad(all_grads, student_parts)
-
-    slice_width = width // size
+    grad_head = head_grad(all_grads, turned, 0, [])
+    grad_head = head_grad(all_grads, turned, 1, [grad_head])
+
     hidden_cols = lax.dynamic_slice_in_dim(student_hidden, t * slice_width, slice_width, 1)
     gain_cols = lax.dynamic_slice_in_dim(student_gain, t * slice_width, slice_width, 0)
-    grad_hidden, grad_gain = finish(arrived, dots, inv_scale, hidden_cols, gain_cols[None], width)
-    flip = 1
-    while flip < branches:
-        grad_gain = grad_gain + swap(grad_gain, "branch", flip)
-        flip *= 2
+    grad_hidden, grad_gain = finish(arrived, inv_scale, hidden_cols, gain_cols[None], width)
     return (grad_head, grad_hidden, grad_gain[0])
 
 

time: 117 us -> 110 us (0.940)
  waiting for transfers between devices: 44 us -> 39.5 us
  starting transfers between devices: 32.1 us -> 30.9 us
  Pallas kernels: 27.8 us -> 26.6 us
    ppermute x4, waiting for transfers between devices: 7.96 us -> 2.65 us  [per_device(): lax.ppermute(owned[kh * (blocks // 4) + kl], ('branch', 'tok'), perm)]
    all_to_all x1 -> x0, starting transfers between devices: 3.5 us -> none  [per_device(): dots = lax.all_to_all(dots, 'tok', 0, 0, tiled=True)]
    pallas_call x6 -> x8, Pallas kernels: 9.73 us -> 8.24 us  [the longest x4 5.88 us: normed_grad_pieces(): pl.pallas_call(functools.partial(pieces_kernel, parity, width), out_shape...]
    ppermute x19 -> x18, starting transfers between devices: 17.7 us -> 18.9 us  [swap(): return lax.ppermute(value, axis, [(i, i ^ flip) for i in range(size)])]
    pallas_call x1 -> x2, Pallas kernels: 6.32 us -> 6.55 us  [head_grad(): pl.pallas_call(functools.partial(head_grad_kernel, count), out_shape=jax....]
    ppermute x19 -> x18, waiting for transfers between devices: 28.8 us -> 28.6 us  [swap(): return lax.ppermute(value, axis, [(i, i ^ flip) for i in range(size)])]
  transfers between devices with their start and end apart: 25 -> 23, of which waited for: 12 -> 12; matrix products, arithmetic and copies ran while one was open for 1% -> 2% of each run, Pallas kernels for 20% -> 20%
where the time goes in v4:
time: 110 us; the launch traced here: 109 us
  waiting for transfers between devices  39.5 us (36%)
  starting transfers between devices  30.9 us (28%)
  Pallas kernels  26.6 us (24%)
  local copies, waits for them, and re-layouts  11.1 us (10%)
    ppermute x18, waiting for transfers between devices, swap(): return lax.ppermute(value, axis, [(i, i ^ flip) for i in range(size)])  28.6 us
    ppermute x18, starting transfers between devices, swap(): return lax.ppermute(value, axis, [(i, i ^ flip) for i in range(size)])  18.9 us
    unnamed x24, local copies, waits for them, and re-layouts  9.49 us
    all_to_all x1, waiting for transfers between devices, per_device(): stats = lax.all_to_all(stats, ('branch', 'tok'), 0, 0, tiled=True)  8.19 us
    pallas_call x2, Pallas kernels, head_grad(): pl.pallas_call(functools.partial(head_grad_kernel, count), out_shape=jax....  6.55 us
    ppermute x4, starting transfers between devices, per_device(): lax.ppermute(owned[kh * (blocks // 4) + kl], ('branch', 'tok'), perm)  6.36 us
    pallas_call x4, Pallas kernels, normed_grad_pieces(): pl.pallas_call(functools.partial(pieces_kernel, parity, width), out_shape...  5.88 us
    all_to_all x1, starting transfers between devices, per_device(): stats = lax.all_to_all(stats, ('branch', 'tok'), 0, 0, tiled=True)  5.63 us
  transfers between devices with their start and end apart: 23, of which 12 were waited for; matrix products, arithmetic and copies ran while one was open for 2% of the time, Pallas kernels for 20%

profile of v4, /device:TPU:0, one launch (start us, length us, event | category | flops | bytes accessed | tf_op | source)
XLA Modules:
  0.0 109.2 jit_solution(13687339329243274625)
XLA Ops:
  0.7 1.4 %copy-done.3 = bf16[128,4096]{1,0:T(8,128)(2,1)S(1)} copy-done((bf16[128,4096]{1,0:T(8,128)(2,1)S(1)}, bf16[128,4096]{1,0:T(8,128)(2,1)}, u32[]{:S(2)}) %copy-start.3) | copy-done | bytes 1048600
  2.1 0.9 copy-done.4
  3.0 0.7 copy-done.5
  3.7 0.7 copy-done.6
  4.4 1.4 %first.1 = (bf16[16,4096]{1,0:T(8,128)(2,1)S(1)}, bf16[128,2048]{1,0:T(8,128)(2,1)S(1)}, bf16[2048,128]{1,0:T(8,128)(2,1)S(1)}, f32[128,1]{1,0:T(8,128)S(1)}, bf16[64,2048]{1,0:T(8,128)(2,1)S(1)}) custom-call(s32[4]{0:T(128)S(1)} %pad_add_fusion.place_ref, bf16[1,16,4096]{2,1,0:T(8,128)(2,1)S(1)} %copy-done.4, f32[1,4096]{1,0:T(1,128)S(1)} %copy-done.6, ...), custom_call_target="tpu_custom_call" | custom-call | flops 4194304 | bytes 2097152 | tf_op jit(solution)/shard_map/first/pallas_call | solution.py:61
  5.8 4.1 %collective-permute-start.6 = (bf16[16,4096]{1,0:T(8,128)(2,1)S(1)}, bf16[16,4096]{1,0:T(8,128)(2,1)S(1)}, u32[]{:S(2)}, u32[]{:S(2)}) collective-permute-start(bf16[16,4096]{1,0:T(8,128)(2,1)S(1)} %get-tuple-element.28.refs_0_), channel_id=1, source_target_pairs={{0,8},{1,9},{2,10},{3,11},{4,12},{5,13},{6,14},{7,15},{8,0},{9,1},... | collective-permute-start | bytes 393224 | tf_op jit(solution)/shard_map/ppermute | solution.py:20
  9.9 1.6 %collective-permute-start.4 = (bf16[16,4096]{1,0:T(8,128)(2,1)S(1)}, bf16[16,4096]{1,0:T(8,128)(2,1)S(1)}, u32[]{:S(2)}, u32[]{:S(2)}) collective-permute-start(bf16[16,4096]{1,0:T(8,128)(2,1)S(1)} %get-tuple-element.28.refs_0_), channel_id=1, source_target_pairs={{0,4},{1,5},{2,6},{3,7},{4,0},{5,1},{6,2},{7,3},{8,12},{9,13},{10,... | collective-permute-start | bytes 393224 | tf_op jit(solution)/shard_map/ppermute | solution.py:20
  11.5 4.8 %collective-permute-done.6.refs_4_ = bf16[16,4096]{1,0:T(8,128)(2,1)S(1)} collective-permute-done((bf16[16,4096]{1,0:T(8,128)(2,1)S(1)}, bf16[16,4096]{1,0:T(8,128)(2,1)S(1)}, u32[]{:S(2)}, u32[]{:S(2)}) %collective-permute-start.6) | collective-permute-done | bytes 131104 | tf_op jit(solution)/shard_map/ppermute | solution.py:20
  16.3 0.6 collective-permute-start.8
  17.0 1.5 %collective-permute-start.3 = (bf16[16,4096]{1,0:T(8,128)(2,1)S(1)}, bf16[16,4096]{1,0:T(8,128)(2,1)S(1)}, u32[]{:S(2)}, u32[]{:S(2)}) collective-permute-start(bf16[16,4096]{1,0:T(8,128)(2,1)S(1)} %get-tuple-element.28.refs_0_), channel_id=1, source_target_pairs={{0,2},{1,3},{2,0},{3,1},{4,6},{5,7},{6,4},{7,5},{8,10},{9,11},{10,... | collective-permute-start | bytes 393224 | tf_op jit(solution)/shard_map/ppermute | solution.py:20
  18.5 0.5 collective-permute-start.5
  19.0 1.5 %collective-permute-start = (bf16[64,2048]{1,0:T(8,128)(2,1)S(1)}, bf16[64,2048]{1,0:T(8,128)(2,1)S(1)}, u32[]{:S(2)}, u32[]{:S(2)}) collective-permute-start(bf16[64,2048]{1,0:T(8,128)(2,1)S(1)} %get-tuple-element.26), channel_id=1, source_target_pairs={{0,16},{16,0},{1,17},{17,1},{2,18},{18,2},{3,19},{19,3},{4,20},{20... | collective-permute-start | bytes 786440 | tf_op jit(solution)/shard_map/ppermute | solution.py:20
  20.5 1.5 %collective-permute-start.7 = (bf16[16,4096]{1,0:T(8,128)(2,1)S(1)}, bf16[16,4096]{1,0:T(8,128)(2,1)S(1)}, u32[]{:S(2)}, u32[]{:S(2)}) collective-permute-start(bf16[16,4096]{1,0:T(8,128)(2,1)S(1)} %collective-permute-done.6.refs_4_), channel_id=1, source_target_pairs={{0,2},{1,3},{2,0},{3,1},{4,6},{5,7},{6,4},{7,5},{8,10},{9,11},{10,... | collective-permute-start | bytes 393224 | tf_op jit(solution)/shard_map/ppermute | solution.py:20
  22.0 0.9 collective-permute-start.9
  23.3 2.8 %collective-permute-done.5.refs_3_ = bf16[16,4096]{1,0:T(8,128)(2,1)S(1)} collective-permute-done((bf16[16,4096]{1,0:T(8,128)(2,1)S(1)}, bf16[16,4096]{1,0:T(8,128)(2,1)S(1)}, u32[]{:S(2)}, u32[]{:S(2)}) %collective-permute-start.5) | collective-permute-done | bytes 131104 | tf_op jit(solution)/shard_map/ppermute | solution.py:20
  26.8 2.2 %collective-permute-done.7.refs_5_ = bf16[16,4096]{1,0:T(8,128)(2,1)S(1)} collective-permute-done((bf16[16,4096]{1,0:T(8,128)(2,1)S(1)}, bf16[16,4096]{1,0:T(8,128)(2,1)S(1)}, u32[]{:S(2)}, u32[]{:S(2)}) %collective-permute-start.7) | collective-permute-done | bytes 131104 | tf_op jit(solution)/shard_map/ppermute | solution.py:20
  28.9 1.6 %collective-permute-done.9.refs_7_ = bf16[16,4096]{1,0:T(8,128)(2,1)S(1)} collective-permute-done((bf16[16,4096]{1,0:T(8,128)(2,1)S(1)}, bf16[16,4096]{1,0:T(8,128)(2,1)S(1)}, u32[]{:S(2)}, u32[]{:S(2)}) %collective-permute-start.9) | collective-permute-done | bytes 131104 | tf_op jit(solution)/shard_map/ppermute | solution.py:20
  30.7 2.6 %copy-done.2 = bf16[2048,1280]{1,0:T(8,128)(2,1)S(1)} copy-done((bf16[2048,1280]{1,0:T(8,128)(2,1)S(1)}, bf16[2048,1280]{1,0:T(8,128)(2,1)}, u32[]{:S(2)}) %copy-start.2) | copy-done | bytes 5242904
  33.7 1.5 %otherdot.1 = (f32[128,1280]{1,0:T(8,128)S(1)}, bf16[2048,128]{1,0:T(8,128)(2,1)S(1)}) custom-call(s32[4]{0:T(128)S(1)} %pad_add_fusion.place_ref, bf16[64,2048]{1,0:T(8,128)(2,1)S(1)} %collective-permute-done.mine_ref, bf16[64,2048]{1,0:T(8,128)(2,1)S(1)} %collective-permute-done.1.other_ref, bf16[2048,1280]{1,0:T(8,128)(2,1)S(1)} %load.1.w_ref), custom_call_target="tpu_custom_call" | custom-call | flops 671088640 | bytes 5242880 | tf_op jit(solution)/shard_map/otherdot/pallas_call | solution.py:124
  35.3 1.6 %collective-permute-start.2 = (f32[128,1280]{1,0:T(8,128)S(1)}, f32[128,1280]{1,0:T(8,128)S(1)}, u32[]{:S(2)}, u32[]{:S(2)}) collective-permute-start(f32[128,1280]{1,0:T(8,128)S(1)} %get-tuple-element.27), channel_id=1, source_target_pairs={{0,16},{16,0},{1,17},{17,1},{2,18},{18,2},{3,19},{19,3},{4,20},{20... | collective-permute-start | bytes 1966088 | tf_op jit(solution)/shard_map/ppermute | solution.py:20
  36.8 0.6 slice-done.2
  37.5 5.3 %teacher.1 = (f32[2,256]{1,0:T(2,128)S(1)}, bf16[128,1280]{1,0:T(8,128)(2,1)S(1)}, bf16[128,1280]{1,0:T(8,128)(2,1)}) custom-call(s32[4]{0:T(128)S(1)} %pad_add_fusion.place_ref, bf16[16,4096]{1,0:T(8,128)(2,1)S(1)} %get-tuple-element.28.refs_0_, bf16[16,4096]{1,0:T(8,128)(2,1)S(1)} %collective-permute-done.3.refs_1_, ...), custom_call_target="tpu_custom_call" | custom-call | flops 2684354560 | bytes 10485760 | tf_op jit(solution)/shard_map/teacher/pallas_call | solution.py:202
  42.8 1.5 %collective-permute-start.12 = (bf16[128,1280]{1,0:T(8,128)(2,1)}, bf16[128,1280]{1,0:T(8,128)(2,1)S(1)}, u32[]{:S(2)}, u32[]{:S(2)}) collective-permute-start(bf16[128,1280]{1,0:T(8,128)(2,1)} %get-tuple-element.33), channel_id=1, source_target_pairs={{0,16},{16,0},{1,17},{17,1},{2,18},{18,2},{3,19},{19,3},{4,20},{20... | collective-permute-start | bytes 983048 | tf_op jit(solution)/shard_map/ppermute | solution.py:20
  44.3 0.9 owndot.1.refs_0_
  45.2 7.6 %collective-permute-done.2.refs_1_ = f32[128,1280]{1,0:T(8,128)S(1)} collective-permute-done((f32[128,1280]{1,0:T(8,128)S(1)}, f32[128,1280]{1,0:T(8,128)S(1)}, u32[]{:S(2)}, u32[]{:S(2)}) %collective-permute-start.2) | collective-permute-done | bytes 655392 | tf_op jit(solution)/shard_map/ppermute | solution.py:20
  52.8 1.5 %stats.1 = (f32[128,1280]{1,0:T(8,128)S(1)}, f32[32,8,128]{2,1,0:T(8,128)}) custom-call(s32[4]{0:T(128)S(1)} %pad_add_fusion.place_ref, f32[128,1280]{1,0:T(8,128)S(1)} %owndot.1.refs_0_, f32[128,1280]{1,0:T(8,128)S(1)} %collective-permute-done.2.refs_1_, f32[2,256]{1,0:T(2,128)S(1)} %get-tuple-element.29.refs_2_, s32[2,128]{1,0:T(2,128)S(1)} %bitcast.13), custom_call_target="tpu_custom_call" | custom-call | flops 1310720 | bytes 1966080 | tf_op jit(solution)/shard_map/stats/pallas_call | solution.py:246
  54.3 5.6 %all-to-all-start = ((f32[32,8,128]{2,1,0:T(8,128)}), f32[32,8,128]{2,1,0:T(8,128)S(1)}, u32[]{:S(2)}, u32[]{:S(2)}) async-start(f32[32,8,128]{2,1,0:T(8,128)} %get-tuple-element.30), calls=%async_computation | async-start | bytes 262144 | tf_op jit(solution)/shard_map/all_to_all | solution.py:528
  60.0 8.2 %all-to-all-done.stats_ref = f32[32,8,128]{2,1,0:T(8,128)S(1)} async-done(((f32[32,8,128]{2,1,0:T(8,128)}), f32[32,8,128]{2,1,0:T(8,128)S(1)}, u32[]{:S(2)}, u32[]{:S(2)}) %all-to-all-start) | async-done | bytes 131104 | tf_op jit(solution)/shard_map/all_to_all | solution.py:528
  68.2 1.3 %grads.1.refs_0_.grads_ref = bf16[136,1280]{1,0:T(8,128)(2,1)S(1)} custom-call(s32[4]{0:T(128)S(1)} %pad_add_fusion.place_ref, f32[32,8,128]{2,1,0:T(8,128)S(1)} %all-to-all-done.stats_ref, f32[128,1280]{1,0:T(8,128)S(1)} %get-tuple-element.31.logits_ref, s32[1,128]{1,0:T(1,128)S(1)} %bitcast.14, bf16[128,1280]{1,0:T(8,128)(2,1)S(1)} %get-tuple-element.32.refs_0_, ...), custom_call_target="tpu_custom_call" | custom-call | flops 2621440 | bytes 1638400 | tf_op jit(solution)/shard_map/grads/pallas_call | solution.py:291
  69.4 0.8 collective-permute-start.13
  70.3 2.5 %copy-done.1 = bf16[2048,1280]{1,0:T(8,128)(2,1)S(1)} copy-done((bf16[2048,1280]{1,0:T(8,128)(2,1)S(1)}, bf16[2048,1280]{1,0:T(8,128)(2,1)}, u32[]{:S(2)}) %copy-start.1) | copy-done | bytes 5242904
  72.7 1.5 %pieces.5 = bf16[1032,128]{1,0:T(8,128)(2,1)S(1)} custom-call(s32[4]{0:T(128)S(1)} %pad_add_fusion.place_ref, bf16[136,1280]{1,0:T(8,128)(2,1)S(1)} %grads.1.refs_0_.grads_ref, bf16[2048,1280]{1,0:T(8,128)(2,1)S(1)} %copy-done.1), custom_call_target="tpu_custom_call" | custom-call | flops 335544320 | bytes 2621440 | tf_op jit(solution)/shard_map/pieces/pallas_call | solution.py:316
  74.3 5.5 %collective-permute-done.13.refs_1_.grads_ref = bf16[136,1280]{1,0:T(8,128)(2,1)S(1)} collective-permute-done((bf16[136,1280]{1,0:T(8,128)(2,1)S(1)}, bf16[136,1280]{1,0:T(8,128)(2,1)S(1)}, u32[]{:S(2)}, u32[]{:S(2)}) %collective-permute-start.13) | collective-permute-done | bytes 348192 | tf_op jit(solution)/shard_map/ppermute | solution.py:20
  79.8 1.5 %pieces.7 = bf16[1032,128]{1,0:T(8,128)(2,1)S(1)} custom-call(s32[4]{0:T(128)S(1)} %pad_add_fusion.place_ref, bf16[136,1280]{1,0:T(8,128)(2,1)S(1)} %collective-permute-done.13.refs_1_.grads_ref, bf16[2048,1280]{1,0:T(8,128)(2,1)S(1)} %copy-done.1), custom_call_target="tpu_custom_call" | custom-call | flops 335544320 | bytes 2621440 | tf_op jit(solution)/shard_map/pieces/pallas_call | solution.py:316
  81.3 1.5 %pieces.4.mine_ref = bf16[1032,128]{1,0:T(8,128)(2,1)S(1)} custom-call(s32[4]{0:T(128)S(1)} %pad_add_fusion.place_ref, bf16[136,1280]{1,0:T(8,128)(2,1)S(1)} %grads.1.refs_0_.grads_ref, bf16[2048,1280]{1,0:T(8,128)(2,1)S(1)} %copy-done.1), custom_call_target="tpu_custom_call" | custom-call | flops 335544320 | bytes 2621440 | tf_op jit(solution)/shard_map/pieces/pallas_call | solution.py:316
  83.3 1.5 %pieces.6.mine_ref = bf16[1032,128]{1,0:T(8,128)(2,1)S(1)} custom-call(s32[4]{0:T(128)S(1)} %pad_add_fusion.place_ref, bf16[136,1280]{1,0:T(8,128)(2,1)S(1)} %collective-permute-done.13.refs_1_.grads_ref, bf16[2048,1280]{1,0:T(8,128)(2,1)S(1)} %copy-done.1), custom_call_target="tpu_custom_call" | custom-call | flops 335544320 | bytes 2621440 | tf_op jit(solution)/shard_map/pieces/pallas_call | solution.py:316
  84.8 1.8 %collective-permute-start.17 = (bf16[520,128]{1,0:T(8,128)(2,1)S(1)}, bf16[520,128]{1,0:T(8,128)(2,1)S(1)}, u32[]{:S(2)}, u32[]{:S(2)}) collective-permute-start(bf16[520,128]{1,0:T(8,128)(2,1)S(1)} %get-tuple-element.40), channel_id=1, source_target_pairs={{0,2},{1,3},{2,0},{3,1},{4,6},{5,7},{6,4},{7,5},{8,10},{9,11},{10,... | collective-permute-start | bytes 399368 | tf_op jit(solution)/shard_map/ppermute | solution.py:20
  86.6 0.8 dynamic_slice.7
  87.4 0.8 constant_dynamic-slice_fusion.hidden_ref
  88.2 1.2 %collective-permute-done.16.refs_2_ = bf16[520,128]{1,0:T(8,128)(2,1)S(1)} collective-permute-done((bf16[520,128]{1,0:T(8,128)(2,1)S(1)}, bf16[520,128]{1,0:T(8,128)(2,1)S(1)}, u32[]{:S(2)}, u32[]{:S(2)}) %collective-permute-start.16) | collective-permute-done | bytes 133152 | tf_op jit(solution)/shard_map/ppermute | solution.py:20
  89.4 2.4 %collective-permute-done.17.refs_3_ = bf16[520,128]{1,0:T(8,128)(2,1)S(1)} collective-permute-done((bf16[520,128]{1,0:T(8,128)(2,1)S(1)}, bf16[520,128]{1,0:T(8,128)(2,1)S(1)}, u32[]{:S(2)}, u32[]{:S(2)}) %collective-permute-start.17) | collective-permute-done | bytes 133152 | tf_op jit(solution)/shard_map/ppermute | solution.py:20
  91.8 1.0 split.1
  92.7 0.7 collective-permute-start.18
  93.5 5.3 %collective-permute-start.20 = (bf16[264,128]{1,0:T(8,128)(2,1)S(1)}, bf16[264,128]{1,0:T(8,128)(2,1)S(1)}, u32[]{:S(2)}, u32[]{:S(2)}) collective-permute-start(bf16[264,128]{1,0:T(8,128)(2,1)S(1)} %get-tuple-element.43), channel_id=1, source_target_pairs={{0,16},{1,17},{2,18},{3,19},{4,20},{5,21},{6,22},{7,23},{8,0},{9,1... | collective-permute-start | bytes 202760 | tf_op jit(solution)/shard_map/ppermute | solution.py:549
  99.1 3.3 %headgrad.2.refs_4_ = f32[2048,1280]{1,0:T(8,128)} custom-call(bf16[136,1280]{1,0:T(8,128)(2,1)S(1)} %grads.1.refs_0_.grads_ref, bf16[136,1280]{1,0:T(8,128)(2,1)S(1)} %collective-permute-done.13.refs_1_.grads_ref, bf16[2048,128]{1,0:T(8,128)(2,1)S(1)} %get-tuple-element.34.refs_2_.refs_4_, bf16[2048,128]{1,0:T(8,128)(2,1)S(1)} %get-tuple-element.35.refs_3_.refs_5_), custom_call_target="tpu_custom_call" | custom-call | flops 671088640 | bytes 5242880 | tf_op jit(solution)/shard_map/headgrad/pallas_call | solution.py:424
  102.4 3.3 %headgrad.3 = f32[2048,1280]{1,0:T(8,128)} custom-call(bf16[136,1280]{1,0:T(8,128)(2,1)S(1)} %grads.1.refs_0_.grads_ref, bf16[136,1280]{1,0:T(8,128)(2,1)S(1)} %collective-permute-done.13.refs_1_.grads_ref, bf16[2048,128]{1,0:T(8,128)(2,1)S(1)} %get-tuple-element.34.refs_2_.refs_4_, ...), custom_call_target="tpu_custom_call", output_to_operand_aliasing={{}: (4, {})} | custom-call | flops 671088640 | bytes 5242880 | tf_op jit(solution)/shard_map/headgrad/pallas_call | solution.py:424
  105.7 2.6 %collective-permute-done.20.refs_2_ = bf16[264,128]{1,0:T(8,128)(2,1)S(1)} collective-permute-done((bf16[264,128]{1,0:T(8,128)(2,1)S(1)}, bf16[264,128]{1,0:T(8,128)(2,1)S(1)}, u32[]{:S(2)}, u32[]{:S(2)}) %collective-permute-start.20) | collective-permute-done | bytes 67616 | tf_op jit(solution)/shard_map/ppermute | solution.py:549
  108.3 0.9 last.1
  (45 shorter events, 2.7 us)
Async XLA Ops:
  0.6 36.2 %slice-start = ((s8[10485760]{0:T(1024)(128)(4,1)}), s8[2097152]{0:T(1024)(128)(4,1)S(1)}, s32[]{:S(2)}) async-start(s8[10485760]{0:T(1024)(128)(4,1)} %bitcast.9), calls=%async_computation.1 | async-start | bytes 4194304
  0.7 1.4 %copy-start.3 = (bf16[128,4096]{1,0:T(8,128)(2,1)S(1)}, bf16[128,4096]{1,0:T(8,128)(2,1)}, u32[]{:S(2)}) copy-start(bf16[128,4096]{1,0:T(8,128)(2,1)} %sh_ref.1) | copy-start | bytes 3145732
  2.1 0.9 copy-start.4
  3.0 0.7 copy-start.5
  3.7 0.7 copy-start.6
  5.8 10.5 %collective-permute-start.6 = (bf16[16,4096]{1,0:T(8,128)(2,1)S(1)}, bf16[16,4096]{1,0:T(8,128)(2,1)S(1)}, u32[]{:S(2)}, u32[]{:S(2)}) collective-permute-start(bf16[16,4096]{1,0:T(8,128)(2,1)S(1)} %get-tuple-element.28.refs_0_), channel_id=1, source_target_pairs={{0,8},{1,9},{2,10},{3,11},{4,12},{5,13},{6,14},{7,15},{8,0},{9,1},... | collective-permute-start | bytes 393224 | tf_op jit(solution)/shard_map/ppermute | solution.py:20
  9.9 8.6 %collective-permute-start.4 = (bf16[16,4096]{1,0:T(8,128)(2,1)S(1)}, bf16[16,4096]{1,0:T(8,128)(2,1)S(1)}, u32[]{:S(2)}, u32[]{:S(2)}) collective-permute-start(bf16[16,4096]{1,0:T(8,128)(2,1)S(1)} %get-tuple-element.28.refs_0_), channel_id=1, source_target_pairs={{0,4},{1,5},{2,6},{3,7},{4,0},{5,1},{6,2},{7,3},{8,12},{9,13},{10,... | collective-permute-start | bytes 393224 | tf_op jit(solution)/shard_map/ppermute | solution.py:20
  16.3 5.7 %collective-permute-start.8 = (bf16[16,4096]{1,0:T(8,128)(2,1)S(1)}, bf16[16,4096]{1,0:T(8,128)(2,1)S(1)}, u32[]{:S(2)}, u32[]{:S(2)}) collective-permute-start(bf16[16,4096]{1,0:T(8,128)(2,1)S(1)} %collective-permute-done.6.refs_4_), channel_id=1, source_target_pairs={{0,4},{1,5},{2,6},{3,7},{4,0},{5,1},{6,2},{7,3},{8,12},{9,13},{10,... | collective-permute-start | bytes 393224 | tf_op jit(solution)/shard_map/ppermute | solution.py:20
  17.0 6.4 %collective-permute-start.3 = (bf16[16,4096]{1,0:T(8,128)(2,1)S(1)}, bf16[16,4096]{1,0:T(8,128)(2,1)S(1)}, u32[]{:S(2)}, u32[]{:S(2)}) collective-permute-start(bf16[16,4096]{1,0:T(8,128)(2,1)S(1)} %get-tuple-element.28.refs_0_), channel_id=1, source_target_pairs={{0,2},{1,3},{2,0},{3,1},{4,6},{5,7},{6,4},{7,5},{8,10},{9,11},{10,... | collective-permute-start | bytes 393224 | tf_op jit(solution)/shard_map/ppermute | solution.py:20
  18.5 7.7 %collective-permute-start.5 = (bf16[16,4096]{1,0:T(8,128)(2,1)S(1)}, bf16[16,4096]{1,0:T(8,128)(2,1)S(1)}, u32[]{:S(2)}, u32[]{:S(2)}) collective-permute-start(bf16[16,4096]{1,0:T(8,128)(2,1)S(1)} %collective-permute-done.4.refs_2_), channel_id=1, source_target_pairs={{0,2},{1,3},{2,0},{3,1},{4,6},{5,7},{6,4},{7,5},{8,10},{9,11},{10,... | collective-permute-start | bytes 393224 | tf_op jit(solution)/shard_map/ppermute | solution.py:20
  19.0 7.4 %collective-permute-start = (bf16[64,2048]{1,0:T(8,128)(2,1)S(1)}, bf16[64,2048]{1,0:T(8,128)(2,1)S(1)}, u32[]{:S(2)}, u32[]{:S(2)}) collective-permute-start(bf16[64,2048]{1,0:T(8,128)(2,1)S(1)} %get-tuple-element.26), channel_id=1, source_target_pairs={{0,16},{16,0},{1,17},{17,1},{2,18},{18,2},{3,19},{19,3},{4,20},{20... | collective-permute-start | bytes 786440 | tf_op jit(solution)/shard_map/ppermute | solution.py:20
  20.5 8.5 %collective-permute-start.7 = (bf16[16,4096]{1,0:T(8,128)(2,1)S(1)}, bf16[16,4096]{1,0:T(8,128)(2,1)S(1)}, u32[]{:S(2)}, u32[]{:S(2)}) collective-permute-start(bf16[16,4096]{1,0:T(8,128)(2,1)S(1)} %collective-permute-done.6.refs_4_), channel_id=1, source_target_pairs={{0,2},{1,3},{2,0},{3,1},{4,6},{5,7},{6,4},{7,5},{8,10},{9,11},{10,... | collective-permute-start | bytes 393224 | tf_op jit(solution)/shard_map/ppermute | solution.py:20
  22.0 8.5 %collective-permute-start.9 = (bf16[16,4096]{1,0:T(8,128)(2,1)S(1)}, bf16[16,4096]{1,0:T(8,128)(2,1)S(1)}, u32[]{:S(2)}, u32[]{:S(2)}) collective-permute-start(bf16[16,4096]{1,0:T(8,128)(2,1)S(1)} %collective-permute-done.8.refs_6_), channel_id=1, source_target_pairs={{0,2},{1,3},{2,0},{3,1},{4,6},{5,7},{6,4},{7,5},{8,10},{9,11},{10,... | collective-permute-start | bytes 393224 | tf_op jit(solution)/shard_map/ppermute | solution.py:20
  26.2 10.6 %collective-permute-start.10 = (bf16[64,4096]{1,0:T(8,128)(2,1)S(1)}, bf16[64,4096]{1,0:T(8,128)(2,1)S(1)}, u32[]{:S(2)}, u32[]{:S(2)}) collective-permute-start(bf16[64,4096]{1,0:T(8,128)(2,1)S(1)} %pad_maximum_fusion), channel_id=1, source_target_pairs={{0,1},{1,0},{2,3},{3,2},{4,5},{5,4},{6,7},{7,6},{8,9},{9,8},{10,11... | collective-permute-start | bytes 1572872 | tf_op jit(solution)/shard_map/ppermute | solution.py:20
  26.4 7.3 %collective-permute-start.1 = (bf16[64,2048]{1,0:T(8,128)(2,1)S(1)}, bf16[64,2048]{1,0:T(8,128)(2,1)S(1)}, u32[]{:S(2)}, u32[]{:S(2)}) collective-permute-start(bf16[64,2048]{1,0:T(8,128)(2,1)S(1)} %collective-permute-done.mine_ref), channel_id=1, source_target_pairs={{0,1},{1,0},{2,3},{3,2},{4,5},{5,4},{6,7},{7,6},{8,9},{9,8},{10,11... | collective-permute-start | bytes 786440 | tf_op jit(solution)/shard_map/ppermute | solution.py:20
  30.6 6.3 %slice-start.1 = ((s8[10485760]{0:T(1024)(128)(4,1)}), s8[4194304]{0:T(1024)(128)(4,1)S(1)}, s32[]{:S(2)}) async-start(s8[10485760]{0:T(1024)(128)(4,1)} %bitcast.9), calls=%async_computation.2 | async-start | bytes 8388608
  30.6 6.9 %slice-start.2 = ((s8[10485760]{0:T(1024)(128)(4,1)}), s8[4194304]{0:T(1024)(128)(4,1)S(1)}, s32[]{:S(2)}) async-start(s8[10485760]{0:T(1024)(128)(4,1)} %bitcast.9), calls=%async_computation.3 | async-start | bytes 8388608
  30.6 6.2 %collective-permute-start.11 = (bf16[64,4096]{1,0:T(8,128)(2,1)S(1)}, bf16[64,4096]{1,0:T(8,128)(2,1)S(1)}, u32[]{:S(2)}, u32[]{:S(2)}) collective-permute-start(bf16[64,4096]{1,0:T(8,128)(2,1)S(1)} %pad_maximum_fusion.1), channel_id=1, source_target_pairs={{0,1},{1,0},{2,3},{3,2},{4,5},{5,4},{6,7},{7,6},{8,9},{9,8},{10,11... | collective-permute-start | bytes 1572872 | tf_op jit(solution)/shard_map/ppermute | solution.py:20
  30.7 2.6 %copy-start.2 = (bf16[2048,1280]{1,0:T(8,128)(2,1)S(1)}, bf16[2048,1280]{1,0:T(8,128)(2,1)}, u32[]{:S(2)}) copy-start(bf16[2048,1280]{1,0:T(8,128)(2,1)} %from_ref.1) | copy-start | bytes 15728644
  33.7 11.5 %copy-start = (bf16[2048,1280]{1,0:T(8,128)(2,1)}, bf16[2048,1280]{1,0:T(8,128)(2,1)S(1)}, u32[]{:S(2)}) copy-start(bf16[2048,1280]{1,0:T(8,128)(2,1)S(1)} %load.1.w_ref) | copy-start | bytes 15728644
  35.2 17.6 %copy-start.7 = (s32[256,1]{0,1:T(1,128)S(1)}, s32[256,1]{0,1:T(1,128)}, u32[]{:S(2)}) copy-start(s32[256,1]{0,1:T(1,128)} %param.14) | copy-start | bytes 3076
  35.2 32.9 %copy-start.8 = (s32[128]{0:T(128)S(1)}, s32[128]{0:T(128)}, u32[]{:S(2)}) copy-start(s32[128]{0:T(128)} %param.15) | copy-start | bytes 1540
  35.3 17.6 %collective-permute-start.2 = (f32[128,1280]{1,0:T(8,128)S(1)}, f32[128,1280]{1,0:T(8,128)S(1)}, u32[]{:S(2)}, u32[]{:S(2)}) collective-permute-start(f32[128,1280]{1,0:T(8,128)S(1)} %get-tuple-element.27), channel_id=1, source_target_pairs={{0,16},{16,0},{1,17},{17,1},{2,18},{18,2},{3,19},{19,3},{4,20},{20... | collective-permute-start | bytes 1966088 | tf_op jit(solution)/shard_map/ppermute | solution.py:20
  42.8 17.1 %collective-permute-start.12 = (bf16[128,1280]{1,0:T(8,128)(2,1)}, bf16[128,1280]{1,0:T(8,128)(2,1)S(1)}, u32[]{:S(2)}, u32[]{:S(2)}) collective-permute-start(bf16[128,1280]{1,0:T(8,128)(2,1)} %get-tuple-element.33), channel_id=1, source_target_pairs={{0,16},{16,0},{1,17},{17,1},{2,18},{18,2},{3,19},{19,3},{4,20},{20... | collective-permute-start | bytes 983048 | tf_op jit(solution)/shard_map/ppermute | solution.py:20
  54.3 13.8 %all-to-all-start = ((f32[32,8,128]{2,1,0:T(8,128)}), f32[32,8,128]{2,1,0:T(8,128)S(1)}, u32[]{:S(2)}, u32[]{:S(2)}) async-start(f32[32,8,128]{2,1,0:T(8,128)} %get-tuple-element.30), calls=%async_computation | async-start | bytes 262144 | tf_op jit(solution)/shard_map/all_to_all | solution.py:528
  69.4 10.4 %collective-permute-start.13 = (bf16[136,1280]{1,0:T(8,128)(2,1)S(1)}, bf16[136,1280]{1,0:T(8,128)(2,1)S(1)}, u32[]{:S(2)}, u32[]{:S(2)}) collective-permute-start(bf16[136,1280]{1,0:T(8,128)(2,1)S(1)} %grads.1.refs_0_.grads_ref), channel_id=1, source_target_pairs={{0,16},{16,0},{1,17},{17,1},{2,18},{18,2},{3,19},{19,3},{4,20},{20... | collective-permute-start | bytes 1044488 | tf_op jit(solution)/shard_map/ppermute | solution.py:20
  70.3 2.5 %copy-start.1 = (bf16[2048,1280]{1,0:T(8,128)(2,1)S(1)}, bf16[2048,1280]{1,0:T(8,128)(2,1)}, u32[]{:S(2)}) copy-start(bf16[2048,1280]{1,0:T(8,128)(2,1)} %copy-done) | copy-start | bytes 15728644
  74.2 8.6 %collective-permute-start.14 = (bf16[1032,128]{1,0:T(8,128)(2,1)S(1)}, bf16[1032,128]{1,0:T(8,128)(2,1)S(1)}, u32[]{:S(2)}, u32[]{:S(2)}) collective-permute-start(bf16[1032,128]{1,0:T(8,128)(2,1)S(1)} %pieces.5), channel_id=1, source_target_pairs={{0,1},{1,0},{2,3},{3,2},{4,5},{5,4},{6,7},{7,6},{8,9},{9,8},{10,11... | collective-permute-start | bytes 792584 | tf_op jit(solution)/shard_map/ppermute | solution.py:20
  81.3 3.5 %collective-permute-start.15 = (bf16[1032,128]{1,0:T(8,128)(2,1)S(1)}, bf16[1032,128]{1,0:T(8,128)(2,1)S(1)}, u32[]{:S(2)}, u32[]{:S(2)}) collective-permute-start(bf16[1032,128]{1,0:T(8,128)(2,1)S(1)} %pieces.7), channel_id=1, source_target_pairs={{0,1},{1,0},{2,3},{3,2},{4,5},{5,4},{6,7},{7,6},{8,9},{9,8},{10,11... | collective-permute-start | bytes 792584 | tf_op jit(solution)/shard_map/ppermute | solution.py:20
  82.9 6.5 %collective-permute-start.16 = (bf16[520,128]{1,0:T(8,128)(2,1)S(1)}, bf16[520,128]{1,0:T(8,128)(2,1)S(1)}, u32[]{:S(2)}, u32[]{:S(2)}) collective-permute-start(bf16[520,128]{1,0:T(8,128)(2,1)S(1)} %get-tuple-element.39), channel_id=1, source_target_pairs={{0,2},{1,3},{2,0},{3,1},{4,6},{5,7},{6,4},{7,5},{8,10},{9,11},{10,... | collective-permute-start | bytes 399368 | tf_op jit(solution)/shard_map/ppermute | solution.py:20
  84.8 6.9 %collective-permute-start.17 = (bf16[520,128]{1,0:T(8,128)(2,1)S(1)}, bf16[520,128]{1,0:T(8,128)(2,1)S(1)}, u32[]{:S(2)}, u32[]{:S(2)}) collective-permute-start(bf16[520,128]{1,0:T(8,128)(2,1)S(1)} %get-tuple-element.40), channel_id=1, source_target_pairs={{0,2},{1,3},{2,0},{3,1},{4,6},{5,7},{6,4},{7,5},{8,10},{9,11},{10,... | collective-permute-start | bytes 399368 | tf_op jit(solution)/shard_map/ppermute | solution.py:20
  92.7 12.9 %collective-permute-start.18 = (bf16[264,128]{1,0:T(8,128)(2,1)S(1)}, bf16[264,128]{1,0:T(8,128)(2,1)S(1)}, u32[]{:S(2)}, u32[]{:S(2)}) collective-permute-start(bf16[264,128]{1,0:T(8,128)(2,1)S(1)} %get-tuple-element.41), channel_id=1, source_target_pairs={{0,0},{1,1},{2,2},{3,3},{4,4},{5,5},{6,6},{7,7},{8,16},{9,17},{10,... | collective-permute-start | bytes 202760 | tf_op jit(solution)/shard_map/ppermute | solution.py:549
  93.4 12.2 %collective-permute-start.19 = (bf16[264,128]{1,0:T(8,128)(2,1)S(1)}, bf16[264,128]{1,0:T(8,128)(2,1)S(1)}, u32[]{:S(2)}, u32[]{:S(2)}) collective-permute-start(bf16[264,128]{1,0:T(8,128)(2,1)S(1)} %get-tuple-element.42), channel_id=1, source_target_pairs={{0,4},{1,5},{2,6},{3,7},{4,0},{5,1},{6,2},{7,3},{8,20},{9,21},{10,... | collective-permute-start | bytes 202760 | tf_op jit(solution)/shard_map/ppermute | solution.py:549
  93.5 14.8 %collective-permute-start.20 = (bf16[264,128]{1,0:T(8,128)(2,1)S(1)}, bf16[264,128]{1,0:T(8,128)(2,1)S(1)}, u32[]{:S(2)}, u32[]{:S(2)}) collective-permute-start(bf16[264,128]{1,0:T(8,128)(2,1)S(1)} %get-tuple-element.43), channel_id=1, source_target_pairs={{0,16},{1,17},{2,18},{3,19},{4,20},{5,21},{6,22},{7,23},{8,0},{9,1... | collective-permute-start | bytes 202760 | tf_op jit(solution)/shard_map/ppermute | solution.py:549
  98.8 9.5 %collective-permute-start.21 = (bf16[264,128]{1,0:T(8,128)(2,1)S(1)}, bf16[264,128]{1,0:T(8,128)(2,1)S(1)}, u32[]{:S(2)}, u32[]{:S(2)}) collective-permute-start(bf16[264,128]{1,0:T(8,128)(2,1)S(1)} %get-tuple-element.44), channel_id=1, source_target_pairs={{0,20},{1,21},{2,22},{3,23},{4,16},{5,17},{6,18},{7,19},{8,4},{9,5... | collective-permute-start | bytes 202760 | tf_op jit(solution)/shard_map/ppermute | solution.py:549

commit v5 on v4

--- a/solution.py
+++ b/solution.py
@@ -33,11 +33,22 @@
     return pl.CostEstimate(flops=flops, bytes_accessed=nbytes, transcendentals=exps)
 
 
-def first_kernel(branches, place_ref, th_ref, tg_ref, sh_ref, sg_ref, block_ref, own_ref, turned_ref, inv_ref, *refs):
-    sent, normed_ref = refs[:-1], refs[-1]
+def first_kernel(branches, place_ref, *refs):
+    sources, (block_ref, own_ref, inv_ref) = refs[:4], refs[4:7]
+    sent, (normed_ref, th_ref, tg_ref, sh_ref, sg_ref, sems) = refs[7 : 6 + branches], refs[6 + branches :]
+    copies = [
+        pltpu.make_async_copy(source, target, sems.at[i])
+        for i, (source, target) in enumerate(zip(sources, (th_ref, tg_ref, sh_ref, sg_ref)))
+    ]
+    for copy in copies:
+        copy.start()
+    for copy in copies[:2]:
+        copy.wait()
     values = th_ref[0].astype(jnp.float32)
     scale = lax.rsqrt(jnp.mean(values * values, axis=-1, keepdims=True) + eps)
     block_ref[...] = (values * scale * tg_ref[...]).astype(jnp.bfloat16)
+    for copy in copies[2:]:
+        copy.wait()
     values = sh_ref[...].astype(jnp.float32)
     scale = lax.rsqrt(jnp.mean(values * values, axis=-1, keepdims=True) + eps)
     inv_ref[...] = scale
@@ -45,9 +56,7 @@
     part = own_ref.shape[1]
     half = own_ref.shape[0] // 2
     b = place_ref[0]
-    own = normed_ref[:, pl.ds(pl.multiple_of(b * part, part), part)]
-    own_ref[...] = own
-    turned_ref[...] = jnp.transpose(own)
+    own_ref[...] = normed_ref[:, pl.ds(pl.multiple_of(b * part, part), part)]
     start = pl.multiple_of((place_ref[1] % 2) * half, half)
     for r in range(1, branches):
         cols = pl.ds(pl.multiple_of((b ^ r) * part, part), part)
@@ -63,14 +72,15 @@
         out_shape=(
             jax.ShapeDtypeStruct(teacher_hidden.shape[1:], bf16),
             jax.ShapeDtypeStruct((rows, part), bf16),
-            jax.ShapeDtypeStruct((part, rows), bf16),
             jax.ShapeDtypeStruct((rows, 1), jnp.float32),
             *[jax.ShapeDtypeStruct((rows // 2, part), bf16)] * (branches - 1),
         ),
-        in_specs=[SMEM] + [VMEM] * 4,
-        out_specs=(VMEM,) * (3 + branches),
-        scratch_shapes=[pltpu.VMEM((rows, width), bf16)],
-        compiler_params=params(16),
+        in_specs=[SMEM] + [pl.BlockSpec(memory_space=pl.ANY)] * 4,
+        out_specs=(VMEM,) * (2 + branches),
+        scratch_shapes=[pltpu.VMEM((rows, width), bf16)]
+        + [pltpu.VMEM(value.shape, value.dtype) for value in (teacher_hidden, teacher_gain, student_hidden)]
+        + [pltpu.VMEM((1, width), jnp.float32), pltpu.SemaphoreType.DMA((4,))],
+        compiler_params=params(60),
         cost_estimate=cost(8 * rows * width, 4 * rows * width),
         name="first",
     )(place, teacher_hidden, teacher_gain, student_hidden, student_gain[None])
@@ -94,16 +104,20 @@
     return arrays, tuple(keys)
 
 
-def own_dot_kernel(rows_ref, w_ref, out_ref):
+def own_dot_kernel(rows_ref, w_ref, out_ref, turned_ref):
+    turned_ref[...] = jnp.transpose(rows_ref[...])
     out_ref[...] = jnp.dot(rows_ref[...], w_ref[...], preferred_element_type=jnp.float32)
 
 
 def own_dot(rows, head):
     return pl.pallas_call(
         own_dot_kernel,
-        out_shape=jax.ShapeDtypeStruct((rows.shape[0], head.shape[1]), jnp.float32),
+        out_shape=(
+            jax.ShapeDtypeStruct((rows.shape[0], head.shape[1]), jnp.float32),
+            jax.ShapeDtypeStruct(rows.shape[::-1], rows.dtype),
+        ),
         in_specs=[VMEM, VMEM],
-        out_specs=VMEM,
+        out_specs=(VMEM, VMEM),
         compiler_params=params(16),
         cost_estimate=cost(2 * rows.size * head.shape[1], 2 * head.size),
         name="owndot",
@@ -325,80 +339,74 @@
     )(place, grads, head)
 
 
-def fold_kernel(width, mine_ref, got_ref, keep_ref, send_ref):
+def fold_kernel(mine_ref, got_ref, *out):
     f32 = jnp.float32
-    count = (mine_ref.shape[0] - EXTRA) // width
-    for k in range(count):
+    width = out[0].shape[0] - EXTRA
+    full = len(out) * width
+    dots = extra_values(mine_ref[full:], 1)[0] + extra_values(got_ref[full:], 1)[0]
+    for k, ref in enumerate(out):
         at = slice(k * width, (k + 1) * width)
-        total = mine_ref[at].astype(f32) + got_ref[at].astype(f32)
-        to = slice(k // 2 * width, (k // 2 + 1) * width)
-        (send_ref if k % 2 else keep_ref)[to] = total.astype(keep_ref.dtype)
-    dots = extra_values(mine_ref[count * width :], 1)[0] + extra_values(got_ref[count * width :], 1)[0]
-    extra = extra_rows([dots], keep_ref.dtype)
-    keep_ref[count // 2 * width :] = extra
-    send_ref[count // 2 * width :] = extra
+        ref[:width] = (mine_ref[at].astype(f32) + got_ref[at].astype(f32)).astype(ref.dtype)
+        ref[width:] = extra_rows([dots], ref.dtype)
 
 
 def fold(mine, got, width):
     full, rows = mine.shape
-    half = (full - EXTRA) // 2 + EXTRA
-    return pl.pallas_call(
-        functools.partial(fold_kernel, width),
-        out_shape=(jax.ShapeDtypeStruct((half, rows), mine.dtype),) * 2,
+    count = (full - EXTRA) // width
+    return pl.pallas_call(
+        fold_kernel,
+        out_shape=(jax.ShapeDtypeStruct((width + EXTRA, rows), mine.dtype),) * count,
         in_specs=[VMEM, VMEM],
-        out_specs=(VMEM, VMEM),
+        out_specs=(VMEM,) * count,
         compiler_params=params(8),
         cost_estimate=cost(mine.size, 6 * mine.size),
         name="fold",
     )(mine, got)
 
 
-def split_kernel(count, width, place_ref, *refs):
-    mine, got, turned = (refs[i * count : (i + 1) * count] for i in range(3))
-    out = refs[3 * count :]
+def split_kernel(count, place_ref, *refs):
+    turned, out = refs[-2 * count : -count], refs[-count:]
+    each = len(refs) // count - 2
     f32 = jnp.float32
-    lows = (mine[0].shape[0] - EXTRA) // width
-    rows = mine[0].shape[1]
-    dots = [
-        extra_values(mine[r][lows * width :], 1)[0] + extra_values(got[r][lows * width :], 1)[0] for r in range(count)
-    ]
-    for low in range(lows):
-        at = slice(low * width, (low + 1) * width)
-        block = pl.multiple_of((place_ref[2] ^ (4 * low)) * width, width)
-        totals = [mine[r][at].astype(f32) + got[r][at].astype(f32) for r in range(count)]
-        gain = sum(
-            jnp.sum(totals[r] * turned[r][pl.ds(block, width)].astype(f32), axis=1, keepdims=True)
-            for r in range(count)
-        )
-        gain = as_row(gain)
-        lanes = min(width, rows)
-        gains = [gain[:, i : i + lanes] for i in range(0, width, lanes)]
-        if lanes < rows:
-            gains = [jnp.concatenate([row, jnp.zeros((1, rows - lanes), f32)], axis=1) for row in gains]
-        for r in range(count):
-            total = totals[r].astype(mine[r].dtype)
-            extra = extra_rows([dots[r]] + gains, mine[r].dtype)
-            for kh in range(count):
-
-                @pl.when((place_ref[3] ^ kh) == r)
-                def _():
-                    out[kh * lows + low][:width] = total
-                    out[kh * lows + low][width:] = extra
-
-
-def split(mine, got, turned, width, place):
-    count = len(mine)
-    rows = mine[0].shape[1]
-    lows = (mine[0].shape[0] - EXTRA) // width
-    return pl.pallas_call(
-        functools.partial(split_kernel, count, width),
-        out_shape=(jax.ShapeDtypeStruct((width + EXTRA, rows), mine[0].dtype),) * (count * lows),
-        in_specs=[SMEM] + [VMEM] * (3 * count),
-        out_specs=(VMEM,) * (count * lows),
+    width, rows = out[0].shape[0] - EXTRA, out[0].shape[1]
+    block = pl.multiple_of(place_ref[2] * width, width)
+    totals, dots, gain = [], [], 0.0
+    for r in range(count):
+        total = refs[r * each][...].astype(f32)
+        for ref in refs[r * each + 1 : (r + 1) * each]:
+            total = total + ref[...].astype(f32)
+        dots.append(extra_values(total[width:], 1)[0])
+        totals.append(total[:width])
+        gain = gain + jnp.sum(totals[r] * turned[r][pl.ds(block, width)].astype(f32), axis=1, keepdims=True)
+    gain = as_row(gain)
+    lanes = min(width, rows)
+    gains = [gain[:, i : i + lanes] for i in range(0, width, lanes)]
+    if lanes < rows:
+        gains = [jnp.concatenate([row, jnp.zeros((1, rows - lanes), f32)], axis=1) for row in gains]
+    for r in range(count):
+        total = totals[r].astype(out[0].dtype)
+        extra = extra_rows([dots[r]] + gains, out[0].dtype)
+        for kh in range(count):
+
+            @pl.when((place_ref[3] ^ kh) == r)
+            def _():
+                out[kh][:width] = total
+                out[kh][width:] = extra
+
+
+def split(parts, turned, place):
+    count = len(parts)
+    shape = parts[0][0].shape
+    each = len(parts[0])
+    return pl.pallas_call(
+        functools.partial(split_kernel, count),
+        out_shape=(jax.ShapeDtypeStruct(shape, parts[0][0].dtype),) * count,
+        in_specs=[SMEM] + [VMEM] * (count * (each + 1)),
+        out_specs=(VMEM,) * count,
         compiler_params=params(8),
-        cost_estimate=cost(4 * count * mine[0].size, 8 * count * mine[0].size),
+        cost_estimate=cost(8 * count * shape[0] * shape[1], 12 * count * shape[0] * shape[1]),
         name="split",
-    )(place, *mine, *got, *turned)
+    )(place, *[part for some in parts for part in some], *turned)
 
 
 def head_grad_kernel(count, *refs):
@@ -505,19 +513,19 @@
     rows, width = student_hidden.shape
     blocks = size // branches
     place = jnp.stack([b, t, t % blocks, (t // blocks) ^ b]).astype(jnp.int32)
-    teacher_block, own, own_turned, inv_scale, *sent = normalize_all(
+    teacher_block, own, inv_scale, *sent = normalize_all(
         teacher_hidden, teacher_gain, student_hidden, student_gain, place, branches
     )
 
     loaded = load(student_head)
-    turned, partials = [own_turned], []
+    own_partial, own_turned = own_dot(own, loaded)
+    turned, partials = [own_turned], [own_partial]
     for r in range(1, branches):
         mine = swap(sent[r - 1], "branch", r)
         other = swap(mine, "tok", 1)
         partial, fetched = other_dot(mine, other, loaded, place)
         turned.append(fetched)
         partials.append(swap(partial, "branch", r))
-    partials = [own_dot(own, loaded)] + partials
 
     got, keys = gather_blocks(teacher_block, size)
     teacher_stats, *exps = teacher_softmax(got, keys, teacher_head, place, blocks, branches)
@@ -530,23 +538,21 @@
     all_grads = [logit_grads] + [swap(logit_grads, "branch", r) for r in range(1, branches)]
 
     slice_width = width // size
-    kept, got = [], []
+    parts = []
     for r in range(branches):
         send = normed_grad_pieces(all_grads[r], loaded, place, blocks, 1)
         send = swap(send, "tok", 1)
         keep = normed_grad_pieces(all_grads[r], loaded, place, blocks, 0)
-        keep, send = fold(keep, send, slice_width)
-        kept.append(keep)
-        got.append(swap(send, "tok", 2))
-    owned = split(kept, got, turned, slice_width, place)
+        folded = fold(keep, send, slice_width)
+        parts.append([folded[0]] + [swap(folded[k], "tok", 2 * k) for k in range(1, blocks // 2)])
+    owned = split(parts, turned, place)
     arrived = []
     for kh in range(branches):
-        for kl in range(blocks // 4):
-            perm = []
-            for i in range(branches * size):
-                bb, h, l, rest = i // size, (i % size) // blocks, (i % blocks) // 4, i % 4
-                perm.append((i, (h ^ kh) * size + bb * blocks + (l ^ kl) * 4 + rest))
-            arrived.append(lax.ppermute(owned[kh * (blocks // 4) + kl], ("branch", "tok"), perm))
+        perm = []
+        for i in range(branches * size):
+            bb, h, rest = i // size, (i % size) // blocks, i % blocks
+            perm.append((i, (h ^ kh) * size + bb * blocks + rest))
+        arrived.append(lax.ppermute(owned[kh], ("branch", "tok"), perm))
 
     grad_head = head_grad(all_grads, turned, 0, [])
     grad_head = head_grad(all_grads, turned, 1, [grad_head])

time: 110 us -> 110 us (level)
  waiting for transfers between devices: 39.5 us -> 35.5 us
  starting transfers between devices: 30.9 us -> 33.7 us
  Pallas kernels: 26.6 us -> 28.1 us
  other arithmetic: 0.15 us -> 1.63 us
  local copies, waits for them, and re-layouts: 11.1 us -> 9.88 us
    ppermute x18 -> x22, starting transfers between devices: 18.9 us -> 24.1 us  [swap(): return lax.ppermute(value, axis, [(i, i ^ flip) for i in range(size)])]
    ppermute x4 -> x2, waiting for transfers between devices: 2.65 us -> 0.01 us  [per_device(): arrived.append(lax.ppermute(owned[kh], ('branch', 'tok'), perm))]
    pallas_call x1, Pallas kernels: 1.36 us -> 3.66 us  [normalize_all(): pl.pallas_call(functools.partial(first_kernel, branches), out_shape=(jax....]
    ppermute x4 -> x2, starting transfers between devices: 6.36 us -> 4.11 us  [per_device(): arrived.append(lax.ppermute(owned[kh], ('branch', 'tok'), perm))]
    ppermute x18 -> x22, waiting for transfers between devices: 28.6 us -> 27.3 us  [swap(): return lax.ppermute(value, axis, [(i, i ^ flip) for i in range(size)])]
    unnamed x24 -> x26, local copies, waits for them, and re-layouts: 9.49 us -> 8.27 us
  transfers between devices with their start and end apart: 23 -> 25, of which waited for: 12 -> 10; matrix products, arithmetic and copies ran while one was open for 2% -> 2% of each run, Pallas kernels for 20% -> 20%
where the time goes in v5:
time: 110 us
  waiting for transfers between devices  35.5 us (32%)
  starting transfers between devices  33.7 us (31%)
  Pallas kernels  28.1 us (26%)
  local copies, waits for them, and re-layouts  9.88 us (9%)
  other arithmetic  1.63 us (1%)
    ppermute x22, waiting for transfers between devices, swap(): return lax.ppermute(value, axis, [(i, i ^ flip) for i in range(size)])  27.3 us
    ppermute x22, starting transfers between devices, swap(): return lax.ppermute(value, axis, [(i, i ^ flip) for i in range(size)])  24.1 us
    unnamed x26, local copies, waits for them, and re-layouts  8.27 us
    all_to_all x1, waiting for transfers between devices, per_device(): stats = lax.all_to_all(stats, ('branch', 'tok'), 0, 0, tiled=True)  8.19 us
    pallas_call x2, Pallas kernels, head_grad(): pl.pallas_call(functools.partial(head_grad_kernel, count), out_shape=jax....  6.56 us
    pallas_call x4, Pallas kernels, normed_grad_pieces(): pl.pallas_call(functools.partial(pieces_kernel, parity, width), out_shape...  5.88 us
    all_to_all x1, starting transfers between devices, per_device(): stats = lax.all_to_all(stats, ('branch', 'tok'), 0, 0, tiled=True)  5.53 us
    pallas_call x1, Pallas kernels, teacher_softmax(): pl.pallas_call(functools.partial(teacher_kernel, keys, half), out_shape=(...  4.72 us
  transfers between devices with their start and end apart: 25, of which 10 were waited for; matrix products, arithmetic and copies ran while one was open for 2% of the time, Pallas kernels for 20%

profile of v5, /device:TPU:0, one launch (start us, length us, event | category | flops | bytes accessed | tf_op | source)
XLA Modules:
  0.0 109.8 jit_solution(13162490984589445362)
XLA Ops:
  0.7 0.7 pad_add_fusion.place_ref
  1.3 3.7 %first.1 = (bf16[16,4096]{1,0:T(8,128)(2,1)}, bf16[128,2048]{1,0:T(8,128)(2,1)}, f32[128,1]{1,0:T(8,128)}, bf16[64,2048]{1,0:T(8,128)(2,1)}) custom-call(s32[4]{0:T(128)} %pad_add_fusion.place_ref, bf16[1,16,4096]{2,1,0:T(8,128)(2,1)} %refs_0_.1, f32[1,4096]{1,0:T(1,128)} %refs_1_.1, bf16[128,4096]{1,0:T(8,128)(2,1)} %refs_2_.1, f32[1,4096]{1,0:T(1,128)} %bitcast.14), custom_call_target="tpu_custom_call" | custom-call | flops 4194304 | bytes 2097152 | tf_op jit(solution)/shard_map/first/pallas_call | solution.py:70
  5.0 4.1 %collective-permute-start.6 = (bf16[16,4096]{1,0:T(8,128)(2,1)}, bf16[16,4096]{1,0:T(8,128)(2,1)S(1)}, u32[]{:S(2)}, u32[]{:S(2)}) collective-permute-start(bf16[16,4096]{1,0:T(8,128)(2,1)} %get-tuple-element.32.refs_0_), channel_id=1, source_target_pairs={{0,8},{1,9},{2,10},{3,11},{4,12},{5,13},{6,14},{7,15},{8,0},{9,1},... | collective-permute-start | bytes 393224 | tf_op jit(solution)/shard_map/ppermute | solution.py:20
  9.1 1.6 %collective-permute-start.4 = (bf16[16,4096]{1,0:T(8,128)(2,1)}, bf16[16,4096]{1,0:T(8,128)(2,1)S(1)}, u32[]{:S(2)}, u32[]{:S(2)}) collective-permute-start(bf16[16,4096]{1,0:T(8,128)(2,1)} %get-tuple-element.32.refs_0_), channel_id=1, source_target_pairs={{0,4},{1,5},{2,6},{3,7},{4,0},{5,1},{6,2},{7,3},{8,12},{9,13},{10,... | collective-permute-start | bytes 393224 | tf_op jit(solution)/shard_map/ppermute | solution.py:20
  10.7 5.0 %collective-permute-done.6.refs_4_ = bf16[16,4096]{1,0:T(8,128)(2,1)S(1)} collective-permute-done((bf16[16,4096]{1,0:T(8,128)(2,1)}, bf16[16,4096]{1,0:T(8,128)(2,1)S(1)}, u32[]{:S(2)}, u32[]{:S(2)}) %collective-permute-start.6) | collective-permute-done | bytes 131104 | tf_op jit(solution)/shard_map/ppermute | solution.py:20
  15.7 0.7 collective-permute-start.8
  16.5 1.5 %collective-permute-start.3 = (bf16[16,4096]{1,0:T(8,128)(2,1)}, bf16[16,4096]{1,0:T(8,128)(2,1)S(1)}, u32[]{:S(2)}, u32[]{:S(2)}) collective-permute-start(bf16[16,4096]{1,0:T(8,128)(2,1)} %get-tuple-element.32.refs_0_), channel_id=1, source_target_pairs={{0,2},{1,3},{2,0},{3,1},{4,6},{5,7},{6,4},{7,5},{8,10},{9,11},{10,... | collective-permute-start | bytes 393224 | tf_op jit(solution)/shard_map/ppermute | solution.py:20
  18.0 0.5 collective-permute-start.5
  18.5 1.5 %collective-permute-start = (bf16[64,2048]{1,0:T(8,128)(2,1)}, bf16[64,2048]{1,0:T(8,128)(2,1)S(1)}, u32[]{:S(2)}, u32[]{:S(2)}) collective-permute-start(bf16[64,2048]{1,0:T(8,128)(2,1)} %get-tuple-element.30), channel_id=1, source_target_pairs={{0,16},{16,0},{1,17},{17,1},{2,18},{18,2},{3,19},{19,3},{4,20},{20... | collective-permute-start | bytes 786440 | tf_op jit(solution)/shard_map/ppermute | solution.py:20
  20.0 1.5 %collective-permute-start.7 = (bf16[16,4096]{1,0:T(8,128)(2,1)S(1)}, bf16[16,4096]{1,0:T(8,128)(2,1)S(1)}, u32[]{:S(2)}, u32[]{:S(2)}) collective-permute-start(bf16[16,4096]{1,0:T(8,128)(2,1)S(1)} %collective-permute-done.6.refs_4_), channel_id=1, source_target_pairs={{0,2},{1,3},{2,0},{3,1},{4,6},{5,7},{6,4},{7,5},{8,10},{9,11},{10,... | collective-permute-start | bytes 393224 | tf_op jit(solution)/shard_map/ppermute | solution.py:20
  21.5 0.8 collective-permute-start.9
  22.3 0.8 collective-permute-done.3.refs_1_
  23.1 2.8 %collective-permute-done.5.refs_3_ = bf16[16,4096]{1,0:T(8,128)(2,1)S(1)} collective-permute-done((bf16[16,4096]{1,0:T(8,128)(2,1)S(1)}, bf16[16,4096]{1,0:T(8,128)(2,1)S(1)}, u32[]{:S(2)}, u32[]{:S(2)}) %collective-permute-start.5) | collective-permute-done | bytes 131104 | tf_op jit(solution)/shard_map/ppermute | solution.py:20
  25.9 0.9 pad_maximum_fusion
  27.4 1.3 %collective-permute-done.7.refs_5_ = bf16[16,4096]{1,0:T(8,128)(2,1)S(1)} collective-permute-done((bf16[16,4096]{1,0:T(8,128)(2,1)S(1)}, bf16[16,4096]{1,0:T(8,128)(2,1)S(1)}, u32[]{:S(2)}, u32[]{:S(2)}) %collective-permute-start.7) | collective-permute-done | bytes 131104 | tf_op jit(solution)/shard_map/ppermute | solution.py:20
  28.7 1.6 %collective-permute-done.9.refs_7_ = bf16[16,4096]{1,0:T(8,128)(2,1)S(1)} collective-permute-done((bf16[16,4096]{1,0:T(8,128)(2,1)S(1)}, bf16[16,4096]{1,0:T(8,128)(2,1)S(1)}, u32[]{:S(2)}, u32[]{:S(2)}) %collective-permute-start.9) | collective-permute-done | bytes 131104 | tf_op jit(solution)/shard_map/ppermute | solution.py:20
  30.4 2.6 %copy-done.3 = bf16[2048,1280]{1,0:T(8,128)(2,1)S(1)} copy-done((bf16[2048,1280]{1,0:T(8,128)(2,1)S(1)}, bf16[2048,1280]{1,0:T(8,128)(2,1)}, u32[]{:S(2)}) %copy-start.3) | copy-done | bytes 5242904
  33.4 1.5 %otherdot.1 = (f32[128,1280]{1,0:T(8,128)S(1)}, bf16[2048,128]{1,0:T(8,128)(2,1)S(1)}) custom-call(s32[4]{0:T(128)S(1)} %copy-done.7, bf16[64,2048]{1,0:T(8,128)(2,1)S(1)} %collective-permute-done.mine_ref, bf16[64,2048]{1,0:T(8,128)(2,1)S(1)} %collective-permute-done.1.other_ref, bf16[2048,1280]{1,0:T(8,128)(2,1)S(1)} %load.1.w_ref), custom_call_target="tpu_custom_call" | custom-call | flops 671088640 | bytes 5242880 | tf_op jit(solution)/shard_map/otherdot/pallas_call | solution.py:138
  35.0 1.6 %collective-permute-start.2 = (f32[128,1280]{1,0:T(8,128)S(1)}, f32[128,1280]{1,0:T(8,128)S(1)}, u32[]{:S(2)}, u32[]{:S(2)}) collective-permute-start(f32[128,1280]{1,0:T(8,128)S(1)} %get-tuple-element.31), channel_id=1, source_target_pairs={{0,16},{16,0},{1,17},{17,1},{2,18},{18,2},{3,19},{19,3},{4,20},{20... | collective-permute-start | bytes 1966088 | tf_op jit(solution)/shard_map/ppermute | solution.py:20
  36.6 0.6 slice-done.2
  37.2 4.7 %teacher.1 = (f32[2,256]{1,0:T(2,128)S(1)}, bf16[128,1280]{1,0:T(8,128)(2,1)S(1)}, bf16[128,1280]{1,0:T(8,128)(2,1)S(1)}) custom-call(s32[4]{0:T(128)S(1)} %copy-done.7, bf16[16,4096]{1,0:T(8,128)(2,1)S(1)} %copy-done.4, bf16[16,4096]{1,0:T(8,128)(2,1)S(1)} %collective-permute-done.3.refs_1_, bf16[16,4096]{1,0:T(8,128)(2,1)S(1)} %collective-permute-done.4.refs_2_, ...), custom_call_target="tpu_custom_call" | custom-call | flops 2684354560 | bytes 10485760 | tf_op jit(solution)/shard_map/teacher/pallas_call | solution.py:216
  41.9 1.6 %collective-permute-start.12 = (bf16[128,1280]{1,0:T(8,128)(2,1)S(1)}, bf16[128,1280]{1,0:T(8,128)(2,1)S(1)}, u32[]{:S(2)}, u32[]{:S(2)}) collective-permute-start(bf16[128,1280]{1,0:T(8,128)(2,1)S(1)} %get-tuple-element.37), channel_id=1, source_target_pairs={{0,16},{16,0},{1,17},{17,1},{2,18},{18,2},{3,19},{19,3},{4,20},{20... | collective-permute-start | bytes 983048 | tf_op jit(solution)/shard_map/ppermute | solution.py:20
  43.5 0.9 owndot.1
  44.4 8.2 %collective-permute-done.2.refs_1_ = f32[128,1280]{1,0:T(8,128)S(1)} collective-permute-done((f32[128,1280]{1,0:T(8,128)S(1)}, f32[128,1280]{1,0:T(8,128)S(1)}, u32[]{:S(2)}, u32[]{:S(2)}) %collective-permute-start.2) | collective-permute-done | bytes 655392 | tf_op jit(solution)/shard_map/ppermute | solution.py:20
  52.6 1.5 %stats.1 = (f32[128,1280]{1,0:T(8,128)S(1)}, f32[32,8,128]{2,1,0:T(8,128)}) custom-call(s32[4]{0:T(128)S(1)} %copy-done.7, f32[128,1280]{1,0:T(8,128)S(1)} %get-tuple-element.29.refs_0_, f32[128,1280]{1,0:T(8,128)S(1)} %collective-permute-done.2.refs_1_, f32[2,256]{1,0:T(2,128)S(1)} %get-tuple-element.33.refs_2_, s32[2,128]{1,0:T(2,128)S(1)} %bitcast.12), custom_call_target="tpu_custom_call" | custom-call | flops 1310720 | bytes 1966080 | tf_op jit(solution)/shard_map/stats/pallas_call | solution.py:260
  54.1 5.5 %all-to-all-start = ((f32[32,8,128]{2,1,0:T(8,128)}), f32[32,8,128]{2,1,0:T(8,128)S(1)}, u32[]{:S(2)}, u32[]{:S(2)}) async-start(f32[32,8,128]{2,1,0:T(8,128)} %get-tuple-element.34), calls=%async_computation | async-start | bytes 262144 | tf_op jit(solution)/shard_map/all_to_all | solution.py:536
  59.6 8.2 %all-to-all-done.stats_ref = f32[32,8,128]{2,1,0:T(8,128)S(1)} async-done(((f32[32,8,128]{2,1,0:T(8,128)}), f32[32,8,128]{2,1,0:T(8,128)S(1)}, u32[]{:S(2)}, u32[]{:S(2)}) %all-to-all-start) | async-done | bytes 131104 | tf_op jit(solution)/shard_map/all_to_all | solution.py:536
  67.8 1.3 %grads.1.refs_0_.grads_ref = bf16[136,1280]{1,0:T(8,128)(2,1)S(1)} custom-call(s32[4]{0:T(128)S(1)} %copy-done.7, f32[32,8,128]{2,1,0:T(8,128)S(1)} %all-to-all-done.stats_ref, f32[128,1280]{1,0:T(8,128)S(1)} %get-tuple-element.35.logits_ref, s32[1,128]{1,0:T(1,128)S(1)} %bitcast.13, bf16[128,1280]{1,0:T(8,128)(2,1)S(1)} %get-tuple-element.36.refs_0_, ...), custom_call_target="tpu_custom_call" | custom-call | flops 2621440 | bytes 1638400 | tf_op jit(solution)/shard_map/grads/pallas_call | solution.py:305
  69.1 0.8 collective-permute-start.13
  69.9 2.5 %copy-done.1 = bf16[2048,1280]{1,0:T(8,128)(2,1)S(1)} copy-done((bf16[2048,1280]{1,0:T(8,128)(2,1)S(1)}, bf16[2048,1280]{1,0:T(8,128)(2,1)}, u32[]{:S(2)}) %copy-start.1) | copy-done | bytes 5242904
  72.4 1.5 %pieces.5 = bf16[1032,128]{1,0:T(8,128)(2,1)S(1)} custom-call(s32[4]{0:T(128)S(1)} %copy-done.7, bf16[136,1280]{1,0:T(8,128)(2,1)S(1)} %grads.1.refs_0_.grads_ref, bf16[2048,1280]{1,0:T(8,128)(2,1)S(1)} %copy-done.1), custom_call_target="tpu_custom_call" | custom-call | flops 335544320 | bytes 2621440 | tf_op jit(solution)/shard_map/pieces/pallas_call | solution.py:330
  73.9 5.5 %collective-permute-done.13.refs_1_.grads_ref = bf16[136,1280]{1,0:T(8,128)(2,1)S(1)} collective-permute-done((bf16[136,1280]{1,0:T(8,128)(2,1)S(1)}, bf16[136,1280]{1,0:T(8,128)(2,1)S(1)}, u32[]{:S(2)}, u32[]{:S(2)}) %collective-permute-start.13) | collective-permute-done | bytes 348192 | tf_op jit(solution)/shard_map/ppermute | solution.py:20
  79.4 1.5 %pieces.7 = bf16[1032,128]{1,0:T(8,128)(2,1)S(1)} custom-call(s32[4]{0:T(128)S(1)} %copy-done.7, bf16[136,1280]{1,0:T(8,128)(2,1)S(1)} %collective-permute-done.13.refs_1_.grads_ref, bf16[2048,1280]{1,0:T(8,128)(2,1)S(1)} %copy-done.1), custom_call_target="tpu_custom_call" | custom-call | flops 335544320 | bytes 2621440 | tf_op jit(solution)/shard_map/pieces/pallas_call | solution.py:330
  81.0 1.5 %pieces.4.mine_ref = bf16[1032,128]{1,0:T(8,128)(2,1)S(1)} custom-call(s32[4]{0:T(128)S(1)} %copy-done.7, bf16[136,1280]{1,0:T(8,128)(2,1)S(1)} %grads.1.refs_0_.grads_ref, bf16[2048,1280]{1,0:T(8,128)(2,1)S(1)} %copy-done.1), custom_call_target="tpu_custom_call" | custom-call | flops 335544320 | bytes 2621440 | tf_op jit(solution)/shard_map/pieces/pallas_call | solution.py:330
  82.9 0.8 dynamic_slice.7
  84.0 2.8 %collective-permute-start.17 = (bf16[264,128]{1,0:T(8,128)(2,1)S(1)}, bf16[264,128]{1,0:T(8,128)(2,1)S(1)}, u32[]{:S(2)}, u32[]{:S(2)}) collective-permute-start(bf16[264,128]{1,0:T(8,128)(2,1)S(1)} %get-tuple-element.44), channel_id=1, source_target_pairs={{0,6},{1,7},{2,4},{3,5},{4,2},{5,3},{6,0},{7,1},{8,14},{9,15},{10,... | collective-permute-start | bytes 202760 | tf_op jit(solution)/shard_map/ppermute | solution.py:20
  86.9 2.5 %copy-done.2 = bf16[2048,1280]{1,0:T(8,128)(2,1)S(1)} copy-done((bf16[2048,1280]{1,0:T(8,128)(2,1)S(1)}, bf16[2048,1280]{1,0:T(8,128)(2,1)}, u32[]{:S(2)}) %copy-start.2) | copy-done | bytes 5242904
  89.3 1.5 %pieces.6.mine_ref = bf16[1032,128]{1,0:T(8,128)(2,1)S(1)} custom-call(s32[4]{0:T(128)S(1)} %copy-done.7, bf16[136,1280]{1,0:T(8,128)(2,1)S(1)} %collective-permute-done.13.refs_1_.grads_ref, bf16[2048,1280]{1,0:T(8,128)(2,1)S(1)} %copy-done.2), custom_call_target="tpu_custom_call" | custom-call | flops 335544320 | bytes 2621440 | tf_op jit(solution)/shard_map/pieces/pallas_call | solution.py:330
  91.6 2.8 %collective-permute-start.21 = (bf16[264,128]{1,0:T(8,128)(2,1)S(1)}, bf16[264,128]{1,0:T(8,128)(2,1)S(1)}, u32[]{:S(2)}, u32[]{:S(2)}) collective-permute-start(bf16[264,128]{1,0:T(8,128)(2,1)S(1)} %get-tuple-element.48), channel_id=1, source_target_pairs={{0,6},{1,7},{2,4},{3,5},{4,2},{5,3},{6,0},{7,1},{8,14},{9,15},{10,... | collective-permute-start | bytes 202760 | tf_op jit(solution)/shard_map/ppermute | solution.py:20
  94.5 0.8 constant_dynamic-slice_fusion.hidden_ref
  95.3 0.7 collective-permute-done.19.refs_5_
  96.0 1.5 %collective-permute-done.21.refs_7_ = bf16[264,128]{1,0:T(8,128)(2,1)S(1)} collective-permute-done((bf16[264,128]{1,0:T(8,128)(2,1)S(1)}, bf16[264,128]{1,0:T(8,128)(2,1)S(1)}, u32[]{:S(2)}, u32[]{:S(2)}) %collective-permute-start.21) | collective-permute-done | bytes 67616 | tf_op jit(solution)/shard_map/ppermute | solution.py:20
  97.4 0.8 split.1
  98.2 0.7 collective-permute-start.22
  98.9 3.4 %collective-permute-start.23 = (bf16[264,128]{1,0:T(8,128)(2,1)S(1)}, bf16[264,128]{1,0:T(8,128)(2,1)S(1)}, u32[]{:S(2)}, u32[]{:S(2)}) collective-permute-start(bf16[264,128]{1,0:T(8,128)(2,1)S(1)} %get-tuple-element.50), channel_id=1, source_target_pairs={{0,16},{1,17},{2,18},{3,19},{4,20},{5,21},{6,22},{7,23},{8,0},{9,1... | collective-permute-start | bytes 202760 | tf_op jit(solution)/shard_map/ppermute | solution.py:555
  102.3 3.3 %headgrad.2.refs_4_ = f32[2048,1280]{1,0:T(8,128)} custom-call(bf16[136,1280]{1,0:T(8,128)(2,1)S(1)} %grads.1.refs_0_.grads_ref, bf16[136,1280]{1,0:T(8,128)(2,1)S(1)} %collective-permute-done.13.refs_1_.grads_ref, bf16[2048,128]{1,0:T(8,128)(2,1)S(1)} %get-tuple-element.38.refs_2_.refs_8_, bf16[2048,128]{1,0:T(8,128)(2,1)S(1)} %get-tuple-element.39.refs_3_.refs_9_), custom_call_target="tpu_custom_call" | custom-call | flops 671088640 | bytes 5242880 | tf_op jit(solution)/shard_map/headgrad/pallas_call | solution.py:432
  105.6 3.3 %headgrad.3 = f32[2048,1280]{1,0:T(8,128)} custom-call(bf16[136,1280]{1,0:T(8,128)(2,1)S(1)} %grads.1.refs_0_.grads_ref, bf16[136,1280]{1,0:T(8,128)(2,1)S(1)} %collective-permute-done.13.refs_1_.grads_ref, bf16[2048,128]{1,0:T(8,128)(2,1)S(1)} %get-tuple-element.38.refs_2_.refs_8_, ...), custom_call_target="tpu_custom_call", output_to_operand_aliasing={{}: (4, {})} | custom-call | flops 671088640 | bytes 5242880 | tf_op jit(solution)/shard_map/headgrad/pallas_call | solution.py:432
  108.9 0.9 last.1
  (51 shorter events, 2.9 us)
Async XLA Ops:
  0.6 35.9 %slice-start = ((s8[10485760]{0:T(1024)(128)(4,1)}), s8[2097152]{0:T(1024)(128)(4,1)S(1)}, s32[]{:S(2)}) async-start(s8[10485760]{0:T(1024)(128)(4,1)} %bitcast.9), calls=%async_computation.1 | async-start | bytes 4194304
  1.3 32.1 %copy-start.7 = (s32[4]{0:T(128)S(1)}, s32[4]{0:T(128)}, u32[]{:S(2)}) copy-start(s32[4]{0:T(128)} %pad_add_fusion.place_ref) | copy-start | bytes 52
  5.0 31.6 %copy-start.4 = (bf16[16,4096]{1,0:T(8,128)(2,1)S(1)}, bf16[16,4096]{1,0:T(8,128)(2,1)}, u32[]{:S(2)}) copy-start(bf16[16,4096]{1,0:T(8,128)(2,1)} %get-tuple-element.32.refs_0_) | copy-start | bytes 393220
  5.0 10.7 %collective-permute-start.6 = (bf16[16,4096]{1,0:T(8,128)(2,1)}, bf16[16,4096]{1,0:T(8,128)(2,1)S(1)}, u32[]{:S(2)}, u32[]{:S(2)}) collective-permute-start(bf16[16,4096]{1,0:T(8,128)(2,1)} %get-tuple-element.32.refs_0_), channel_id=1, source_target_pairs={{0,8},{1,9},{2,10},{3,11},{4,12},{5,13},{6,14},{7,15},{8,0},{9,1},... | collective-permute-start | bytes 393224 | tf_op jit(solution)/shard_map/ppermute | solution.py:20
  9.1 8.9 %collective-permute-start.4 = (bf16[16,4096]{1,0:T(8,128)(2,1)}, bf16[16,4096]{1,0:T(8,128)(2,1)S(1)}, u32[]{:S(2)}, u32[]{:S(2)}) collective-permute-start(bf16[16,4096]{1,0:T(8,128)(2,1)} %get-tuple-element.32.refs_0_), channel_id=1, source_target_pairs={{0,4},{1,5},{2,6},{3,7},{4,0},{5,1},{6,2},{7,3},{8,12},{9,13},{10,... | collective-permute-start | bytes 393224 | tf_op jit(solution)/shard_map/ppermute | solution.py:20
  15.7 5.8 %collective-permute-start.8 = (bf16[16,4096]{1,0:T(8,128)(2,1)S(1)}, bf16[16,4096]{1,0:T(8,128)(2,1)S(1)}, u32[]{:S(2)}, u32[]{:S(2)}) collective-permute-start(bf16[16,4096]{1,0:T(8,128)(2,1)S(1)} %collective-permute-done.6.refs_4_), channel_id=1, source_target_pairs={{0,4},{1,5},{2,6},{3,7},{4,0},{5,1},{6,2},{7,3},{8,12},{9,13},{10,... | collective-permute-start | bytes 393224 | tf_op jit(solution)/shard_map/ppermute | solution.py:20
  16.5 6.6 %collective-permute-start.3 = (bf16[16,4096]{1,0:T(8,128)(2,1)}, bf16[16,4096]{1,0:T(8,128)(2,1)S(1)}, u32[]{:S(2)}, u32[]{:S(2)}) collective-permute-start(bf16[16,4096]{1,0:T(8,128)(2,1)} %get-tuple-element.32.refs_0_), channel_id=1, source_target_pairs={{0,2},{1,3},{2,0},{3,1},{4,6},{5,7},{6,4},{7,5},{8,10},{9,11},{10,... | collective-permute-start | bytes 393224 | tf_op jit(solution)/shard_map/ppermute | solution.py:20
  18.0 7.9 %collective-permute-start.5 = (bf16[16,4096]{1,0:T(8,128)(2,1)S(1)}, bf16[16,4096]{1,0:T(8,128)(2,1)S(1)}, u32[]{:S(2)}, u32[]{:S(2)}) collective-permute-start(bf16[16,4096]{1,0:T(8,128)(2,1)S(1)} %collective-permute-done.4.refs_2_), channel_id=1, source_target_pairs={{0,2},{1,3},{2,0},{3,1},{4,6},{5,7},{6,4},{7,5},{8,10},{9,11},{10,... | collective-permute-start | bytes 393224 | tf_op jit(solution)/shard_map/ppermute | solution.py:20
  18.5 8.4 %collective-permute-start = (bf16[64,2048]{1,0:T(8,128)(2,1)}, bf16[64,2048]{1,0:T(8,128)(2,1)S(1)}, u32[]{:S(2)}, u32[]{:S(2)}) collective-permute-start(bf16[64,2048]{1,0:T(8,128)(2,1)} %get-tuple-element.30), channel_id=1, source_target_pairs={{0,16},{16,0},{1,17},{17,1},{2,18},{18,2},{3,19},{19,3},{4,20},{20... | collective-permute-start | bytes 786440 | tf_op jit(solution)/shard_map/ppermute | solution.py:20
  20.0 8.7 %collective-permute-start.7 = (bf16[16,4096]{1,0:T(8,128)(2,1)S(1)}, bf16[16,4096]{1,0:T(8,128)(2,1)S(1)}, u32[]{:S(2)}, u32[]{:S(2)}) collective-permute-start(bf16[16,4096]{1,0:T(8,128)(2,1)S(1)} %collective-permute-done.6.refs_4_), channel_id=1, source_target_pairs={{0,2},{1,3},{2,0},{3,1},{4,6},{5,7},{6,4},{7,5},{8,10},{9,11},{10,... | collective-permute-start | bytes 393224 | tf_op jit(solution)/shard_map/ppermute | solution.py:20
  21.5 8.7 %collective-permute-start.9 = (bf16[16,4096]{1,0:T(8,128)(2,1)S(1)}, bf16[16,4096]{1,0:T(8,128)(2,1)S(1)}, u32[]{:S(2)}, u32[]{:S(2)}) collective-permute-start(bf16[16,4096]{1,0:T(8,128)(2,1)S(1)} %collective-permute-done.8.refs_6_), channel_id=1, source_target_pairs={{0,2},{1,3},{2,0},{3,1},{4,6},{5,7},{6,4},{7,5},{8,10},{9,11},{10,... | collective-permute-start | bytes 393224 | tf_op jit(solution)/shard_map/ppermute | solution.py:20
  26.8 9.8 %collective-permute-start.10 = (bf16[64,4096]{1,0:T(8,128)(2,1)S(1)}, bf16[64,4096]{1,0:T(8,128)(2,1)S(1)}, u32[]{:S(2)}, u32[]{:S(2)}) collective-permute-start(bf16[64,4096]{1,0:T(8,128)(2,1)S(1)} %pad_maximum_fusion), channel_id=1, source_target_pairs={{0,1},{1,0},{2,3},{3,2},{4,5},{5,4},{6,7},{7,6},{8,9},{9,8},{10,11... | collective-permute-start | bytes 1572872 | tf_op jit(solution)/shard_map/ppermute | solution.py:20
  26.9 6.5 %collective-permute-start.1 = (bf16[64,2048]{1,0:T(8,128)(2,1)S(1)}, bf16[64,2048]{1,0:T(8,128)(2,1)S(1)}, u32[]{:S(2)}, u32[]{:S(2)}) collective-permute-start(bf16[64,2048]{1,0:T(8,128)(2,1)S(1)} %collective-permute-done.mine_ref), channel_id=1, source_target_pairs={{0,1},{1,0},{2,3},{3,2},{4,5},{5,4},{6,7},{7,6},{8,9},{9,8},{10,11... | collective-permute-start | bytes 786440 | tf_op jit(solution)/shard_map/ppermute | solution.py:20
  30.3 6.3 %slice-start.1 = ((s8[10485760]{0:T(1024)(128)(4,1)}), s8[4194304]{0:T(1024)(128)(4,1)S(1)}, s32[]{:S(2)}) async-start(s8[10485760]{0:T(1024)(128)(4,1)} %bitcast.9), calls=%async_computation.2 | async-start | bytes 8388608
  30.3 6.9 %slice-start.2 = ((s8[10485760]{0:T(1024)(128)(4,1)}), s8[4194304]{0:T(1024)(128)(4,1)S(1)}, s32[]{:S(2)}) async-start(s8[10485760]{0:T(1024)(128)(4,1)} %bitcast.9), calls=%async_computation.3 | async-start | bytes 8388608
  30.3 6.3 %collective-permute-start.11 = (bf16[64,4096]{1,0:T(8,128)(2,1)S(1)}, bf16[64,4096]{1,0:T(8,128)(2,1)S(1)}, u32[]{:S(2)}, u32[]{:S(2)}) collective-permute-start(bf16[64,4096]{1,0:T(8,128)(2,1)S(1)} %pad_maximum_fusion.1), channel_id=1, source_target_pairs={{0,1},{1,0},{2,3},{3,2},{4,5},{5,4},{6,7},{7,6},{8,9},{9,8},{10,11... | collective-permute-start | bytes 1572872 | tf_op jit(solution)/shard_map/ppermute | solution.py:20
  30.4 2.6 %copy-start.3 = (bf16[2048,1280]{1,0:T(8,128)(2,1)S(1)}, bf16[2048,1280]{1,0:T(8,128)(2,1)}, u32[]{:S(2)}) copy-start(bf16[2048,1280]{1,0:T(8,128)(2,1)} %from_ref.1) | copy-start | bytes 15728644
  33.4 11.0 %copy-start = (bf16[2048,1280]{1,0:T(8,128)(2,1)}, bf16[2048,1280]{1,0:T(8,128)(2,1)S(1)}, u32[]{:S(2)}) copy-start(bf16[2048,1280]{1,0:T(8,128)(2,1)S(1)} %load.1.w_ref) | copy-start | bytes 15728644
  33.4 10.1 %copy-start.5 = (bf16[128,2048]{1,0:T(8,128)(2,1)S(1)}, bf16[128,2048]{1,0:T(8,128)(2,1)}, u32[]{:S(2)}) copy-start(bf16[128,2048]{1,0:T(8,128)(2,1)} %get-tuple-element.28.rows_ref) | copy-start | bytes 1572868
  35.0 17.6 %copy-start.8 = (s32[256,1]{0,1:T(1,128)S(1)}, s32[256,1]{0,1:T(1,128)}, u32[]{:S(2)}) copy-start(s32[256,1]{0,1:T(1,128)} %param.14) | copy-start | bytes 3076
  35.0 32.8 %copy-start.9 = (s32[128]{0:T(128)S(1)}, s32[128]{0:T(128)}, u32[]{:S(2)}) copy-start(s32[128]{0:T(128)} %param.15) | copy-start | bytes 1540
  35.0 17.5 %collective-permute-start.2 = (f32[128,1280]{1,0:T(8,128)S(1)}, f32[128,1280]{1,0:T(8,128)S(1)}, u32[]{:S(2)}, u32[]{:S(2)}) collective-permute-start(f32[128,1280]{1,0:T(8,128)S(1)} %get-tuple-element.31), channel_id=1, source_target_pairs={{0,16},{16,0},{1,17},{17,1},{2,18},{18,2},{3,19},{19,3},{4,20},{20... | collective-permute-start | bytes 1966088 | tf_op jit(solution)/shard_map/ppermute | solution.py:20
  41.9 17.7 %collective-permute-start.12 = (bf16[128,1280]{1,0:T(8,128)(2,1)S(1)}, bf16[128,1280]{1,0:T(8,128)(2,1)S(1)}, u32[]{:S(2)}, u32[]{:S(2)}) collective-permute-start(bf16[128,1280]{1,0:T(8,128)(2,1)S(1)} %get-tuple-element.37), channel_id=1, source_target_pairs={{0,16},{16,0},{1,17},{17,1},{2,18},{18,2},{3,19},{19,3},{4,20},{20... | collective-permute-start | bytes 983048 | tf_op jit(solution)/shard_map/ppermute | solution.py:20
  54.1 13.7 %all-to-all-start = ((f32[32,8,128]{2,1,0:T(8,128)}), f32[32,8,128]{2,1,0:T(8,128)S(1)}, u32[]{:S(2)}, u32[]{:S(2)}) async-start(f32[32,8,128]{2,1,0:T(8,128)} %get-tuple-element.34), calls=%async_computation | async-start | bytes 262144 | tf_op jit(solution)/shard_map/all_to_all | solution.py:536
  69.1 10.4 %collective-permute-start.13 = (bf16[136,1280]{1,0:T(8,128)(2,1)S(1)}, bf16[136,1280]{1,0:T(8,128)(2,1)S(1)}, u32[]{:S(2)}, u32[]{:S(2)}) collective-permute-start(bf16[136,1280]{1,0:T(8,128)(2,1)S(1)} %grads.1.refs_0_.grads_ref), channel_id=1, source_target_pairs={{0,16},{16,0},{1,17},{17,1},{2,18},{18,2},{3,19},{19,3},{4,20},{20... | collective-permute-start | bytes 1044488 | tf_op jit(solution)/shard_map/ppermute | solution.py:20
  69.9 2.5 %copy-start.1 = (bf16[2048,1280]{1,0:T(8,128)(2,1)S(1)}, bf16[2048,1280]{1,0:T(8,128)(2,1)}, u32[]{:S(2)}) copy-start(bf16[2048,1280]{1,0:T(8,128)(2,1)} %copy-done) | copy-start | bytes 15728644
  73.9 8.6 %collective-permute-start.14 = (bf16[1032,128]{1,0:T(8,128)(2,1)S(1)}, bf16[1032,128]{1,0:T(8,128)(2,1)S(1)}, u32[]{:S(2)}, u32[]{:S(2)}) collective-permute-start(bf16[1032,128]{1,0:T(8,128)(2,1)S(1)} %pieces.5), channel_id=1, source_target_pairs={{0,1},{1,0},{2,3},{3,2},{4,5},{5,4},{6,7},{7,6},{8,9},{9,8},{10,11... | collective-permute-start | bytes 792584 | tf_op jit(solution)/shard_map/ppermute | solution.py:20
  80.9 9.9 %collective-permute-start.18 = (bf16[1032,128]{1,0:T(8,128)(2,1)S(1)}, bf16[1032,128]{1,0:T(8,128)(2,1)S(1)}, u32[]{:S(2)}, u32[]{:S(2)}) collective-permute-start(bf16[1032,128]{1,0:T(8,128)(2,1)S(1)} %pieces.7), channel_id=1, source_target_pairs={{0,1},{1,0},{2,3},{3,2},{4,5},{5,4},{6,7},{7,6},{8,9},{9,8},{10,11... | collective-permute-start | bytes 792584 | tf_op jit(solution)/shard_map/ppermute | solution.py:20
  82.5 9.1 %collective-permute-start.15 = (bf16[264,128]{1,0:T(8,128)(2,1)S(1)}, bf16[264,128]{1,0:T(8,128)(2,1)S(1)}, u32[]{:S(2)}, u32[]{:S(2)}) collective-permute-start(bf16[264,128]{1,0:T(8,128)(2,1)S(1)} %get-tuple-element.42), channel_id=1, source_target_pairs={{0,2},{1,3},{2,0},{3,1},{4,6},{5,7},{6,4},{7,5},{8,10},{9,11},{10,... | collective-permute-start | bytes 202760 | tf_op jit(solution)/shard_map/ppermute | solution.py:20
  83.7 11.6 %collective-permute-start.16 = (bf16[264,128]{1,0:T(8,128)(2,1)S(1)}, bf16[264,128]{1,0:T(8,128)(2,1)S(1)}, u32[]{:S(2)}, u32[]{:S(2)}) collective-permute-start(bf16[264,128]{1,0:T(8,128)(2,1)S(1)} %get-tuple-element.43), channel_id=1, source_target_pairs={{0,4},{1,5},{2,6},{3,7},{4,0},{5,1},{6,2},{7,3},{8,12},{9,13},{10,... | collective-permute-start | bytes 202760 | tf_op jit(solution)/shard_map/ppermute | solution.py:20
  84.0 11.3 %collective-permute-start.17 = (bf16[264,128]{1,0:T(8,128)(2,1)S(1)}, bf16[264,128]{1,0:T(8,128)(2,1)S(1)}, u32[]{:S(2)}, u32[]{:S(2)}) collective-permute-start(bf16[264,128]{1,0:T(8,128)(2,1)S(1)} %get-tuple-element.44), channel_id=1, source_target_pairs={{0,6},{1,7},{2,4},{3,5},{4,2},{5,3},{6,0},{7,1},{8,14},{9,15},{10,... | collective-permute-start | bytes 202760 | tf_op jit(solution)/shard_map/ppermute | solution.py:20
  86.9 2.5 %copy-start.2 = (bf16[2048,1280]{1,0:T(8,128)(2,1)S(1)}, bf16[2048,1280]{1,0:T(8,128)(2,1)}, u32[]{:S(2)}) copy-start(bf16[2048,1280]{1,0:T(8,128)(2,1)} %copy-done) | copy-start | bytes 15728644
  90.9 5.1 %collective-permute-start.19 = (bf16[264,128]{1,0:T(8,128)(2,1)S(1)}, bf16[264,128]{1,0:T(8,128)(2,1)S(1)}, u32[]{:S(2)}, u32[]{:S(2)}) collective-permute-start(bf16[264,128]{1,0:T(8,128)(2,1)S(1)} %get-tuple-element.46), channel_id=1, source_target_pairs={{0,2},{1,3},{2,0},{3,1},{4,6},{5,7},{6,4},{7,5},{8,10},{9,11},{10,... | collective-permute-start | bytes 202760 | tf_op jit(solution)/shard_map/ppermute | solution.py:20
  91.3 4.7 %collective-permute-start.20 = (bf16[264,128]{1,0:T(8,128)(2,1)S(1)}, bf16[264,128]{1,0:T(8,128)(2,1)S(1)}, u32[]{:S(2)}, u32[]{:S(2)}) collective-permute-start(bf16[264,128]{1,0:T(8,128)(2,1)S(1)} %get-tuple-element.47), channel_id=1, source_target_pairs={{0,4},{1,5},{2,6},{3,7},{4,0},{5,1},{6,2},{7,3},{8,12},{9,13},{10,... | collective-permute-start | bytes 202760 | tf_op jit(solution)/shard_map/ppermute | solution.py:20
  91.6 5.8 %collective-permute-start.21 = (bf16[264,128]{1,0:T(8,128)(2,1)S(1)}, bf16[264,128]{1,0:T(8,128)(2,1)S(1)}, u32[]{:S(2)}, u32[]{:S(2)}) collective-permute-start(bf16[264,128]{1,0:T(8,128)(2,1)S(1)} %get-tuple-element.48), channel_id=1, source_target_pairs={{0,6},{1,7},{2,4},{3,5},{4,2},{5,3},{6,0},{7,1},{8,14},{9,15},{10,... | collective-permute-start | bytes 202760 | tf_op jit(solution)/shard_map/ppermute | solution.py:20
  98.2 10.7 %collective-permute-start.22 = (bf16[264,128]{1,0:T(8,128)(2,1)S(1)}, bf16[264,128]{1,0:T(8,128)(2,1)S(1)}, u32[]{:S(2)}, u32[]{:S(2)}) collective-permute-start(bf16[264,128]{1,0:T(8,128)(2,1)S(1)} %get-tuple-element.49), channel_id=1, source_target_pairs={{0,0},{1,1},{2,2},{3,3},{4,4},{5,5},{6,6},{7,7},{8,16},{9,17},{10,... | collective-permute-start | bytes 202760 | tf_op jit(solution)/shard_map/ppermute | solution.py:555
  98.9 10.0 %collective-permute-start.23 = (bf16[264,128]{1,0:T(8,128)(2,1)S(1)}, bf16[264,128]{1,0:T(8,128)(2,1)S(1)}, u32[]{:S(2)}, u32[]{:S(2)}) collective-permute-start(bf16[264,128]{1,0:T(8,128)(2,1)S(1)} %get-tuple-element.50), channel_id=1, source_target_pairs={{0,16},{1,17},{2,18},{3,19},{4,20},{5,21},{6,22},{7,23},{8,0},{9,1... | collective-permute-start | bytes 202760 | tf_op jit(solution)/shard_map/ppermute | solution.py:555
  105.6 3.3 %copy-start.6 = (f32[128,1]{1,0:T(8,128)S(1)}, f32[128,1]{1,0:T(8,128)}, u32[]{:S(2)}) copy-start(f32[128,1]{1,0:T(8,128)} %get-tuple-element.40.inv_ref) | copy-start | bytes 1540

commit v6 on v5

--- a/solution.py
+++ b/solution.py
@@ -21,7 +21,6 @@
 
 
 VMEM = pl.BlockSpec(memory_space=pltpu.VMEM)
-SMEM = pl.BlockSpec(memory_space=pltpu.SMEM)
 MIB = 1 << 20
 
 
@@ -33,57 +32,67 @@
     return pl.CostEstimate(flops=flops, bytes_accessed=nbytes, transcendentals=exps)
 
 
-def first_kernel(branches, place_ref, *refs):
-    sources, (block_ref, own_ref, inv_ref) = refs[:4], refs[4:7]
-    sent, (normed_ref, th_ref, tg_ref, sh_ref, sg_ref, sems) = refs[7 : 6 + branches], refs[6 + branches :]
+def position():
+    b, t = lax.axis_index("branch"), lax.axis_index("tok")
+    blocks = lax.axis_size("tok") // lax.axis_size("branch")
+    return b, t, lax.rem(t, blocks), lax.div(t, blocks) ^ b
+
+
+def normalized(values, gain):
+    values = values.astype(jnp.float32)
+    scale = lax.rsqrt(jnp.mean(values * values, axis=-1, keepdims=True) + eps)
+    return (values * scale * gain).astype(jnp.bfloat16), scale
+
+
+def first_kernel(branches, *refs):
+    teacher, teacher_gain, student, student_gain = refs[:4]
+    block_ref, *sent = refs[4 : 4 + branches]
+    th_ref, tg_ref, sh_ref, sg_ref, normed_ref, sems = refs[4 + branches :]
+    b = lax.axis_index("branch")
+    half, part = sent[0].shape
+    rows = pl.ds(pl.multiple_of(lax.axis_index("tok") % 2 * half, half), half)
     copies = [
         pltpu.make_async_copy(source, target, sems.at[i])
-        for i, (source, target) in enumerate(zip(sources, (th_ref, tg_ref, sh_ref, sg_ref)))
+        for i, (source, target) in enumerate(
+            ((student.at[rows], sh_ref), (student_gain, sg_ref), (teacher, th_ref), (teacher_gain, tg_ref))
+        )
     ]
     for copy in copies:
         copy.start()
     for copy in copies[:2]:
         copy.wait()
-    values = th_ref[0].astype(jnp.float32)
-    scale = lax.rsqrt(jnp.mean(values * values, axis=-1, keepdims=True) + eps)
-    block_ref[...] = (values * scale * tg_ref[...]).astype(jnp.bfloat16)
+    normed_ref[...], unused = normalized(sh_ref[...], sg_ref[...])
+    for r in range(1, branches):
+        sent[r - 1][...] = normed_ref[:, pl.ds(pl.multiple_of((b ^ r) * part, part), part)]
     for copy in copies[2:]:
         copy.wait()
-    values = sh_ref[...].astype(jnp.float32)
-    scale = lax.rsqrt(jnp.mean(values * values, axis=-1, keepdims=True) + eps)
-    inv_ref[...] = scale
-    normed_ref[...] = (values * scale * sg_ref[...]).astype(jnp.bfloat16)
-    part = own_ref.shape[1]
-    half = own_ref.shape[0] // 2
-    b = place_ref[0]
-    own_ref[...] = normed_ref[:, pl.ds(pl.multiple_of(b * part, part), part)]
-    start = pl.multiple_of((place_ref[1] % 2) * half, half)
-    for r in range(1, branches):
-        cols = pl.ds(pl.multiple_of((b ^ r) * part, part), part)
-        sent[r - 1][...] = normed_ref[pl.ds(start, half), cols]
-
-
-def normalize_all(teacher_hidden, teacher_gain, student_hidden, student_gain, place, branches):
+    block_ref[...], unused = normalized(th_ref[0], tg_ref[...])
+
+
+def first_blocks(teacher_hidden, teacher_gain, student_hidden, student_gain, branches):
     rows, width = student_hidden.shape
     part = width // branches
-    bf16 = jnp.bfloat16
+    bf16, f32 = jnp.bfloat16, jnp.float32
     return pl.pallas_call(
         functools.partial(first_kernel, branches),
         out_shape=(
             jax.ShapeDtypeStruct(teacher_hidden.shape[1:], bf16),
-            jax.ShapeDtypeStruct((rows, part), bf16),
-            jax.ShapeDtypeStruct((rows, 1), jnp.float32),
             *[jax.ShapeDtypeStruct((rows // 2, part), bf16)] * (branches - 1),
         ),
-        in_specs=[SMEM] + [pl.BlockSpec(memory_space=pl.ANY)] * 4,
-        out_specs=(VMEM,) * (2 + branches),
-        scratch_shapes=[pltpu.VMEM((rows, width), bf16)]
-        + [pltpu.VMEM(value.shape, value.dtype) for value in (teacher_hidden, teacher_gain, student_hidden)]
-        + [pltpu.VMEM((1, width), jnp.float32), pltpu.SemaphoreType.DMA((4,))],
+        in_specs=[pl.BlockSpec(memory_space=pl.ANY)] * 4,
+        out_specs=(VMEM,) * branches,
+        scratch_shapes=[
+            pltpu.VMEM(teacher_hidden.shape, bf16),
+            pltpu.VMEM((1, width), f32),
+            pltpu.VMEM((rows // 2, width), bf16),
+            pltpu.VMEM((1, width), f32),
+            pltpu.VMEM((rows // 2, width), bf16),
+            pltpu.SemaphoreType.DMA((4,)),
+        ],
         compiler_params=params(60),
         cost_estimate=cost(8 * rows * width, 4 * rows * width),
         name="first",
-    )(place, teacher_hidden, teacher_gain, student_hidden, student_gain[None])
+    )(teacher_hidden, teacher_gain, student_hidden, student_gain[None])
 
 
 def gather_blocks(block, size):
@@ -92,8 +101,10 @@
         got[k] = swap(block, "tok", k)
     for k in range(0, size, 8):
         got[k + 4] = swap(got[k], "tok", 4)
+    got[6] = swap(block, "tok", 6)
     for k in range(0, size, 4):
-        got[k + 2] = swap(got[k], "tok", 2)
+        if k != 4:
+            got[k + 2] = swap(got[k], "tok", 2)
     evens = sorted(got)
     half = len(evens) // 2
     arrays = [got[k] for k in evens]
@@ -104,36 +115,44 @@
     return arrays, tuple(keys)
 
 
-def own_dot_kernel(rows_ref, w_ref, out_ref, turned_ref):
-    turned_ref[...] = jnp.transpose(rows_ref[...])
-    out_ref[...] = jnp.dot(rows_ref[...], w_ref[...], preferred_element_type=jnp.float32)
-
-
-def own_dot(rows, head):
+def own_dot_kernel(rows_ref, gain_ref, w_ref, out_ref, turned_ref, inv_ref, normed_ref):
+    place = position()
+    normed_ref[...], inv_ref[...] = normalized(rows_ref[...], gain_ref[...])
+    part = turned_ref.shape[0]
+    own = normed_ref[:, pl.ds(pl.multiple_of(place[0] * part, part), part)]
+    turned_ref[...] = jnp.transpose(own)
+    out_ref[...] = jnp.dot(own, w_ref[...], preferred_element_type=jnp.float32)
+
+
+def own_dot(hidden, gain, head):
+    rows, width = hidden.shape
     return pl.pallas_call(
         own_dot_kernel,
         out_shape=(
-            jax.ShapeDtypeStruct((rows.shape[0], head.shape[1]), jnp.float32),
-            jax.ShapeDtypeStruct(rows.shape[::-1], rows.dtype),
+            jax.ShapeDtypeStruct((rows, head.shape[1]), jnp.float32),
+            jax.ShapeDtypeStruct((head.shape[0], rows), jnp.bfloat16),
+            jax.ShapeDtypeStruct((rows, 1), jnp.float32),
         ),
-        in_specs=[VMEM, VMEM],
-        out_specs=(VMEM, VMEM),
+        in_specs=[VMEM] * 3,
+        out_specs=(VMEM,) * 3,
+        scratch_shapes=[pltpu.VMEM((rows, width), jnp.bfloat16)],
         compiler_params=params(16),
-        cost_estimate=cost(2 * rows.size * head.shape[1], 2 * head.size),
+        cost_estimate=cost(2 * rows * head.size, 2 * head.size),
         name="owndot",
-    )(rows, head)
-
-
-def other_dot_kernel(place_ref, mine_ref, other_ref, w_ref, out_ref, turned_ref, rows_ref):
+    )(hidden, gain[None], head)
+
+
+def other_dot_kernel(mine_ref, other_ref, w_ref, out_ref, turned_ref, rows_ref):
+    place = position()
     half = mine_ref.shape[0]
-    core = place_ref[1] % 2
+    core = place[1] % 2
     rows_ref[pl.ds(pl.multiple_of(core * half, half), half), :] = mine_ref[...]
     rows_ref[pl.ds(pl.multiple_of((1 - core) * half, half), half), :] = other_ref[...]
     out_ref[...] = jnp.dot(rows_ref[...], w_ref[...], preferred_element_type=jnp.float32)
     turned_ref[...] = jnp.transpose(rows_ref[...])
 
 
-def other_dot(mine, other, head, place):
+def other_dot(mine, other, head):
     rows = 2 * mine.shape[0]
     return pl.pallas_call(
         other_dot_kernel,
@@ -141,13 +160,13 @@
             jax.ShapeDtypeStruct((rows, head.shape[1]), jnp.float32),
             jax.ShapeDtypeStruct((mine.shape[1], rows), jnp.bfloat16),
         ),
-        in_specs=[SMEM, VMEM, VMEM, VMEM],
+        in_specs=[VMEM] * 3,
         out_specs=(VMEM, VMEM),
         scratch_shapes=[pltpu.VMEM((rows, mine.shape[1]), jnp.bfloat16)],
         compiler_params=params(16),
         cost_estimate=cost(2 * rows * head.size, 2 * head.size),
         name="otherdot",
-    )(place, mine, other, head)
+    )(mine, other, head)
 
 
 EXTRA = 8
@@ -178,11 +197,12 @@
     return jnp.transpose(jnp.broadcast_to(col, (col.shape[0], 128)))[:1]
 
 
-def teacher_kernel(keys, half, place_ref, *refs):
+def teacher_kernel(keys, half, *refs):
+    place = position()
     blocks = refs[: len(keys)]
     w_ref, stat_ref, *exps = refs[len(keys) : -2]
     rows_ref, logits_ref = refs[-2:]
-    mine = place_ref[1] ^ (place_ref[0] * half)
+    mine = place[1] ^ (place[0] * half)
     for ref, owned in zip(blocks, keys):
         count = ref.shape[0] // len(owned)
         for j, k in enumerate(owned):
@@ -210,7 +230,7 @@
     stat_ref[1:2, :] = as_row(jnp.sum(scaled, axis=1, keepdims=True))
 
 
-def teacher_softmax(got, keys, head, place, half, branches):
+def teacher_softmax(got, keys, head, half, branches):
     width, cols = head.shape[1:]
     tokens = sum(part.shape[0] for part in got)
     return pl.pallas_call(
@@ -219,16 +239,17 @@
             jax.ShapeDtypeStruct((2, tokens), jnp.float32),
             *[jax.ShapeDtypeStruct((tokens // branches, cols), jnp.bfloat16)] * branches,
         ),
-        in_specs=[SMEM] + [VMEM] * (len(got) + 1),
+        in_specs=[VMEM] * (len(got) + 1),
         out_specs=(VMEM,) * (1 + branches),
         scratch_shapes=[pltpu.VMEM((tokens, width), jnp.bfloat16), pltpu.VMEM((tokens, cols), jnp.float32)],
         compiler_params=params(28),
         cost_estimate=cost(2 * tokens * width * cols, 2 * width * cols, tokens * cols),
         name="teacher",
-    )(place, *got, head)
-
-
-def stats_kernel(count, place_ref, *refs):
+    )(*got, head)
+
+
+def stats_kernel(count, *refs):
+    place = position()
     parts = refs[:count]
     teacher_ref, weight_ref, logits_ref, out_ref = refs[count:]
     logits = parts[0][...]
@@ -241,7 +262,7 @@
     size = out_ref.shape[0] // count
     student = jnp.concatenate([as_row(top), as_row(total)], axis=0)
     for r in range(count):
-        there = place_ref[0] ^ r
+        there = place[0] ^ r
         block = jnp.concatenate(
             [
                 teacher_ref[:, r * rows : (r + 1) * rows],
@@ -254,7 +275,7 @@
         out_ref[pl.ds(there * size, size)] = jnp.broadcast_to(block[None], (size, 8, rows))
 
 
-def student_stats(parts, teacher_stats, weights, place, size):
+def student_stats(parts, teacher_stats, weights, size):
     rows, cols = parts[0].shape
     count = len(parts)
     return pl.pallas_call(
@@ -263,18 +284,19 @@
             jax.ShapeDtypeStruct((rows, cols), jnp.float32),
             jax.ShapeDtypeStruct((count * size, 8, rows), jnp.float32),
         ),
-        in_specs=[SMEM] + [VMEM] * (count + 2),
+        in_specs=[VMEM] * (count + 2),
         out_specs=(VMEM, VMEM),
         compiler_params=params(12),
         cost_estimate=cost(8 * rows * cols, 12 * rows * cols, rows * cols),
         name="stats",
-    )(place, *parts, teacher_stats, weights)
-
-
-def grads_kernel(count, size, place_ref, stats_ref, logits_ref, ids_ref, *refs):
+    )(*parts, teacher_stats, weights)
+
+
+def grads_kernel(count, size, stats_ref, logits_ref, ids_ref, *refs):
+    place = position()
     terms = refs[:count]
     grads_ref = refs[count]
-    b, t = place_ref[0], place_ref[1]
+    b, t = place[0], place[1]
     rows, cols = logits_ref.shape
     logits = logits_ref[...]
     shard = lax.broadcasted_iota(jnp.int32, (rows, cols), 1)
@@ -299,44 +321,45 @@
     grads_ref[rows:, :rows] = extra_rows([dots], grads.dtype)
 
 
-def make_grads(stats, logits, ids, terms, place, size):
+def make_grads(stats, logits, ids, terms, size):
     rows, cols = logits.shape
     count = len(terms)
     return pl.pallas_call(
         functools.partial(grads_kernel, count, size),
         out_shape=jax.ShapeDtypeStruct((rows + EXTRA, cols), jnp.bfloat16),
-        in_specs=[SMEM] + [VMEM] * (count + 3),
+        in_specs=[VMEM] * (count + 3),
         out_specs=VMEM,
         compiler_params=params(12),
         cost_estimate=cost(16 * rows * cols, 10 * rows * cols, rows * cols),
         name="grads",
-    )(place, stats, logits, ids, *terms)
-
-
-def pieces_kernel(parity, width, place_ref, grads_ref, w_ref, out_ref, turned_ref):
+    )(stats, logits, ids, *terms)
+
+
+def pieces_kernel(parity, width, grads_ref, w_ref, out_ref, turned_ref):
+    place = position()
     rows = out_ref.shape[1]
     turned_ref[...] = jnp.transpose(grads_ref[:rows])
     count = (out_ref.shape[0] - EXTRA) // width
     for k in range(count):
-        start = pl.multiple_of((place_ref[2] ^ (2 * k + parity)) * width, width)
+        start = pl.multiple_of((place[2] ^ (2 * k + parity)) * width, width)
         acc = jnp.dot(w_ref[pl.ds(start, width)], turned_ref[...], preferred_element_type=jnp.float32)
         out_ref[k * width : (k + 1) * width] = acc.astype(out_ref.dtype)
     out_ref[count * width :] = grads_ref[rows:, :rows]
 
 
-def normed_grad_pieces(grads, head, place, blocks, parity):
+def normed_grad_pieces(grads, head, blocks, parity):
     rows, cols = grads.shape[0] - EXTRA, grads.shape[1]
     width = head.shape[0] // blocks
     return pl.pallas_call(
         functools.partial(pieces_kernel, parity, width),
         out_shape=jax.ShapeDtypeStruct((blocks // 2 * width + EXTRA, rows), jnp.bfloat16),
-        in_specs=[SMEM, VMEM, VMEM],
+        in_specs=[VMEM] * 2,
         out_specs=VMEM,
         scratch_shapes=[pltpu.VMEM((cols, rows), jnp.bfloat16)],
         compiler_params=params(16),
         cost_estimate=cost(rows * head.size, head.size),
         name="pieces",
-    )(place, grads, head)
+    )(grads, head)
 
 
 def fold_kernel(mine_ref, got_ref, *out):
@@ -364,12 +387,13 @@
     )(mine, got)
 
 
-def split_kernel(count, place_ref, *refs):
+def split_kernel(count, *refs):
+    place = position()
     turned, out = refs[-2 * count : -count], refs[-count:]
     each = len(refs) // count - 2
     f32 = jnp.float32
     width, rows = out[0].shape[0] - EXTRA, out[0].shape[1]
-    block = pl.multiple_of(place_ref[2] * width, width)
+    block = pl.multiple_of(place[2] * width, width)
     totals, dots, gain = [], [], 0.0
     for r in range(count):
         total = refs[r * each][...].astype(f32)
@@ -388,25 +412,25 @@
         extra = extra_rows([dots[r]] + gains, out[0].dtype)
         for kh in range(count):
 
-            @pl.when((place_ref[3] ^ kh) == r)
+            @pl.when((place[3] ^ kh) == r)
             def _():
                 out[kh][:width] = total
                 out[kh][width:] = extra
 
 
-def split(parts, turned, place):
+def split(parts, turned):
     count = len(parts)
     shape = parts[0][0].shape
     each = len(parts[0])
     return pl.pallas_call(
         functools.partial(split_kernel, count),
         out_shape=(jax.ShapeDtypeStruct(shape, parts[0][0].dtype),) * count,
-        in_specs=[SMEM] + [VMEM] * (count * (each + 1)),
+        in_specs=[VMEM] * (count * (each + 1)),
         out_specs=(VMEM,) * count,
         compiler_params=params(8),
         cost_estimate=cost(8 * count * shape[0] * shape[1], 12 * count * shape[0] * shape[1]),
         name="split",
-    )(place, *[part for some in parts for part in some], *turned)
+    )(*[part for some in parts for part in some], *turned)
 
 
 def head_grad_kernel(count, *refs):
@@ -508,44 +532,40 @@
 ):
     branches = lax.axis_size("branch")
     size = lax.axis_size("tok")
-    b = lax.axis_index("branch")
     t = lax.axis_index("tok")
     rows, width = student_hidden.shape
     blocks = size // branches
-    place = jnp.stack([b, t, t % blocks, (t // blocks) ^ b]).astype(jnp.int32)
-    teacher_block, own, inv_scale, *sent = normalize_all(
-        teacher_hidden, teacher_gain, student_hidden, student_gain, place, branches
-    )
+    teacher_block, *sent = first_blocks(teacher_hidden, teacher_gain, student_hidden, student_gain, branches)
 
     loaded = load(student_head)
-    own_partial, own_turned = own_dot(own, loaded)
+    own_partial, own_turned, inv_scale = own_dot(student_hidden, student_gain, loaded)
     turned, partials = [own_turned], [own_partial]
     for r in range(1, branches):
         mine = swap(sent[r - 1], "branch", r)
         other = swap(mine, "tok", 1)
-        partial, fetched = other_dot(mine, other, loaded, place)
+        partial, fetched = other_dot(mine, other, loaded)
         turned.append(fetched)
         partials.append(swap(partial, "branch", r))
 
     got, keys = gather_blocks(teacher_block, size)
-    teacher_stats, *exps = teacher_softmax(got, keys, teacher_head, place, blocks, branches)
+    teacher_stats, *exps = teacher_softmax(got, keys, teacher_head, blocks, branches)
     terms = [exps[0]] + [swap(exps[r], "branch", r) for r in range(1, branches)]
 
     weights = cluster_weights[:, 0].reshape(branches, rows)
-    logits, stats = student_stats(partials, teacher_stats, weights, place, size)
+    logits, stats = student_stats(partials, teacher_stats, weights, size)
     stats = lax.all_to_all(stats, ("branch", "tok"), 0, 0, tiled=True)
-    logit_grads = make_grads(stats, logits, token_ids[None], terms, place, size)
+    logit_grads = make_grads(stats, logits, token_ids[None], terms, size)
     all_grads = [logit_grads] + [swap(logit_grads, "branch", r) for r in range(1, branches)]
 
     slice_width = width // size
     parts = []
     for r in range(branches):
-        send = normed_grad_pieces(all_grads[r], loaded, place, blocks, 1)
+        send = normed_grad_pieces(all_grads[r], loaded, blocks, 1)
         send = swap(send, "tok", 1)
-        keep = normed_grad_pieces(all_grads[r], loaded, place, blocks, 0)
+        keep = normed_grad_pieces(all_grads[r], loaded, blocks, 0)
         folded = fold(keep, send, slice_width)
         parts.append([folded[0]] + [swap(folded[k], "tok", 2 * k) for k in range(1, blocks // 2)])
-    owned = split(parts, turned, place)
+    owned = split(parts, turned)
     arrived = []
     for kh in range(branches):
         perm = []

time: 110 us -> 108 us (0.982)
  local copies, waits for them, and re-layouts: 9.88 us -> 12.9 us
  Pallas kernels: 28.1 us -> 25.4 us
  waiting for transfers between devices: 35.5 us -> 33.7 us
    unnamed x26 -> x36, local copies, waits for them, and re-layouts: 8.27 us -> 12.9 us
    pallas_call x4, Pallas kernels: 5.88 us -> 3.69 us  [normed_grad_pieces(): pl.pallas_call(functools.partial(pieces_kernel, parity, width), out_shape...]
    ppermute x22, waiting for transfers between devices: 27.3 us -> 25.5 us  [swap(): return lax.ppermute(value, axis, [(i, i ^ flip) for i in range(size)])]
    pallas_call x2, Pallas kernels: 0.13 us -> 1.68 us  [fold(): pl.pallas_call(fold_kernel, out_shape=(jax.ShapeDtypeStruct((width + EXTR...]
  transfers between devices with their start and end apart: 25 -> 25, of which waited for: 10 -> 11; matrix products, arithmetic and copies ran while one was open for 2% -> 1% of each run, Pallas kernels for 20% -> 19%
where the time goes in v6:
time: 108 us; the launch traced here: 107 us
  waiting for transfers between devices  33.7 us (31%)
  starting transfers between devices  33.3 us (31%)
  Pallas kernels  25.4 us (24%)
  local copies, waits for them, and re-layouts  12.9 us (12%)
    ppermute x22, waiting for transfers between devices, swap(): return lax.ppermute(value, axis, [(i, i ^ flip) for i in range(size)])  25.5 us
    ppermute x22, starting transfers between devices, swap(): return lax.ppermute(value, axis, [(i, i ^ flip) for i in range(size)])  23.4 us
    unnamed x36, local copies, waits for them, and re-layouts  12.9 us
    all_to_all x1, waiting for transfers between devices, per_device(): stats = lax.all_to_all(stats, ('branch', 'tok'), 0, 0, tiled=True)  8.19 us
    pallas_call x2, Pallas kernels, head_grad(): pl.pallas_call(functools.partial(head_grad_kernel, count), out_shape=jax....  6.57 us
    all_to_all x1, starting transfers between devices, per_device(): stats = lax.all_to_all(stats, ('branch', 'tok'), 0, 0, tiled=True)  5.85 us
    pallas_call x1, Pallas kernels, teacher_softmax(): pl.pallas_call(functools.partial(teacher_kernel, keys, half), out_shape=(...  4.82 us
    ppermute x2, starting transfers between devices, per_device(): arrived.append(lax.ppermute(owned[kh], ('branch', 'tok'), perm))  4.1 us
  transfers between devices with their start and end apart: 25, of which 11 were waited for; matrix products, arithmetic and copies ran while one was open for 1% of the time, Pallas kernels for 19%

profile of v6, /device:TPU:0, one launch (start us, length us, event | category | flops | bytes accessed | tf_op | source)
XLA Modules:
  0.0 107.3 jit_solution(14086341163347900407)
XLA Ops:
  0.6 2.3 %first.1 = (bf16[16,4096]{1,0:T(8,128)(2,1)}, bf16[64,2048]{1,0:T(8,128)(2,1)}) custom-call(bf16[1,16,4096]{2,1,0:T(8,128)(2,1)} %refs_0_.1, f32[1,4096]{1,0:T(1,128)} %refs_1_.1, bf16[128,4096]{1,0:T(8,128)(2,1)} %refs_2_.1, f32[1,4096]{1,0:T(1,128)} %bitcast.7), custom_call_target="tpu_custom_call" | custom-call | flops 4194304 | bytes 2097152 | tf_op jit(solution)/shard_map/first/pallas_call | solution.py:76
  3.0 4.1 %collective-permute-start.6 = (bf16[16,4096]{1,0:T(8,128)(2,1)}, bf16[16,4096]{1,0:T(8,128)(2,1)S(1)}, u32[]{:S(2)}, u32[]{:S(2)}) collective-permute-start(bf16[16,4096]{1,0:T(8,128)(2,1)} %get-tuple-element.30.refs_0_), channel_id=1, source_target_pairs={{0,8},{1,9},{2,10},{3,11},{4,12},{5,13},{6,14},{7,15},{8,0},{9,1},... | collective-permute-start | bytes 393224 | tf_op jit(solution)/shard_map/ppermute | solution.py:20
  7.1 2.5 %collective-permute-start.5 = (bf16[16,4096]{1,0:T(8,128)(2,1)}, bf16[16,4096]{1,0:T(8,128)(2,1)S(1)}, u32[]{:S(2)}, u32[]{:S(2)}) collective-permute-start(bf16[16,4096]{1,0:T(8,128)(2,1)} %get-tuple-element.30.refs_0_), channel_id=1, source_target_pairs={{0,6},{1,7},{2,4},{3,5},{4,2},{5,3},{6,0},{7,1},{8,14},{9,15},{10,... | collective-permute-start | bytes 393224 | tf_op jit(solution)/shard_map/ppermute | solution.py:20
  9.7 4.1 %collective-permute-done.6.refs_4_ = bf16[16,4096]{1,0:T(8,128)(2,1)S(1)} collective-permute-done((bf16[16,4096]{1,0:T(8,128)(2,1)}, bf16[16,4096]{1,0:T(8,128)(2,1)S(1)}, u32[]{:S(2)}, u32[]{:S(2)}) %collective-permute-start.6) | collective-permute-done | bytes 131104 | tf_op jit(solution)/shard_map/ppermute | solution.py:20
  13.7 0.8 collective-permute-start.8
  14.5 1.3 %collective-permute-start.4 = (bf16[16,4096]{1,0:T(8,128)(2,1)}, bf16[16,4096]{1,0:T(8,128)(2,1)S(1)}, u32[]{:S(2)}, u32[]{:S(2)}) collective-permute-start(bf16[16,4096]{1,0:T(8,128)(2,1)} %get-tuple-element.30.refs_0_), channel_id=1, source_target_pairs={{0,4},{1,5},{2,6},{3,7},{4,0},{5,1},{6,2},{7,3},{8,12},{9,13},{10,... | collective-permute-start | bytes 393224 | tf_op jit(solution)/shard_map/ppermute | solution.py:20
  15.8 1.6 %collective-permute-start.3 = (bf16[16,4096]{1,0:T(8,128)(2,1)}, bf16[16,4096]{1,0:T(8,128)(2,1)S(1)}, u32[]{:S(2)}, u32[]{:S(2)}) collective-permute-start(bf16[16,4096]{1,0:T(8,128)(2,1)} %get-tuple-element.30.refs_0_), channel_id=1, source_target_pairs={{0,2},{1,3},{2,0},{3,1},{4,6},{5,7},{6,4},{7,5},{8,10},{9,11},{10,... | collective-permute-start | bytes 393224 | tf_op jit(solution)/shard_map/ppermute | solution.py:20
  17.3 1.5 %collective-permute-start = (bf16[64,2048]{1,0:T(8,128)(2,1)}, bf16[64,2048]{1,0:T(8,128)(2,1)S(1)}, u32[]{:S(2)}, u32[]{:S(2)}) collective-permute-start(bf16[64,2048]{1,0:T(8,128)(2,1)} %get-tuple-element.28), channel_id=1, source_target_pairs={{0,16},{16,0},{1,17},{17,1},{2,18},{18,2},{3,19},{19,3},{4,20},{20... | collective-permute-start | bytes 786440 | tf_op jit(solution)/shard_map/ppermute | solution.py:20
  19.9 1.5 %collective-permute-start.9 = (bf16[16,4096]{1,0:T(8,128)(2,1)S(1)}, bf16[16,4096]{1,0:T(8,128)(2,1)S(1)}, u32[]{:S(2)}, u32[]{:S(2)}) collective-permute-start(bf16[16,4096]{1,0:T(8,128)(2,1)S(1)} %collective-permute-done.8.refs_6_), channel_id=1, source_target_pairs={{0,2},{1,3},{2,0},{3,1},{4,6},{5,7},{6,4},{7,5},{8,10},{9,11},{10,... | collective-permute-start | bytes 393224 | tf_op jit(solution)/shard_map/ppermute | solution.py:20
  21.3 1.0 collective-permute-done.3.refs_1_
  22.4 0.9 pad_maximum_fusion
  23.9 1.0 collective-permute-done.7.refs_5_
  24.9 1.4 %collective-permute-done.9.refs_7_ = bf16[16,4096]{1,0:T(8,128)(2,1)S(1)} collective-permute-done((bf16[16,4096]{1,0:T(8,128)(2,1)S(1)}, bf16[16,4096]{1,0:T(8,128)(2,1)S(1)}, u32[]{:S(2)}, u32[]{:S(2)}) %collective-permute-start.9) | collective-permute-done | bytes 131104 | tf_op jit(solution)/shard_map/ppermute | solution.py:20
  26.5 2.6 %copy-done.3 = bf16[2048,1280]{1,0:T(8,128)(2,1)S(1)} copy-done((bf16[2048,1280]{1,0:T(8,128)(2,1)S(1)}, bf16[2048,1280]{1,0:T(8,128)(2,1)}, u32[]{:S(2)}) %copy-start.3) | copy-done | bytes 5242904
  29.5 1.0 otherdot.1
  30.5 0.8 collective-permute-start.2
  31.3 2.0 %slice-done.2 = s8[4194304]{0:T(1024)(128)(4,1)S(1)} async-done(((s8[10485760]{0:T(1024)(128)(4,1)}), s8[4194304]{0:T(1024)(128)(4,1)S(1)}, s32[]{:S(2)}) %slice-start.2) | async-done | bytes 4194328
  33.3 4.8 %teacher.1 = (f32[2,256]{1,0:T(2,128)S(1)}, bf16[128,1280]{1,0:T(8,128)(2,1)S(1)}, bf16[128,1280]{1,0:T(8,128)(2,1)}) custom-call(bf16[16,4096]{1,0:T(8,128)(2,1)S(1)} %copy-done.7, bf16[16,4096]{1,0:T(8,128)(2,1)S(1)} %collective-permute-done.3.refs_1_, bf16[16,4096]{1,0:T(8,128)(2,1)S(1)} %collective-permute-done.4.refs_2_, ...), custom_call_target="tpu_custom_call" | custom-call | flops 2684354560 | bytes 10485760 | tf_op jit(solution)/shard_map/teacher/pallas_call | solution.py:236
  38.1 0.7 collective-permute-start.12
  38.8 1.4 %owndot.1 = (f32[128,1280]{1,0:T(8,128)S(1)}, bf16[2048,128]{1,0:T(8,128)(2,1)S(1)}, f32[128,1]{1,0:T(8,128)S(1)}) custom-call(bf16[128,4096]{1,0:T(8,128)(2,1)S(1)} %copy-done.4, f32[1,4096]{1,0:T(1,128)S(1)} %bitcast.8, bf16[2048,1280]{1,0:T(8,128)(2,1)S(1)} %load.1.w_ref), custom_call_target="tpu_custom_call" | custom-call | flops 671088640 | bytes 5242880 | tf_op jit(solution)/shard_map/owndot/pallas_call | solution.py:129
  40.2 8.0 %collective-permute-done.2.refs_1_ = f32[128,1280]{1,0:T(8,128)S(1)} collective-permute-done((f32[128,1280]{1,0:T(8,128)S(1)}, f32[128,1280]{1,0:T(8,128)S(1)}, u32[]{:S(2)}, u32[]{:S(2)}) %collective-permute-start.2) | collective-permute-done | bytes 655392 | tf_op jit(solution)/shard_map/ppermute | solution.py:20
  48.2 1.0 stats.1
  49.1 0.9 copy-done.5
  50.0 5.9 %all-to-all-start = ((f32[32,8,128]{2,1,0:T(8,128)}), f32[32,8,128]{2,1,0:T(8,128)S(1)}, u32[]{:S(2)}, u32[]{:S(2)}) async-start(f32[32,8,128]{2,1,0:T(8,128)} %get-tuple-element.32), calls=%async_computation | async-start | bytes 262144 | tf_op jit(solution)/shard_map/all_to_all | solution.py:556
  55.9 8.2 %all-to-all-done.stats_ref = f32[32,8,128]{2,1,0:T(8,128)S(1)} async-done(((f32[32,8,128]{2,1,0:T(8,128)}), f32[32,8,128]{2,1,0:T(8,128)S(1)}, u32[]{:S(2)}, u32[]{:S(2)}) %all-to-all-start) | async-done | bytes 131104 | tf_op jit(solution)/shard_map/all_to_all | solution.py:556
  64.1 1.1 %copy-done.6 = f32[128,1280]{1,0:T(8,128)S(1)} copy-done((f32[128,1280]{1,0:T(8,128)S(1)}, f32[128,1280]{1,0:T(8,128)}, u32[]{:S(2)}) %copy-start.6) | copy-done | bytes 655384
  65.1 0.7 grads.1.refs_0_.grads_ref
  65.9 0.8 collective-permute-start.13
  66.7 2.5 %copy-done.1 = bf16[2048,1280]{1,0:T(8,128)(2,1)S(1)} copy-done((bf16[2048,1280]{1,0:T(8,128)(2,1)S(1)}, bf16[2048,1280]{1,0:T(8,128)(2,1)}, u32[]{:S(2)}) %copy-start.1) | copy-done | bytes 5242904
  69.2 0.9 pieces.5
  70.2 6.0 %collective-permute-done.13.refs_1_.grads_ref = bf16[136,1280]{1,0:T(8,128)(2,1)S(1)} collective-permute-done((bf16[136,1280]{1,0:T(8,128)(2,1)S(1)}, bf16[136,1280]{1,0:T(8,128)(2,1)S(1)}, u32[]{:S(2)}, u32[]{:S(2)}) %collective-permute-start.13) | collective-permute-done | bytes 348192 | tf_op jit(solution)/shard_map/ppermute | solution.py:20
  76.2 0.9 pieces.7
  77.2 0.9 pieces.4.mine_ref
  78.2 0.7 fold.2
  79.5 0.6 copy-done.14
  80.8 2.8 %collective-permute-start.17 = (bf16[264,128]{1,0:T(8,128)(2,1)}, bf16[264,128]{1,0:T(8,128)(2,1)S(1)}, u32[]{:S(2)}, u32[]{:S(2)}) collective-permute-start(bf16[264,128]{1,0:T(8,128)(2,1)} %copy-done.13), channel_id=1, source_target_pairs={{0,6},{1,7},{2,4},{3,5},{4,2},{5,3},{6,0},{7,1},{8,14},{9,15},{10,... | collective-permute-start | bytes 202760 | tf_op jit(solution)/shard_map/ppermute | solution.py:20
  83.6 2.5 %copy-done.2 = bf16[2048,1280]{1,0:T(8,128)(2,1)S(1)} copy-done((bf16[2048,1280]{1,0:T(8,128)(2,1)S(1)}, bf16[2048,1280]{1,0:T(8,128)(2,1)}, u32[]{:S(2)}) %copy-start.2) | copy-done | bytes 5242904
  86.1 0.9 pieces.6.mine_ref
  87.1 1.0 fold.3
  88.8 2.8 %collective-permute-start.21 = (bf16[264,128]{1,0:T(8,128)(2,1)S(1)}, bf16[264,128]{1,0:T(8,128)(2,1)S(1)}, u32[]{:S(2)}, u32[]{:S(2)}) collective-permute-start(bf16[264,128]{1,0:T(8,128)(2,1)S(1)} %get-tuple-element.46), channel_id=1, source_target_pairs={{0,6},{1,7},{2,4},{3,5},{4,2},{5,3},{6,0},{7,1},{8,14},{9,15},{10,... | collective-permute-start | bytes 202760 | tf_op jit(solution)/shard_map/ppermute | solution.py:20
  91.7 1.5 %collective-permute-done.19.refs_5_ = bf16[264,128]{1,0:T(8,128)(2,1)S(1)} collective-permute-done((bf16[264,128]{1,0:T(8,128)(2,1)S(1)}, bf16[264,128]{1,0:T(8,128)(2,1)S(1)}, u32[]{:S(2)}, u32[]{:S(2)}) %collective-permute-start.19) | collective-permute-done | bytes 67616 | tf_op jit(solution)/shard_map/ppermute | solution.py:20
  93.2 1.5 %collective-permute-done.21.refs_7_ = bf16[264,128]{1,0:T(8,128)(2,1)S(1)} collective-permute-done((bf16[264,128]{1,0:T(8,128)(2,1)S(1)}, bf16[264,128]{1,0:T(8,128)(2,1)S(1)}, u32[]{:S(2)}, u32[]{:S(2)}) %collective-permute-start.21) | collective-permute-done | bytes 67616 | tf_op jit(solution)/shard_map/ppermute | solution.py:20
  94.6 1.1 %split.1 = (bf16[264,128]{1,0:T(8,128)(2,1)S(1)}, bf16[264,128]{1,0:T(8,128)(2,1)S(1)}) custom-call(bf16[264,128]{1,0:T(8,128)(2,1)S(1)} %get-tuple-element.39.refs_0_, bf16[264,128]{1,0:T(8,128)(2,1)} %collective-permute-done.15.refs_1_, bf16[264,128]{1,0:T(8,128)(2,1)S(1)} %collective-permute-done.16.refs_2_, ...), custom_call_target="tpu_custom_call" | custom-call | flops 540672 | bytes 811008 | tf_op jit(solution)/shard_map/split/pallas_call | solution.py:425
  95.7 0.7 collective-permute-start.22
  96.4 3.4 %collective-permute-start.23 = (bf16[264,128]{1,0:T(8,128)(2,1)S(1)}, bf16[264,128]{1,0:T(8,128)(2,1)S(1)}, u32[]{:S(2)}, u32[]{:S(2)}) collective-permute-start(bf16[264,128]{1,0:T(8,128)(2,1)S(1)} %get-tuple-element.48), channel_id=1, source_target_pairs={{0,16},{1,17},{2,18},{3,19},{4,20},{5,21},{6,22},{7,23},{8,0},{9,1... | collective-permute-start | bytes 202760 | tf_op jit(solution)/shard_map/ppermute | solution.py:575
  99.8 3.3 %headgrad.2.refs_4_ = f32[2048,1280]{1,0:T(8,128)} custom-call(bf16[136,1280]{1,0:T(8,128)(2,1)S(1)} %grads.1.refs_0_.grads_ref, bf16[136,1280]{1,0:T(8,128)(2,1)S(1)} %collective-permute-done.13.refs_1_.grads_ref, bf16[2048,128]{1,0:T(8,128)(2,1)S(1)} %get-tuple-element.36.refs_2_.refs_8_, bf16[2048,128]{1,0:T(8,128)(2,1)S(1)} %get-tuple-element.37.refs_3_.refs_9_), custom_call_target="tpu_custom_call" | custom-call | flops 671088640 | bytes 5242880 | tf_op jit(solution)/shard_map/headgrad/pallas_call | solution.py:456
  103.1 3.3 %headgrad.3 = f32[2048,1280]{1,0:T(8,128)} custom-call(bf16[136,1280]{1,0:T(8,128)(2,1)S(1)} %grads.1.refs_0_.grads_ref, bf16[136,1280]{1,0:T(8,128)(2,1)S(1)} %collective-permute-done.13.refs_1_.grads_ref, bf16[2048,128]{1,0:T(8,128)(2,1)S(1)} %get-tuple-element.36.refs_2_.refs_8_, ...), custom_call_target="tpu_custom_call", output_to_operand_aliasing={{}: (4, {})} | custom-call | flops 671088640 | bytes 5242880 | tf_op jit(solution)/shard_map/headgrad/pallas_call | solution.py:456
  106.4 0.9 last.1
  (60 shorter events, 4.5 us)
Async XLA Ops:
  0.6 30.6 %slice-start = ((s8[10485760]{0:T(1024)(128)(4,1)}), s8[2097152]{0:T(1024)(128)(4,1)S(1)}, s32[]{:S(2)}) async-start(s8[10485760]{0:T(1024)(128)(4,1)} %bitcast.5), calls=%async_computation.1 | async-start | bytes 4194304
  3.0 28.3 %copy-start.7 = (bf16[16,4096]{1,0:T(8,128)(2,1)S(1)}, bf16[16,4096]{1,0:T(8,128)(2,1)}, u32[]{:S(2)}) copy-start(bf16[16,4096]{1,0:T(8,128)(2,1)} %get-tuple-element.30.refs_0_) | copy-start | bytes 393220
  3.0 10.7 %collective-permute-start.6 = (bf16[16,4096]{1,0:T(8,128)(2,1)}, bf16[16,4096]{1,0:T(8,128)(2,1)S(1)}, u32[]{:S(2)}, u32[]{:S(2)}) collective-permute-start(bf16[16,4096]{1,0:T(8,128)(2,1)} %get-tuple-element.30.refs_0_), channel_id=1, source_target_pairs={{0,8},{1,9},{2,10},{3,11},{4,12},{5,13},{6,14},{7,15},{8,0},{9,1},... | collective-permute-start | bytes 393224 | tf_op jit(solution)/shard_map/ppermute | solution.py:20
  7.1 11.7 %collective-permute-start.5 = (bf16[16,4096]{1,0:T(8,128)(2,1)}, bf16[16,4096]{1,0:T(8,128)(2,1)S(1)}, u32[]{:S(2)}, u32[]{:S(2)}) collective-permute-start(bf16[16,4096]{1,0:T(8,128)(2,1)} %get-tuple-element.30.refs_0_), channel_id=1, source_target_pairs={{0,6},{1,7},{2,4},{3,5},{4,2},{5,3},{6,0},{7,1},{8,14},{9,15},{10,... | collective-permute-start | bytes 393224 | tf_op jit(solution)/shard_map/ppermute | solution.py:20
  13.7 6.1 %collective-permute-start.8 = (bf16[16,4096]{1,0:T(8,128)(2,1)S(1)}, bf16[16,4096]{1,0:T(8,128)(2,1)S(1)}, u32[]{:S(2)}, u32[]{:S(2)}) collective-permute-start(bf16[16,4096]{1,0:T(8,128)(2,1)S(1)} %collective-permute-done.6.refs_4_), channel_id=1, source_target_pairs={{0,4},{1,5},{2,6},{3,7},{4,0},{5,1},{6,2},{7,3},{8,12},{9,13},{10,... | collective-permute-start | bytes 393224 | tf_op jit(solution)/shard_map/ppermute | solution.py:20
  14.5 6.8 %collective-permute-start.4 = (bf16[16,4096]{1,0:T(8,128)(2,1)}, bf16[16,4096]{1,0:T(8,128)(2,1)S(1)}, u32[]{:S(2)}, u32[]{:S(2)}) collective-permute-start(bf16[16,4096]{1,0:T(8,128)(2,1)} %get-tuple-element.30.refs_0_), channel_id=1, source_target_pairs={{0,4},{1,5},{2,6},{3,7},{4,0},{5,1},{6,2},{7,3},{8,12},{9,13},{10,... | collective-permute-start | bytes 393224 | tf_op jit(solution)/shard_map/ppermute | solution.py:20
  15.8 6.6 %collective-permute-start.3 = (bf16[16,4096]{1,0:T(8,128)(2,1)}, bf16[16,4096]{1,0:T(8,128)(2,1)S(1)}, u32[]{:S(2)}, u32[]{:S(2)}) collective-permute-start(bf16[16,4096]{1,0:T(8,128)(2,1)} %get-tuple-element.30.refs_0_), channel_id=1, source_target_pairs={{0,2},{1,3},{2,0},{3,1},{4,6},{5,7},{6,4},{7,5},{8,10},{9,11},{10,... | collective-permute-start | bytes 393224 | tf_op jit(solution)/shard_map/ppermute | solution.py:20
  17.3 6.6 %collective-permute-start = (bf16[64,2048]{1,0:T(8,128)(2,1)}, bf16[64,2048]{1,0:T(8,128)(2,1)S(1)}, u32[]{:S(2)}, u32[]{:S(2)}) collective-permute-start(bf16[64,2048]{1,0:T(8,128)(2,1)} %get-tuple-element.28), channel_id=1, source_target_pairs={{0,16},{16,0},{1,17},{17,1},{2,18},{18,2},{3,19},{19,3},{4,20},{20... | collective-permute-start | bytes 786440 | tf_op jit(solution)/shard_map/ppermute | solution.py:20
  18.8 6.1 %collective-permute-start.7 = (bf16[16,4096]{1,0:T(8,128)(2,1)S(1)}, bf16[16,4096]{1,0:T(8,128)(2,1)S(1)}, u32[]{:S(2)}, u32[]{:S(2)}) collective-permute-start(bf16[16,4096]{1,0:T(8,128)(2,1)S(1)} %collective-permute-done.6.refs_4_), channel_id=1, source_target_pairs={{0,2},{1,3},{2,0},{3,1},{4,6},{5,7},{6,4},{7,5},{8,10},{9,11},{10,... | collective-permute-start | bytes 393224 | tf_op jit(solution)/shard_map/ppermute | solution.py:20
  19.9 6.4 %collective-permute-start.9 = (bf16[16,4096]{1,0:T(8,128)(2,1)S(1)}, bf16[16,4096]{1,0:T(8,128)(2,1)S(1)}, u32[]{:S(2)}, u32[]{:S(2)}) collective-permute-start(bf16[16,4096]{1,0:T(8,128)(2,1)S(1)} %collective-permute-done.8.refs_6_), channel_id=1, source_target_pairs={{0,2},{1,3},{2,0},{3,1},{4,6},{5,7},{6,4},{7,5},{8,10},{9,11},{10,... | collective-permute-start | bytes 393224 | tf_op jit(solution)/shard_map/ppermute | solution.py:20
  23.3 8.0 %collective-permute-start.10 = (bf16[64,4096]{1,0:T(8,128)(2,1)S(1)}, bf16[64,4096]{1,0:T(8,128)(2,1)S(1)}, u32[]{:S(2)}, u32[]{:S(2)}) collective-permute-start(bf16[64,4096]{1,0:T(8,128)(2,1)S(1)} %pad_maximum_fusion), channel_id=1, source_target_pairs={{0,1},{1,0},{2,3},{3,2},{4,5},{5,4},{6,7},{7,6},{8,9},{9,8},{10,11... | collective-permute-start | bytes 1572872 | tf_op jit(solution)/shard_map/ppermute | solution.py:20
  23.9 5.6 %collective-permute-start.1 = (bf16[64,2048]{1,0:T(8,128)(2,1)S(1)}, bf16[64,2048]{1,0:T(8,128)(2,1)S(1)}, u32[]{:S(2)}, u32[]{:S(2)}) collective-permute-start(bf16[64,2048]{1,0:T(8,128)(2,1)S(1)} %collective-permute-done.mine_ref), channel_id=1, source_target_pairs={{0,1},{1,0},{2,3},{3,2},{4,5},{5,4},{6,7},{7,6},{8,9},{9,8},{10,11... | collective-permute-start | bytes 786440 | tf_op jit(solution)/shard_map/ppermute | solution.py:20
  26.3 4.9 %slice-start.1 = ((s8[10485760]{0:T(1024)(128)(4,1)}), s8[4194304]{0:T(1024)(128)(4,1)S(1)}, s32[]{:S(2)}) async-start(s8[10485760]{0:T(1024)(128)(4,1)} %bitcast.5), calls=%async_computation.2 | async-start | bytes 8388608
  26.4 6.9 %slice-start.2 = ((s8[10485760]{0:T(1024)(128)(4,1)}), s8[4194304]{0:T(1024)(128)(4,1)S(1)}, s32[]{:S(2)}) async-start(s8[10485760]{0:T(1024)(128)(4,1)} %bitcast.5), calls=%async_computation.3 | async-start | bytes 8388608
  26.4 4.9 %collective-permute-start.11 = (bf16[64,4096]{1,0:T(8,128)(2,1)S(1)}, bf16[64,4096]{1,0:T(8,128)(2,1)S(1)}, u32[]{:S(2)}, u32[]{:S(2)}) collective-permute-start(bf16[64,4096]{1,0:T(8,128)(2,1)S(1)} %pad_maximum_fusion.1), channel_id=1, source_target_pairs={{0,1},{1,0},{2,3},{3,2},{4,5},{5,4},{6,7},{7,6},{8,9},{9,8},{10,11... | collective-permute-start | bytes 1572872 | tf_op jit(solution)/shard_map/ppermute | solution.py:20
  26.4 2.6 %copy-start.3 = (bf16[2048,1280]{1,0:T(8,128)(2,1)S(1)}, bf16[2048,1280]{1,0:T(8,128)(2,1)}, u32[]{:S(2)}) copy-start(bf16[2048,1280]{1,0:T(8,128)(2,1)} %from_ref.1) | copy-start | bytes 15728644
  29.5 10.7 %copy-start = (bf16[2048,1280]{1,0:T(8,128)(2,1)}, bf16[2048,1280]{1,0:T(8,128)(2,1)S(1)}, u32[]{:S(2)}) copy-start(bf16[2048,1280]{1,0:T(8,128)(2,1)S(1)} %load.1.w_ref) | copy-start | bytes 15728644
  29.5 9.3 %copy-start.4 = (bf16[128,4096]{1,0:T(8,128)(2,1)S(1)}, bf16[128,4096]{1,0:T(8,128)(2,1)}, u32[]{:S(2)}) copy-start(bf16[128,4096]{1,0:T(8,128)(2,1)} %refs_2_.1) | copy-start | bytes 3145732
  29.5 9.3 %copy-start.8 = (f32[4096]{0:T(1024)S(1)}, f32[4096]{0:T(1024)}, u32[]{:S(2)}) copy-start(f32[4096]{0:T(1024)} %param.12) | copy-start | bytes 49156
  30.5 17.7 %copy-start.11 = (s32[256,1]{0,1:T(1,128)S(1)}, s32[256,1]{0,1:T(1,128)}, u32[]{:S(2)}) copy-start(s32[256,1]{0,1:T(1,128)} %param.14) | copy-start | bytes 3076
  30.5 33.6 %copy-start.12 = (s32[128]{0:T(128)S(1)}, s32[128]{0:T(128)}, u32[]{:S(2)}) copy-start(s32[128]{0:T(128)} %param.15) | copy-start | bytes 1540
  30.5 17.7 %collective-permute-start.2 = (f32[128,1280]{1,0:T(8,128)S(1)}, f32[128,1280]{1,0:T(8,128)S(1)}, u32[]{:S(2)}, u32[]{:S(2)}) collective-permute-start(f32[128,1280]{1,0:T(8,128)S(1)} %get-tuple-element.29), channel_id=1, source_target_pairs={{0,16},{16,0},{1,17},{17,1},{2,18},{18,2},{3,19},{19,3},{4,20},{20... | collective-permute-start | bytes 1966088 | tf_op jit(solution)/shard_map/ppermute | solution.py:20
  38.1 17.8 %collective-permute-start.12 = (bf16[128,1280]{1,0:T(8,128)(2,1)}, bf16[128,1280]{1,0:T(8,128)(2,1)S(1)}, u32[]{:S(2)}, u32[]{:S(2)}) collective-permute-start(bf16[128,1280]{1,0:T(8,128)(2,1)} %get-tuple-element.35), channel_id=1, source_target_pairs={{0,16},{16,0},{1,17},{17,1},{2,18},{18,2},{3,19},{19,3},{4,20},{20... | collective-permute-start | bytes 983048 | tf_op jit(solution)/shard_map/ppermute | solution.py:20
  40.2 9.8 %copy-start.9 = (f32[128,1]{1,0:T(8,128)}, f32[128,1]{1,0:T(8,128)S(1)}, u32[]{:S(2)}) copy-start(f32[128,1]{1,0:T(8,128)S(1)} %get-tuple-element.38.inv_ref) | copy-start | bytes 1540
  49.1 0.9 copy-start.5
  50.0 14.1 %all-to-all-start = ((f32[32,8,128]{2,1,0:T(8,128)}), f32[32,8,128]{2,1,0:T(8,128)S(1)}, u32[]{:S(2)}, u32[]{:S(2)}) async-start(f32[32,8,128]{2,1,0:T(8,128)} %get-tuple-element.32), calls=%async_computation | async-start | bytes 262144 | tf_op jit(solution)/shard_map/all_to_all | solution.py:556
  64.1 1.1 %copy-start.6 = (f32[128,1280]{1,0:T(8,128)S(1)}, f32[128,1280]{1,0:T(8,128)}, u32[]{:S(2)}) copy-start(f32[128,1280]{1,0:T(8,128)} %copy-done.5) | copy-start | bytes 1966084
  65.9 10.4 %collective-permute-start.13 = (bf16[136,1280]{1,0:T(8,128)(2,1)S(1)}, bf16[136,1280]{1,0:T(8,128)(2,1)S(1)}, u32[]{:S(2)}, u32[]{:S(2)}) collective-permute-start(bf16[136,1280]{1,0:T(8,128)(2,1)S(1)} %grads.1.refs_0_.grads_ref), channel_id=1, source_target_pairs={{0,16},{16,0},{1,17},{17,1},{2,18},{18,2},{3,19},{19,3},{4,20},{20... | collective-permute-start | bytes 1044488 | tf_op jit(solution)/shard_map/ppermute | solution.py:20
  66.7 2.5 %copy-start.1 = (bf16[2048,1280]{1,0:T(8,128)(2,1)S(1)}, bf16[2048,1280]{1,0:T(8,128)(2,1)}, u32[]{:S(2)}) copy-start(bf16[2048,1280]{1,0:T(8,128)(2,1)} %copy-done) | copy-start | bytes 15728644
  70.1 8.1 %collective-permute-start.14 = (bf16[1032,128]{1,0:T(8,128)(2,1)S(1)}, bf16[1032,128]{1,0:T(8,128)(2,1)S(1)}, u32[]{:S(2)}, u32[]{:S(2)}) collective-permute-start(bf16[1032,128]{1,0:T(8,128)(2,1)S(1)} %pieces.5), channel_id=1, source_target_pairs={{0,1},{1,0},{2,3},{3,2},{4,5},{5,4},{6,7},{7,6},{8,9},{9,8},{10,11... | collective-permute-start | bytes 792584 | tf_op jit(solution)/shard_map/ppermute | solution.py:20
  77.1 9.9 %collective-permute-start.18 = (bf16[1032,128]{1,0:T(8,128)(2,1)S(1)}, bf16[1032,128]{1,0:T(8,128)(2,1)}, u32[]{:S(2)}, u32[]{:S(2)}) collective-permute-start(bf16[1032,128]{1,0:T(8,128)(2,1)S(1)} %pieces.7), channel_id=1, source_target_pairs={{0,1},{1,0},{2,3},{3,2},{4,5},{5,4},{6,7},{7,6},{8,9},{9,8},{10,11... | collective-permute-start | bytes 792584 | tf_op jit(solution)/shard_map/ppermute | solution.py:20
  78.8 0.6 copy-start.13
  79.5 0.6 copy-start.14
  80.1 8.8 %collective-permute-start.15 = (bf16[264,128]{1,0:T(8,128)(2,1)}, bf16[264,128]{1,0:T(8,128)(2,1)}, u32[]{:S(2)}, u32[]{:S(2)}) collective-permute-start(bf16[264,128]{1,0:T(8,128)(2,1)} %get-tuple-element.40), channel_id=1, source_target_pairs={{0,2},{1,3},{2,0},{3,1},{4,6},{5,7},{6,4},{7,5},{8,10},{9,11},{10,... | collective-permute-start | bytes 202760 | tf_op jit(solution)/shard_map/ppermute | solution.py:20
  80.5 11.2 %collective-permute-start.16 = (bf16[264,128]{1,0:T(8,128)(2,1)}, bf16[264,128]{1,0:T(8,128)(2,1)S(1)}, u32[]{:S(2)}, u32[]{:S(2)}) collective-permute-start(bf16[264,128]{1,0:T(8,128)(2,1)} %copy-done.14), channel_id=1, source_target_pairs={{0,4},{1,5},{2,6},{3,7},{4,0},{5,1},{6,2},{7,3},{8,12},{9,13},{10,... | collective-permute-start | bytes 202760 | tf_op jit(solution)/shard_map/ppermute | solution.py:20
  80.8 10.8 %collective-permute-start.17 = (bf16[264,128]{1,0:T(8,128)(2,1)}, bf16[264,128]{1,0:T(8,128)(2,1)S(1)}, u32[]{:S(2)}, u32[]{:S(2)}) collective-permute-start(bf16[264,128]{1,0:T(8,128)(2,1)} %copy-done.13), channel_id=1, source_target_pairs={{0,6},{1,7},{2,4},{3,5},{4,2},{5,3},{6,0},{7,1},{8,14},{9,15},{10,... | collective-permute-start | bytes 202760 | tf_op jit(solution)/shard_map/ppermute | solution.py:20
  83.6 2.5 %copy-start.2 = (bf16[2048,1280]{1,0:T(8,128)(2,1)S(1)}, bf16[2048,1280]{1,0:T(8,128)(2,1)}, u32[]{:S(2)}) copy-start(bf16[2048,1280]{1,0:T(8,128)(2,1)} %copy-done) | copy-start | bytes 15728644
  88.1 5.1 %collective-permute-start.19 = (bf16[264,128]{1,0:T(8,128)(2,1)S(1)}, bf16[264,128]{1,0:T(8,128)(2,1)S(1)}, u32[]{:S(2)}, u32[]{:S(2)}) collective-permute-start(bf16[264,128]{1,0:T(8,128)(2,1)S(1)} %get-tuple-element.44), channel_id=1, source_target_pairs={{0,2},{1,3},{2,0},{3,1},{4,6},{5,7},{6,4},{7,5},{8,10},{9,11},{10,... | collective-permute-start | bytes 202760 | tf_op jit(solution)/shard_map/ppermute | solution.py:20
  88.5 4.7 %collective-permute-start.20 = (bf16[264,128]{1,0:T(8,128)(2,1)S(1)}, bf16[264,128]{1,0:T(8,128)(2,1)S(1)}, u32[]{:S(2)}, u32[]{:S(2)}) collective-permute-start(bf16[264,128]{1,0:T(8,128)(2,1)S(1)} %get-tuple-element.45), channel_id=1, source_target_pairs={{0,4},{1,5},{2,6},{3,7},{4,0},{5,1},{6,2},{7,3},{8,12},{9,13},{10,... | collective-permute-start | bytes 202760 | tf_op jit(solution)/shard_map/ppermute | solution.py:20
  88.8 5.8 %collective-permute-start.21 = (bf16[264,128]{1,0:T(8,128)(2,1)S(1)}, bf16[264,128]{1,0:T(8,128)(2,1)S(1)}, u32[]{:S(2)}, u32[]{:S(2)}) collective-permute-start(bf16[264,128]{1,0:T(8,128)(2,1)S(1)} %get-tuple-element.46), channel_id=1, source_target_pairs={{0,6},{1,7},{2,4},{3,5},{4,2},{5,3},{6,0},{7,1},{8,14},{9,15},{10,... | collective-permute-start | bytes 202760 | tf_op jit(solution)/shard_map/ppermute | solution.py:20
  95.7 10.7 %collective-permute-start.22 = (bf16[264,128]{1,0:T(8,128)(2,1)S(1)}, bf16[264,128]{1,0:T(8,128)(2,1)S(1)}, u32[]{:S(2)}, u32[]{:S(2)}) collective-permute-start(bf16[264,128]{1,0:T(8,128)(2,1)S(1)} %get-tuple-element.47), channel_id=1, source_target_pairs={{0,0},{1,1},{2,2},{3,3},{4,4},{5,5},{6,6},{7,7},{8,16},{9,17},{10,... | collective-permute-start | bytes 202760 | tf_op jit(solution)/shard_map/ppermute | solution.py:575
  96.4 10.0 %collective-permute-start.23 = (bf16[264,128]{1,0:T(8,128)(2,1)S(1)}, bf16[264,128]{1,0:T(8,128)(2,1)S(1)}, u32[]{:S(2)}, u32[]{:S(2)}) collective-permute-start(bf16[264,128]{1,0:T(8,128)(2,1)S(1)} %get-tuple-element.48), channel_id=1, source_target_pairs={{0,16},{1,17},{2,18},{3,19},{4,20},{5,21},{6,22},{7,23},{8,0},{9,1... | collective-permute-start | bytes 202760 | tf_op jit(solution)/shard_map/ppermute | solution.py:575
  103.1 3.3 %copy-start.10 = (f32[128,1]{1,0:T(8,128)S(1)}, f32[128,1]{1,0:T(8,128)}, u32[]{:S(2)}) copy-start(f32[128,1]{1,0:T(8,128)} %copy-done.9) | copy-start | bytes 1540

commit v7 on v6

--- a/solution.py
+++ b/solution.py
@@ -110,7 +110,8 @@
     arrays = [got[k] for k in evens]
     keys = [(k,) for k in evens]
     for group in (evens[:half], evens[half:]):
-        arrays.append(swap(jnp.concatenate([got[k] for k in group], axis=0), "tok", 1))
+        joined = jnp.concatenate([got[k] for k in group], axis=0) if len(group) > 1 else got[group[0]]
+        arrays.append(swap(joined, "tok", 1))
         keys.append(tuple(k + 1 for k in group))
     return arrays, tuple(keys)
 
@@ -387,81 +388,109 @@
     )(mine, got)
 
 
-def split_kernel(count, *refs):
+def join_kernel(gains, *refs):
+    out = refs[-1]
+    width, rows = out.shape[0] - EXTRA, out.shape[1]
+    total = refs[0][...].astype(jnp.float32)
+    for ref in refs[1:-1]:
+        total = total + ref[...].astype(jnp.float32)
+    dots = extra_values(total[width:], 1)
+    out[:width] = total[:width].astype(out.dtype)
+    out[width:] = extra_rows(dots + [jnp.zeros((1, rows), jnp.float32)] * gains, out.dtype)
+
+
+def join(parts, gains):
+    shape, dtype = parts[0].shape, parts[0].dtype
+    return pl.pallas_call(
+        functools.partial(join_kernel, gains),
+        out_shape=jax.ShapeDtypeStruct(shape, dtype),
+        in_specs=[VMEM] * len(parts),
+        out_specs=VMEM,
+        compiler_params=params(8),
+        cost_estimate=cost(4 * shape[0] * shape[1], 10 * shape[0] * shape[1]),
+        name="join",
+    )(*parts)
+
+
+def split_kernel(count, own_ref, *refs):
     place = position()
-    turned, out = refs[-2 * count : -count], refs[-count:]
-    each = len(refs) // count - 2
+    turned, out, rest_ref = refs[-2 * count : -count], refs[-count:-1], refs[-1]
+    each = (len(refs) - 2 * count) // (count - 1)
     f32 = jnp.float32
-    width, rows = out[0].shape[0] - EXTRA, out[0].shape[1]
-    block = pl.multiple_of(place[2] * width, width)
-    totals, dots, gain = [], [], 0.0
-    for r in range(count):
+    width, rows = own_ref.shape[0] - EXTRA, own_ref.shape[1]
+    block = pl.ds(pl.multiple_of(place[2] * width, width), width)
+    totals, dots = [own_ref[:width].astype(f32)], [jnp.zeros((1, rows), f32)]
+    for r in range(count - 1):
         total = refs[r * each][...].astype(f32)
         for ref in refs[r * each + 1 : (r + 1) * each]:
             total = total + ref[...].astype(f32)
         dots.append(extra_values(total[width:], 1)[0])
         totals.append(total[:width])
-        gain = gain + jnp.sum(totals[r] * turned[r][pl.ds(block, width)].astype(f32), axis=1, keepdims=True)
+    gain = sum(
+        jnp.sum(totals[r] * turned[r][block].astype(f32), axis=1, keepdims=True) for r in range(count)
+    )
     gain = as_row(gain)
     lanes = min(width, rows)
     gains = [gain[:, i : i + lanes] for i in range(0, width, lanes)]
     if lanes < rows:
         gains = [jnp.concatenate([row, jnp.zeros((1, rows - lanes), f32)], axis=1) for row in gains]
-    for r in range(count):
-        total = totals[r].astype(out[0].dtype)
-        extra = extra_rows([dots[r]] + gains, out[0].dtype)
-        for kh in range(count):
-
-            @pl.when((place[3] ^ kh) == r)
-            def _():
-                out[kh][:width] = total
-                out[kh][width:] = extra
-
-
-def split(parts, turned):
-    count = len(parts)
-    shape = parts[0][0].shape
-    each = len(parts[0])
+    for r in range(1, count):
+        out[r - 1][:width] = totals[r].astype(own_ref.dtype)
+        out[r - 1][width:] = extra_rows([dots[r]] + gains, own_ref.dtype)
+    rest_ref[...] = extra_rows([dots[0]] + gains, own_ref.dtype)
+
+
+def split(own, parts, turned):
+    shape, dtype = own.shape, own.dtype
+    count = len(turned)
+    flat = [part for some in parts for part in some]
     return pl.pallas_call(
         functools.partial(split_kernel, count),
-        out_shape=(jax.ShapeDtypeStruct(shape, parts[0][0].dtype),) * count,
-        in_specs=[VMEM] * (count * (each + 1)),
+        out_shape=(*[jax.ShapeDtypeStruct(shape, dtype)] * (count - 1), jax.ShapeDtypeStruct((EXTRA, shape[1]), dtype)),
+        in_specs=[VMEM] * (1 + len(flat) + count),
         out_specs=(VMEM,) * count,
         compiler_params=params(8),
         cost_estimate=cost(8 * count * shape[0] * shape[1], 12 * count * shape[0] * shape[1]),
         name="split",
-    )(*[part for some in parts for part in some], *turned)
-
-
-def head_grad_kernel(count, *refs):
+    )(own, *flat, *turned)
+
+
+def head_grad_kernel(count, half, tile, *refs):
     grads, turned = refs[:count], refs[count : 2 * count]
-    out_ref, grads_ref = refs[-2:]
+    out_ref, grads_ref, total_ref, sems = refs[-4:]
     rows = grads_ref.shape[0] // count
-
-    @pl.when(pl.program_id(0) == 0)
-    def _():
-        for r in range(count):
-            grads_ref[r * rows : (r + 1) * rows, :] = grads[r][:rows]
-
-    lhs = jnp.concatenate([ref[...] for ref in turned], axis=1)
-    out_ref[...] = jnp.dot(lhs, grads_ref[...], preferred_element_type=jnp.float32)
+    for r in range(count):
+        grads_ref[r * rows : (r + 1) * rows, :] = grads[r][:rows]
+    copies = []
+    for i in range(total_ref.shape[0] // tile):
+        here = slice(i * tile, (i + 1) * tile)
+        start = half * total_ref.shape[0] + i * tile
+        lhs = jnp.concatenate([ref[start : start + tile] for ref in turned], axis=1)
+        total_ref[here] = jnp.dot(lhs, grads_ref[...], preferred_element_type=jnp.float32)
+        copy = pltpu.make_async_copy(total_ref.at[here], out_ref.at[pl.ds(start, tile)], sems.at[i])
+        copy.start()
+        copies.append(copy)
+    for copy in copies:
+        copy.wait()
 
 
 def head_grad(grads, turned, half, done):
     count = len(grads)
-    full, cols = grads[0].shape
+    cols = grads[0].shape[1]
     part, rows = turned[0].shape
-    tile = tile_of(part)
+    tile = tile_of(part // 2)
     steps = part // tile // 2
-    return pl.pallas_call(
-        functools.partial(head_grad_kernel, count),
+    whole = pl.BlockSpec(memory_space=pl.ANY)
+    return pl.pallas_call(
+        functools.partial(head_grad_kernel, count, half, tile),
         out_shape=jax.ShapeDtypeStruct((part, cols), jnp.float32),
-        grid=(steps,),
-        in_specs=[pl.BlockSpec((full, cols), lambda i: (0, 0))] * count
-        + [pl.BlockSpec((tile, rows), lambda i: (i + half * steps, 0))] * count
-        + [pl.BlockSpec(memory_space=pl.ANY)] * len(done),
-        out_specs=pl.BlockSpec((tile, cols), lambda i: (i + half * steps, 0)),
-        scratch_shapes=[pltpu.VMEM((count * rows, cols), jnp.bfloat16)],
+        in_specs=[VMEM] * (2 * count) + [whole] * len(done),
+        out_specs=whole,
+        scratch_shapes=[
+            pltpu.VMEM((count * rows, cols), jnp.bfloat16),
+            pltpu.VMEM((part // 2, cols), jnp.float32),
+            pltpu.SemaphoreType.DMA((steps,)),
+        ],
         input_output_aliases={2 * count: 0} if done else {},
         compiler_params=params(16),
         cost_estimate=cost(count * rows * part * cols, 2 * part * cols),
@@ -469,15 +498,19 @@
     )(*grads, *turned, *done)
 
 
-def last_kernel(count, width, inv_ref, hidden_ref, gain_ref, *refs):
-    parts = refs[:count]
-    out_ref, gain_out_ref = refs[count:]
-    total = parts[0][...].astype(jnp.float32)
+def last_kernel(count, extras, width, inv_ref, hidden_ref, gain_ref, *refs):
+    parts, rests = refs[:count], refs[count : count + extras]
+    out_ref, gain_out_ref = refs[-2:]
+    mine = jnp.where(position()[3] == 0, 1.0, 0.0)
+    total = parts[0][...].astype(jnp.float32) * mine
     for ref in parts[1:]:
         total = total + ref[...].astype(jnp.float32)
     piece, rows = total.shape[0] - EXTRA, total.shape[1]
+    extra = total[piece:] + rests[0][...].astype(jnp.float32) * mine
+    for ref in rests[1:]:
+        extra = extra + ref[...].astype(jnp.float32)
     lanes = min(piece, rows)
-    dots, *gains = extra_values(total[piece:], 1 + piece // lanes)
+    dots, *gains = extra_values(extra, 1 + piece // lanes)
     gain_out_ref[...] = jnp.concatenate([row[:, :lanes] for row in gains], axis=1) / gain_ref[...]
     normed_grads = jnp.transpose(total[:piece])
     inv = inv_ref[...]
@@ -485,20 +518,20 @@
     out_ref[...] = inv * gain_ref[...] * normed_grads - scaled * (inv * column(dots) / width)
 
 
-def finish(parts, inv, hidden, gain, width):
+def finish(parts, rests, inv, hidden, gain, width):
     piece, rows = parts[0].shape[0] - EXTRA, parts[0].shape[1]
     return pl.pallas_call(
-        functools.partial(last_kernel, len(parts), width),
+        functools.partial(last_kernel, len(parts), len(rests), width),
         out_shape=(
             jax.ShapeDtypeStruct((rows, piece), jnp.float32),
             jax.ShapeDtypeStruct((1, piece), jnp.float32),
         ),
-        in_specs=[VMEM] * (3 + len(parts)),
+        in_specs=[VMEM] * (3 + len(parts) + len(rests)),
         out_specs=(VMEM, VMEM),
         compiler_params=params(12),
         cost_estimate=cost(16 * rows * piece, 12 * rows * piece),
         name="last",
-    )(inv, hidden, gain, *parts)
+    )(inv, hidden, gain, *parts, *rests)
 
 
 def load_kernel(from_ref, to_ref, sem):
@@ -565,21 +598,26 @@
         keep = normed_grad_pieces(all_grads[r], loaded, blocks, 0)
         folded = fold(keep, send, slice_width)
         parts.append([folded[0]] + [swap(folded[k], "tok", 2 * k) for k in range(1, blocks // 2)])
-    owned = split(parts, turned)
-    arrived = []
-    for kh in range(branches):
+    def to_owner(value, r, kz):
         perm = []
-        for i in range(branches * size):
-            bb, h, rest = i // size, (i % size) // blocks, i % blocks
-            perm.append((i, (h ^ kh) * size + bb * blocks + rest))
-        arrived.append(lax.ppermute(owned[kh], ("branch", "tok"), perm))
+        for bb in range(branches):
+            for rest in range(blocks):
+                perm.append((bb * size + (bb ^ kz) * blocks + rest, (bb ^ r) * size + bb * blocks + rest))
+        return lax.ppermute(value, ("branch", "tok"), perm)
+
+    early = join(parts[0], max(1, slice_width // rows))
+    arrived = [early] + [to_owner(early, 0, kz) for kz in range(1, branches)]
+    *late, rest = split(early, parts[1:], turned)
+    for r in range(1, branches):
+        arrived += [to_owner(late[r - 1], r, kz) for kz in range(branches)]
+    rests = [rest] + [to_owner(rest, 0, kz) for kz in range(1, branches)]
 
     grad_head = head_grad(all_grads, turned, 0, [])
     grad_head = head_grad(all_grads, turned, 1, [grad_head])
 
     hidden_cols = lax.dynamic_slice_in_dim(student_hidden, t * slice_width, slice_width, 1)
     gain_cols = lax.dynamic_slice_in_dim(student_gain, t * slice_width, slice_width, 0)
-    grad_hidden, grad_gain = finish(arrived, inv_scale, hidden_cols, gain_cols[None], width)
+    grad_hidden, grad_gain = finish(arrived, rests, inv_scale, hidden_cols, gain_cols[None], width)
     return (grad_head, grad_hidden, grad_gain[0])
 
 

time: 108 us -> 114 us (1.056)
  starting transfers between devices: 33.3 us -> 40.1 us
    ppermute x2 -> x4, starting transfers between devices: 4.1 us -> 10.8 us  [to_owner(): return lax.ppermute(value, ('branch', 'tok'), perm)]
    ppermute x2 -> x4, waiting for transfers between devices: 0.01 us -> 2.3 us  [to_owner(): return lax.ppermute(value, ('branch', 'tok'), perm)]
    ppermute x22, waiting for transfers between devices: 25.5 us -> 23.3 us  [swap(): return lax.ppermute(value, axis, [(i, i ^ flip) for i in range(size)])]
    pallas_call x4 -> x5, Pallas kernels: 8.56 us -> 7.55 us  [the longest x2 5.53 us: head_grad(): pl.pallas_call(functools.partial(head_grad_kernel, count, half, tile), ou...]
  transfers between devices with their start and end apart: 25 -> 27, of which waited for: 11 -> 11; matrix products, arithmetic and copies ran while one was open for 1% -> 1% of each run, Pallas kernels for 19% -> 18%
where the time goes in v7:
time: 114 us; the launch traced here: 113 us
  starting transfers between devices  40.1 us (35%)
  waiting for transfers between devices  33.8 us (30%)
  Pallas kernels  24.4 us (21%)
  local copies, waits for them, and re-layouts  12.9 us (11%)
    ppermute x22, starting transfers between devices, swap(): return lax.ppermute(value, axis, [(i, i ^ flip) for i in range(size)])  23.4 us
    ppermute x22, waiting for transfers between devices, swap(): return lax.ppermute(value, axis, [(i, i ^ flip) for i in range(size)])  23.3 us
    unnamed x36, local copies, waits for them, and re-layouts  12.8 us
    ppermute x4, starting transfers between devices, to_owner(): return lax.ppermute(value, ('branch', 'tok'), perm)  10.8 us
    all_to_all x1, waiting for transfers between devices, per_device(): stats = lax.all_to_all(stats, ('branch', 'tok'), 0, 0, tiled=True)  8.19 us
    all_to_all x1, starting transfers between devices, per_device(): stats = lax.all_to_all(stats, ('branch', 'tok'), 0, 0, tiled=True)  5.85 us
    pallas_call x2, Pallas kernels, head_grad(): pl.pallas_call(functools.partial(head_grad_kernel, count, half, tile), ou...  5.53 us
    pallas_call x1, Pallas kernels, teacher_softmax(): pl.pallas_call(functools.partial(teacher_kernel, keys, half), out_shape=(...  4.81 us
  transfers between devices with their start and end apart: 27, of which 11 were waited for; matrix products, arithmetic and copies ran while one was open for 1% of the time, Pallas kernels for 18%

profile of v7, /device:TPU:0, one launch (start us, length us, event | category | flops | bytes accessed | tf_op | source)
XLA Modules:
  0.0 113.2 jit_solution(6351132672490819320)
XLA Ops:
  0.6 2.3 %first.1 = (bf16[16,4096]{1,0:T(8,128)(2,1)}, bf16[64,2048]{1,0:T(8,128)(2,1)}) custom-call(bf16[1,16,4096]{2,1,0:T(8,128)(2,1)} %refs_0_.1, f32[1,4096]{1,0:T(1,128)} %refs_1_.1, bf16[128,4096]{1,0:T(8,128)(2,1)} %refs_2_.1, f32[1,4096]{1,0:T(1,128)} %bitcast.7), custom_call_target="tpu_custom_call" | custom-call | flops 4194304 | bytes 2097152 | tf_op jit(solution)/shard_map/first/pallas_call | solution.py:76
  3.0 4.1 %collective-permute-start.6 = (bf16[16,4096]{1,0:T(8,128)(2,1)}, bf16[16,4096]{1,0:T(8,128)(2,1)S(1)}, u32[]{:S(2)}, u32[]{:S(2)}) collective-permute-start(bf16[16,4096]{1,0:T(8,128)(2,1)} %get-tuple-element.30.refs_0_), channel_id=1, source_target_pairs={{0,8},{1,9},{2,10},{3,11},{4,12},{5,13},{6,14},{7,15},{8,0},{9,1},... | collective-permute-start | bytes 393224 | tf_op jit(solution)/shard_map/ppermute | solution.py:20
  7.1 2.5 %collective-permute-start.5 = (bf16[16,4096]{1,0:T(8,128)(2,1)}, bf16[16,4096]{1,0:T(8,128)(2,1)S(1)}, u32[]{:S(2)}, u32[]{:S(2)}) collective-permute-start(bf16[16,4096]{1,0:T(8,128)(2,1)} %get-tuple-element.30.refs_0_), channel_id=1, source_target_pairs={{0,6},{1,7},{2,4},{3,5},{4,2},{5,3},{6,0},{7,1},{8,14},{9,15},{10,... | collective-permute-start | bytes 393224 | tf_op jit(solution)/shard_map/ppermute | solution.py:20
  9.7 4.1 %collective-permute-done.6.refs_4_ = bf16[16,4096]{1,0:T(8,128)(2,1)S(1)} collective-permute-done((bf16[16,4096]{1,0:T(8,128)(2,1)}, bf16[16,4096]{1,0:T(8,128)(2,1)S(1)}, u32[]{:S(2)}, u32[]{:S(2)}) %collective-permute-start.6) | collective-permute-done | bytes 131104 | tf_op jit(solution)/shard_map/ppermute | solution.py:20
  13.7 0.8 collective-permute-start.8
  14.5 1.3 %collective-permute-start.4 = (bf16[16,4096]{1,0:T(8,128)(2,1)}, bf16[16,4096]{1,0:T(8,128)(2,1)S(1)}, u32[]{:S(2)}, u32[]{:S(2)}) collective-permute-start(bf16[16,4096]{1,0:T(8,128)(2,1)} %get-tuple-element.30.refs_0_), channel_id=1, source_target_pairs={{0,4},{1,5},{2,6},{3,7},{4,0},{5,1},{6,2},{7,3},{8,12},{9,13},{10,... | collective-permute-start | bytes 393224 | tf_op jit(solution)/shard_map/ppermute | solution.py:20
  15.8 1.6 %collective-permute-start.3 = (bf16[16,4096]{1,0:T(8,128)(2,1)}, bf16[16,4096]{1,0:T(8,128)(2,1)S(1)}, u32[]{:S(2)}, u32[]{:S(2)}) collective-permute-start(bf16[16,4096]{1,0:T(8,128)(2,1)} %get-tuple-element.30.refs_0_), channel_id=1, source_target_pairs={{0,2},{1,3},{2,0},{3,1},{4,6},{5,7},{6,4},{7,5},{8,10},{9,11},{10,... | collective-permute-start | bytes 393224 | tf_op jit(solution)/shard_map/ppermute | solution.py:20
  17.3 1.5 %collective-permute-start = (bf16[64,2048]{1,0:T(8,128)(2,1)}, bf16[64,2048]{1,0:T(8,128)(2,1)S(1)}, u32[]{:S(2)}, u32[]{:S(2)}) collective-permute-start(bf16[64,2048]{1,0:T(8,128)(2,1)} %get-tuple-element.28), channel_id=1, source_target_pairs={{0,16},{16,0},{1,17},{17,1},{2,18},{18,2},{3,19},{19,3},{4,20},{20... | collective-permute-start | bytes 786440 | tf_op jit(solution)/shard_map/ppermute | solution.py:20
  19.9 1.5 %collective-permute-start.9 = (bf16[16,4096]{1,0:T(8,128)(2,1)S(1)}, bf16[16,4096]{1,0:T(8,128)(2,1)S(1)}, u32[]{:S(2)}, u32[]{:S(2)}) collective-permute-start(bf16[16,4096]{1,0:T(8,128)(2,1)S(1)} %collective-permute-done.8.refs_6_), channel_id=1, source_target_pairs={{0,2},{1,3},{2,0},{3,1},{4,6},{5,7},{6,4},{7,5},{8,10},{9,11},{10,... | collective-permute-start | bytes 393224 | tf_op jit(solution)/shard_map/ppermute | solution.py:20
  21.3 1.0 collective-permute-done.3.refs_1_
  22.4 0.9 pad_maximum_fusion
  23.9 1.0 collective-permute-done.7.refs_5_
  24.9 1.4 %collective-permute-done.9.refs_7_ = bf16[16,4096]{1,0:T(8,128)(2,1)S(1)} collective-permute-done((bf16[16,4096]{1,0:T(8,128)(2,1)S(1)}, bf16[16,4096]{1,0:T(8,128)(2,1)S(1)}, u32[]{:S(2)}, u32[]{:S(2)}) %collective-permute-start.9) | collective-permute-done | bytes 131104 | tf_op jit(solution)/shard_map/ppermute | solution.py:20
  26.5 2.6 %copy-done.3 = bf16[2048,1280]{1,0:T(8,128)(2,1)S(1)} copy-done((bf16[2048,1280]{1,0:T(8,128)(2,1)S(1)}, bf16[2048,1280]{1,0:T(8,128)(2,1)}, u32[]{:S(2)}) %copy-start.3) | copy-done | bytes 5242904
  29.5 1.0 otherdot.1
  30.5 0.8 collective-permute-start.2
  31.3 2.0 %slice-done.2 = s8[4194304]{0:T(1024)(128)(4,1)S(1)} async-done(((s8[10485760]{0:T(1024)(128)(4,1)}), s8[4194304]{0:T(1024)(128)(4,1)S(1)}, s32[]{:S(2)}) %slice-start.2) | async-done | bytes 4194328
  33.3 4.8 %teacher.1 = (f32[2,256]{1,0:T(2,128)S(1)}, bf16[128,1280]{1,0:T(8,128)(2,1)S(1)}, bf16[128,1280]{1,0:T(8,128)(2,1)}) custom-call(bf16[16,4096]{1,0:T(8,128)(2,1)S(1)} %copy-done.7, bf16[16,4096]{1,0:T(8,128)(2,1)S(1)} %collective-permute-done.3.refs_1_, bf16[16,4096]{1,0:T(8,128)(2,1)S(1)} %collective-permute-done.4.refs_2_, ...), custom_call_target="tpu_custom_call" | custom-call | flops 2684354560 | bytes 10485760 | tf_op jit(solution)/shard_map/teacher/pallas_call | solution.py:237
  38.1 0.7 collective-permute-start.12
  38.8 1.4 %owndot.1 = (f32[128,1280]{1,0:T(8,128)S(1)}, bf16[2048,128]{1,0:T(8,128)(2,1)S(1)}, f32[128,1]{1,0:T(8,128)S(1)}) custom-call(bf16[128,4096]{1,0:T(8,128)(2,1)S(1)} %copy-done.4, f32[1,4096]{1,0:T(1,128)S(1)} %bitcast.8, bf16[2048,1280]{1,0:T(8,128)(2,1)S(1)} %load.1.w_ref), custom_call_target="tpu_custom_call" | custom-call | flops 671088640 | bytes 5242880 | tf_op jit(solution)/shard_map/owndot/pallas_call | solution.py:130
  40.2 8.0 %collective-permute-done.2.refs_1_ = f32[128,1280]{1,0:T(8,128)S(1)} collective-permute-done((f32[128,1280]{1,0:T(8,128)S(1)}, f32[128,1280]{1,0:T(8,128)S(1)}, u32[]{:S(2)}, u32[]{:S(2)}) %collective-permute-start.2) | collective-permute-done | bytes 655392 | tf_op jit(solution)/shard_map/ppermute | solution.py:20
  48.2 1.0 stats.1
  49.1 0.9 copy-done.5
  50.0 5.9 %all-to-all-start = ((f32[32,8,128]{2,1,0:T(8,128)}), f32[32,8,128]{2,1,0:T(8,128)S(1)}, u32[]{:S(2)}, u32[]{:S(2)}) async-start(f32[32,8,128]{2,1,0:T(8,128)} %get-tuple-element.32), calls=%async_computation | async-start | bytes 262144 | tf_op jit(solution)/shard_map/all_to_all | solution.py:589
  55.9 8.2 %all-to-all-done.stats_ref = f32[32,8,128]{2,1,0:T(8,128)S(1)} async-done(((f32[32,8,128]{2,1,0:T(8,128)}), f32[32,8,128]{2,1,0:T(8,128)S(1)}, u32[]{:S(2)}, u32[]{:S(2)}) %all-to-all-start) | async-done | bytes 131104 | tf_op jit(solution)/shard_map/all_to_all | solution.py:589
  64.0 1.1 copy-done.6
  65.1 0.7 grads.1.refs_0_.grads_ref
  65.8 0.8 collective-permute-start.13
  66.7 2.5 %copy-done.1 = bf16[2048,1280]{1,0:T(8,128)(2,1)S(1)} copy-done((bf16[2048,1280]{1,0:T(8,128)(2,1)S(1)}, bf16[2048,1280]{1,0:T(8,128)(2,1)}, u32[]{:S(2)}) %copy-start.1) | copy-done | bytes 5242904
  69.2 0.9 pieces.5
  70.2 6.0 %collective-permute-done.13.refs_1_.grads_ref = bf16[136,1280]{1,0:T(8,128)(2,1)S(1)} collective-permute-done((bf16[136,1280]{1,0:T(8,128)(2,1)S(1)}, bf16[136,1280]{1,0:T(8,128)(2,1)S(1)}, u32[]{:S(2)}, u32[]{:S(2)}) %collective-permute-start.13) | collective-permute-done | bytes 348192 | tf_op jit(solution)/shard_map/ppermute | solution.py:20
  76.2 0.9 pieces.7
  77.2 0.9 pieces.4.mine_ref
  78.2 0.7 fold.2
  80.8 2.8 %collective-permute-start.17 = (bf16[264,128]{1,0:T(8,128)(2,1)}, bf16[264,128]{1,0:T(8,128)(2,1)S(1)}, u32[]{:S(2)}, u32[]{:S(2)}) collective-permute-start(bf16[264,128]{1,0:T(8,128)(2,1)} %copy-done.13), channel_id=1, source_target_pairs={{0,6},{1,7},{2,4},{3,5},{4,2},{5,3},{6,0},{7,1},{8,14},{9,15},{10,... | collective-permute-start | bytes 202760 | tf_op jit(solution)/shard_map/ppermute | solution.py:20
  83.6 2.5 %copy-done.2 = bf16[2048,1280]{1,0:T(8,128)(2,1)S(1)} copy-done((bf16[2048,1280]{1,0:T(8,128)(2,1)S(1)}, bf16[2048,1280]{1,0:T(8,128)(2,1)}, u32[]{:S(2)}) %copy-start.2) | copy-done | bytes 5242904
  86.1 0.9 pieces.6.mine_ref
  87.1 1.0 fold.3
  88.8 2.8 %collective-permute-start.22 = (bf16[264,128]{1,0:T(8,128)(2,1)S(1)}, bf16[264,128]{1,0:T(8,128)(2,1)S(1)}, u32[]{:S(2)}, u32[]{:S(2)}) collective-permute-start(bf16[264,128]{1,0:T(8,128)(2,1)S(1)} %get-tuple-element.46), channel_id=1, source_target_pairs={{0,6},{1,7},{2,4},{3,5},{4,2},{5,3},{6,0},{7,1},{8,14},{9,15},{10,... | collective-permute-start | bytes 202760 | tf_op jit(solution)/shard_map/ppermute | solution.py:20
  91.7 0.9 join.1.own_ref.refs_0_
  92.6 1.3 %collective-permute-start.18 = (bf16[264,128]{1,0:T(8,128)(2,1)S(1)}, bf16[264,128]{1,0:T(8,128)(2,1)S(1)}, u32[]{:S(2)}, u32[]{:S(2)}) collective-permute-start(bf16[264,128]{1,0:T(8,128)(2,1)S(1)} %join.1.own_ref.refs_0_), channel_id=1, source_target_pairs={{8,0},{9,1},{10,2},{11,3},{12,4},{13,5},{14,6},{15,7},{16,24},{17,... | collective-permute-start | bytes 202760 | tf_op jit(solution)/shard_map/ppermute | solution.py:606
  93.9 0.7 collective-permute-done.22.refs_3_
  95.5 7.5 %collective-permute-start.23 = (bf16[264,128]{1,0:T(8,128)(2,1)S(1)}, bf16[264,128]{1,0:T(8,128)(2,1)S(1)}, u32[]{:S(2)}, u32[]{:S(2)}) collective-permute-start(bf16[264,128]{1,0:T(8,128)(2,1)S(1)} %get-tuple-element.47), channel_id=1, source_target_pairs={{0,16},{1,17},{2,18},{3,19},{4,20},{5,21},{6,22},{7,23},{24,8},{25... | collective-permute-start | bytes 202760 | tf_op jit(solution)/shard_map/ppermute | solution.py:606
  103.0 2.8 %headgrad.2.refs_4_ = f32[2048,1280]{1,0:T(8,128)} custom-call(bf16[136,1280]{1,0:T(8,128)(2,1)S(1)} %grads.1.refs_0_.grads_ref, bf16[136,1280]{1,0:T(8,128)(2,1)S(1)} %collective-permute-done.13.refs_1_.grads_ref, bf16[2048,128]{1,0:T(8,128)(2,1)S(1)} %get-tuple-element.36.refs_2_.refs_4_, bf16[2048,128]{1,0:T(8,128)(2,1)S(1)} %get-tuple-element.37.refs_3_.refs_5_), custom_call_target="tpu_custom_call" | custom-call | flops 671088640 | bytes 5242880 | tf_op jit(solution)/shard_map/headgrad/pallas_call | solution.py:484
  105.8 1.4 %collective-permute-start.25 = (bf16[8,128]{1,0:T(8,128)(2,1)S(1)}, bf16[8,128]{1,0:T(8,128)(2,1)S(1)}, u32[]{:S(2)}, u32[]{:S(2)}) collective-permute-start(bf16[8,128]{1,0:T(8,128)(2,1)S(1)} %get-tuple-element.48.refs_4_), channel_id=1, source_target_pairs={{8,0},{9,1},{10,2},{11,3},{12,4},{13,5},{14,6},{15,7},{16,24},{17,... | collective-permute-start | bytes 6152 | tf_op jit(solution)/shard_map/ppermute | solution.py:606
  107.2 2.8 %headgrad.3 = f32[2048,1280]{1,0:T(8,128)} custom-call(bf16[136,1280]{1,0:T(8,128)(2,1)S(1)} %grads.1.refs_0_.grads_ref, bf16[136,1280]{1,0:T(8,128)(2,1)S(1)} %collective-permute-done.13.refs_1_.grads_ref, bf16[2048,128]{1,0:T(8,128)(2,1)S(1)} %get-tuple-element.36.refs_2_.refs_4_, ...), custom_call_target="tpu_custom_call", output_to_operand_aliasing={{}: (4, {})} | custom-call | flops 671088640 | bytes 5242880 | tf_op jit(solution)/shard_map/headgrad/pallas_call | solution.py:484
  110.0 2.3 %collective-permute-done.25.refs_5_ = bf16[8,128]{1,0:T(8,128)(2,1)S(1)} collective-permute-done((bf16[8,128]{1,0:T(8,128)(2,1)S(1)}, bf16[8,128]{1,0:T(8,128)(2,1)S(1)}, u32[]{:S(2)}, u32[]{:S(2)}) %collective-permute-start.25) | collective-permute-done | bytes 2080 | tf_op jit(solution)/shard_map/ppermute | solution.py:606
  112.3 0.9 last.1
  (65 shorter events, 6.0 us)
Async XLA Ops:
  0.6 30.6 %slice-start = ((s8[10485760]{0:T(1024)(128)(4,1)}), s8[2097152]{0:T(1024)(128)(4,1)S(1)}, s32[]{:S(2)}) async-start(s8[10485760]{0:T(1024)(128)(4,1)} %bitcast.5), calls=%async_computation.1 | async-start | bytes 4194304
  3.0 28.3 %copy-start.7 = (bf16[16,4096]{1,0:T(8,128)(2,1)S(1)}, bf16[16,4096]{1,0:T(8,128)(2,1)}, u32[]{:S(2)}) copy-start(bf16[16,4096]{1,0:T(8,128)(2,1)} %get-tuple-element.30.refs_0_) | copy-start | bytes 393220
  3.0 10.7 %collective-permute-start.6 = (bf16[16,4096]{1,0:T(8,128)(2,1)}, bf16[16,4096]{1,0:T(8,128)(2,1)S(1)}, u32[]{:S(2)}, u32[]{:S(2)}) collective-permute-start(bf16[16,4096]{1,0:T(8,128)(2,1)} %get-tuple-element.30.refs_0_), channel_id=1, source_target_pairs={{0,8},{1,9},{2,10},{3,11},{4,12},{5,13},{6,14},{7,15},{8,0},{9,1},... | collective-permute-start | bytes 393224 | tf_op jit(solution)/shard_map/ppermute | solution.py:20
  7.1 11.7 %collective-permute-start.5 = (bf16[16,4096]{1,0:T(8,128)(2,1)}, bf16[16,4096]{1,0:T(8,128)(2,1)S(1)}, u32[]{:S(2)}, u32[]{:S(2)}) collective-permute-start(bf16[16,4096]{1,0:T(8,128)(2,1)} %get-tuple-element.30.refs_0_), channel_id=1, source_target_pairs={{0,6},{1,7},{2,4},{3,5},{4,2},{5,3},{6,0},{7,1},{8,14},{9,15},{10,... | collective-permute-start | bytes 393224 | tf_op jit(solution)/shard_map/ppermute | solution.py:20
  13.7 6.1 %collective-permute-start.8 = (bf16[16,4096]{1,0:T(8,128)(2,1)S(1)}, bf16[16,4096]{1,0:T(8,128)(2,1)S(1)}, u32[]{:S(2)}, u32[]{:S(2)}) collective-permute-start(bf16[16,4096]{1,0:T(8,128)(2,1)S(1)} %collective-permute-done.6.refs_4_), channel_id=1, source_target_pairs={{0,4},{1,5},{2,6},{3,7},{4,0},{5,1},{6,2},{7,3},{8,12},{9,13},{10,... | collective-permute-start | bytes 393224 | tf_op jit(solution)/shard_map/ppermute | solution.py:20
  14.5 6.8 %collective-permute-start.4 = (bf16[16,4096]{1,0:T(8,128)(2,1)}, bf16[16,4096]{1,0:T(8,128)(2,1)S(1)}, u32[]{:S(2)}, u32[]{:S(2)}) collective-permute-start(bf16[16,4096]{1,0:T(8,128)(2,1)} %get-tuple-element.30.refs_0_), channel_id=1, source_target_pairs={{0,4},{1,5},{2,6},{3,7},{4,0},{5,1},{6,2},{7,3},{8,12},{9,13},{10,... | collective-permute-start | bytes 393224 | tf_op jit(solution)/shard_map/ppermute | solution.py:20
  15.8 6.6 %collective-permute-start.3 = (bf16[16,4096]{1,0:T(8,128)(2,1)}, bf16[16,4096]{1,0:T(8,128)(2,1)S(1)}, u32[]{:S(2)}, u32[]{:S(2)}) collective-permute-start(bf16[16,4096]{1,0:T(8,128)(2,1)} %get-tuple-element.30.refs_0_), channel_id=1, source_target_pairs={{0,2},{1,3},{2,0},{3,1},{4,6},{5,7},{6,4},{7,5},{8,10},{9,11},{10,... | collective-permute-start | bytes 393224 | tf_op jit(solution)/shard_map/ppermute | solution.py:20
  17.3 6.6 %collective-permute-start = (bf16[64,2048]{1,0:T(8,128)(2,1)}, bf16[64,2048]{1,0:T(8,128)(2,1)S(1)}, u32[]{:S(2)}, u32[]{:S(2)}) collective-permute-start(bf16[64,2048]{1,0:T(8,128)(2,1)} %get-tuple-element.28), channel_id=1, source_target_pairs={{0,16},{16,0},{1,17},{17,1},{2,18},{18,2},{3,19},{19,3},{4,20},{20... | collective-permute-start | bytes 786440 | tf_op jit(solution)/shard_map/ppermute | solution.py:20
  18.8 6.1 %collective-permute-start.7 = (bf16[16,4096]{1,0:T(8,128)(2,1)S(1)}, bf16[16,4096]{1,0:T(8,128)(2,1)S(1)}, u32[]{:S(2)}, u32[]{:S(2)}) collective-permute-start(bf16[16,4096]{1,0:T(8,128)(2,1)S(1)} %collective-permute-done.6.refs_4_), channel_id=1, source_target_pairs={{0,2},{1,3},{2,0},{3,1},{4,6},{5,7},{6,4},{7,5},{8,10},{9,11},{10,... | collective-permute-start | bytes 393224 | tf_op jit(solution)/shard_map/ppermute | solution.py:20
  19.9 6.4 %collective-permute-start.9 = (bf16[16,4096]{1,0:T(8,128)(2,1)S(1)}, bf16[16,4096]{1,0:T(8,128)(2,1)S(1)}, u32[]{:S(2)}, u32[]{:S(2)}) collective-permute-start(bf16[16,4096]{1,0:T(8,128)(2,1)S(1)} %collective-permute-done.8.refs_6_), channel_id=1, source_target_pairs={{0,2},{1,3},{2,0},{3,1},{4,6},{5,7},{6,4},{7,5},{8,10},{9,11},{10,... | collective-permute-start | bytes 393224 | tf_op jit(solution)/shard_map/ppermute | solution.py:20
  23.3 8.0 %collective-permute-start.10 = (bf16[64,4096]{1,0:T(8,128)(2,1)S(1)}, bf16[64,4096]{1,0:T(8,128)(2,1)S(1)}, u32[]{:S(2)}, u32[]{:S(2)}) collective-permute-start(bf16[64,4096]{1,0:T(8,128)(2,1)S(1)} %pad_maximum_fusion), channel_id=1, source_target_pairs={{0,1},{1,0},{2,3},{3,2},{4,5},{5,4},{6,7},{7,6},{8,9},{9,8},{10,11... | collective-permute-start | bytes 1572872 | tf_op jit(solution)/shard_map/ppermute | solution.py:20
  23.9 5.6 %collective-permute-start.1 = (bf16[64,2048]{1,0:T(8,128)(2,1)S(1)}, bf16[64,2048]{1,0:T(8,128)(2,1)S(1)}, u32[]{:S(2)}, u32[]{:S(2)}) collective-permute-start(bf16[64,2048]{1,0:T(8,128)(2,1)S(1)} %collective-permute-done.mine_ref), channel_id=1, source_target_pairs={{0,1},{1,0},{2,3},{3,2},{4,5},{5,4},{6,7},{7,6},{8,9},{9,8},{10,11... | collective-permute-start | bytes 786440 | tf_op jit(solution)/shard_map/ppermute | solution.py:20
  26.3 4.9 %slice-start.1 = ((s8[10485760]{0:T(1024)(128)(4,1)}), s8[4194304]{0:T(1024)(128)(4,1)S(1)}, s32[]{:S(2)}) async-start(s8[10485760]{0:T(1024)(128)(4,1)} %bitcast.5), calls=%async_computation.2 | async-start | bytes 8388608
  26.4 6.9 %slice-start.2 = ((s8[10485760]{0:T(1024)(128)(4,1)}), s8[4194304]{0:T(1024)(128)(4,1)S(1)}, s32[]{:S(2)}) async-start(s8[10485760]{0:T(1024)(128)(4,1)} %bitcast.5), calls=%async_computation.3 | async-start | bytes 8388608
  26.4 4.9 %collective-permute-start.11 = (bf16[64,4096]{1,0:T(8,128)(2,1)S(1)}, bf16[64,4096]{1,0:T(8,128)(2,1)S(1)}, u32[]{:S(2)}, u32[]{:S(2)}) collective-permute-start(bf16[64,4096]{1,0:T(8,128)(2,1)S(1)} %pad_maximum_fusion.1), channel_id=1, source_target_pairs={{0,1},{1,0},{2,3},{3,2},{4,5},{5,4},{6,7},{7,6},{8,9},{9,8},{10,11... | collective-permute-start | bytes 1572872 | tf_op jit(solution)/shard_map/ppermute | solution.py:20
  26.4 2.6 %copy-start.3 = (bf16[2048,1280]{1,0:T(8,128)(2,1)S(1)}, bf16[2048,1280]{1,0:T(8,128)(2,1)}, u32[]{:S(2)}) copy-start(bf16[2048,1280]{1,0:T(8,128)(2,1)} %from_ref.1) | copy-start | bytes 15728644
  29.5 10.7 %copy-start = (bf16[2048,1280]{1,0:T(8,128)(2,1)}, bf16[2048,1280]{1,0:T(8,128)(2,1)S(1)}, u32[]{:S(2)}) copy-start(bf16[2048,1280]{1,0:T(8,128)(2,1)S(1)} %load.1.w_ref) | copy-start | bytes 15728644
  29.5 9.3 %copy-start.4 = (bf16[128,4096]{1,0:T(8,128)(2,1)S(1)}, bf16[128,4096]{1,0:T(8,128)(2,1)}, u32[]{:S(2)}) copy-start(bf16[128,4096]{1,0:T(8,128)(2,1)} %refs_2_.1) | copy-start | bytes 3145732
  29.5 9.3 %copy-start.8 = (f32[4096]{0:T(1024)S(1)}, f32[4096]{0:T(1024)}, u32[]{:S(2)}) copy-start(f32[4096]{0:T(1024)} %param.12) | copy-start | bytes 49156
  30.5 17.7 %copy-start.11 = (s32[256,1]{0,1:T(1,128)S(1)}, s32[256,1]{0,1:T(1,128)}, u32[]{:S(2)}) copy-start(s32[256,1]{0,1:T(1,128)} %param.14) | copy-start | bytes 3076
  30.5 33.6 %copy-start.12 = (s32[128]{0:T(128)S(1)}, s32[128]{0:T(128)}, u32[]{:S(2)}) copy-start(s32[128]{0:T(128)} %param.15) | copy-start | bytes 1540
  30.5 17.7 %collective-permute-start.2 = (f32[128,1280]{1,0:T(8,128)S(1)}, f32[128,1280]{1,0:T(8,128)S(1)}, u32[]{:S(2)}, u32[]{:S(2)}) collective-permute-start(f32[128,1280]{1,0:T(8,128)S(1)} %get-tuple-element.29), channel_id=1, source_target_pairs={{0,16},{16,0},{1,17},{17,1},{2,18},{18,2},{3,19},{19,3},{4,20},{20... | collective-permute-start | bytes 1966088 | tf_op jit(solution)/shard_map/ppermute | solution.py:20
  38.1 17.8 %collective-permute-start.12 = (bf16[128,1280]{1,0:T(8,128)(2,1)}, bf16[128,1280]{1,0:T(8,128)(2,1)S(1)}, u32[]{:S(2)}, u32[]{:S(2)}) collective-permute-start(bf16[128,1280]{1,0:T(8,128)(2,1)} %get-tuple-element.35), channel_id=1, source_target_pairs={{0,16},{16,0},{1,17},{17,1},{2,18},{18,2},{3,19},{19,3},{4,20},{20... | collective-permute-start | bytes 983048 | tf_op jit(solution)/shard_map/ppermute | solution.py:20
  40.1 9.8 %copy-start.9 = (f32[128,1]{1,0:T(8,128)}, f32[128,1]{1,0:T(8,128)S(1)}, u32[]{:S(2)}) copy-start(f32[128,1]{1,0:T(8,128)S(1)} %get-tuple-element.38.inv_ref) | copy-start | bytes 1540
  49.1 0.9 copy-start.5
  50.0 14.1 %all-to-all-start = ((f32[32,8,128]{2,1,0:T(8,128)}), f32[32,8,128]{2,1,0:T(8,128)S(1)}, u32[]{:S(2)}, u32[]{:S(2)}) async-start(f32[32,8,128]{2,1,0:T(8,128)} %get-tuple-element.32), calls=%async_computation | async-start | bytes 262144 | tf_op jit(solution)/shard_map/all_to_all | solution.py:589
  64.0 1.1 copy-start.6
  65.8 10.4 %collective-permute-start.13 = (bf16[136,1280]{1,0:T(8,128)(2,1)S(1)}, bf16[136,1280]{1,0:T(8,128)(2,1)S(1)}, u32[]{:S(2)}, u32[]{:S(2)}) collective-permute-start(bf16[136,1280]{1,0:T(8,128)(2,1)S(1)} %grads.1.refs_0_.grads_ref), channel_id=1, source_target_pairs={{0,16},{16,0},{1,17},{17,1},{2,18},{18,2},{3,19},{19,3},{4,20},{20... | collective-permute-start | bytes 1044488 | tf_op jit(solution)/shard_map/ppermute | solution.py:20
  66.7 2.5 %copy-start.1 = (bf16[2048,1280]{1,0:T(8,128)(2,1)S(1)}, bf16[2048,1280]{1,0:T(8,128)(2,1)}, u32[]{:S(2)}) copy-start(bf16[2048,1280]{1,0:T(8,128)(2,1)} %copy-done) | copy-start | bytes 15728644
  70.1 8.1 %collective-permute-start.14 = (bf16[1032,128]{1,0:T(8,128)(2,1)S(1)}, bf16[1032,128]{1,0:T(8,128)(2,1)S(1)}, u32[]{:S(2)}, u32[]{:S(2)}) collective-permute-start(bf16[1032,128]{1,0:T(8,128)(2,1)S(1)} %pieces.5), channel_id=1, source_target_pairs={{0,1},{1,0},{2,3},{3,2},{4,5},{5,4},{6,7},{7,6},{8,9},{9,8},{10,11... | collective-permute-start | bytes 792584 | tf_op jit(solution)/shard_map/ppermute | solution.py:20
  77.1 9.9 %collective-permute-start.19 = (bf16[1032,128]{1,0:T(8,128)(2,1)S(1)}, bf16[1032,128]{1,0:T(8,128)(2,1)}, u32[]{:S(2)}, u32[]{:S(2)}) collective-permute-start(bf16[1032,128]{1,0:T(8,128)(2,1)S(1)} %pieces.7), channel_id=1, source_target_pairs={{0,1},{1,0},{2,3},{3,2},{4,5},{5,4},{6,7},{7,6},{8,9},{9,8},{10,11... | collective-permute-start | bytes 792584 | tf_op jit(solution)/shard_map/ppermute | solution.py:20
  78.8 0.6 copy-start.13
  79.5 0.6 copy-start.14
  80.1 8.8 %collective-permute-start.15 = (bf16[264,128]{1,0:T(8,128)(2,1)}, bf16[264,128]{1,0:T(8,128)(2,1)}, u32[]{:S(2)}, u32[]{:S(2)}) collective-permute-start(bf16[264,128]{1,0:T(8,128)(2,1)} %get-tuple-element.40), channel_id=1, source_target_pairs={{0,2},{1,3},{2,0},{3,1},{4,6},{5,7},{6,4},{7,5},{8,10},{9,11},{10,... | collective-permute-start | bytes 202760 | tf_op jit(solution)/shard_map/ppermute | solution.py:20
  80.4 11.2 %collective-permute-start.16 = (bf16[264,128]{1,0:T(8,128)(2,1)}, bf16[264,128]{1,0:T(8,128)(2,1)S(1)}, u32[]{:S(2)}, u32[]{:S(2)}) collective-permute-start(bf16[264,128]{1,0:T(8,128)(2,1)} %copy-done.14), channel_id=1, source_target_pairs={{0,4},{1,5},{2,6},{3,7},{4,0},{5,1},{6,2},{7,3},{8,12},{9,13},{10,... | collective-permute-start | bytes 202760 | tf_op jit(solution)/shard_map/ppermute | solution.py:20
  80.8 10.8 %collective-permute-start.17 = (bf16[264,128]{1,0:T(8,128)(2,1)}, bf16[264,128]{1,0:T(8,128)(2,1)S(1)}, u32[]{:S(2)}, u32[]{:S(2)}) collective-permute-start(bf16[264,128]{1,0:T(8,128)(2,1)} %copy-done.13), channel_id=1, source_target_pairs={{0,6},{1,7},{2,4},{3,5},{4,2},{5,3},{6,0},{7,1},{8,14},{9,15},{10,... | collective-permute-start | bytes 202760 | tf_op jit(solution)/shard_map/ppermute | solution.py:20
  83.6 2.5 %copy-start.2 = (bf16[2048,1280]{1,0:T(8,128)(2,1)S(1)}, bf16[2048,1280]{1,0:T(8,128)(2,1)}, u32[]{:S(2)}) copy-start(bf16[2048,1280]{1,0:T(8,128)(2,1)} %copy-done) | copy-start | bytes 15728644
  88.1 5.8 %collective-permute-start.20 = (bf16[264,128]{1,0:T(8,128)(2,1)S(1)}, bf16[264,128]{1,0:T(8,128)(2,1)S(1)}, u32[]{:S(2)}, u32[]{:S(2)}) collective-permute-start(bf16[264,128]{1,0:T(8,128)(2,1)S(1)} %get-tuple-element.44), channel_id=1, source_target_pairs={{0,2},{1,3},{2,0},{3,1},{4,6},{5,7},{6,4},{7,5},{8,10},{9,11},{10,... | collective-permute-start | bytes 202760 | tf_op jit(solution)/shard_map/ppermute | solution.py:20
  88.5 5.5 %collective-permute-start.21 = (bf16[264,128]{1,0:T(8,128)(2,1)S(1)}, bf16[264,128]{1,0:T(8,128)(2,1)S(1)}, u32[]{:S(2)}, u32[]{:S(2)}) collective-permute-start(bf16[264,128]{1,0:T(8,128)(2,1)S(1)} %get-tuple-element.45), channel_id=1, source_target_pairs={{0,4},{1,5},{2,6},{3,7},{4,0},{5,1},{6,2},{7,3},{8,12},{9,13},{10,... | collective-permute-start | bytes 202760 | tf_op jit(solution)/shard_map/ppermute | solution.py:20
  88.8 5.8 %collective-permute-start.22 = (bf16[264,128]{1,0:T(8,128)(2,1)S(1)}, bf16[264,128]{1,0:T(8,128)(2,1)S(1)}, u32[]{:S(2)}, u32[]{:S(2)}) collective-permute-start(bf16[264,128]{1,0:T(8,128)(2,1)S(1)} %get-tuple-element.46), channel_id=1, source_target_pairs={{0,6},{1,7},{2,4},{3,5},{4,2},{5,3},{6,0},{7,1},{8,14},{9,15},{10,... | collective-permute-start | bytes 202760 | tf_op jit(solution)/shard_map/ppermute | solution.py:20
  92.6 17.4 %collective-permute-start.18 = (bf16[264,128]{1,0:T(8,128)(2,1)S(1)}, bf16[264,128]{1,0:T(8,128)(2,1)S(1)}, u32[]{:S(2)}, u32[]{:S(2)}) collective-permute-start(bf16[264,128]{1,0:T(8,128)(2,1)S(1)} %join.1.own_ref.refs_0_), channel_id=1, source_target_pairs={{8,0},{9,1},{10,2},{11,3},{12,4},{13,5},{14,6},{15,7},{16,24},{17,... | collective-permute-start | bytes 202760 | tf_op jit(solution)/shard_map/ppermute | solution.py:606
  94.8 17.4 %collective-permute-start.24 = (bf16[264,128]{1,0:T(8,128)(2,1)S(1)}, bf16[264,128]{1,0:T(8,128)(2,1)S(1)}, u32[]{:S(2)}, u32[]{:S(2)}) collective-permute-start(bf16[264,128]{1,0:T(8,128)(2,1)S(1)} %get-tuple-element.47), channel_id=1, source_target_pairs={{8,16},{9,17},{10,18},{11,19},{12,20},{13,21},{14,22},{15,23},{16,... | collective-permute-start | bytes 202760 | tf_op jit(solution)/shard_map/ppermute | solution.py:606
  95.5 16.8 %collective-permute-start.23 = (bf16[264,128]{1,0:T(8,128)(2,1)S(1)}, bf16[264,128]{1,0:T(8,128)(2,1)S(1)}, u32[]{:S(2)}, u32[]{:S(2)}) collective-permute-start(bf16[264,128]{1,0:T(8,128)(2,1)S(1)} %get-tuple-element.47), channel_id=1, source_target_pairs={{0,16},{1,17},{2,18},{3,19},{4,20},{5,21},{6,22},{7,23},{24,8},{25... | collective-permute-start | bytes 202760 | tf_op jit(solution)/shard_map/ppermute | solution.py:606
  105.7 6.5 %copy-start.10 = (f32[128,1]{1,0:T(8,128)S(1)}, f32[128,1]{1,0:T(8,128)}, u32[]{:S(2)}) copy-start(f32[128,1]{1,0:T(8,128)} %copy-done.9) | copy-start | bytes 1540
  105.8 6.5 %collective-permute-start.25 = (bf16[8,128]{1,0:T(8,128)(2,1)S(1)}, bf16[8,128]{1,0:T(8,128)(2,1)S(1)}, u32[]{:S(2)}, u32[]{:S(2)}) collective-permute-start(bf16[8,128]{1,0:T(8,128)(2,1)S(1)} %get-tuple-element.48.refs_4_), channel_id=1, source_target_pairs={{8,0},{9,1},{10,2},{11,3},{12,4},{13,5},{14,6},{15,7},{16,24},{17,... | collective-permute-start | bytes 6152 | tf_op jit(solution)/shard_map/ppermute | solution.py:606

commit v8 on v6

--- a/solution.py
+++ b/solution.py
@@ -200,7 +200,7 @@
 def teacher_kernel(keys, half, *refs):
     place = position()
     blocks = refs[: len(keys)]
-    w_ref, stat_ref, *exps = refs[len(keys) : -2]
+    w_ref, weight_ref, stat_ref, *exps = refs[len(keys) : -2]
     rows_ref, logits_ref = refs[-2:]
     mine = place[1] ^ (place[0] * half)
     for ref, owned in zip(blocks, keys):
@@ -223,35 +223,39 @@
     logits = logits_ref[...]
     top = jnp.max(logits, axis=1, keepdims=True)
     scaled = jnp.exp(logits - top)
-    rows = exps[0].shape[0]
+    rows = exps[0].shape[0] - EXTRA
     for r, ref in enumerate(exps):
-        ref[...] = scaled[r * rows : (r + 1) * rows].astype(ref.dtype)
+        ref[:rows] = scaled[r * rows : (r + 1) * rows].astype(ref.dtype)
+        ref[rows:] = jnp.zeros((EXTRA, cols), ref.dtype)
+        weight = weight_ref[pl.ds(place[0] ^ r, 1), :].astype(jnp.float32)
+        ref[rows:, :rows] = extra_rows([weight], ref.dtype)
     stat_ref[0:1, :] = as_row(top)
     stat_ref[1:2, :] = as_row(jnp.sum(scaled, axis=1, keepdims=True))
 
 
-def teacher_softmax(got, keys, head, half, branches):
+def teacher_softmax(got, keys, head, weights, half):
+    branches = weights.shape[0]
     width, cols = head.shape[1:]
     tokens = sum(part.shape[0] for part in got)
     return pl.pallas_call(
         functools.partial(teacher_kernel, keys, half),
         out_shape=(
             jax.ShapeDtypeStruct((2, tokens), jnp.float32),
-            *[jax.ShapeDtypeStruct((tokens // branches, cols), jnp.bfloat16)] * branches,
+            *[jax.ShapeDtypeStruct((tokens // branches + EXTRA, cols), jnp.bfloat16)] * branches,
         ),
-        in_specs=[VMEM] * (len(got) + 1),
+        in_specs=[VMEM] * (len(got) + 2),
         out_specs=(VMEM,) * (1 + branches),
         scratch_shapes=[pltpu.VMEM((tokens, width), jnp.bfloat16), pltpu.VMEM((tokens, cols), jnp.float32)],
         compiler_params=params(28),
         cost_estimate=cost(2 * tokens * width * cols, 2 * width * cols, tokens * cols),
         name="teacher",
-    )(*got, head)
+    )(*got, head, weights)
 
 
 def stats_kernel(count, *refs):
     place = position()
     parts = refs[:count]
-    teacher_ref, weight_ref, logits_ref, out_ref = refs[count:]
+    teacher_ref, logits_ref, out_ref = refs[count:]
     logits = parts[0][...]
     for ref in parts[1:]:
         logits = logits + ref[...]
@@ -263,33 +267,25 @@
     student = jnp.concatenate([as_row(top), as_row(total)], axis=0)
     for r in range(count):
         there = place[0] ^ r
-        block = jnp.concatenate(
-            [
-                teacher_ref[:, r * rows : (r + 1) * rows],
-                student,
-                weight_ref[pl.ds(there, 1), :].astype(jnp.float32),
-                jnp.zeros((3, rows), jnp.float32),
-            ],
-            axis=0,
-        )
-        out_ref[pl.ds(there * size, size)] = jnp.broadcast_to(block[None], (size, 8, rows))
-
-
-def student_stats(parts, teacher_stats, weights, size):
+        block = jnp.concatenate([teacher_ref[:, r * rows : (r + 1) * rows], student], axis=0)
+        out_ref[pl.ds(there * size, size)] = jnp.broadcast_to(block[None], (size, 4, rows))
+
+
+def student_stats(parts, teacher_stats, size):
     rows, cols = parts[0].shape
     count = len(parts)
     return pl.pallas_call(
         functools.partial(stats_kernel, count),
         out_shape=(
             jax.ShapeDtypeStruct((rows, cols), jnp.float32),
-            jax.ShapeDtypeStruct((count * size, 8, rows), jnp.float32),
+            jax.ShapeDtypeStruct((count * size, 4, rows), jnp.float32),
         ),
-        in_specs=[VMEM] * (count + 2),
+        in_specs=[VMEM] * (count + 1),
         out_specs=(VMEM, VMEM),
         compiler_params=params(12),
         cost_estimate=cost(8 * rows * cols, 12 * rows * cols, rows * cols),
         name="stats",
-    )(*parts, teacher_stats, weights)
+    )(*parts, teacher_stats)
 
 
 def grads_kernel(count, size, stats_ref, logits_ref, ids_ref, *refs):
@@ -308,8 +304,9 @@
         here = stats_ref[start + t]
         peak = jnp.max(block[:, 0, :], axis=0, keepdims=True)
         total = jnp.sum(block[:, 1, :] * jnp.exp(block[:, 0, :] - peak), axis=0, keepdims=True)
-        scale = ((1.0 - mix_label) / DEN) * here[4:5] * jnp.exp(here[0:1] - peak) / total
-        targets = targets + terms[r][...].astype(jnp.float32) * column(scale)
+        weight = extra_values(terms[r][rows:, :rows], 1)[0]
+        scale = ((1.0 - mix_label) / DEN) * weight * jnp.exp(here[0:1] - peak) / total
+        targets = targets + terms[r][:rows].astype(jnp.float32) * column(scale)
         if r == 0:
             peak = jnp.max(block[:, 2, :], axis=0, keepdims=True)
             total = jnp.sum(block[:, 3, :] * jnp.exp(block[:, 2, :] - peak), axis=0, keepdims=True)
@@ -433,35 +430,42 @@
     )(*[part for some in parts for part in some], *turned)
 
 
-def head_grad_kernel(count, *refs):
+def head_grad_kernel(count, half, tile, *refs):
     grads, turned = refs[:count], refs[count : 2 * count]
-    out_ref, grads_ref = refs[-2:]
+    out_ref, grads_ref, total_ref, sems = refs[-4:]
     rows = grads_ref.shape[0] // count
-
-    @pl.when(pl.program_id(0) == 0)
-    def _():
-        for r in range(count):
-            grads_ref[r * rows : (r + 1) * rows, :] = grads[r][:rows]
-
-    lhs = jnp.concatenate([ref[...] for ref in turned], axis=1)
-    out_ref[...] = jnp.dot(lhs, grads_ref[...], preferred_element_type=jnp.float32)
+    for r in range(count):
+        grads_ref[r * rows : (r + 1) * rows, :] = grads[r][:rows]
+    copies = []
+    for i in range(total_ref.shape[0] // tile):
+        here = slice(i * tile, (i + 1) * tile)
+        start = half * total_ref.shape[0] + i * tile
+        lhs = jnp.concatenate([ref[start : start + tile] for ref in turned], axis=1)
+        total_ref[here] = jnp.dot(lhs, grads_ref[...], preferred_element_type=jnp.float32)
+        copy = pltpu.make_async_copy(total_ref.at[here], out_ref.at[pl.ds(start, tile)], sems.at[i])
+        copy.start()
+        copies.append(copy)
+    for copy in copies:
+        copy.wait()
 
 
 def head_grad(grads, turned, half, done):
     count = len(grads)
-    full, cols = grads[0].shape
+    cols = grads[0].shape[1]
     part, rows = turned[0].shape
-    tile = tile_of(part)
+    tile = tile_of(part // 2)
     steps = part // tile // 2
-    return pl.pallas_call(
-        functools.partial(head_grad_kernel, count),
+    whole = pl.BlockSpec(memory_space=pl.ANY)
+    return pl.pallas_call(
+        functools.partial(head_grad_kernel, count, half, tile),
         out_shape=jax.ShapeDtypeStruct((part, cols), jnp.float32),
-        grid=(steps,),
-        in_specs=[pl.BlockSpec((full, cols), lambda i: (0, 0))] * count
-        + [pl.BlockSpec((tile, rows), lambda i: (i + half * steps, 0))] * count
-        + [pl.BlockSpec(memory_space=pl.ANY)] * len(done),
-        out_specs=pl.BlockSpec((tile, cols), lambda i: (i + half * steps, 0)),
-        scratch_shapes=[pltpu.VMEM((count * rows, cols), jnp.bfloat16)],
+        in_specs=[VMEM] * (2 * count) + [whole] * len(done),
+        out_specs=whole,
+        scratch_shapes=[
+            pltpu.VMEM((count * rows, cols), jnp.bfloat16),
+            pltpu.VMEM((part // 2, cols), jnp.float32),
+            pltpu.SemaphoreType.DMA((steps,)),
+        ],
         input_output_aliases={2 * count: 0} if done else {},
         compiler_params=params(16),
         cost_estimate=cost(count * rows * part * cols, 2 * part * cols),
@@ -548,11 +552,11 @@
         partials.append(swap(partial, "branch", r))
 
     got, keys = gather_blocks(teacher_block, size)
-    teacher_stats, *exps = teacher_softmax(got, keys, teacher_head, blocks, branches)
+    weights = cluster_weights[:, 0].reshape(branches, rows)
+    teacher_stats, *exps = teacher_softmax(got, keys, teacher_head, weights, blocks)
     terms = [exps[0]] + [swap(exps[r], "branch", r) for r in range(1, branches)]
 
-    weights = cluster_weights[:, 0].reshape(branches, rows)
-    logits, stats = student_stats(partials, teacher_stats, weights, size)
+    logits, stats = student_stats(partials, teacher_stats, size)
     stats = lax.all_to_all(stats, ("branch", "tok"), 0, 0, tiled=True)
     logit_grads = make_grads(stats, logits, token_ids[None], terms, size)
     all_grads = [logit_grads] + [swap(logit_grads, "branch", r) for r in range(1, branches)]

time: 108 us -> 105 us (0.972)
  Pallas kernels: 25.4 us -> 23.5 us
  local copies, waits for them, and re-layouts: 12.9 us -> 11.2 us
    unnamed x36, local copies, waits for them, and re-layouts: 12.9 us -> 11.1 us
    ppermute x22, waiting for transfers between devices: 25.5 us -> 26.8 us  [swap(): return lax.ppermute(value, axis, [(i, i ^ flip) for i in range(size)])]
  transfers between devices with their start and end apart: 25 -> 25, of which waited for: 11 -> 10; matrix products, arithmetic and copies ran while one was open for 1% -> 1% of each run, Pallas kernels for 19% -> 18%
where the time goes in v8:
time: 105 us
  starting transfers between devices  34.2 us (33%)
  waiting for transfers between devices  34.2 us (33%)
  Pallas kernels  23.5 us (22%)
  local copies, waits for them, and re-layouts  11.2 us (11%)
    ppermute x22, waiting for transfers between devices, swap(): return lax.ppermute(value, axis, [(i, i ^ flip) for i in range(size)])  26.8 us
    ppermute x22, starting transfers between devices, swap(): return lax.ppermute(value, axis, [(i, i ^ flip) for i in range(size)])  24.3 us
    unnamed x36, local copies, waits for them, and re-layouts  11.1 us
    all_to_all x1, waiting for transfers between devices, per_device(): stats = lax.all_to_all(stats, ('branch', 'tok'), 0, 0, tiled=True)  7.4 us
    all_to_all x1, starting transfers between devices, per_device(): stats = lax.all_to_all(stats, ('branch', 'tok'), 0, 0, tiled=True)  5.84 us
    pallas_call x2, Pallas kernels, head_grad(): pl.pallas_call(functools.partial(head_grad_kernel, count, half, tile), ou...  5.53 us
    pallas_call x1, Pallas kernels, teacher_softmax(): pl.pallas_call(functools.partial(teacher_kernel, keys, half), out_shape=(...  4.89 us
    ppermute x2, starting transfers between devices, per_device(): arrived.append(lax.ppermute(owned[kh], ('branch', 'tok'), perm))  4.06 us
  transfers between devices with their start and end apart: 25, of which 10 were waited for; matrix products, arithmetic and copies ran while one was open for 1% of the time, Pallas kernels for 18%

profile of v8, /device:TPU:0, one launch (start us, length us, event | category | flops | bytes accessed | tf_op | source)
XLA Modules:
  0.0 105.1 jit_solution(5767878727284813656)
XLA Ops:
  0.7 2.3 %first.1 = (bf16[16,4096]{1,0:T(8,128)(2,1)}, bf16[64,2048]{1,0:T(8,128)(2,1)}) custom-call(bf16[1,16,4096]{2,1,0:T(8,128)(2,1)} %refs_0_.1, f32[1,4096]{1,0:T(1,128)} %refs_1_.1, bf16[128,4096]{1,0:T(8,128)(2,1)} %refs_2_.1, f32[1,4096]{1,0:T(1,128)} %bitcast.7), custom_call_target="tpu_custom_call" | custom-call | flops 4194304 | bytes 2097152 | tf_op jit(solution)/shard_map/first/pallas_call | solution.py:76
  3.0 4.1 %collective-permute-start.6 = (bf16[16,4096]{1,0:T(8,128)(2,1)}, bf16[16,4096]{1,0:T(8,128)(2,1)S(1)}, u32[]{:S(2)}, u32[]{:S(2)}) collective-permute-start(bf16[16,4096]{1,0:T(8,128)(2,1)} %get-tuple-element.30.refs_0_), channel_id=1, source_target_pairs={{0,8},{1,9},{2,10},{3,11},{4,12},{5,13},{6,14},{7,15},{8,0},{9,1},... | collective-permute-start | bytes 393224 | tf_op jit(solution)/shard_map/ppermute | solution.py:20
  7.1 2.5 %collective-permute-start.5 = (bf16[16,4096]{1,0:T(8,128)(2,1)}, bf16[16,4096]{1,0:T(8,128)(2,1)S(1)}, u32[]{:S(2)}, u32[]{:S(2)}) collective-permute-start(bf16[16,4096]{1,0:T(8,128)(2,1)} %get-tuple-element.30.refs_0_), channel_id=1, source_target_pairs={{0,6},{1,7},{2,4},{3,5},{4,2},{5,3},{6,0},{7,1},{8,14},{9,15},{10,... | collective-permute-start | bytes 393224 | tf_op jit(solution)/shard_map/ppermute | solution.py:20
  9.7 4.1 %collective-permute-done.6.refs_4_ = bf16[16,4096]{1,0:T(8,128)(2,1)S(1)} collective-permute-done((bf16[16,4096]{1,0:T(8,128)(2,1)}, bf16[16,4096]{1,0:T(8,128)(2,1)S(1)}, u32[]{:S(2)}, u32[]{:S(2)}) %collective-permute-start.6) | collective-permute-done | bytes 131104 | tf_op jit(solution)/shard_map/ppermute | solution.py:20
  13.8 0.8 collective-permute-start.8
  14.5 1.3 %collective-permute-start.4 = (bf16[16,4096]{1,0:T(8,128)(2,1)}, bf16[16,4096]{1,0:T(8,128)(2,1)S(1)}, u32[]{:S(2)}, u32[]{:S(2)}) collective-permute-start(bf16[16,4096]{1,0:T(8,128)(2,1)} %get-tuple-element.30.refs_0_), channel_id=1, source_target_pairs={{0,4},{1,5},{2,6},{3,7},{4,0},{5,1},{6,2},{7,3},{8,12},{9,13},{10,... | collective-permute-start | bytes 393224 | tf_op jit(solution)/shard_map/ppermute | solution.py:20
  15.8 1.6 %collective-permute-start.3 = (bf16[16,4096]{1,0:T(8,128)(2,1)}, bf16[16,4096]{1,0:T(8,128)(2,1)S(1)}, u32[]{:S(2)}, u32[]{:S(2)}) collective-permute-start(bf16[16,4096]{1,0:T(8,128)(2,1)} %get-tuple-element.30.refs_0_), channel_id=1, source_target_pairs={{0,2},{1,3},{2,0},{3,1},{4,6},{5,7},{6,4},{7,5},{8,10},{9,11},{10,... | collective-permute-start | bytes 393224 | tf_op jit(solution)/shard_map/ppermute | solution.py:20
  17.4 1.5 %collective-permute-start = (bf16[64,2048]{1,0:T(8,128)(2,1)}, bf16[64,2048]{1,0:T(8,128)(2,1)S(1)}, u32[]{:S(2)}, u32[]{:S(2)}) collective-permute-start(bf16[64,2048]{1,0:T(8,128)(2,1)} %get-tuple-element.28), channel_id=1, source_target_pairs={{0,16},{16,0},{1,17},{17,1},{2,18},{18,2},{3,19},{19,3},{4,20},{20... | collective-permute-start | bytes 786440 | tf_op jit(solution)/shard_map/ppermute | solution.py:20
  19.4 0.5 collective-permute-done.8.refs_6_
  19.9 1.5 %collective-permute-start.9 = (bf16[16,4096]{1,0:T(8,128)(2,1)S(1)}, bf16[16,4096]{1,0:T(8,128)(2,1)S(1)}, u32[]{:S(2)}, u32[]{:S(2)}) collective-permute-start(bf16[16,4096]{1,0:T(8,128)(2,1)S(1)} %collective-permute-done.8.refs_6_), channel_id=1, source_target_pairs={{0,2},{1,3},{2,0},{3,1},{4,6},{5,7},{6,4},{7,5},{8,10},{9,11},{10,... | collective-permute-start | bytes 393224 | tf_op jit(solution)/shard_map/ppermute | solution.py:20
  21.4 1.0 collective-permute-done.3.refs_1_
  22.4 0.9 pad_maximum_fusion
  23.4 1.5 %collective-permute-done.7.refs_5_ = bf16[16,4096]{1,0:T(8,128)(2,1)S(1)} collective-permute-done((bf16[16,4096]{1,0:T(8,128)(2,1)S(1)}, bf16[16,4096]{1,0:T(8,128)(2,1)S(1)}, u32[]{:S(2)}, u32[]{:S(2)}) %collective-permute-start.7) | collective-permute-done | bytes 131104 | tf_op jit(solution)/shard_map/ppermute | solution.py:20
  24.9 1.4 %collective-permute-done.9.refs_7_ = bf16[16,4096]{1,0:T(8,128)(2,1)S(1)} collective-permute-done((bf16[16,4096]{1,0:T(8,128)(2,1)S(1)}, bf16[16,4096]{1,0:T(8,128)(2,1)S(1)}, u32[]{:S(2)}, u32[]{:S(2)}) %collective-permute-start.9) | collective-permute-done | bytes 131104 | tf_op jit(solution)/shard_map/ppermute | solution.py:20
  27.0 2.8 %copy-done.3 = bf16[2048,1280]{1,0:T(8,128)(2,1)S(1)} copy-done((bf16[2048,1280]{1,0:T(8,128)(2,1)S(1)}, bf16[2048,1280]{1,0:T(8,128)(2,1)}, u32[]{:S(2)}) %copy-start.3) | copy-done | bytes 5242904
  30.1 0.9 otherdot.1
  31.1 0.8 collective-permute-start.2
  32.0 4.9 %teacher.1 = (f32[2,256]{1,0:T(2,128)S(1)}, bf16[136,1280]{1,0:T(8,128)(2,1)S(1)}, bf16[136,1280]{1,0:T(8,128)(2,1)}) custom-call(bf16[16,4096]{1,0:T(8,128)(2,1)S(1)} %copy-done.7, bf16[16,4096]{1,0:T(8,128)(2,1)S(1)} %collective-permute-done.3.refs_1_, bf16[16,4096]{1,0:T(8,128)(2,1)S(1)} %collective-permute-done.4.refs_2_, ...), custom_call_target="tpu_custom_call" | custom-call | flops 2684354560 | bytes 10485760 | tf_op jit(solution)/shard_map/teacher/pallas_call | solution.py:240
  36.9 1.3 %collective-permute-start.12 = (bf16[136,1280]{1,0:T(8,128)(2,1)}, bf16[136,1280]{1,0:T(8,128)(2,1)S(1)}, u32[]{:S(2)}, u32[]{:S(2)}) collective-permute-start(bf16[136,1280]{1,0:T(8,128)(2,1)} %get-tuple-element.35), channel_id=1, source_target_pairs={{0,16},{16,0},{1,17},{17,1},{2,18},{18,2},{3,19},{19,3},{4,20},{20... | collective-permute-start | bytes 1044488 | tf_op jit(solution)/shard_map/ppermute | solution.py:20
  38.2 1.3 %owndot.1 = (f32[128,1280]{1,0:T(8,128)S(1)}, bf16[2048,128]{1,0:T(8,128)(2,1)S(1)}, f32[128,1]{1,0:T(8,128)S(1)}) custom-call(bf16[128,4096]{1,0:T(8,128)(2,1)S(1)} %copy-done.4, f32[1,4096]{1,0:T(1,128)S(1)} %bitcast.8, bf16[2048,1280]{1,0:T(8,128)(2,1)S(1)} %load.1.w_ref), custom_call_target="tpu_custom_call" | custom-call | flops 671088640 | bytes 5242880 | tf_op jit(solution)/shard_map/owndot/pallas_call | solution.py:129
  39.5 9.3 %collective-permute-done.2.refs_1_ = f32[128,1280]{1,0:T(8,128)S(1)} collective-permute-done((f32[128,1280]{1,0:T(8,128)S(1)}, f32[128,1280]{1,0:T(8,128)S(1)}, u32[]{:S(2)}, u32[]{:S(2)}) %collective-permute-start.2) | collective-permute-done | bytes 655392 | tf_op jit(solution)/shard_map/ppermute | solution.py:20
  48.8 0.9 stats.1
  49.7 0.9 copy-done.5
  50.6 5.8 %all-to-all-start = ((f32[32,4,128]{2,1,0:T(4,128)}), f32[32,4,128]{2,1,0:T(4,128)S(1)}, u32[]{:S(2)}, u32[]{:S(2)}) async-start(f32[32,4,128]{2,1,0:T(4,128)} %get-tuple-element.32), calls=%async_computation | async-start | bytes 131072 | tf_op jit(solution)/shard_map/all_to_all | solution.py:560
  56.4 7.4 %all-to-all-done.stats_ref = f32[32,4,128]{2,1,0:T(4,128)S(1)} async-done(((f32[32,4,128]{2,1,0:T(4,128)}), f32[32,4,128]{2,1,0:T(4,128)S(1)}, u32[]{:S(2)}, u32[]{:S(2)}) %all-to-all-start) | async-done | bytes 65568 | tf_op jit(solution)/shard_map/all_to_all | solution.py:560
  63.8 1.1 %copy-done.6 = f32[128,1280]{1,0:T(8,128)S(1)} copy-done((f32[128,1280]{1,0:T(8,128)S(1)}, f32[128,1280]{1,0:T(8,128)}, u32[]{:S(2)}) %copy-start.6) | copy-done | bytes 655384
  64.9 0.7 grads.1.refs_0_.grads_ref
  65.7 0.7 collective-permute-start.13
  66.4 2.5 %copy-done.1 = bf16[2048,1280]{1,0:T(8,128)(2,1)S(1)} copy-done((bf16[2048,1280]{1,0:T(8,128)(2,1)S(1)}, bf16[2048,1280]{1,0:T(8,128)(2,1)}, u32[]{:S(2)}) %copy-start.1) | copy-done | bytes 5242904
  68.9 0.9 pieces.5
  69.9 6.0 %collective-permute-done.13.refs_1_.grads_ref = bf16[136,1280]{1,0:T(8,128)(2,1)S(1)} collective-permute-done((bf16[136,1280]{1,0:T(8,128)(2,1)S(1)}, bf16[136,1280]{1,0:T(8,128)(2,1)S(1)}, u32[]{:S(2)}, u32[]{:S(2)}) %collective-permute-start.13) | collective-permute-done | bytes 348192 | tf_op jit(solution)/shard_map/ppermute | solution.py:20
  75.9 0.9 pieces.7
  76.9 0.9 pieces.4.mine_ref
  77.8 0.7 fold.2
  78.5 0.6 copy-done.13
  79.1 0.6 copy-done.14
  80.8 2.5 %collective-permute-start.17 = (bf16[264,128]{1,0:T(8,128)(2,1)}, bf16[264,128]{1,0:T(8,128)(2,1)S(1)}, u32[]{:S(2)}, u32[]{:S(2)}) collective-permute-start(bf16[264,128]{1,0:T(8,128)(2,1)} %copy-done.13), channel_id=1, source_target_pairs={{0,6},{1,7},{2,4},{3,5},{4,2},{5,3},{6,0},{7,1},{8,14},{9,15},{10,... | collective-permute-start | bytes 202760 | tf_op jit(solution)/shard_map/ppermute | solution.py:20
  83.3 2.5 %copy-done.2 = bf16[2048,1280]{1,0:T(8,128)(2,1)S(1)} copy-done((bf16[2048,1280]{1,0:T(8,128)(2,1)S(1)}, bf16[2048,1280]{1,0:T(8,128)(2,1)}, u32[]{:S(2)}) %copy-start.2) | copy-done | bytes 5242904
  85.8 0.9 pieces.6.mine_ref
  86.7 1.0 fold.3
  88.8 2.5 %collective-permute-start.21 = (bf16[264,128]{1,0:T(8,128)(2,1)S(1)}, bf16[264,128]{1,0:T(8,128)(2,1)S(1)}, u32[]{:S(2)}, u32[]{:S(2)}) collective-permute-start(bf16[264,128]{1,0:T(8,128)(2,1)S(1)} %get-tuple-element.46), channel_id=1, source_target_pairs={{0,6},{1,7},{2,4},{3,5},{4,2},{5,3},{6,0},{7,1},{8,14},{9,15},{10,... | collective-permute-start | bytes 202760 | tf_op jit(solution)/shard_map/ppermute | solution.py:20
  91.3 1.5 %collective-permute-done.19.refs_5_ = bf16[264,128]{1,0:T(8,128)(2,1)S(1)} collective-permute-done((bf16[264,128]{1,0:T(8,128)(2,1)S(1)}, bf16[264,128]{1,0:T(8,128)(2,1)S(1)}, u32[]{:S(2)}, u32[]{:S(2)}) %collective-permute-start.19) | collective-permute-done | bytes 67616 | tf_op jit(solution)/shard_map/ppermute | solution.py:20
  92.8 1.5 %collective-permute-done.21.refs_7_ = bf16[264,128]{1,0:T(8,128)(2,1)S(1)} collective-permute-done((bf16[264,128]{1,0:T(8,128)(2,1)S(1)}, bf16[264,128]{1,0:T(8,128)(2,1)S(1)}, u32[]{:S(2)}, u32[]{:S(2)}) %collective-permute-start.21) | collective-permute-done | bytes 67616 | tf_op jit(solution)/shard_map/ppermute | solution.py:20
  94.5 0.7 collective-permute-start.22
  95.2 3.4 %collective-permute-start.23 = (bf16[264,128]{1,0:T(8,128)(2,1)S(1)}, bf16[264,128]{1,0:T(8,128)(2,1)S(1)}, u32[]{:S(2)}, u32[]{:S(2)}) collective-permute-start(bf16[264,128]{1,0:T(8,128)(2,1)S(1)} %get-tuple-element.48), channel_id=1, source_target_pairs={{0,16},{1,17},{2,18},{3,19},{4,20},{5,21},{6,22},{7,23},{8,0},{9,1... | collective-permute-start | bytes 202760 | tf_op jit(solution)/shard_map/ppermute | solution.py:579
  98.6 2.8 %headgrad.2.refs_4_ = f32[2048,1280]{1,0:T(8,128)} custom-call(bf16[136,1280]{1,0:T(8,128)(2,1)S(1)} %grads.1.refs_0_.grads_ref, bf16[136,1280]{1,0:T(8,128)(2,1)S(1)} %collective-permute-done.13.refs_1_.grads_ref, bf16[2048,128]{1,0:T(8,128)(2,1)S(1)} %get-tuple-element.36.refs_2_.refs_8_, bf16[2048,128]{1,0:T(8,128)(2,1)S(1)} %get-tuple-element.37.refs_3_.refs_9_), custom_call_target="tpu_custom_call" | custom-call | flops 671088640 | bytes 5242880 | tf_op jit(solution)/shard_map/headgrad/pallas_call | solution.py:459
  101.4 2.8 %headgrad.3 = f32[2048,1280]{1,0:T(8,128)} custom-call(bf16[136,1280]{1,0:T(8,128)(2,1)S(1)} %grads.1.refs_0_.grads_ref, bf16[136,1280]{1,0:T(8,128)(2,1)S(1)} %collective-permute-done.13.refs_1_.grads_ref, bf16[2048,128]{1,0:T(8,128)(2,1)S(1)} %get-tuple-element.36.refs_2_.refs_8_, ...), custom_call_target="tpu_custom_call", output_to_operand_aliasing={{}: (4, {})} | custom-call | flops 671088640 | bytes 5242880 | tf_op jit(solution)/shard_map/headgrad/pallas_call | solution.py:459
  104.2 0.9 last.1
  (60 shorter events, 4.2 us)
Async XLA Ops:
  0.6 31.3 %copy-start.11 = (s32[256,1]{0,1:T(1,128)S(1)}, s32[256,1]{0,1:T(1,128)}, u32[]{:S(2)}) copy-start(s32[256,1]{0,1:T(1,128)} %param.14) | copy-start | bytes 3076
  0.6 31.2 %slice-start = ((s8[10485760]{0:T(1024)(128)(4,1)}), s8[2097152]{0:T(1024)(128)(4,1)S(1)}, s32[]{:S(2)}) async-start(s8[10485760]{0:T(1024)(128)(4,1)} %bitcast.5), calls=%async_computation.1 | async-start | bytes 4194304
  3.0 28.9 %copy-start.7 = (bf16[16,4096]{1,0:T(8,128)(2,1)S(1)}, bf16[16,4096]{1,0:T(8,128)(2,1)}, u32[]{:S(2)}) copy-start(bf16[16,4096]{1,0:T(8,128)(2,1)} %get-tuple-element.30.refs_0_) | copy-start | bytes 393220
  3.0 10.7 %collective-permute-start.6 = (bf16[16,4096]{1,0:T(8,128)(2,1)}, bf16[16,4096]{1,0:T(8,128)(2,1)S(1)}, u32[]{:S(2)}, u32[]{:S(2)}) collective-permute-start(bf16[16,4096]{1,0:T(8,128)(2,1)} %get-tuple-element.30.refs_0_), channel_id=1, source_target_pairs={{0,8},{1,9},{2,10},{3,11},{4,12},{5,13},{6,14},{7,15},{8,0},{9,1},... | collective-permute-start | bytes 393224 | tf_op jit(solution)/shard_map/ppermute | solution.py:20
  7.1 11.7 %collective-permute-start.5 = (bf16[16,4096]{1,0:T(8,128)(2,1)}, bf16[16,4096]{1,0:T(8,128)(2,1)S(1)}, u32[]{:S(2)}, u32[]{:S(2)}) collective-permute-start(bf16[16,4096]{1,0:T(8,128)(2,1)} %get-tuple-element.30.refs_0_), channel_id=1, source_target_pairs={{0,6},{1,7},{2,4},{3,5},{4,2},{5,3},{6,0},{7,1},{8,14},{9,15},{10,... | collective-permute-start | bytes 393224 | tf_op jit(solution)/shard_map/ppermute | solution.py:20
  13.8 6.1 %collective-permute-start.8 = (bf16[16,4096]{1,0:T(8,128)(2,1)S(1)}, bf16[16,4096]{1,0:T(8,128)(2,1)S(1)}, u32[]{:S(2)}, u32[]{:S(2)}) collective-permute-start(bf16[16,4096]{1,0:T(8,128)(2,1)S(1)} %collective-permute-done.6.refs_4_), channel_id=1, source_target_pairs={{0,4},{1,5},{2,6},{3,7},{4,0},{5,1},{6,2},{7,3},{8,12},{9,13},{10,... | collective-permute-start | bytes 393224 | tf_op jit(solution)/shard_map/ppermute | solution.py:20
  14.5 6.8 %collective-permute-start.4 = (bf16[16,4096]{1,0:T(8,128)(2,1)}, bf16[16,4096]{1,0:T(8,128)(2,1)S(1)}, u32[]{:S(2)}, u32[]{:S(2)}) collective-permute-start(bf16[16,4096]{1,0:T(8,128)(2,1)} %get-tuple-element.30.refs_0_), channel_id=1, source_target_pairs={{0,4},{1,5},{2,6},{3,7},{4,0},{5,1},{6,2},{7,3},{8,12},{9,13},{10,... | collective-permute-start | bytes 393224 | tf_op jit(solution)/shard_map/ppermute | solution.py:20
  15.8 6.6 %collective-permute-start.3 = (bf16[16,4096]{1,0:T(8,128)(2,1)}, bf16[16,4096]{1,0:T(8,128)(2,1)S(1)}, u32[]{:S(2)}, u32[]{:S(2)}) collective-permute-start(bf16[16,4096]{1,0:T(8,128)(2,1)} %get-tuple-element.30.refs_0_), channel_id=1, source_target_pairs={{0,2},{1,3},{2,0},{3,1},{4,6},{5,7},{6,4},{7,5},{8,10},{9,11},{10,... | collective-permute-start | bytes 393224 | tf_op jit(solution)/shard_map/ppermute | solution.py:20
  17.4 9.1 %collective-permute-start = (bf16[64,2048]{1,0:T(8,128)(2,1)}, bf16[64,2048]{1,0:T(8,128)(2,1)S(1)}, u32[]{:S(2)}, u32[]{:S(2)}) collective-permute-start(bf16[64,2048]{1,0:T(8,128)(2,1)} %get-tuple-element.28), channel_id=1, source_target_pairs={{0,16},{16,0},{1,17},{17,1},{2,18},{18,2},{3,19},{19,3},{4,20},{20... | collective-permute-start | bytes 786440 | tf_op jit(solution)/shard_map/ppermute | solution.py:20
  18.9 6.1 %collective-permute-start.7 = (bf16[16,4096]{1,0:T(8,128)(2,1)S(1)}, bf16[16,4096]{1,0:T(8,128)(2,1)S(1)}, u32[]{:S(2)}, u32[]{:S(2)}) collective-permute-start(bf16[16,4096]{1,0:T(8,128)(2,1)S(1)} %collective-permute-done.6.refs_4_), channel_id=1, source_target_pairs={{0,2},{1,3},{2,0},{3,1},{4,6},{5,7},{6,4},{7,5},{8,10},{9,11},{10,... | collective-permute-start | bytes 393224 | tf_op jit(solution)/shard_map/ppermute | solution.py:20
  19.9 6.4 %collective-permute-start.9 = (bf16[16,4096]{1,0:T(8,128)(2,1)S(1)}, bf16[16,4096]{1,0:T(8,128)(2,1)S(1)}, u32[]{:S(2)}, u32[]{:S(2)}) collective-permute-start(bf16[16,4096]{1,0:T(8,128)(2,1)S(1)} %collective-permute-done.8.refs_6_), channel_id=1, source_target_pairs={{0,2},{1,3},{2,0},{3,1},{4,6},{5,7},{6,4},{7,5},{8,10},{9,11},{10,... | collective-permute-start | bytes 393224 | tf_op jit(solution)/shard_map/ppermute | solution.py:20
  23.3 8.6 %collective-permute-start.10 = (bf16[64,4096]{1,0:T(8,128)(2,1)S(1)}, bf16[64,4096]{1,0:T(8,128)(2,1)S(1)}, u32[]{:S(2)}, u32[]{:S(2)}) collective-permute-start(bf16[64,4096]{1,0:T(8,128)(2,1)S(1)} %pad_maximum_fusion), channel_id=1, source_target_pairs={{0,1},{1,0},{2,3},{3,2},{4,5},{5,4},{6,7},{7,6},{8,9},{9,8},{10,11... | collective-permute-start | bytes 1572872 | tf_op jit(solution)/shard_map/ppermute | solution.py:20
  26.4 5.6 %slice-start.1 = ((s8[10485760]{0:T(1024)(128)(4,1)}), s8[4194304]{0:T(1024)(128)(4,1)S(1)}, s32[]{:S(2)}) async-start(s8[10485760]{0:T(1024)(128)(4,1)} %bitcast.5), calls=%async_computation.2 | async-start | bytes 8388608
  26.4 5.6 %slice-start.2 = ((s8[10485760]{0:T(1024)(128)(4,1)}), s8[4194304]{0:T(1024)(128)(4,1)S(1)}, s32[]{:S(2)}) async-start(s8[10485760]{0:T(1024)(128)(4,1)} %bitcast.5), calls=%async_computation.3 | async-start | bytes 8388608
  26.4 5.5 %collective-permute-start.11 = (bf16[64,4096]{1,0:T(8,128)(2,1)S(1)}, bf16[64,4096]{1,0:T(8,128)(2,1)S(1)}, u32[]{:S(2)}, u32[]{:S(2)}) collective-permute-start(bf16[64,4096]{1,0:T(8,128)(2,1)S(1)} %pad_maximum_fusion.1), channel_id=1, source_target_pairs={{0,1},{1,0},{2,3},{3,2},{4,5},{5,4},{6,7},{7,6},{8,9},{9,8},{10,11... | collective-permute-start | bytes 1572872 | tf_op jit(solution)/shard_map/ppermute | solution.py:20
  26.5 3.7 %collective-permute-start.1 = (bf16[64,2048]{1,0:T(8,128)(2,1)S(1)}, bf16[64,2048]{1,0:T(8,128)(2,1)S(1)}, u32[]{:S(2)}, u32[]{:S(2)}) collective-permute-start(bf16[64,2048]{1,0:T(8,128)(2,1)S(1)} %collective-permute-done.mine_ref), channel_id=1, source_target_pairs={{0,1},{1,0},{2,3},{3,2},{4,5},{5,4},{6,7},{7,6},{8,9},{9,8},{10,11... | collective-permute-start | bytes 786440 | tf_op jit(solution)/shard_map/ppermute | solution.py:20
  27.0 2.8 %copy-start.3 = (bf16[2048,1280]{1,0:T(8,128)(2,1)S(1)}, bf16[2048,1280]{1,0:T(8,128)(2,1)}, u32[]{:S(2)}) copy-start(bf16[2048,1280]{1,0:T(8,128)(2,1)} %from_ref.1) | copy-start | bytes 15728644
  30.1 9.4 %copy-start = (bf16[2048,1280]{1,0:T(8,128)(2,1)}, bf16[2048,1280]{1,0:T(8,128)(2,1)S(1)}, u32[]{:S(2)}) copy-start(bf16[2048,1280]{1,0:T(8,128)(2,1)S(1)} %load.1.w_ref) | copy-start | bytes 15728644
  30.1 8.1 %copy-start.4 = (bf16[128,4096]{1,0:T(8,128)(2,1)S(1)}, bf16[128,4096]{1,0:T(8,128)(2,1)}, u32[]{:S(2)}) copy-start(bf16[128,4096]{1,0:T(8,128)(2,1)} %refs_2_.1) | copy-start | bytes 3145732
  30.1 8.0 %copy-start.8 = (f32[4096]{0:T(1024)S(1)}, f32[4096]{0:T(1024)}, u32[]{:S(2)}) copy-start(f32[4096]{0:T(1024)} %param.12) | copy-start | bytes 49156
  31.1 32.7 %copy-start.12 = (s32[128]{0:T(128)S(1)}, s32[128]{0:T(128)}, u32[]{:S(2)}) copy-start(s32[128]{0:T(128)} %param.15) | copy-start | bytes 1540
  31.1 17.7 %collective-permute-start.2 = (f32[128,1280]{1,0:T(8,128)S(1)}, f32[128,1280]{1,0:T(8,128)S(1)}, u32[]{:S(2)}, u32[]{:S(2)}) collective-permute-start(f32[128,1280]{1,0:T(8,128)S(1)} %get-tuple-element.29), channel_id=1, source_target_pairs={{0,16},{16,0},{1,17},{17,1},{2,18},{18,2},{3,19},{19,3},{4,20},{20... | collective-permute-start | bytes 1966088 | tf_op jit(solution)/shard_map/ppermute | solution.py:20
  36.9 19.5 %collective-permute-start.12 = (bf16[136,1280]{1,0:T(8,128)(2,1)}, bf16[136,1280]{1,0:T(8,128)(2,1)S(1)}, u32[]{:S(2)}, u32[]{:S(2)}) collective-permute-start(bf16[136,1280]{1,0:T(8,128)(2,1)} %get-tuple-element.35), channel_id=1, source_target_pairs={{0,16},{16,0},{1,17},{17,1},{2,18},{18,2},{3,19},{19,3},{4,20},{20... | collective-permute-start | bytes 1044488 | tf_op jit(solution)/shard_map/ppermute | solution.py:20
  39.5 11.1 %copy-start.9 = (f32[128,1]{1,0:T(8,128)}, f32[128,1]{1,0:T(8,128)S(1)}, u32[]{:S(2)}) copy-start(f32[128,1]{1,0:T(8,128)S(1)} %get-tuple-element.38.inv_ref) | copy-start | bytes 1540
  49.7 0.9 copy-start.5
  50.6 13.3 %all-to-all-start = ((f32[32,4,128]{2,1,0:T(4,128)}), f32[32,4,128]{2,1,0:T(4,128)S(1)}, u32[]{:S(2)}, u32[]{:S(2)}) async-start(f32[32,4,128]{2,1,0:T(4,128)} %get-tuple-element.32), calls=%async_computation | async-start | bytes 131072 | tf_op jit(solution)/shard_map/all_to_all | solution.py:560
  63.8 1.1 %copy-start.6 = (f32[128,1280]{1,0:T(8,128)S(1)}, f32[128,1280]{1,0:T(8,128)}, u32[]{:S(2)}) copy-start(f32[128,1280]{1,0:T(8,128)} %copy-done.5) | copy-start | bytes 1966084
  65.7 10.2 %collective-permute-start.13 = (bf16[136,1280]{1,0:T(8,128)(2,1)S(1)}, bf16[136,1280]{1,0:T(8,128)(2,1)S(1)}, u32[]{:S(2)}, u32[]{:S(2)}) collective-permute-start(bf16[136,1280]{1,0:T(8,128)(2,1)S(1)} %grads.1.refs_0_.grads_ref), channel_id=1, source_target_pairs={{0,16},{16,0},{1,17},{17,1},{2,18},{18,2},{3,19},{19,3},{4,20},{20... | collective-permute-start | bytes 1044488 | tf_op jit(solution)/shard_map/ppermute | solution.py:20
  66.4 2.5 %copy-start.1 = (bf16[2048,1280]{1,0:T(8,128)(2,1)S(1)}, bf16[2048,1280]{1,0:T(8,128)(2,1)}, u32[]{:S(2)}) copy-start(bf16[2048,1280]{1,0:T(8,128)(2,1)} %copy-done) | copy-start | bytes 15728644
  69.8 8.0 %collective-permute-start.14 = (bf16[1032,128]{1,0:T(8,128)(2,1)S(1)}, bf16[1032,128]{1,0:T(8,128)(2,1)S(1)}, u32[]{:S(2)}, u32[]{:S(2)}) collective-permute-start(bf16[1032,128]{1,0:T(8,128)(2,1)S(1)} %pieces.5), channel_id=1, source_target_pairs={{0,1},{1,0},{2,3},{3,2},{4,5},{5,4},{6,7},{7,6},{8,9},{9,8},{10,11... | collective-permute-start | bytes 792584 | tf_op jit(solution)/shard_map/ppermute | solution.py:20
  76.8 9.9 %collective-permute-start.18 = (bf16[1032,128]{1,0:T(8,128)(2,1)S(1)}, bf16[1032,128]{1,0:T(8,128)(2,1)}, u32[]{:S(2)}, u32[]{:S(2)}) collective-permute-start(bf16[1032,128]{1,0:T(8,128)(2,1)S(1)} %pieces.7), channel_id=1, source_target_pairs={{0,1},{1,0},{2,3},{3,2},{4,5},{5,4},{6,7},{7,6},{8,9},{9,8},{10,11... | collective-permute-start | bytes 792584 | tf_op jit(solution)/shard_map/ppermute | solution.py:20
  78.5 0.6 copy-start.13
  79.1 0.6 copy-start.14
  79.7 9.1 %collective-permute-start.15 = (bf16[264,128]{1,0:T(8,128)(2,1)}, bf16[264,128]{1,0:T(8,128)(2,1)S(1)}, u32[]{:S(2)}, u32[]{:S(2)}) collective-permute-start(bf16[264,128]{1,0:T(8,128)(2,1)} %get-tuple-element.40), channel_id=1, source_target_pairs={{0,2},{1,3},{2,0},{3,1},{4,6},{5,7},{6,4},{7,5},{8,10},{9,11},{10,... | collective-permute-start | bytes 202760 | tf_op jit(solution)/shard_map/ppermute | solution.py:20
  80.3 11.1 %collective-permute-start.16 = (bf16[264,128]{1,0:T(8,128)(2,1)}, bf16[264,128]{1,0:T(8,128)(2,1)S(1)}, u32[]{:S(2)}, u32[]{:S(2)}) collective-permute-start(bf16[264,128]{1,0:T(8,128)(2,1)} %copy-done.14), channel_id=1, source_target_pairs={{0,4},{1,5},{2,6},{3,7},{4,0},{5,1},{6,2},{7,3},{8,12},{9,13},{10,... | collective-permute-start | bytes 202760 | tf_op jit(solution)/shard_map/ppermute | solution.py:20
  80.8 10.5 %collective-permute-start.17 = (bf16[264,128]{1,0:T(8,128)(2,1)}, bf16[264,128]{1,0:T(8,128)(2,1)S(1)}, u32[]{:S(2)}, u32[]{:S(2)}) collective-permute-start(bf16[264,128]{1,0:T(8,128)(2,1)} %copy-done.13), channel_id=1, source_target_pairs={{0,6},{1,7},{2,4},{3,5},{4,2},{5,3},{6,0},{7,1},{8,14},{9,15},{10,... | collective-permute-start | bytes 202760 | tf_op jit(solution)/shard_map/ppermute | solution.py:20
  83.3 2.5 %copy-start.2 = (bf16[2048,1280]{1,0:T(8,128)(2,1)S(1)}, bf16[2048,1280]{1,0:T(8,128)(2,1)}, u32[]{:S(2)}) copy-start(bf16[2048,1280]{1,0:T(8,128)(2,1)} %copy-done) | copy-start | bytes 15728644
  87.7 5.1 %collective-permute-start.19 = (bf16[264,128]{1,0:T(8,128)(2,1)S(1)}, bf16[264,128]{1,0:T(8,128)(2,1)S(1)}, u32[]{:S(2)}, u32[]{:S(2)}) collective-permute-start(bf16[264,128]{1,0:T(8,128)(2,1)S(1)} %get-tuple-element.44), channel_id=1, source_target_pairs={{0,2},{1,3},{2,0},{3,1},{4,6},{5,7},{6,4},{7,5},{8,10},{9,11},{10,... | collective-permute-start | bytes 202760 | tf_op jit(solution)/shard_map/ppermute | solution.py:20
  88.3 4.6 %collective-permute-start.20 = (bf16[264,128]{1,0:T(8,128)(2,1)S(1)}, bf16[264,128]{1,0:T(8,128)(2,1)S(1)}, u32[]{:S(2)}, u32[]{:S(2)}) collective-permute-start(bf16[264,128]{1,0:T(8,128)(2,1)S(1)} %get-tuple-element.45), channel_id=1, source_target_pairs={{0,4},{1,5},{2,6},{3,7},{4,0},{5,1},{6,2},{7,3},{8,12},{9,13},{10,... | collective-permute-start | bytes 202760 | tf_op jit(solution)/shard_map/ppermute | solution.py:20
  88.8 5.5 %collective-permute-start.21 = (bf16[264,128]{1,0:T(8,128)(2,1)S(1)}, bf16[264,128]{1,0:T(8,128)(2,1)S(1)}, u32[]{:S(2)}, u32[]{:S(2)}) collective-permute-start(bf16[264,128]{1,0:T(8,128)(2,1)S(1)} %get-tuple-element.46), channel_id=1, source_target_pairs={{0,6},{1,7},{2,4},{3,5},{4,2},{5,3},{6,0},{7,1},{8,14},{9,15},{10,... | collective-permute-start | bytes 202760 | tf_op jit(solution)/shard_map/ppermute | solution.py:20
  94.5 9.6 %collective-permute-start.22 = (bf16[264,128]{1,0:T(8,128)(2,1)S(1)}, bf16[264,128]{1,0:T(8,128)(2,1)S(1)}, u32[]{:S(2)}, u32[]{:S(2)}) collective-permute-start(bf16[264,128]{1,0:T(8,128)(2,1)S(1)} %get-tuple-element.47), channel_id=1, source_target_pairs={{0,0},{1,1},{2,2},{3,3},{4,4},{5,5},{6,6},{7,7},{8,16},{9,17},{10,... | collective-permute-start | bytes 202760 | tf_op jit(solution)/shard_map/ppermute | solution.py:579
  95.2 9.0 %collective-permute-start.23 = (bf16[264,128]{1,0:T(8,128)(2,1)S(1)}, bf16[264,128]{1,0:T(8,128)(2,1)S(1)}, u32[]{:S(2)}, u32[]{:S(2)}) collective-permute-start(bf16[264,128]{1,0:T(8,128)(2,1)S(1)} %get-tuple-element.48), channel_id=1, source_target_pairs={{0,16},{1,17},{2,18},{3,19},{4,20},{5,21},{6,22},{7,23},{8,0},{9,1... | collective-permute-start | bytes 202760 | tf_op jit(solution)/shard_map/ppermute | solution.py:579
  101.3 2.8 %copy-start.10 = (f32[128,1]{1,0:T(8,128)S(1)}, f32[128,1]{1,0:T(8,128)}, u32[]{:S(2)}) copy-start(f32[128,1]{1,0:T(8,128)} %copy-done.9) | copy-start | bytes 1540

commit v9 on v8

--- a/solution.py
+++ b/solution.py
@@ -291,7 +291,7 @@
 def grads_kernel(count, size, stats_ref, logits_ref, ids_ref, *refs):
     place = position()
     terms = refs[:count]
-    grads_ref = refs[count]
+    grads_ref, dots_ref = refs[count:]
     b, t = place[0], place[1]
     rows, cols = logits_ref.shape
     logits = logits_ref[...]
@@ -312,10 +312,9 @@
             total = jnp.sum(block[:, 3, :] * jnp.exp(block[:, 2, :] - peak), axis=0, keepdims=True)
             probs = jnp.exp(logits - column(peak)) / column(total)
     grads = (loss_scale * (probs - targets)).astype(grads_ref.dtype)
-    grads_ref[:rows] = grads
-    grads_ref[rows:] = jnp.zeros((EXTRA, cols), grads.dtype)
+    grads_ref[...] = grads
     dots = as_row(jnp.sum(grads.astype(jnp.float32) * logits, axis=1, keepdims=True))
-    grads_ref[rows:, :rows] = extra_rows([dots], grads.dtype)
+    dots_ref[...] = extra_rows([dots], grads.dtype)
 
 
 def make_grads(stats, logits, ids, terms, size):
@@ -323,40 +322,39 @@
     count = len(terms)
     return pl.pallas_call(
         functools.partial(grads_kernel, count, size),
-        out_shape=jax.ShapeDtypeStruct((rows + EXTRA, cols), jnp.bfloat16),
+        out_shape=(jax.ShapeDtypeStruct((rows, cols), jnp.bfloat16), jax.ShapeDtypeStruct((EXTRA, rows), jnp.bfloat16)),
         in_specs=[VMEM] * (count + 3),
-        out_specs=VMEM,
+        out_specs=(VMEM, VMEM),
         compiler_params=params(12),
         cost_estimate=cost(16 * rows * cols, 10 * rows * cols, rows * cols),
         name="grads",
     )(stats, logits, ids, *terms)
 
 
-def pieces_kernel(parity, width, grads_ref, w_ref, out_ref, turned_ref):
+def pieces_kernel(parity, width, grads_ref, dots_ref, w_ref, out_ref, turned_ref):
     place = position()
-    rows = out_ref.shape[1]
-    turned_ref[...] = jnp.transpose(grads_ref[:rows])
+    turned_ref[...] = jnp.transpose(grads_ref[...])
     count = (out_ref.shape[0] - EXTRA) // width
     for k in range(count):
         start = pl.multiple_of((place[2] ^ (2 * k + parity)) * width, width)
         acc = jnp.dot(w_ref[pl.ds(start, width)], turned_ref[...], preferred_element_type=jnp.float32)
         out_ref[k * width : (k + 1) * width] = acc.astype(out_ref.dtype)
-    out_ref[count * width :] = grads_ref[rows:, :rows]
-
-
-def normed_grad_pieces(grads, head, blocks, parity):
-    rows, cols = grads.shape[0] - EXTRA, grads.shape[1]
+    out_ref[count * width :] = dots_ref[...]
+
+
+def normed_grad_pieces(grads, dots, head, blocks, parity):
+    rows, cols = grads.shape
     width = head.shape[0] // blocks
     return pl.pallas_call(
         functools.partial(pieces_kernel, parity, width),
         out_shape=jax.ShapeDtypeStruct((blocks // 2 * width + EXTRA, rows), jnp.bfloat16),
-        in_specs=[VMEM] * 2,
+        in_specs=[VMEM] * 3,
         out_specs=VMEM,
         scratch_shapes=[pltpu.VMEM((cols, rows), jnp.bfloat16)],
         compiler_params=params(16),
         cost_estimate=cost(rows * head.size, head.size),
         name="pieces",
-    )(grads, head)
+    )(grads, dots, head)
 
 
 def fold_kernel(mine_ref, got_ref, *out):
@@ -364,10 +362,11 @@
     width = out[0].shape[0] - EXTRA
     full = len(out) * width
     dots = extra_values(mine_ref[full:], 1)[0] + extra_values(got_ref[full:], 1)[0]
+    extra = extra_rows([dots], out[0].dtype)
     for k, ref in enumerate(out):
         at = slice(k * width, (k + 1) * width)
         ref[:width] = (mine_ref[at].astype(f32) + got_ref[at].astype(f32)).astype(ref.dtype)
-        ref[width:] = extra_rows([dots], ref.dtype)
+        ref[width:] = extra
 
 
 def fold(mine, got, width):
@@ -558,15 +557,16 @@
 
     logits, stats = student_stats(partials, teacher_stats, size)
     stats = lax.all_to_all(stats, ("branch", "tok"), 0, 0, tiled=True)
-    logit_grads = make_grads(stats, logits, token_ids[None], terms, size)
+    logit_grads, dots = make_grads(stats, logits, token_ids[None], terms, size)
     all_grads = [logit_grads] + [swap(logit_grads, "branch", r) for r in range(1, branches)]
+    all_dots = [dots] + [swap(dots, "branch", r) for r in range(1, branches)]
 
     slice_width = width // size
     parts = []
     for r in range(branches):
-        send = normed_grad_pieces(all_grads[r], loaded, blocks, 1)
+        send = normed_grad_pieces(all_grads[r], all_dots[r], loaded, blocks, 1)
         send = swap(send, "tok", 1)
-        keep = normed_grad_pieces(all_grads[r], loaded, blocks, 0)
+        keep = normed_grad_pieces(all_grads[r], all_dots[r], loaded, blocks, 0)
         folded = fold(keep, send, slice_width)
         parts.append([folded[0]] + [swap(folded[k], "tok", 2 * k) for k in range(1, blocks // 2)])
     owned = split(parts, turned)

time: 105 us -> 105 us (level)
  waiting for transfers between devices: 34.2 us -> 31.6 us
  local copies, waits for them, and re-layouts: 11.2 us -> 12.9 us
  starting transfers between devices: 34.2 us -> 35.6 us
    ppermute x22 -> x23, waiting for transfers between devices: 26.8 us -> 25 us  [swap(): return lax.ppermute(value, axis, [(i, i ^ flip) for i in range(size)])]
    unnamed x36, local copies, waits for them, and re-layouts: 11.1 us -> 12.8 us
    ppermute x22 -> x23, starting transfers between devices: 24.3 us -> 25.7 us  [swap(): return lax.ppermute(value, axis, [(i, i ^ flip) for i in range(size)])]
  transfers between devices with their start and end apart: 25 -> 26, of which waited for: 10 -> 10; matrix products, arithmetic and copies ran while one was open for 1% -> 1% of each run, Pallas kernels for 18% -> 18%
where the time goes in v9:
time: 105 us
  starting transfers between devices  35.6 us (34%)
  waiting for transfers between devices  31.6 us (30%)
  Pallas kernels  22.6 us (22%)
  local copies, waits for them, and re-layouts  12.9 us (12%)
    ppermute x23, starting transfers between devices, swap(): return lax.ppermute(value, axis, [(i, i ^ flip) for i in range(size)])  25.7 us
    ppermute x23, waiting for transfers between devices, swap(): return lax.ppermute(value, axis, [(i, i ^ flip) for i in range(size)])  25 us
    unnamed x36, local copies, waits for them, and re-layouts  12.8 us
    all_to_all x1, waiting for transfers between devices, per_device(): stats = lax.all_to_all(stats, ('branch', 'tok'), 0, 0, tiled=True)  6.67 us
    all_to_all x1, starting transfers between devices, per_device(): stats = lax.all_to_all(stats, ('branch', 'tok'), 0, 0, tiled=True)  5.84 us
    pallas_call x2, Pallas kernels, head_grad(): pl.pallas_call(functools.partial(head_grad_kernel, count, half, tile), ou...  5.51 us
    pallas_call x1, Pallas kernels, teacher_softmax(): pl.pallas_call(functools.partial(teacher_kernel, keys, half), out_shape=(...  4.89 us
    ppermute x2, starting transfers between devices, per_device(): arrived.append(lax.ppermute(owned[kh], ('branch', 'tok'), perm))  4.06 us
  transfers between devices with their start and end apart: 26, of which 10 were waited for; matrix products, arithmetic and copies ran while one was open for 1% of the time, Pallas kernels for 18%

profile of v9, /device:TPU:0, one launch (start us, length us, event | category | flops | bytes accessed | tf_op | source)
XLA Modules:
  0.0 104.7 jit_solution(17665781930061107944)
XLA Ops:
  0.7 2.3 %first.1 = (bf16[16,4096]{1,0:T(8,128)(2,1)}, bf16[64,2048]{1,0:T(8,128)(2,1)}) custom-call(bf16[1,16,4096]{2,1,0:T(8,128)(2,1)} %refs_0_.1, f32[1,4096]{1,0:T(1,128)} %refs_1_.1, bf16[128,4096]{1,0:T(8,128)(2,1)} %refs_2_.1, f32[1,4096]{1,0:T(1,128)} %bitcast.7), custom_call_target="tpu_custom_call" | custom-call | flops 4194304 | bytes 2097152 | tf_op jit(solution)/shard_map/first/pallas_call | solution.py:76
  3.0 4.1 %collective-permute-start.6 = (bf16[16,4096]{1,0:T(8,128)(2,1)}, bf16[16,4096]{1,0:T(8,128)(2,1)S(1)}, u32[]{:S(2)}, u32[]{:S(2)}) collective-permute-start(bf16[16,4096]{1,0:T(8,128)(2,1)} %get-tuple-element.32.refs_0_), channel_id=1, source_target_pairs={{0,8},{1,9},{2,10},{3,11},{4,12},{5,13},{6,14},{7,15},{8,0},{9,1},... | collective-permute-start | bytes 393224 | tf_op jit(solution)/shard_map/ppermute | solution.py:20
  7.1 2.5 %collective-permute-start.5 = (bf16[16,4096]{1,0:T(8,128)(2,1)}, bf16[16,4096]{1,0:T(8,128)(2,1)S(1)}, u32[]{:S(2)}, u32[]{:S(2)}) collective-permute-start(bf16[16,4096]{1,0:T(8,128)(2,1)} %get-tuple-element.32.refs_0_), channel_id=1, source_target_pairs={{0,6},{1,7},{2,4},{3,5},{4,2},{5,3},{6,0},{7,1},{8,14},{9,15},{10,... | collective-permute-start | bytes 393224 | tf_op jit(solution)/shard_map/ppermute | solution.py:20
  9.7 4.1 %collective-permute-done.6.refs_4_ = bf16[16,4096]{1,0:T(8,128)(2,1)S(1)} collective-permute-done((bf16[16,4096]{1,0:T(8,128)(2,1)}, bf16[16,4096]{1,0:T(8,128)(2,1)S(1)}, u32[]{:S(2)}, u32[]{:S(2)}) %collective-permute-start.6) | collective-permute-done | bytes 131104 | tf_op jit(solution)/shard_map/ppermute | solution.py:20
  13.8 0.8 collective-permute-start.8
  14.5 1.3 %collective-permute-start.4 = (bf16[16,4096]{1,0:T(8,128)(2,1)}, bf16[16,4096]{1,0:T(8,128)(2,1)S(1)}, u32[]{:S(2)}, u32[]{:S(2)}) collective-permute-start(bf16[16,4096]{1,0:T(8,128)(2,1)} %get-tuple-element.32.refs_0_), channel_id=1, source_target_pairs={{0,4},{1,5},{2,6},{3,7},{4,0},{5,1},{6,2},{7,3},{8,12},{9,13},{10,... | collective-permute-start | bytes 393224 | tf_op jit(solution)/shard_map/ppermute | solution.py:20
  15.8 1.6 %collective-permute-start.3 = (bf16[16,4096]{1,0:T(8,128)(2,1)}, bf16[16,4096]{1,0:T(8,128)(2,1)S(1)}, u32[]{:S(2)}, u32[]{:S(2)}) collective-permute-start(bf16[16,4096]{1,0:T(8,128)(2,1)} %get-tuple-element.32.refs_0_), channel_id=1, source_target_pairs={{0,2},{1,3},{2,0},{3,1},{4,6},{5,7},{6,4},{7,5},{8,10},{9,11},{10,... | collective-permute-start | bytes 393224 | tf_op jit(solution)/shard_map/ppermute | solution.py:20
  17.4 1.5 %collective-permute-start = (bf16[64,2048]{1,0:T(8,128)(2,1)}, bf16[64,2048]{1,0:T(8,128)(2,1)S(1)}, u32[]{:S(2)}, u32[]{:S(2)}) collective-permute-start(bf16[64,2048]{1,0:T(8,128)(2,1)} %get-tuple-element.30), channel_id=1, source_target_pairs={{0,16},{16,0},{1,17},{17,1},{2,18},{18,2},{3,19},{19,3},{4,20},{20... | collective-permute-start | bytes 786440 | tf_op jit(solution)/shard_map/ppermute | solution.py:20
  19.9 1.5 %collective-permute-start.9 = (bf16[16,4096]{1,0:T(8,128)(2,1)S(1)}, bf16[16,4096]{1,0:T(8,128)(2,1)S(1)}, u32[]{:S(2)}, u32[]{:S(2)}) collective-permute-start(bf16[16,4096]{1,0:T(8,128)(2,1)S(1)} %collective-permute-done.8.refs_6_), channel_id=1, source_target_pairs={{0,2},{1,3},{2,0},{3,1},{4,6},{5,7},{6,4},{7,5},{8,10},{9,11},{10,... | collective-permute-start | bytes 393224 | tf_op jit(solution)/shard_map/ppermute | solution.py:20
  21.4 1.0 collective-permute-done.3.refs_1_
  22.4 0.9 pad_maximum_fusion
  23.4 1.5 %collective-permute-done.7.refs_5_ = bf16[16,4096]{1,0:T(8,128)(2,1)S(1)} collective-permute-done((bf16[16,4096]{1,0:T(8,128)(2,1)S(1)}, bf16[16,4096]{1,0:T(8,128)(2,1)S(1)}, u32[]{:S(2)}, u32[]{:S(2)}) %collective-permute-start.7) | collective-permute-done | bytes 131104 | tf_op jit(solution)/shard_map/ppermute | solution.py:20
  24.9 1.4 %collective-permute-done.9.refs_7_ = bf16[16,4096]{1,0:T(8,128)(2,1)S(1)} collective-permute-done((bf16[16,4096]{1,0:T(8,128)(2,1)S(1)}, bf16[16,4096]{1,0:T(8,128)(2,1)S(1)}, u32[]{:S(2)}, u32[]{:S(2)}) %collective-permute-start.9) | collective-permute-done | bytes 131104 | tf_op jit(solution)/shard_map/ppermute | solution.py:20
  27.0 2.8 %copy-done.3 = bf16[2048,1280]{1,0:T(8,128)(2,1)S(1)} copy-done((bf16[2048,1280]{1,0:T(8,128)(2,1)S(1)}, bf16[2048,1280]{1,0:T(8,128)(2,1)}, u32[]{:S(2)}) %copy-start.3) | copy-done | bytes 5242904
  30.1 0.9 otherdot.1
  31.1 0.8 collective-permute-start.2
  32.0 4.9 %teacher.1 = (f32[2,256]{1,0:T(2,128)S(1)}, bf16[136,1280]{1,0:T(8,128)(2,1)S(1)}, bf16[136,1280]{1,0:T(8,128)(2,1)}) custom-call(bf16[16,4096]{1,0:T(8,128)(2,1)S(1)} %copy-done.7, bf16[16,4096]{1,0:T(8,128)(2,1)S(1)} %collective-permute-done.3.refs_1_, bf16[16,4096]{1,0:T(8,128)(2,1)S(1)} %collective-permute-done.4.refs_2_, ...), custom_call_target="tpu_custom_call" | custom-call | flops 2684354560 | bytes 10485760 | tf_op jit(solution)/shard_map/teacher/pallas_call | solution.py:240
  36.9 1.3 %collective-permute-start.12 = (bf16[136,1280]{1,0:T(8,128)(2,1)}, bf16[136,1280]{1,0:T(8,128)(2,1)S(1)}, u32[]{:S(2)}, u32[]{:S(2)}) collective-permute-start(bf16[136,1280]{1,0:T(8,128)(2,1)} %get-tuple-element.37), channel_id=1, source_target_pairs={{0,16},{16,0},{1,17},{17,1},{2,18},{18,2},{3,19},{19,3},{4,20},{20... | collective-permute-start | bytes 1044488 | tf_op jit(solution)/shard_map/ppermute | solution.py:20
  38.2 1.3 %owndot.1 = (f32[128,1280]{1,0:T(8,128)S(1)}, bf16[2048,128]{1,0:T(8,128)(2,1)S(1)}, f32[128,1]{1,0:T(8,128)S(1)}) custom-call(bf16[128,4096]{1,0:T(8,128)(2,1)S(1)} %copy-done.4, f32[1,4096]{1,0:T(1,128)S(1)} %bitcast.8, bf16[2048,1280]{1,0:T(8,128)(2,1)S(1)} %load.1.w_ref), custom_call_target="tpu_custom_call" | custom-call | flops 671088640 | bytes 5242880 | tf_op jit(solution)/shard_map/owndot/pallas_call | solution.py:129
  39.5 9.3 %collective-permute-done.2.refs_1_ = f32[128,1280]{1,0:T(8,128)S(1)} collective-permute-done((f32[128,1280]{1,0:T(8,128)S(1)}, f32[128,1280]{1,0:T(8,128)S(1)}, u32[]{:S(2)}, u32[]{:S(2)}) %collective-permute-start.2) | collective-permute-done | bytes 655392 | tf_op jit(solution)/shard_map/ppermute | solution.py:20
  48.8 0.9 stats.1
  49.7 0.9 copy-done.5
  50.6 5.8 %all-to-all-start = ((f32[32,4,128]{2,1,0:T(4,128)}), f32[32,4,128]{2,1,0:T(4,128)S(1)}, u32[]{:S(2)}, u32[]{:S(2)}) async-start(f32[32,4,128]{2,1,0:T(4,128)} %get-tuple-element.34), calls=%async_computation | async-start | bytes 131072 | tf_op jit(solution)/shard_map/all_to_all | solution.py:559
  56.4 0.7 copy-done.8
  57.2 6.7 %all-to-all-done.stats_ref = f32[32,4,128]{2,1,0:T(4,128)S(1)} async-done(((f32[32,4,128]{2,1,0:T(4,128)}), f32[32,4,128]{2,1,0:T(4,128)S(1)}, u32[]{:S(2)}, u32[]{:S(2)}) %all-to-all-start) | async-done | bytes 65568 | tf_op jit(solution)/shard_map/all_to_all | solution.py:559
  63.8 1.1 %copy-done.6 = f32[128,1280]{1,0:T(8,128)S(1)} copy-done((f32[128,1280]{1,0:T(8,128)S(1)}, f32[128,1280]{1,0:T(8,128)}, u32[]{:S(2)}) %copy-start.6) | copy-done | bytes 655384
  64.9 1.0 copy-done.9
  65.9 0.7 grads.1
  66.6 0.7 collective-permute-start.13
  67.3 2.5 %copy-done.1 = bf16[2048,1280]{1,0:T(8,128)(2,1)S(1)} copy-done((bf16[2048,1280]{1,0:T(8,128)(2,1)S(1)}, bf16[2048,1280]{1,0:T(8,128)(2,1)}, u32[]{:S(2)}) %copy-start.1) | copy-done | bytes 5242904
  69.8 0.9 pieces.5
  70.8 1.4 %collective-permute-start.18 = (bf16[8,128]{1,0:T(8,128)(2,1)S(1)}, bf16[8,128]{1,0:T(8,128)(2,1)S(1)}, u32[]{:S(2)}, u32[]{:S(2)}) collective-permute-start(bf16[8,128]{1,0:T(8,128)(2,1)S(1)} %get-tuple-element.42.dots_ref), channel_id=1, source_target_pairs={{0,16},{16,0},{1,17},{17,1},{2,18},{18,2},{3,19},{19,3},{4,20},{20... | collective-permute-start | bytes 6152 | tf_op jit(solution)/shard_map/ppermute | solution.py:20
  72.3 4.2 %collective-permute-done.18.dots_ref = bf16[8,128]{1,0:T(8,128)(2,1)S(1)} collective-permute-done((bf16[8,128]{1,0:T(8,128)(2,1)S(1)}, bf16[8,128]{1,0:T(8,128)(2,1)S(1)}, u32[]{:S(2)}, u32[]{:S(2)}) %collective-permute-start.18) | collective-permute-done | bytes 2080 | tf_op jit(solution)/shard_map/ppermute | solution.py:20
  76.4 0.9 pieces.7
  77.5 0.9 pieces.4.mine_ref
  78.4 0.7 fold.2
  79.1 0.6 copy-done.13
  81.4 2.5 %collective-permute-start.17 = (bf16[264,128]{1,0:T(8,128)(2,1)}, bf16[264,128]{1,0:T(8,128)(2,1)S(1)}, u32[]{:S(2)}, u32[]{:S(2)}) collective-permute-start(bf16[264,128]{1,0:T(8,128)(2,1)} %copy-done.13), channel_id=1, source_target_pairs={{0,6},{1,7},{2,4},{3,5},{4,2},{5,3},{6,0},{7,1},{8,14},{9,15},{10,... | collective-permute-start | bytes 202760 | tf_op jit(solution)/shard_map/ppermute | solution.py:20
  83.9 2.5 %copy-done.2 = bf16[2048,1280]{1,0:T(8,128)(2,1)S(1)} copy-done((bf16[2048,1280]{1,0:T(8,128)(2,1)S(1)}, bf16[2048,1280]{1,0:T(8,128)(2,1)}, u32[]{:S(2)}) %copy-start.2) | copy-done | bytes 5242904
  86.4 0.9 pieces.6.mine_ref
  88.4 2.5 %collective-permute-start.22 = (bf16[264,128]{1,0:T(8,128)(2,1)S(1)}, bf16[264,128]{1,0:T(8,128)(2,1)S(1)}, u32[]{:S(2)}, u32[]{:S(2)}) collective-permute-start(bf16[264,128]{1,0:T(8,128)(2,1)S(1)} %get-tuple-element.50), channel_id=1, source_target_pairs={{0,6},{1,7},{2,4},{3,5},{4,2},{5,3},{6,0},{7,1},{8,14},{9,15},{10,... | collective-permute-start | bytes 202760 | tf_op jit(solution)/shard_map/ppermute | solution.py:20
  91.0 1.5 %collective-permute-done.20.refs_5_ = bf16[264,128]{1,0:T(8,128)(2,1)S(1)} collective-permute-done((bf16[264,128]{1,0:T(8,128)(2,1)S(1)}, bf16[264,128]{1,0:T(8,128)(2,1)S(1)}, u32[]{:S(2)}, u32[]{:S(2)}) %collective-permute-start.20) | collective-permute-done | bytes 67616 | tf_op jit(solution)/shard_map/ppermute | solution.py:20
  92.5 1.5 %collective-permute-done.22.refs_7_ = bf16[264,128]{1,0:T(8,128)(2,1)S(1)} collective-permute-done((bf16[264,128]{1,0:T(8,128)(2,1)S(1)}, bf16[264,128]{1,0:T(8,128)(2,1)S(1)}, u32[]{:S(2)}, u32[]{:S(2)}) %collective-permute-start.22) | collective-permute-done | bytes 67616 | tf_op jit(solution)/shard_map/ppermute | solution.py:20
  94.1 0.7 collective-permute-start.23
  94.8 3.4 %collective-permute-start.24 = (bf16[264,128]{1,0:T(8,128)(2,1)S(1)}, bf16[264,128]{1,0:T(8,128)(2,1)S(1)}, u32[]{:S(2)}, u32[]{:S(2)}) collective-permute-start(bf16[264,128]{1,0:T(8,128)(2,1)S(1)} %get-tuple-element.52), channel_id=1, source_target_pairs={{0,16},{1,17},{2,18},{3,19},{4,20},{5,21},{6,22},{7,23},{8,0},{9,1... | collective-permute-start | bytes 202760 | tf_op jit(solution)/shard_map/ppermute | solution.py:579
  98.2 2.8 %headgrad.2.refs_4_ = f32[2048,1280]{1,0:T(8,128)} custom-call(bf16[128,1280]{1,0:T(8,128)(2,1)S(1)} %get-tuple-element.38.refs_0_.grads_ref, bf16[128,1280]{1,0:T(8,128)(2,1)S(1)} %collective-permute-done.13.refs_1_.grads_ref, bf16[2048,128]{1,0:T(8,128)(2,1)S(1)} %get-tuple-element.39.refs_2_.refs_8_, bf16[2048,128]{1,0:T(8,128)(2,1)S(1)} %get-tuple-element.40.refs_3_.refs_9_), custom_call_target="tpu_custom_call" | custom-call | flops 671088640 | bytes 5242880 | tf_op jit(solution)/shard_map/headgrad/pallas_call | solution.py:458
  101.0 2.8 %headgrad.3 = f32[2048,1280]{1,0:T(8,128)} custom-call(bf16[128,1280]{1,0:T(8,128)(2,1)S(1)} %get-tuple-element.38.refs_0_.grads_ref, bf16[128,1280]{1,0:T(8,128)(2,1)S(1)} %collective-permute-done.13.refs_1_.grads_ref, bf16[2048,128]{1,0:T(8,128)(2,1)S(1)} %get-tuple-element.39.refs_2_.refs_8_, ...), custom_call_target="tpu_custom_call", output_to_operand_aliasing={{}: (4, {})} | custom-call | flops 671088640 | bytes 5242880 | tf_op jit(solution)/shard_map/headgrad/pallas_call | solution.py:458
  103.8 0.9 last.1
  (62 shorter events, 5.4 us)
Async XLA Ops:
  0.6 31.3 %copy-start.11 = (s32[256,1]{0,1:T(1,128)S(1)}, s32[256,1]{0,1:T(1,128)}, u32[]{:S(2)}) copy-start(s32[256,1]{0,1:T(1,128)} %param.14) | copy-start | bytes 3076
  0.6 31.2 %slice-start = ((s8[10485760]{0:T(1024)(128)(4,1)}), s8[2097152]{0:T(1024)(128)(4,1)S(1)}, s32[]{:S(2)}) async-start(s8[10485760]{0:T(1024)(128)(4,1)} %bitcast.5), calls=%async_computation.1 | async-start | bytes 4194304
  3.0 28.9 %copy-start.7 = (bf16[16,4096]{1,0:T(8,128)(2,1)S(1)}, bf16[16,4096]{1,0:T(8,128)(2,1)}, u32[]{:S(2)}) copy-start(bf16[16,4096]{1,0:T(8,128)(2,1)} %get-tuple-element.32.refs_0_) | copy-start | bytes 393220
  3.0 10.7 %collective-permute-start.6 = (bf16[16,4096]{1,0:T(8,128)(2,1)}, bf16[16,4096]{1,0:T(8,128)(2,1)S(1)}, u32[]{:S(2)}, u32[]{:S(2)}) collective-permute-start(bf16[16,4096]{1,0:T(8,128)(2,1)} %get-tuple-element.32.refs_0_), channel_id=1, source_target_pairs={{0,8},{1,9},{2,10},{3,11},{4,12},{5,13},{6,14},{7,15},{8,0},{9,1},... | collective-permute-start | bytes 393224 | tf_op jit(solution)/shard_map/ppermute | solution.py:20
  7.1 11.7 %collective-permute-start.5 = (bf16[16,4096]{1,0:T(8,128)(2,1)}, bf16[16,4096]{1,0:T(8,128)(2,1)S(1)}, u32[]{:S(2)}, u32[]{:S(2)}) collective-permute-start(bf16[16,4096]{1,0:T(8,128)(2,1)} %get-tuple-element.32.refs_0_), channel_id=1, source_target_pairs={{0,6},{1,7},{2,4},{3,5},{4,2},{5,3},{6,0},{7,1},{8,14},{9,15},{10,... | collective-permute-start | bytes 393224 | tf_op jit(solution)/shard_map/ppermute | solution.py:20
  13.8 6.1 %collective-permute-start.8 = (bf16[16,4096]{1,0:T(8,128)(2,1)S(1)}, bf16[16,4096]{1,0:T(8,128)(2,1)S(1)}, u32[]{:S(2)}, u32[]{:S(2)}) collective-permute-start(bf16[16,4096]{1,0:T(8,128)(2,1)S(1)} %collective-permute-done.6.refs_4_), channel_id=1, source_target_pairs={{0,4},{1,5},{2,6},{3,7},{4,0},{5,1},{6,2},{7,3},{8,12},{9,13},{10,... | collective-permute-start | bytes 393224 | tf_op jit(solution)/shard_map/ppermute | solution.py:20
  14.5 6.8 %collective-permute-start.4 = (bf16[16,4096]{1,0:T(8,128)(2,1)}, bf16[16,4096]{1,0:T(8,128)(2,1)S(1)}, u32[]{:S(2)}, u32[]{:S(2)}) collective-permute-start(bf16[16,4096]{1,0:T(8,128)(2,1)} %get-tuple-element.32.refs_0_), channel_id=1, source_target_pairs={{0,4},{1,5},{2,6},{3,7},{4,0},{5,1},{6,2},{7,3},{8,12},{9,13},{10,... | collective-permute-start | bytes 393224 | tf_op jit(solution)/shard_map/ppermute | solution.py:20
  15.8 6.6 %collective-permute-start.3 = (bf16[16,4096]{1,0:T(8,128)(2,1)}, bf16[16,4096]{1,0:T(8,128)(2,1)S(1)}, u32[]{:S(2)}, u32[]{:S(2)}) collective-permute-start(bf16[16,4096]{1,0:T(8,128)(2,1)} %get-tuple-element.32.refs_0_), channel_id=1, source_target_pairs={{0,2},{1,3},{2,0},{3,1},{4,6},{5,7},{6,4},{7,5},{8,10},{9,11},{10,... | collective-permute-start | bytes 393224 | tf_op jit(solution)/shard_map/ppermute | solution.py:20
  17.4 9.1 %collective-permute-start = (bf16[64,2048]{1,0:T(8,128)(2,1)}, bf16[64,2048]{1,0:T(8,128)(2,1)S(1)}, u32[]{:S(2)}, u32[]{:S(2)}) collective-permute-start(bf16[64,2048]{1,0:T(8,128)(2,1)} %get-tuple-element.30), channel_id=1, source_target_pairs={{0,16},{16,0},{1,17},{17,1},{2,18},{18,2},{3,19},{19,3},{4,20},{20... | collective-permute-start | bytes 786440 | tf_op jit(solution)/shard_map/ppermute | solution.py:20
  18.9 6.1 %collective-permute-start.7 = (bf16[16,4096]{1,0:T(8,128)(2,1)S(1)}, bf16[16,4096]{1,0:T(8,128)(2,1)S(1)}, u32[]{:S(2)}, u32[]{:S(2)}) collective-permute-start(bf16[16,4096]{1,0:T(8,128)(2,1)S(1)} %collective-permute-done.6.refs_4_), channel_id=1, source_target_pairs={{0,2},{1,3},{2,0},{3,1},{4,6},{5,7},{6,4},{7,5},{8,10},{9,11},{10,... | collective-permute-start | bytes 393224 | tf_op jit(solution)/shard_map/ppermute | solution.py:20
  19.9 6.4 %collective-permute-start.9 = (bf16[16,4096]{1,0:T(8,128)(2,1)S(1)}, bf16[16,4096]{1,0:T(8,128)(2,1)S(1)}, u32[]{:S(2)}, u32[]{:S(2)}) collective-permute-start(bf16[16,4096]{1,0:T(8,128)(2,1)S(1)} %collective-permute-done.8.refs_6_), channel_id=1, source_target_pairs={{0,2},{1,3},{2,0},{3,1},{4,6},{5,7},{6,4},{7,5},{8,10},{9,11},{10,... | collective-permute-start | bytes 393224 | tf_op jit(solution)/shard_map/ppermute | solution.py:20
  23.3 8.6 %collective-permute-start.10 = (bf16[64,4096]{1,0:T(8,128)(2,1)S(1)}, bf16[64,4096]{1,0:T(8,128)(2,1)S(1)}, u32[]{:S(2)}, u32[]{:S(2)}) collective-permute-start(bf16[64,4096]{1,0:T(8,128)(2,1)S(1)} %pad_maximum_fusion), channel_id=1, source_target_pairs={{0,1},{1,0},{2,3},{3,2},{4,5},{5,4},{6,7},{7,6},{8,9},{9,8},{10,11... | collective-permute-start | bytes 1572872 | tf_op jit(solution)/shard_map/ppermute | solution.py:20
  26.4 5.6 %slice-start.1 = ((s8[10485760]{0:T(1024)(128)(4,1)}), s8[4194304]{0:T(1024)(128)(4,1)S(1)}, s32[]{:S(2)}) async-start(s8[10485760]{0:T(1024)(128)(4,1)} %bitcast.5), calls=%async_computation.2 | async-start | bytes 8388608
  26.4 5.6 %slice-start.2 = ((s8[10485760]{0:T(1024)(128)(4,1)}), s8[4194304]{0:T(1024)(128)(4,1)S(1)}, s32[]{:S(2)}) async-start(s8[10485760]{0:T(1024)(128)(4,1)} %bitcast.5), calls=%async_computation.3 | async-start | bytes 8388608
  26.4 5.5 %collective-permute-start.11 = (bf16[64,4096]{1,0:T(8,128)(2,1)S(1)}, bf16[64,4096]{1,0:T(8,128)(2,1)S(1)}, u32[]{:S(2)}, u32[]{:S(2)}) collective-permute-start(bf16[64,4096]{1,0:T(8,128)(2,1)S(1)} %pad_maximum_fusion.1), channel_id=1, source_target_pairs={{0,1},{1,0},{2,3},{3,2},{4,5},{5,4},{6,7},{7,6},{8,9},{9,8},{10,11... | collective-permute-start | bytes 1572872 | tf_op jit(solution)/shard_map/ppermute | solution.py:20
  26.5 3.7 %collective-permute-start.1 = (bf16[64,2048]{1,0:T(8,128)(2,1)S(1)}, bf16[64,2048]{1,0:T(8,128)(2,1)S(1)}, u32[]{:S(2)}, u32[]{:S(2)}) collective-permute-start(bf16[64,2048]{1,0:T(8,128)(2,1)S(1)} %collective-permute-done.mine_ref), channel_id=1, source_target_pairs={{0,1},{1,0},{2,3},{3,2},{4,5},{5,4},{6,7},{7,6},{8,9},{9,8},{10,11... | collective-permute-start | bytes 786440 | tf_op jit(solution)/shard_map/ppermute | solution.py:20
  27.0 2.8 %copy-start.3 = (bf16[2048,1280]{1,0:T(8,128)(2,1)S(1)}, bf16[2048,1280]{1,0:T(8,128)(2,1)}, u32[]{:S(2)}) copy-start(bf16[2048,1280]{1,0:T(8,128)(2,1)} %from_ref.1) | copy-start | bytes 15728644
  30.1 9.4 %copy-start = (bf16[2048,1280]{1,0:T(8,128)(2,1)}, bf16[2048,1280]{1,0:T(8,128)(2,1)S(1)}, u32[]{:S(2)}) copy-start(bf16[2048,1280]{1,0:T(8,128)(2,1)S(1)} %load.1.w_ref) | copy-start | bytes 15728644
  30.1 8.1 %copy-start.4 = (bf16[128,4096]{1,0:T(8,128)(2,1)S(1)}, bf16[128,4096]{1,0:T(8,128)(2,1)}, u32[]{:S(2)}) copy-start(bf16[128,4096]{1,0:T(8,128)(2,1)} %refs_2_.1) | copy-start | bytes 3145732
  30.1 8.0 %copy-start.10 = (f32[4096]{0:T(1024)S(1)}, f32[4096]{0:T(1024)}, u32[]{:S(2)}) copy-start(f32[4096]{0:T(1024)} %param.12) | copy-start | bytes 49156
  31.1 32.7 %copy-start.12 = (s32[128]{0:T(128)S(1)}, s32[128]{0:T(128)}, u32[]{:S(2)}) copy-start(s32[128]{0:T(128)} %param.15) | copy-start | bytes 1540
  31.1 17.7 %collective-permute-start.2 = (f32[128,1280]{1,0:T(8,128)S(1)}, f32[128,1280]{1,0:T(8,128)S(1)}, u32[]{:S(2)}, u32[]{:S(2)}) collective-permute-start(f32[128,1280]{1,0:T(8,128)S(1)} %get-tuple-element.31), channel_id=1, source_target_pairs={{0,16},{16,0},{1,17},{17,1},{2,18},{18,2},{3,19},{19,3},{4,20},{20... | collective-permute-start | bytes 1966088 | tf_op jit(solution)/shard_map/ppermute | solution.py:20
  36.9 19.5 %collective-permute-start.12 = (bf16[136,1280]{1,0:T(8,128)(2,1)}, bf16[136,1280]{1,0:T(8,128)(2,1)S(1)}, u32[]{:S(2)}, u32[]{:S(2)}) collective-permute-start(bf16[136,1280]{1,0:T(8,128)(2,1)} %get-tuple-element.37), channel_id=1, source_target_pairs={{0,16},{16,0},{1,17},{17,1},{2,18},{18,2},{3,19},{19,3},{4,20},{20... | collective-permute-start | bytes 1044488 | tf_op jit(solution)/shard_map/ppermute | solution.py:20
  49.7 0.9 copy-start.5
  50.6 13.3 %all-to-all-start = ((f32[32,4,128]{2,1,0:T(4,128)}), f32[32,4,128]{2,1,0:T(4,128)S(1)}, u32[]{:S(2)}, u32[]{:S(2)}) async-start(f32[32,4,128]{2,1,0:T(4,128)} %get-tuple-element.34), calls=%async_computation | async-start | bytes 131072 | tf_op jit(solution)/shard_map/all_to_all | solution.py:559
  56.4 0.7 copy-start.8
  63.8 1.1 %copy-start.6 = (f32[128,1280]{1,0:T(8,128)S(1)}, f32[128,1280]{1,0:T(8,128)}, u32[]{:S(2)}) copy-start(f32[128,1280]{1,0:T(8,128)} %copy-done.5) | copy-start | bytes 1966084
  64.9 1.0 copy-start.9
  66.6 9.8 %collective-permute-start.13 = (bf16[128,1280]{1,0:T(8,128)(2,1)S(1)}, bf16[128,1280]{1,0:T(8,128)(2,1)S(1)}, u32[]{:S(2)}, u32[]{:S(2)}) collective-permute-start(bf16[128,1280]{1,0:T(8,128)(2,1)S(1)} %get-tuple-element.38.refs_0_.grads_ref), channel_id=1, source_target_pairs={{0,16},{16,0},{1,17},{17,1},{2,18},{18,2},{3,19},{19,3},{4,20},{20... | collective-permute-start | bytes 983048 | tf_op jit(solution)/shard_map/ppermute | solution.py:20
  67.3 2.5 %copy-start.1 = (bf16[2048,1280]{1,0:T(8,128)(2,1)S(1)}, bf16[2048,1280]{1,0:T(8,128)(2,1)}, u32[]{:S(2)}) copy-start(bf16[2048,1280]{1,0:T(8,128)(2,1)} %copy-done) | copy-start | bytes 15728644
  70.8 7.6 %collective-permute-start.14 = (bf16[1032,128]{1,0:T(8,128)(2,1)S(1)}, bf16[1032,128]{1,0:T(8,128)(2,1)S(1)}, u32[]{:S(2)}, u32[]{:S(2)}) collective-permute-start(bf16[1032,128]{1,0:T(8,128)(2,1)S(1)} %pieces.5), channel_id=1, source_target_pairs={{0,1},{1,0},{2,3},{3,2},{4,5},{5,4},{6,7},{7,6},{8,9},{9,8},{10,11... | collective-permute-start | bytes 792584 | tf_op jit(solution)/shard_map/ppermute | solution.py:20
  70.8 5.6 %collective-permute-start.18 = (bf16[8,128]{1,0:T(8,128)(2,1)S(1)}, bf16[8,128]{1,0:T(8,128)(2,1)S(1)}, u32[]{:S(2)}, u32[]{:S(2)}) collective-permute-start(bf16[8,128]{1,0:T(8,128)(2,1)S(1)} %get-tuple-element.42.dots_ref), channel_id=1, source_target_pairs={{0,16},{16,0},{1,17},{17,1},{2,18},{18,2},{3,19},{19,3},{4,20},{20... | collective-permute-start | bytes 6152 | tf_op jit(solution)/shard_map/ppermute | solution.py:20
  77.4 9.9 %collective-permute-start.19 = (bf16[1032,128]{1,0:T(8,128)(2,1)S(1)}, bf16[1032,128]{1,0:T(8,128)(2,1)S(1)}, u32[]{:S(2)}, u32[]{:S(2)}) collective-permute-start(bf16[1032,128]{1,0:T(8,128)(2,1)S(1)} %pieces.7), channel_id=1, source_target_pairs={{0,1},{1,0},{2,3},{3,2},{4,5},{5,4},{6,7},{7,6},{8,9},{9,8},{10,11... | collective-permute-start | bytes 792584 | tf_op jit(solution)/shard_map/ppermute | solution.py:20
  79.1 0.6 copy-start.13
  79.7 0.6 copy-start.14
  80.3 8.1 %collective-permute-start.15 = (bf16[264,128]{1,0:T(8,128)(2,1)}, bf16[264,128]{1,0:T(8,128)(2,1)S(1)}, u32[]{:S(2)}, u32[]{:S(2)}) collective-permute-start(bf16[264,128]{1,0:T(8,128)(2,1)} %get-tuple-element.44), channel_id=1, source_target_pairs={{0,2},{1,3},{2,0},{3,1},{4,6},{5,7},{6,4},{7,5},{8,10},{9,11},{10,... | collective-permute-start | bytes 202760 | tf_op jit(solution)/shard_map/ppermute | solution.py:20
  80.8 10.1 %collective-permute-start.16 = (bf16[264,128]{1,0:T(8,128)(2,1)}, bf16[264,128]{1,0:T(8,128)(2,1)S(1)}, u32[]{:S(2)}, u32[]{:S(2)}) collective-permute-start(bf16[264,128]{1,0:T(8,128)(2,1)} %copy-done.14), channel_id=1, source_target_pairs={{0,4},{1,5},{2,6},{3,7},{4,0},{5,1},{6,2},{7,3},{8,12},{9,13},{10,... | collective-permute-start | bytes 202760 | tf_op jit(solution)/shard_map/ppermute | solution.py:20
  81.4 9.6 %collective-permute-start.17 = (bf16[264,128]{1,0:T(8,128)(2,1)}, bf16[264,128]{1,0:T(8,128)(2,1)S(1)}, u32[]{:S(2)}, u32[]{:S(2)}) collective-permute-start(bf16[264,128]{1,0:T(8,128)(2,1)} %copy-done.13), channel_id=1, source_target_pairs={{0,6},{1,7},{2,4},{3,5},{4,2},{5,3},{6,0},{7,1},{8,14},{9,15},{10,... | collective-permute-start | bytes 202760 | tf_op jit(solution)/shard_map/ppermute | solution.py:20
  83.9 2.5 %copy-start.2 = (bf16[2048,1280]{1,0:T(8,128)(2,1)S(1)}, bf16[2048,1280]{1,0:T(8,128)(2,1)}, u32[]{:S(2)}) copy-start(bf16[2048,1280]{1,0:T(8,128)(2,1)} %copy-done) | copy-start | bytes 15728644
  87.4 5.1 %collective-permute-start.20 = (bf16[264,128]{1,0:T(8,128)(2,1)S(1)}, bf16[264,128]{1,0:T(8,128)(2,1)S(1)}, u32[]{:S(2)}, u32[]{:S(2)}) collective-permute-start(bf16[264,128]{1,0:T(8,128)(2,1)S(1)} %get-tuple-element.48), channel_id=1, source_target_pairs={{0,2},{1,3},{2,0},{3,1},{4,6},{5,7},{6,4},{7,5},{8,10},{9,11},{10,... | collective-permute-start | bytes 202760 | tf_op jit(solution)/shard_map/ppermute | solution.py:20
  87.9 4.6 %collective-permute-start.21 = (bf16[264,128]{1,0:T(8,128)(2,1)S(1)}, bf16[264,128]{1,0:T(8,128)(2,1)S(1)}, u32[]{:S(2)}, u32[]{:S(2)}) collective-permute-start(bf16[264,128]{1,0:T(8,128)(2,1)S(1)} %get-tuple-element.49), channel_id=1, source_target_pairs={{0,4},{1,5},{2,6},{3,7},{4,0},{5,1},{6,2},{7,3},{8,12},{9,13},{10,... | collective-permute-start | bytes 202760 | tf_op jit(solution)/shard_map/ppermute | solution.py:20
  88.4 5.5 %collective-permute-start.22 = (bf16[264,128]{1,0:T(8,128)(2,1)S(1)}, bf16[264,128]{1,0:T(8,128)(2,1)S(1)}, u32[]{:S(2)}, u32[]{:S(2)}) collective-permute-start(bf16[264,128]{1,0:T(8,128)(2,1)S(1)} %get-tuple-element.50), channel_id=1, source_target_pairs={{0,6},{1,7},{2,4},{3,5},{4,2},{5,3},{6,0},{7,1},{8,14},{9,15},{10,... | collective-permute-start | bytes 202760 | tf_op jit(solution)/shard_map/ppermute | solution.py:20
  94.1 9.6 %collective-permute-start.23 = (bf16[264,128]{1,0:T(8,128)(2,1)S(1)}, bf16[264,128]{1,0:T(8,128)(2,1)S(1)}, u32[]{:S(2)}, u32[]{:S(2)}) collective-permute-start(bf16[264,128]{1,0:T(8,128)(2,1)S(1)} %get-tuple-element.51), channel_id=1, source_target_pairs={{0,0},{1,1},{2,2},{3,3},{4,4},{5,5},{6,6},{7,7},{8,16},{9,17},{10,... | collective-permute-start | bytes 202760 | tf_op jit(solution)/shard_map/ppermute | solution.py:579
  94.8 8.9 %collective-permute-start.24 = (bf16[264,128]{1,0:T(8,128)(2,1)S(1)}, bf16[264,128]{1,0:T(8,128)(2,1)S(1)}, u32[]{:S(2)}, u32[]{:S(2)}) collective-permute-start(bf16[264,128]{1,0:T(8,128)(2,1)S(1)} %get-tuple-element.52), channel_id=1, source_target_pairs={{0,16},{1,17},{2,18},{3,19},{4,20},{5,21},{6,22},{7,23},{8,0},{9,1... | collective-permute-start | bytes 202760 | tf_op jit(solution)/shard_map/ppermute | solution.py:579
